TPU v7x, 32 devices: a whole 2x2x4 slice. The times are simulated.
32 devices in a mesh: dp: 4 (over z), span: 2 (over core), tensor: 4 (over y, x).
Axes of the slice: x: 2, y: 2, z: 4, core: 2. Of those that a mesh axis runs over, the one named last changes fastest.
Arguments:
- layer_input: bfloat16 [2, 16, 512, 768], P('span', 'dp', 'tensor'), may hold values from -6 to 6
- skip_tokens: bfloat16 [2, 16, 512, 768], P('span', 'dp', 'tensor'), may hold values from -6 to 6
- backbone_cotangent: bfloat16 [2, 16, 512, 768], P('span', 'dp', 'tensor'), may hold values from -6 to 6
- head_cotangent: bfloat16 [2, 16, 512, 768], P('span', 'dp', 'tensor'), may hold values from -6 to 6
- segment_lengths: int32 [2, 16, 4], P('span', 'dp'), may hold values from 1 to 174, 464 in all within a row
- pair_index: int32 [64], replicated, may hold values from 0 to 63, each once
- w_heads: bfloat16 [2, 3, 768, 768], P(None, None, None, 'tensor'), may hold values from -0.21875 to 0.21875
- heads_bias: bfloat16 [2, 2, 768], P(None, None, 'tensor'), may hold values from -1.75 to 1.75
- w_project: bfloat16 [2, 768, 768], P(None, 'tensor'), may hold values from -0.875 to 0.875
- project_bias: bfloat16 [2, 768], replicated, may hold values from -1.75 to 1.75
- norm_gain: bfloat16 [2, 2, 768], replicated, may hold values from 0.5 to 1.5
- norm_shift: bfloat16 [2, 2, 768], replicated, may hold values from -1.75 to 1.75
- w_expand: bfloat16 [2, 768, 3072], P(None, None, 'tensor'), may hold values from -0.21875 to 0.21875
- expand_bias: bfloat16 [2, 3072], P(None, 'tensor'), may hold values from -3 to 3
- w_shrink: bfloat16 [2, 3072, 768], P(None, 'tensor'), may hold values from -0.109375 to 0.109375
- shrink_bias: bfloat16 [2, 768], replicated, may hold values from -1.75 to 1.75
Outputs:
- backbone_out: bfloat16 [2, 16, 512, 768], P('span', 'dp', 'tensor')
- head_out: bfloat16 [2, 16, 512, 768], P('span', 'dp', 'tensor')
- span_loss: float32 [], replicated
- grad_input: bfloat16 [2, 16, 512, 768], P('span', 'dp', 'tensor')
- grad_skip: bfloat16 [2, 16, 512, 768], P('span', 'dp', 'tensor')
- grad_heads: float32 [2, 3, 768, 768], P(None, None, None, 'tensor')
- grad_heads_bias: float32 [2, 2, 768], P(None, None, 'tensor')
- grad_project: float32 [2, 768, 768], P(None, 'tensor')
- grad_project_bias: float32 [2, 768], replicated
- grad_gain: float32 [2, 2, 768], replicated
- grad_shift: float32 [2, 2, 768], replicated
- grad_expand: float32 [2, 768, 3072], P(None, None, 'tensor')
- grad_expand_bias: float32 [2, 3072], P(None, 'tensor')
- grad_shrink: float32 [2, 3072, 768], P(None, 'tensor')
- grad_shrink_bias: float32 [2, 768], replicated
Inputs may be any that keep to these rules, and one draw needn't show every extreme that they name: `segment_lengths`: each row holds 4 spans whose lengths add up to 464, the longest being 174; the rest of the row is padding. `pair_index`: each value occurs exactly once.
All inputs are finite; a program needn't handle non-finite values.
Results may differ from a plain program's by a relative error of at most 0.015.
The roundings to bfloat16 on the way count: a program that leaves them out, or rounds other values in their place, can miss the bound.
Values may be sent and summed in bfloat16 or wider, within the bound.
A program may use at most 192 MiB of HBM per device.

v0:
```python
import math

import jax
import jax.numpy as jnp
from jax import lax
from jax.sharding import PartitionSpec as P

HEAD_DIM = 64


EPSILON = 1e-12
LOSS_WEIGHT = 8.0
HIGHEST = lax.Precision.HIGHEST
MASKED = -1e30


def normalize(values, norm_scale, norm_offset):
    centred = values - jnp.mean(values, axis=-1, keepdims=True)
    spread = jnp.mean(centred * centred, axis=-1, keepdims=True)
    return centred * lax.rsqrt(spread + EPSILON) * norm_scale + norm_offset


def activate(values):
    return jax.nn.gelu(values, approximate=False)


def spread_rows(values):
    return lax.all_gather(values, "tensor", axis=1, tiled=True)


def collect_rows(values):
    return lax.psum_scatter(values, "tensor", scatter_dimension=1, tiled=True)


def split_heads(values):
    return values.reshape(values.shape[0], values.shape[1] // HEAD_DIM, HEAD_DIM)


def scores_of(queries, key_rows, segment):
    scores = (
        jnp.einsum("qhd,khd->hqk", queries, key_rows, preferred_element_type=jnp.float32) * 0.125
    )
    same_span = segment[:, None] == segment[None, :]
    return jnp.where(same_span[None], scores, MASKED)


def attend_forward(pieces):
    queries, key_rows, value_rows, segment = pieces
    queries = split_heads(queries)
    key_rows = split_heads(key_rows)
    value_rows = split_heads(value_rows)
    scores = scores_of(queries, key_rows, segment)
    maximum = jnp.max(scores, axis=-1, keepdims=True)
    raised = jnp.exp(scores - maximum)
    row_total = jnp.sum(raised, axis=-1, keepdims=True)
    attention = (raised / row_total).astype(jnp.bfloat16)
    mixture = jnp.einsum("hqk,khd->qhd", attention, value_rows, preferred_element_type=jnp.float32)
    mixture = mixture.reshape(mixture.shape[0], mixture.shape[1] * HEAD_DIM).astype(jnp.bfloat16)
    return (mixture, (maximum + jnp.log(row_total))[..., 0])


def attend_backward(pieces):
    queries, key_rows, value_rows, segment, upward, log_total = pieces
    local_width = queries.shape[1]
    queries = split_heads(queries)
    key_rows = split_heads(key_rows)
    value_rows = split_heads(value_rows)
    upward = split_heads(upward)
    scores = scores_of(queries, key_rows, segment)
    attention = jnp.exp(scores - log_total[..., None])
    grad_weights = jnp.einsum(
        "qhd,khd->hqk", upward, value_rows, preferred_element_type=jnp.float32
    )
    grad_scores = (
        attention * (grad_weights - jnp.sum(attention * grad_weights, axis=-1, keepdims=True))
    ).astype(jnp.bfloat16)
    grad_query = (
        jnp.einsum("hqk,khd->qhd", grad_scores, key_rows, preferred_element_type=jnp.float32)
        * 0.125
    )
    grad_key = (
        jnp.einsum("hqk,qhd->khd", grad_scores, queries, preferred_element_type=jnp.float32) * 0.125
    )
    grad_value = jnp.einsum(
        "hqk,qhd->khd", attention.astype(jnp.bfloat16), upward, preferred_element_type=jnp.float32
    )
    grad_query = grad_query.reshape(grad_query.shape[0], local_width).astype(jnp.bfloat16)
    grad_key = grad_key.reshape(grad_key.shape[0], local_width).astype(jnp.bfloat16)
    grad_value = grad_value.reshape(grad_value.shape[0], local_width).astype(jnp.bfloat16)
    return (grad_query, grad_key, grad_value)


def layer_forward(share, segment, weights):
    (
        w_heads,
        heads_bias,
        w_project,
        project_bias,
        norm_gain,
        norm_shift,
        w_expand,
        expand_bias,
        w_shrink,
        shrink_bias,
    ) = weights
    rows_in = spread_rows(share.astype(jnp.bfloat16))
    projected = jnp.einsum("std,cde->cste", rows_in, w_heads, preferred_element_type=jnp.float32)
    queries = (projected[0] + heads_bias[0]).astype(jnp.bfloat16)
    key_rows = projected[1].astype(jnp.bfloat16)
    value_rows = (projected[2] + heads_bias[1]).astype(jnp.bfloat16)
    mixture, log_total = lax.map(attend_forward, (queries, key_rows, value_rows, segment))
    first_sum = (
        share
        + collect_rows(
            jnp.einsum("ste,ed->std", mixture, w_project, preferred_element_type=jnp.float32)
        )
        + project_bias
    )
    first_norm = normalize(first_sum, norm_gain[0], norm_shift[0])
    rows_mid = spread_rows(first_norm.astype(jnp.bfloat16))
    expanded = (
        jnp.einsum("std,df->stf", rows_mid, w_expand, preferred_element_type=jnp.float32)
        + expand_bias
    )
    activated = activate(expanded).astype(jnp.bfloat16)
    second_sum = (
        first_norm
        + collect_rows(
            jnp.einsum("stf,fd->std", activated, w_shrink, preferred_element_type=jnp.float32)
        )
        + shrink_bias
    )
    stored = (
        rows_in,
        queries,
        key_rows,
        value_rows,
        mixture,
        log_total,
        first_sum,
        rows_mid,
        expanded,
        activated,
        second_sum,
    )
    return (normalize(second_sum, norm_gain[1], norm_shift[1]), stored)


def layer_backward(upward, segment, weights, stored):
    (
        w_heads,
        heads_bias,
        w_project,
        project_bias,
        norm_gain,
        norm_shift,
        w_expand,
        expand_bias,
        w_shrink,
        shrink_bias,
    ) = weights
    (
        rows_in,
        queries,
        key_rows,
        value_rows,
        mixture,
        log_total,
        first_sum,
        rows_mid,
        expanded,
        activated,
        second_sum,
    ) = stored
    ignored, pull_second = jax.vjp(
        normalize, second_sum, norm_gain[1].astype(jnp.float32), norm_shift[1].astype(jnp.float32)
    )
    grad_second, gain_second, shift_second = pull_second(upward)
    rounded = spread_rows(grad_second.astype(jnp.bfloat16))
    grad_shrink = jnp.einsum("stf,std->fd", activated, rounded, preferred_element_type=jnp.float32)
    grad_act = jnp.einsum("std,fd->stf", rounded, w_shrink, preferred_element_type=jnp.float32)
    ignored, pull_act = jax.vjp(activate, expanded)
    grad_hidden = pull_act(grad_act)[0]
    hidden_low = grad_hidden.astype(jnp.bfloat16)
    grad_expand = jnp.einsum(
        "std,stf->df", rows_mid, hidden_low, preferred_element_type=jnp.float32
    )
    grad_first = grad_second + collect_rows(
        jnp.einsum("stf,df->std", hidden_low, w_expand, preferred_element_type=jnp.float32)
    )
    ignored, pull_first = jax.vjp(
        normalize, first_sum, norm_gain[0].astype(jnp.float32), norm_shift[0].astype(jnp.float32)
    )
    grad_attend, gain_first, shift_first = pull_first(grad_first)
    rounded = spread_rows(grad_attend.astype(jnp.bfloat16))
    grad_project = jnp.einsum("ste,std->ed", mixture, rounded, preferred_element_type=jnp.float32)
    grad_mixture = jnp.einsum(
        "std,ed->ste", rounded, w_project, preferred_element_type=jnp.float32
    ).astype(jnp.bfloat16)
    grad_query, grad_key, grad_value = lax.map(
        attend_backward, (queries, key_rows, value_rows, segment, grad_mixture, log_total)
    )
    grad_heads = jnp.stack(
        [
            jnp.einsum("std,ste->de", rows_in, grad_query, preferred_element_type=jnp.float32),
            jnp.einsum("std,ste->de", rows_in, grad_key, preferred_element_type=jnp.float32),
            jnp.einsum("std,ste->de", rows_in, grad_value, preferred_element_type=jnp.float32),
        ]
    )
    grad_heads_bias = jnp.stack(
        [
            jnp.sum(grad_query.astype(jnp.float32), axis=(0, 1)),
            jnp.sum(grad_value.astype(jnp.float32), axis=(0, 1)),
        ]
    )
    back_terms = jnp.einsum(
        "ste,de->std", grad_query, w_heads[0], preferred_element_type=jnp.float32
    )
    back_terms = back_terms + jnp.einsum(
        "ste,de->std", grad_key, w_heads[1], preferred_element_type=jnp.float32
    )
    back_terms = back_terms + jnp.einsum(
        "ste,de->std", grad_value, w_heads[2], preferred_element_type=jnp.float32
    )
    grad_layer_in = grad_attend + collect_rows(back_terms)
    matrices = (
        grad_heads,
        grad_heads_bias,
        grad_project,
        grad_expand,
        jnp.sum(grad_hidden, axis=(0, 1)),
        grad_shrink,
    )
    vectors = (
        jnp.sum(grad_attend, axis=(0, 1)),
        jnp.stack([gain_first, gain_second]),
        jnp.stack([shift_first, shift_second]),
        jnp.sum(grad_second, axis=(0, 1)),
    )
    return (grad_layer_in, matrices, vectors)


def shards(
    layer_input,
    skip_tokens,
    backbone_cotangent,
    head_cotangent,
    segment_lengths,
    pair_index,
    w_heads,
    heads_bias,
    w_project,
    project_bias,
    norm_gain,
    norm_shift,
    w_expand,
    expand_bias,
    w_shrink,
    shrink_bias,
):
    stacked = (
        w_heads,
        heads_bias,
        w_project,
        project_bias,
        norm_gain,
        norm_shift,
        w_expand,
        expand_bias,
        w_shrink,
        shrink_bias,
    )
    backbone_weights = tuple((member[0] for member in stacked))
    head_weights = tuple((member[1] for member in stacked))
    lengths = segment_lengths[0]
    seq_count = lengths.shape[0]
    span_count = lengths.shape[1]
    share_rows = layer_input.shape[2]
    row_tokens = share_rows * lax.axis_size("tensor")
    starts = jnp.cumsum(lengths, axis=-1) - lengths
    row_length = jnp.sum(lengths, axis=-1)
    places = jnp.arange(row_tokens, dtype=jnp.int32)
    counted = jnp.sum((places[None, :, None] >= starts[:, None, :]).astype(jnp.int32), axis=-1) - 1
    segment = jnp.where(places[None, :] < row_length[:, None], counted, span_count)
    local_places = lax.axis_index("tensor") * share_rows + jnp.arange(share_rows, dtype=jnp.int32)
    valid_rows = (local_places[None, :] < row_length[:, None]).astype(jnp.float32)[..., None]
    picker = (starts[:, :, None] == local_places[None, None, :]).astype(jnp.float32)
    first_mark = jnp.sum(picker, axis=1)[..., None] > 0
    backbone, backbone_stored = layer_forward(
        layer_input[0].astype(jnp.float32), segment, backbone_weights
    )
    chosen = jnp.einsum("sgp,spd->sgd", picker, backbone, precision=HIGHEST)
    slot_count = seq_count * span_count
    feature_count = chosen.shape[2]
    gathered = lax.all_gather(
        chosen.reshape(slot_count, feature_count).astype(jnp.bfloat16),
        ("dp", "span", "tensor"),
        axis=0,
        tiled=True,
    )
    dp_count = lax.axis_size("dp")
    pair_count = lax.axis_size("span")
    tensor_count = lax.axis_size("tensor")
    anchor_rows = jnp.sum(
        gathered.astype(jnp.float32).reshape(
            dp_count, pair_count, tensor_count, slot_count, feature_count
        ),
        axis=2,
    )
    anchor_rows = jnp.transpose(anchor_rows, (1, 0, 2, 3)).reshape(
        pair_count, dp_count * slot_count, feature_count
    )
    head_input = jnp.where(first_mark, backbone, skip_tokens[0].astype(jnp.float32))
    head_rows, head_stored = layer_forward(head_input, segment, head_weights)
    vector_count = dp_count * slot_count
    side_index = lax.axis_index("span")
    block_start = lax.axis_index("dp") * slot_count
    columns = jnp.arange(vector_count, dtype=jnp.int32)
    root_width = math.sqrt(feature_count)
    logits = jnp.dot(anchor_rows[0], anchor_rows[1].T, precision=HIGHEST) / root_width
    target = (pair_index[:, None] == columns[None, :]).astype(jnp.float32)
    lse_rows = jax.nn.logsumexp(logits, axis=1)
    lse_columns = jax.nn.logsumexp(logits, axis=0)
    grad_logits = LOSS_WEIGHT * (
        jnp.exp(logits - lse_rows[:, None]) + jnp.exp(logits - lse_columns[None, :]) - 2.0 * target
    )
    grad_zero = jnp.dot(grad_logits, anchor_rows[1], precision=HIGHEST) / root_width
    grad_one = jnp.dot(grad_logits.T, anchor_rows[0], precision=HIGHEST) / root_width
    both_sides = jnp.stack([grad_zero, grad_one])
    grad_vectors = lax.dynamic_slice(
        lax.dynamic_index_in_dim(both_sides, side_index, 0, keepdims=False),
        (block_start, 0),
        (slot_count, feature_count),
    )
    span_loss = (jnp.sum(lse_rows) + jnp.sum(lse_columns) - 2.0 * jnp.sum(target * logits)) / (
        2 * vector_count
    )
    head_seed = head_cotangent[0].astype(jnp.float32) * valid_rows
    grad_head_in, head_matrices, head_vectors = layer_backward(
        head_seed, segment, head_weights, head_stored
    )
    grad_skip = jnp.where(first_mark, 0.0, grad_head_in)
    from_span = jnp.einsum(
        "sgp,sgd->spd",
        picker,
        grad_vectors.reshape(seq_count, span_count, feature_count),
        precision=HIGHEST,
    )
    backbone_seed = (
        backbone_cotangent[0].astype(jnp.float32) * valid_rows
        + jnp.where(first_mark, grad_head_in, 0.0)
        + from_span
    )
    grad_input, backbone_matrices, backbone_vectors = layer_backward(
        backbone_seed, segment, backbone_weights, backbone_stored
    )
    summed = lax.psum(
        (
            backbone_matrices[0],
            backbone_matrices[1],
            backbone_matrices[2],
            backbone_matrices[3],
            backbone_matrices[4],
            backbone_matrices[5],
            head_matrices[0],
            head_matrices[1],
            head_matrices[2],
            head_matrices[3],
            head_matrices[4],
            head_matrices[5],
        ),
        ("dp", "span"),
    )
    backbone_matrices = summed[:6]
    head_matrices = summed[6:]
    summed_small = lax.psum(
        (
            backbone_vectors[0],
            backbone_vectors[1],
            backbone_vectors[2],
            backbone_vectors[3],
            head_vectors[0],
            head_vectors[1],
            head_vectors[2],
            head_vectors[3],
        ),
        ("dp", "span", "tensor"),
    )
    backbone_vectors = summed_small[:4]
    head_vectors = summed_small[4:]
    return (
        (backbone * valid_rows).astype(jnp.bfloat16)[None],
        (head_rows * valid_rows).astype(jnp.bfloat16)[None],
        span_loss,
        grad_input.astype(jnp.bfloat16)[None],
        grad_skip.astype(jnp.bfloat16)[None],
        jnp.stack([backbone_matrices[0], head_matrices[0]]),
        jnp.stack([backbone_matrices[1], head_matrices[1]]),
        jnp.stack([backbone_matrices[2], head_matrices[2]]),
        jnp.stack([backbone_vectors[0], head_vectors[0]]),
        jnp.stack([backbone_vectors[1], head_vectors[1]]),
        jnp.stack([backbone_vectors[2], head_vectors[2]]),
        jnp.stack([backbone_matrices[3], head_matrices[3]]),
        jnp.stack([backbone_matrices[4], head_matrices[4]]),
        jnp.stack([backbone_matrices[5], head_matrices[5]]),
        jnp.stack([backbone_vectors[3], head_vectors[3]]),
    )


def solution(mesh):
    in_specs = (
        P("span", "dp", "tensor", None),
        P("span", "dp", "tensor", None),
        P("span", "dp", "tensor", None),
        P("span", "dp", "tensor", None),
        P("span", "dp", None),
        P(),
        P(None, None, None, "tensor"),
        P(None, None, "tensor"),
        P(None, "tensor", None),
        P(),
        P(),
        P(),
        P(None, None, "tensor"),
        P(None, "tensor"),
        P(None, "tensor", None),
        P(),
    )
    out_specs = (
        P("span", "dp", "tensor", None),
        P("span", "dp", "tensor", None),
        P(),
        P("span", "dp", "tensor", None),
        P("span", "dp", "tensor", None),
        P(None, None, None, "tensor"),
        P(None, None, "tensor"),
        P(None, "tensor", None),
        P(),
        P(),
        P(),
        P(None, None, "tensor"),
        P(None, "tensor"),
        P(None, "tensor", None),
        P(),
    )
    return jax.shard_map(shards, mesh=mesh, in_specs=in_specs, out_specs=out_specs, check_vma=False)
```

profile of v0, /device:TPU:0, one launch (start us, length us, event | category | flops | bytes accessed | tf_op | source)
XLA Modules:
  0.0 1523.5 jit_solution(11413857618912558488)
XLA Ops:
  11.2 45.2 %all-gather.24.cloned.1.call-done = bf16[1,4,512,768]{3,2,1,0:T(8,128)(2,1)} async-done(((bf16[1,4,128,768]{3,2,1,0:T(8,128)(2,1)}), bf16[1,4,512,768]{3,2,1,0:T(8,128)(2,1)}) %all-gather.24.cloned.1.call-update) | async-done | bytes 3145744 | tf_op jit(solution)/shard_map/all_gather | solution.py:28
  56.4 4.2 fusion.48
  61.1 11.7 while.52
  72.8 4.9 fusion.140
  78.6 69.4 %reduce-scatter.9.cloned.1.call-done = f32[4,128,768]{2,1,0:T(8,128)} async-done(((f32[4,512,768]{2,1,0:T(8,128)}), f32[4,128,768]{2,1,0:T(8,128)}) %reduce-scatter.9.cloned.1.call-update) | async-done | bytes 1572880 | tf_op jit(solution)/shard_map/reduce_scatter | solution.py:32
  151.9 43.4 %all-gather.10.cloned.1.call-done = bf16[4,512,768]{2,1,0:T(8,128)(2,1)} async-done(((bf16[4,128,768]{2,1,0:T(8,128)(2,1)}), bf16[4,512,768]{2,1,0:T(8,128)(2,1)}) %all-gather.10.cloned.1.call-update) | async-done | bytes 3145744 | tf_op jit(solution)/shard_map/all_gather | solution.py:28
  195.3 6.4 fusion.80
  201.8 15.4 %multiply_convert_fusion.3 = (bf16[4,512,768]{2,1,0:T(8,128)(2,1)S(1)}, f32[4,512,768]{2,1,0:T(8,128)}) fusion(f32[4,512,768]{2,1,0:T(8,128)S(1)} %get-tuple-element.398, f32[768]{0:T(1024)S(1)} %get-tuple-element.243, u8[512,768]{1,0:T(8,128)(4,1)S(1)} %get-tuple-element.212, u8[512,768]{1,0:T(8,128)(4,1)S(1)} %get-tuple-element.211), kind=kLoop, calls=%fused_computation.102 | loop fusion | flops 111673344 | bytes 16518144 | tf_op jit(solution)/shard_map/convert_element_type | solution.py:125
  218.8 4.5 fusion.100
  224.1 69.4 %reduce-scatter.11.cloned.1.call-done = f32[4,128,768]{2,1,0:T(8,128)} async-done(((f32[4,512,768]{2,1,0:T(8,128)}), f32[4,128,768]{2,1,0:T(8,128)}) %reduce-scatter.11.cloned.1.call-update) | async-done | bytes 1572880 | tf_op jit(solution)/shard_map/reduce_scatter | solution.py:32
  298.6 43.8 %all-gather.12.cloned.1.call-done = bf16[4,512,768]{2,1,0:T(8,128)(2,1)} async-done(((bf16[4,128,768]{2,1,0:T(8,128)(2,1)}), bf16[4,512,768]{2,1,0:T(8,128)(2,1)}) %all-gather.12.cloned.1.call-update) | async-done | bytes 3145744 | tf_op jit(solution)/shard_map/all_gather | solution.py:28
  342.4 3.9 fusion.51
  347.9 19.1 %while.53 = (s32[]{:T(128)}, bf16[4,512,192]{1,2,0:T(8,128)(2,1)S(1)}, f32[4,3,512]{2,1,0:T(4,128)S(1)}, bf16[4,512,192]{1,2,0:T(8,128)(2,1)}, s32[4,512]{1,0:T(...) while((s32[]{:T(128)}, bf16[4,512,192]{1,2,0:T(8,128)(2,1)S(1)}, ...), condition=%wide.region_17.18_spmd, body=%wide.region_14.17_spmd.sunk | while | flops 211122688 | bytes 12906601 | solution.py:111
  367.0 4.8 fusion.137
  372.0 70.0 %reduce-scatter.13.cloned.1.call-done = f32[4,128,768]{2,1,0:T(8,128)} async-done(((f32[4,512,768]{2,1,0:T(8,128)}), f32[4,128,768]{2,1,0:T(8,128)}) %reduce-scatter.13.cloned.1.call-update) | async-done | bytes 1572880 | tf_op jit(solution)/shard_map/reduce_scatter | solution.py:32
  447.0 43.7 %all-gather.14.cloned.1.call-done = bf16[4,512,768]{2,1,0:T(8,128)(2,1)} async-done(((bf16[4,128,768]{2,1,0:T(8,128)(2,1)}), bf16[4,512,768]{2,1,0:T(8,128)(2,1)}) %all-gather.14.cloned.1.call-update) | async-done | bytes 3145744 | tf_op jit(solution)/shard_map/all_gather | solution.py:28
  490.7 6.4 fusion.81
  497.2 15.4 %multiply_convert_fusion.2 = (bf16[4,512,768]{2,1,0:T(8,128)(2,1)S(1)}, f32[4,512,768]{2,1,0:T(8,128)}) fusion(f32[4,512,768]{2,1,0:T(8,128)S(1)} %get-tuple-element.399, f32[768]{0:T(1024)S(1)} %get-tuple-element.242, u8[512,768]{1,0:T(8,128)(4,1)S(1)} %get-tuple-element.210, u8[512,768]{1,0:T(8,128)(4,1)S(1)} %get-tuple-element.209), kind=kLoop, calls=%fused_computation.89 | loop fusion | flops 111673344 | bytes 16518144 | tf_op jit(solution)/shard_map/convert_element_type | solution.py:125
  514.3 4.5 fusion.94
  518.8 70.1 %reduce-scatter.15.cloned.1.call-done = f32[4,128,768]{2,1,0:T(8,128)} async-done(((f32[4,512,768]{2,1,0:T(8,128)}), f32[4,128,768]{2,1,0:T(8,128)}) %reduce-scatter.15.cloned.1.call-update) | async-done | bytes 1572880 | tf_op jit(solution)/shard_map/reduce_scatter | solution.py:32
  594.3 43.7 %all-gather.16.cloned.1.call-done = bf16[4,512,768]{2,1,0:T(8,128)(2,1)} async-done(((bf16[4,128,768]{2,1,0:T(8,128)(2,1)}), bf16[4,512,768]{2,1,0:T(8,128)(2,1)}) %all-gather.16.cloned.1.call-update) | async-done | bytes 3145744 | tf_op jit(solution)/shard_map/all_gather | solution.py:28
  638.0 11.2 fusion.179
  650.9 4.5 fusion.76
  655.5 70.1 %reduce-scatter.17.cloned.1.call-done = f32[4,128,768]{2,1,0:T(8,128)} async-done(((f32[4,512,768]{2,1,0:T(8,128)}), f32[4,128,768]{2,1,0:T(8,128)}) %reduce-scatter.17.cloned.1.call-update) | async-done | bytes 1572880 | tf_op jit(solution)/shard_map/reduce_scatter | solution.py:32
  725.6 4.6 add_reduce_fusion.3
  734.3 43.5 %all-gather.18.cloned.1.call-done = bf16[4,512,768]{2,1,0:T(8,128)(2,1)} async-done(((bf16[4,128,768]{2,1,0:T(8,128)(2,1)}), bf16[4,512,768]{2,1,0:T(8,128)(2,1)}) %all-gather.18.cloned.1.call-update) | async-done | bytes 3145744 | tf_op jit(solution)/shard_map/all_gather | solution.py:28
  777.7 3.9 convolution_convert_fusion.1
  782.7 36.0 %while.54 = (s32[]{:T(128)}, bf16[4,512,192]{1,2,0:T(8,128)(2,1)S(1)}, bf16[4,512,192]{1,2,0:T(8,128)(2,1)}, bf16[4,512,192]{1,2,0:T(8,128)(2,1)S(1)}, bf16[4,51...) while((s32[]{:T(128)}, ...), condition=%wide.region_39.40_spmd, body=%wide.region_37.39_spmd.sunk | while | flops 511146496 | bytes 28873352 | solution.py:200
  823.6 4.7 add_add_fusion.1
  829.3 74.0 %all_gather.31 = bf16[512,768]{1,0:T(8,128)(2,1)S(1)} all-gather(bf16[16,768]{1,0:T(8,128)(2,1)S(1)} %convert_element_type.392), channel_id=1, replica_groups=mesh['dp'=4,'span'=2,'tensor'=4] {'dp','span','tensor'}, dimensions={0}, use_global_device_ids=true | all-gather | bytes 811008 | tf_op jit(solution)/shard_map/all_gather | solution.py:295
  906.2 4.8 reduce-scatter.19.cloned.1.call-done
  916.5 43.8 %all-gather.20.cloned.1.call-done = bf16[4,512,768]{2,1,0:T(8,128)(2,1)} async-done(((bf16[4,128,768]{2,1,0:T(8,128)(2,1)}), bf16[4,512,768]{2,1,0:T(8,128)(2,1)}) %all-gather.20.cloned.1.call-update) | async-done | bytes 3145744 | tf_op jit(solution)/shard_map/all_gather | solution.py:28
  960.3 10.6 fusion.180
  972.6 4.5 fusion.73
  977.2 70.1 %reduce-scatter.21.cloned.1.call-done = f32[4,128,768]{2,1,0:T(8,128)} async-done(((f32[4,512,768]{2,1,0:T(8,128)}), f32[4,128,768]{2,1,0:T(8,128)}) %reduce-scatter.21.cloned.1.call-update) | async-done | bytes 1572880 | tf_op jit(solution)/shard_map/reduce_scatter | solution.py:32
  1053.0 6.1 convolution_bitcast_fusion
  1059.1 4.2 convolution_bitcast_fusion.2
  1071.5 4.2 convolution_bitcast_fusion.1
  1075.7 4.5 convolution_bitcast_fusion.3
  1080.1 16.4 %all-gather.22.cloned.1.call-done = bf16[4,512,768]{2,1,0:T(8,128)(2,1)} async-done(((bf16[4,128,768]{2,1,0:T(8,128)(2,1)}), bf16[4,512,768]{2,1,0:T(8,128)(2,1)}) %all-gather.22.cloned.1.call-update) | async-done | bytes 3145744 | tf_op jit(solution)/shard_map/all_gather | solution.py:28
  1096.5 4.0 convolution_convert_fusion
  1103.3 41.8 %while.55 = (s32[]{:T(128)}, bf16[4,512,192]{1,2,0:T(8,128)(2,1)}, bf16[4,512,192]{1,2,0:T(8,128)(2,1)}, bf16[4,512,192]{1,2,0:T(8,128)(2,1)}, bf16[4,512,192]{1...) while((s32[]{:T(128)}, bf16[4,512,192]{1,2,0:T(8,128)(2,1)}, ...), condition=%wide.region_48.49_spmd, body=%wide.region_46.48_spmd.sunk | while | flops 511146496 | bytes 28873860 | solution.py:200
  1158.9 4.8 add_add_fusion
  1170.2 41.6 %all-reduce = (f32[1,768]{1,0:T(1,128)S(1)}, f32[1,768]{1,0:T(1,128)S(1)}, f32[1,2,768]{2,1,0:T(2,128)S(1)}, f32[1,2,768]{2,1,0:T(2,128)S(1)}, f32[1,2,768]{2,1,...) all-reduce(f32[1,768]{1,0:T(1,128)S(1)} %stack.204, ...), channel_id=1, replica_groups=mesh['dp'=4,'span'=2,'tensor'=4] {'dp','span','tensor'}, use_global_device_ids=true, to_apply=%region_63.64 | all-reduce | flops 9216 | bytes 73728 | tf_op jit(solution)/shard_map/psum | solution.py:376
  1215.8 29.2 %all-reduce.1 = (f32[1,2,192]{2,1,0:T(2,128)S(1)}, f32[1,2,192]{2,1,0:T(2,128)S(1)}, f32[1,768]{1,0:T(1,128)S(1)}, f32[1,768]{1,0:T(1,128)S(1)}) all-reduce(f32[1,2,192]{2,1,0:T(2,128)S(1)} %maximum_bitcast_fusion.7, f32[1,2,192]{2,1,0:T(2,128)S(1)} %maximum_bitcast_fusion.6, ...), channel_id=1, replica_groups=mesh['dp'=4,'span'=2,'tensor'=4] {'dp','span'}, use_global_device_ids=true, to_apply=%region_57.58 | all-reduce | flops 2304 | bytes 18432 | tf_op jit(solution)/shard_map/psum | solution.py:357
  1246.2 193.5 %all-reduce.5.cloned.1.call-done = (f32[1,3,768,192]{2,3,1,0:T(8,128)}, f32[1,3,768,192]{2,3,1,0:T(8,128)}, f32[1,192,768]{2,1,0:T(8,128)}, f32[1,192,768]{2,1,0...) async-done(((f32[1,3,768,192]{2,3,1,0:T(8,128)}, f32[1,3,768,192]{2,3,1,0:T(8,128)}, ...) | async-done | bytes 14155792 | tf_op jit(solution)/shard_map/psum | solution.py:357
  1442.2 3.7 pad_maximum_fusion.2
  1452.9 59.9 %reduce-scatter.23.cloned.1.call-done = f32[4,128,768]{2,1,0:T(8,128)} async-done(((f32[4,512,768]{2,1,0:T(8,128)}), f32[4,128,768]{2,1,0:T(8,128)}) %reduce-scatter.23.cloned.1.call-update) | async-done | bytes 1572880 | tf_op jit(solution)/shard_map/reduce_scatter | solution.py:32
  (517 shorter events, 211.9 us)
Async XLA Ops:
  7.2 49.3 %all-gather.24.cloned.1.call-start = ((), (), s32[]{:S(2)}) async-start(), calls=%async_computation.23 | async-start | bytes 3932160 | tf_op jit(solution)/shard_map/all_gather | solution.py:28
  7.9 140.1 %reduce-scatter.9.cloned.1.call-start = ((), (), s32[]{:S(2)}) async-start(), calls=%async_computation.8 | async-start | bytes 7864320 | tf_op jit(solution)/shard_map/reduce_scatter | solution.py:32
  72.8 4.9 copy-start.22
  72.8 4.9 copy-start.24
  77.8 70.2 %copy-start.36 = (bf16[1,4,128,768]{3,2,1,0:T(8,128)(2,1)S(1)}, bf16[1,4,128,768]{3,2,1,0:T(8,128)(2,1)}, u32[]{:S(2)}) copy-start(bf16[1,4,128,768]{3,2,1,0:T(8,128)(2,1)} %param.24) | copy-start | bytes 2359300
  77.8 117.5 %all-gather.10.cloned.1.call-start = ((), (), s32[]{:S(2)}) async-start(), calls=%async_computation.9 | async-start | bytes 3932160 | tf_op jit(solution)/shard_map/all_gather | solution.py:28
  78.5 215.0 %copy-start.47 = (f32[768]{0:T(1024)}, f32[768]{0:T(1024)S(1)}, u32[]{:S(2)}) copy-start(f32[768]{0:T(1024)S(1)} %get-tuple-element.234) | copy-start | bytes 9220
  149.7 143.8 %copy-start.2 = (f32[4,128,768]{2,1,0:T(8,128)}, f32[4,128,768]{2,1,0:T(8,128)S(1)}, u32[]{:S(2)}) copy-start(f32[4,128,768]{2,1,0:T(8,128)S(1)} %get-tuple-element.357) | copy-start | bytes 4718596
  149.8 143.8 %copy-start.49 = (f32[4,128]{1,0:T(4,128)}, f32[4,128]{1,0:T(4,128)S(1)}, u32[]{:S(2)}) copy-start(f32[4,128]{1,0:T(4,128)S(1)} %broadcast_multiply_fusion.3) | copy-start | bytes 6148
  150.1 51.7 %copy-start.55 = (f32[4,128]{1,0:T(4,128)}, f32[4,128]{1,0:T(4,128)S(1)}, u32[]{:S(2)}) copy-start(f32[4,128]{1,0:T(4,128)S(1)} %multiply_reduce_fusion.11) | copy-start | bytes 6148
  150.1 143.4 %copy-start.51 = (f32[4,128]{1,0:T(4,128)}, f32[4,128]{1,0:T(4,128)S(1)}, u32[]{:S(2)}) copy-start(f32[4,128]{1,0:T(4,128)S(1)} %fusion.160) | copy-start | bytes 6148
  151.3 142.2 %reduce-scatter.11.cloned.1.call-start = ((), (), s32[]{:S(2)}) async-start(), calls=%async_computation.10 | async-start | bytes 7864320 | tf_op jit(solution)/shard_map/reduce_scatter | solution.py:32
  151.9 49.8 %copy-start.59 = (f32[768]{0:T(1024)}, f32[768]{0:T(1024)S(1)}, u32[]{:S(2)}) copy-start(f32[768]{0:T(1024)S(1)} %get-tuple-element.243) | copy-start | bytes 9220
  201.8 15.4 %copy-start.30 = (f32[4,512,768]{2,1,0:T(8,128)}, f32[4,512,768]{2,1,0:T(8,128)S(1)}, u32[]{:S(2)}) copy-start(f32[4,512,768]{2,1,0:T(8,128)S(1)} %get-tuple-element.398) | copy-start | bytes 18874372
  201.8 17.0 %copy-start.75 = (bf16[2,768,768]{2,1,0:T(8,128)(2,1)S(1)}, bf16[2,768,768]{2,1,0:T(8,128)(2,1)}, u32[]{:S(2)}) copy-start(bf16[2,768,768]{2,1,0:T(8,128)(2,1)} %param.38) | copy-start | bytes 7077892
  223.4 119.0 %all-gather.12.cloned.1.call-start = ((), (), s32[]{:S(2)}) async-start(), calls=%async_computation.11 | async-start | bytes 3932160 | tf_op jit(solution)/shard_map/all_gather | solution.py:28
  295.6 46.8 %copy-start.43 = (bf16[2,3,768,192]{2,3,1,0:T(8,128)(2,1)S(1)}, bf16[2,3,768,192]{2,3,1,0:T(8,128)(2,1)}, u32[]{:S(2)}) copy-start(bf16[2,3,768,192]{2,3,1,0:T(8,128)(2,1)} %param.30) | copy-start | bytes 5308420
  298.4 143.6 %reduce-scatter.13.cloned.1.call-start = ((), (), s32[]{:S(2)}) async-start(), calls=%async_computation.12 | async-start | bytes 7864320 | tf_op jit(solution)/shard_map/reduce_scatter | solution.py:32
  371.9 118.9 %all-gather.14.cloned.1.call-start = ((), (), s32[]{:S(2)}) async-start(), calls=%async_computation.13 | async-start | bytes 3932160 | tf_op jit(solution)/shard_map/all_gather | solution.py:28
  446.7 142.2 %reduce-scatter.15.cloned.1.call-start = ((), (), s32[]{:S(2)}) async-start(), calls=%async_computation.14 | async-start | bytes 7864320 | tf_op jit(solution)/shard_map/reduce_scatter | solution.py:32
  497.2 15.4 %copy-start.31 = (f32[4,512,768]{2,1,0:T(8,128)}, f32[4,512,768]{2,1,0:T(8,128)S(1)}, u32[]{:S(2)}) copy-start(f32[4,512,768]{2,1,0:T(8,128)S(1)} %get-tuple-element.399) | copy-start | bytes 18874372
  497.2 17.1 %copy-start.76 = (bf16[2,768,768]{2,1,0:T(8,128)(2,1)S(1)}, bf16[2,768,768]{2,1,0:T(8,128)(2,1)}, u32[]{:S(2)}) copy-start(bf16[2,768,768]{2,1,0:T(8,128)(2,1)} %param.38) | copy-start | bytes 7077892
  518.8 119.2 %all-gather.16.cloned.1.call-start = ((), (), s32[]{:S(2)}) async-start(), calls=%async_computation.15 | async-start | bytes 3932160 | tf_op jit(solution)/shard_map/all_gather | solution.py:28
  594.0 131.7 %reduce-scatter.17.cloned.1.call-start = ((), (), s32[]{:S(2)}) async-start(), calls=%async_computation.16 | async-start | bytes 7864320 | tf_op jit(solution)/shard_map/reduce_scatter | solution.py:32
  638.0 12.9 copy-start.77
  655.4 122.3 %all-gather.18.cloned.1.call-start = ((), (), s32[]{:S(2)}) async-start(), calls=%async_computation.17 | async-start | bytes 3932160 | tf_op jit(solution)/shard_map/all_gather | solution.py:28
  730.9 46.8 %copy-start.44 = (bf16[2,192,768]{2,1,0:T(8,128)(2,1)S(1)}, bf16[2,192,768]{2,1,0:T(8,128)(2,1)}, u32[]{:S(2)}) copy-start(bf16[2,192,768]{2,1,0:T(8,128)(2,1)} %param.32) | copy-start | bytes 1769476
  733.7 177.3 %reduce-scatter.19.cloned.1.call-start = ((), (), s32[]{:S(2)}) async-start(), calls=%async_computation.18 | async-start | bytes 7864320 | tf_op jit(solution)/shard_map/reduce_scatter | solution.py:32
  828.3 75.6 %copy-start.70 = (s32[64]{0:T(128)S(1)}, s32[64]{0:T(128)}, u32[]{:S(2)}) copy-start(s32[64]{0:T(128)} %param.29) | copy-start | bytes 772
  828.3 132.0 %all-gather.20.cloned.1.call-start = ((), (), s32[]{:S(2)}) async-start(), calls=%async_computation.19 | async-start | bytes 3932160 | tf_op jit(solution)/shard_map/all_gather | solution.py:28
  828.4 82.6 %copy-start.6 = (f32[4,128,768]{2,1,0:T(8,128)S(1)}, f32[4,128,768]{2,1,0:T(8,128)}, u32[]{:S(2)}) copy-start(f32[4,128,768]{2,1,0:T(8,128)} %copy-done.5) | copy-start | bytes 4718596
  906.2 8.3 copy-start.58
  914.6 45.7 %copy-start.60 = (f32[768]{0:T(1024)S(1)}, f32[768]{0:T(1024)}, u32[]{:S(2)}) copy-start(f32[768]{0:T(1024)} %copy-done.59) | copy-start | bytes 9220
  916.3 131.0 %reduce-scatter.21.cloned.1.call-start = ((), (), s32[]{:S(2)}) async-start(), calls=%async_computation.20 | async-start | bytes 7864320 | tf_op jit(solution)/shard_map/reduce_scatter | solution.py:32
  960.3 12.3 copy-start.78
  977.1 70.2 %copy-start.3 = (f32[4,128,768]{2,1,0:T(8,128)S(1)}, f32[4,128,768]{2,1,0:T(8,128)}, u32[]{:S(2)}) copy-start(f32[4,128,768]{2,1,0:T(8,128)} %copy-done.2) | copy-start | bytes 4718596
  977.1 70.2 %copy-start.48 = (f32[768]{0:T(1024)S(1)}, f32[768]{0:T(1024)}, u32[]{:S(2)}) copy-start(f32[768]{0:T(1024)} %copy-done.47) | copy-start | bytes 9220
  977.1 70.2 %copy-start.50 = (f32[4,128]{1,0:T(4,128)S(1)}, f32[4,128]{1,0:T(4,128)}, u32[]{:S(2)}) copy-start(f32[4,128]{1,0:T(4,128)} %copy-done.49) | copy-start | bytes 6148
  977.1 70.2 %copy-start.52 = (f32[4,128]{1,0:T(4,128)S(1)}, f32[4,128]{1,0:T(4,128)}, u32[]{:S(2)}) copy-start(f32[4,128]{1,0:T(4,128)} %copy-done.51) | copy-start | bytes 6148
  977.2 72.4 %copy-start.56 = (f32[4,128]{1,0:T(4,128)S(1)}, f32[4,128]{1,0:T(4,128)}, u32[]{:S(2)}) copy-start(f32[4,128]{1,0:T(4,128)} %copy-done.55) | copy-start | bytes 6148
  977.2 119.3 %all-gather.22.cloned.1.call-start = ((), (), s32[]{:S(2)}) async-start(), calls=%async_computation.21 | async-start | bytes 3932160 | tf_op jit(solution)/shard_map/all_gather | solution.py:28
  1052.5 387.3 %all-reduce.5.cloned.1.call-start = ((), (), s32[]{:S(2)}) async-start(), calls=%async_computation.24 | async-start | bytes 28311552 | tf_op jit(solution)/shard_map/psum | solution.py:357
  1053.0 6.1 copy-start.73
  1053.0 6.1 copy-start.80
  1075.7 20.8 %copy-start.45 = (bf16[2,192,768]{2,1,0:T(8,128)(2,1)S(1)}, bf16[2,192,768]{2,1,0:T(8,128)(2,1)}, u32[]{:S(2)}) copy-start(bf16[2,192,768]{2,1,0:T(8,128)(2,1)} %param.32) | copy-start | bytes 1769476
  1103.3 41.8 %copy-start = (bf16[1,4,512,768]{3,2,1,0:T(8,128)(2,1)S(1)}, bf16[1,4,512,768]{3,2,1,0:T(8,128)(2,1)}, u32[]{:S(2)}) copy-start(bf16[1,4,512,768]{3,2,1,0:T(8,128)(2,1)} %all-gather.24.cloned.1.call-done) | copy-start | bytes 9437188
  1153.5 359.3 %reduce-scatter.23.cloned.1.call-start = ((), (), s32[]{:S(2)}) async-start(), calls=%async_computation.22 | async-start | bytes 7864320 | tf_op jit(solution)/shard_map/reduce_scatter | solution.py:32
  1450.4 62.4 %copy-start.15 = (f32[4,128,768]{2,1,0:T(8,128)S(1)}, f32[4,128,768]{2,1,0:T(8,128)}, u32[]{:S(2)}) copy-start(f32[4,128,768]{2,1,0:T(8,128)} %copy-done.14) | copy-start | bytes 4718596
  (52 other events, 132.7 us)
Sparse Core Ops, SparseCore 0:
  9.8 46.5 all-gather.23
  78.0 70.0 reduce-scatter.8
  151.4 43.8 all-gather.9
  223.5 70.0 reduce-scatter.10
  298.5 43.8 all-gather.11
  372.0 70.0 reduce-scatter.12
  446.9 43.8 all-gather.13
  518.9 70.0 reduce-scatter.14
  594.1 43.8 all-gather.15
  655.6 70.0 reduce-scatter.16
  733.9 43.8 all-gather.17
  828.4 82.5 reduce-scatter.18
  916.4 43.8 all-gather.19
  977.3 70.0 reduce-scatter.20
  1052.6 43.8 all-gather.21
  1153.6 286.0 all-reduce.4
  1442.6 70.1 reduce-scatter.22
where the time goes:
time: 1530 us; the launch traced here: 1520 us
  waiting for transfers between devices  1000 us (65%)
  matrix products  173 us (11%)
  blocking collectives  145 us (9%)
  other arithmetic  109 us (7%)
  local copies, waits for them, and re-layouts  72.2 us (5%)
  between operations  18.9 us (1%)
    reduce_scatter x8, waiting for transfers between devices, collect_rows(): return lax.psum_scatter(values, 'tensor', scatter_dimension=1, tiled=True)  484 us
    all_gather x8, waiting for transfers between devices, spread_rows(): return lax.all_gather(values, 'tensor', axis=1, tiled=True)  323 us
    psum x1, waiting for transfers between devices, shards(): lax.psum((backbone_matrices[0], backbone_matrices[1], backbone_matrices[2...  194 us
    all_gather x1, blocking collectives, shards(): lax.all_gather(chosen.reshape(slot_count, feature_count).astype(jnp.bfloa...  74 us
    psum x1, blocking collectives, shards(): lax.psum((backbone_vectors[0], backbone_vectors[1], backbone_vectors[2],...  41.6 us
    dynamic_slice x64, local copies, waits for them, and re-layouts, layer_forward(): lax.map(attend_forward, (queries, key_rows, value_rows, segment))  38.4 us
    convert_element_type x2, other arithmetic, layer_forward(): activated = activate(expanded).astype(jnp.bfloat16)  30.8 us
  transfers between devices with their start and end apart: 17, of which 17 were waited for; matrix products, arithmetic and copies ran while one was open for 4% of the time, Pallas kernels for 0%

commit v1 on v0

v1 whole, which is shorter than its diff:
```python
import math

import jax
import jax.numpy as jnp
from jax import lax
from jax.sharding import PartitionSpec as P

HEAD_DIM = 64
EPSILON = 1e-12
LOSS_WEIGHT = 8.0
HIGHEST = lax.Precision.HIGHEST
MASKED = -1e30
BF = jnp.bfloat16
F32 = jnp.float32
BOTH = ("span", "tensor")


def mm(a, b, ca, cb):
    return lax.dot_general(a, b, (((ca,), (cb,)), ((), ())), preferred_element_type=F32)


def normal_parts(values):
    centred = values - jnp.mean(values, axis=-1, keepdims=True)
    spread = jnp.mean(centred * centred, axis=-1, keepdims=True)
    scale = lax.rsqrt(spread + EPSILON)
    return centred * scale, scale


def normal_back(upward, normed, scale, gain):
    weighted = upward * gain
    first = jnp.mean(weighted, axis=-1, keepdims=True)
    second = jnp.mean(weighted * normed, axis=-1, keepdims=True)
    return (weighted - first - normed * second) * scale


def split_heads(values):
    return values.reshape(values.shape[0], values.shape[1] // HEAD_DIM, HEAD_DIM)


def attend_forward(queries, keys, values, same):
    scores = (
        jnp.einsum("qhd,khd->hqk", split_heads(queries), split_heads(keys), preferred_element_type=F32)
        * 0.125
    )
    scores = jnp.where(same[None], scores, MASKED)
    maximum = jnp.max(scores, axis=-1, keepdims=True)
    raised = jnp.exp(scores - maximum)
    total = jnp.sum(raised, axis=-1, keepdims=True)
    attention = (raised / total).astype(BF)
    mixture = jnp.einsum("hqk,khd->qhd", attention, split_heads(values), preferred_element_type=F32)
    return mixture.reshape(queries.shape).astype(BF), maximum + jnp.log(total)


def attend_backward(queries, keys, values, same, upward, log_total):
    qh, kh, vh, uh = (split_heads(m) for m in (queries, keys, values, upward))
    scores = jnp.einsum("qhd,khd->hqk", qh, kh, preferred_element_type=F32) * 0.125
    scores = jnp.where(same[None], scores, MASKED)
    attention = jnp.exp(scores - log_total)
    grad_weights = jnp.einsum("qhd,khd->hqk", uh, vh, preferred_element_type=F32)
    inner = jnp.sum(attention * grad_weights, axis=-1, keepdims=True)
    grad_scores = (attention * (grad_weights - inner)).astype(BF)
    dq = jnp.einsum("hqk,khd->qhd", grad_scores, kh, preferred_element_type=F32) * 0.125
    dk = jnp.einsum("hqk,qhd->khd", grad_scores, qh, preferred_element_type=F32) * 0.125
    dv = jnp.einsum("hqk,qhd->khd", attention.astype(BF), uh, preferred_element_type=F32)
    return tuple(m.reshape(queries.shape).astype(BF) for m in (dq, dk, dv))


def gelu_parts(hidden):
    phi = 0.5 * (1.0 + lax.erf(hidden * math.sqrt(0.5)))
    slope = phi + hidden * jnp.exp(-0.5 * hidden * hidden) * (1.0 / math.sqrt(2.0 * math.pi))
    return hidden * phi, slope


def layer_forward(x, same, attn_w, ffn_w, vec):
    wq, wk, wv, wp = attn_w
    we, ws = ffn_w
    xb = x.astype(BF)
    q = (mm(xb, wq, 1, 1) + vec["qb"]).astype(BF)
    k = mm(xb, wk, 1, 1).astype(BF)
    v = (mm(xb, wv, 1, 1) + vec["vb"]).astype(BF)
    o, lse = attend_forward(q, k, v, same)
    z1 = x + mm(o, wp, 1, 0) + vec["pb"]
    n1, r1 = normal_parts(z1)
    y = n1 * vec["g0"] + vec["s0"]
    yb = y.astype(BF)
    hid = jnp.einsum("qd,tdf->tqf", yb, we, preferred_element_type=F32) + vec["eb"][:, None, :]
    act, slope = gelu_parts(hid)
    act = act.astype(BF)
    z2 = y + jnp.einsum("tqf,tfd->qd", act, ws, preferred_element_type=F32) + vec["sb"]
    n2, r2 = normal_parts(z2)
    out = n2 * vec["g1"] + vec["s1"]
    return out, (xb, q, k, v, o, lse, n1, r1, yb, act, slope.astype(BF), n2, r2)


def layer_backward(dout, same, attn_w, ffn_w, vec, kept):
    wq, wk, wv, wp = attn_w
    we, ws = ffn_w
    xb, q, k, v, o, lse, n1, r1, yb, act, slope, n2, r2 = kept
    dz2 = normal_back(dout, n2, r2, vec["g1"])
    dgain1 = jnp.sum(dout * n2, axis=0)
    dshift1 = jnp.sum(dout, axis=0)
    dsb = jnp.sum(dz2, axis=0)
    dzb = dz2.astype(BF)
    dws = jnp.einsum("tqf,qd->tfd", act, dzb, preferred_element_type=F32).astype(BF)
    dact = jnp.einsum("qd,tfd->tqf", dzb, ws, preferred_element_type=F32)
    dhid = dact * slope.astype(F32)
    deb = jnp.sum(dhid, axis=1)
    dhb = dhid.astype(BF)
    dwe = jnp.einsum("qd,tqf->tdf", yb, dhb, preferred_element_type=F32).astype(BF)
    dy = dz2 + jnp.einsum("tqf,tdf->qd", dhb, we, preferred_element_type=F32)
    dz1 = normal_back(dy, n1, r1, vec["g0"])
    dgain0 = jnp.sum(dy * n1, axis=0)
    dshift0 = jnp.sum(dy, axis=0)
    dpb = jnp.sum(dz1, axis=0)
    da = dz1.astype(BF)
    dwp = mm(o, da, 0, 0).astype(BF)
    do = mm(da, wp, 1, 1).astype(BF)
    dq, dk, dv = attend_backward(q, k, v, same, do, lse)
    dwq = mm(dq, xb, 0, 0).astype(BF)
    dwk = mm(dk, xb, 0, 0).astype(BF)
    dwv = mm(dv, xb, 0, 0).astype(BF)
    dqb = jnp.sum(dq.astype(F32), axis=0)
    dvb = jnp.sum(dv.astype(F32), axis=0)
    dx = dz1 + mm(dq, wq, 1, 0) + mm(dk, wk, 1, 0) + mm(dv, wv, 1, 0)
    small = {
        "qb": dqb, "vb": dvb, "pb": dpb, "g0": dgain0, "g1": dgain1,
        "s0": dshift0, "s1": dshift1, "sb": dsb, "eb": deb.reshape(-1),
    }
    return dx, (dwq, dwk, dwv, dwp), (dwe, dws), small


SMALL = ("qb", "vb", "pb", "g0", "g1", "s0", "s1", "sb", "eb")


def to_rows(values):
    return lax.all_to_all(values, "tensor", split_axis=0, concat_axis=1, tiled=True)[0]


def to_places(values):
    return lax.all_to_all(values[None], "tensor", split_axis=1, concat_axis=0, tiled=True)


def shards(
    layer_input, skip_tokens, backbone_cotangent, head_cotangent, segment_lengths, pair_index,
    w_heads, heads_bias, w_project, project_bias, norm_gain, norm_shift,
    w_expand, expand_bias, w_shrink, shrink_bias,
):
    side = lax.axis_index("span")
    mine = lax.axis_index("tensor")
    tensor_count = lax.axis_size("tensor")
    width = layer_input.shape[-1]
    head_cols = w_heads.shape[-1]
    ff_cols = w_expand.shape[-1]

    def gather_attn(l):
        heads = jnp.swapaxes(w_heads[l], 1, 2)
        zero = jnp.stack([heads[0], heads[1]])
        one = jnp.stack([heads[2], w_project[l]])
        got = lax.all_gather(jnp.where(side == 0, zero, one), BOTH, axis=0, tiled=False)
        got = got.reshape(2, tensor_count, 2, head_cols, width)
        return tuple(
            got[i, :, j].reshape(tensor_count * head_cols, width) for i in range(2) for j in range(2)
        )

    def gather_ffn(l):
        got = lax.all_gather(
            jnp.where(side == 0, w_expand[l], w_shrink[l]), BOTH, axis=0, tiled=False
        )
        got = got.reshape(2, tensor_count, width, ff_cols)
        return got[0], got[1]

    small_in = jnp.concatenate([heads_bias.reshape(-1), expand_bias.reshape(-1)])
    small_got = lax.all_gather(small_in, "tensor", axis=0, tiled=False).astype(F32)
    hb_all = jnp.transpose(small_got[:, : 4 * head_cols].reshape(tensor_count, 2, 2, head_cols), (1, 2, 0, 3))
    hb_all = hb_all.reshape(2, 2, tensor_count * head_cols)
    eb_all = jnp.transpose(small_got[:, 4 * head_cols :].reshape(tensor_count, 2, ff_cols), (1, 0, 2))

    def vectors(l):
        return {
            "qb": hb_all[l, 0], "vb": hb_all[l, 1], "pb": project_bias[l].astype(F32),
            "g0": norm_gain[l, 0].astype(F32), "g1": norm_gain[l, 1].astype(F32),
            "s0": norm_shift[l, 0].astype(F32), "s1": norm_shift[l, 1].astype(F32),
            "sb": shrink_bias[l].astype(F32), "eb": eb_all[l],
        }

    attn_w0 = gather_attn(0)
    ffn_w0 = gather_ffn(0)
    attn_w1 = gather_attn(1)
    ffn_w1 = gather_ffn(1)

    x = to_rows(layer_input[0])
    skip = to_rows(skip_tokens[0])
    backbone_cot = to_rows(backbone_cotangent[0])
    head_cot = to_rows(head_cotangent[0])
    tokens = x.shape[0]

    lengths = lax.dynamic_index_in_dim(segment_lengths[0], mine, 0, keepdims=False)
    span_count = lengths.shape[0]
    starts = jnp.cumsum(lengths) - lengths
    row_length = jnp.sum(lengths)
    places = jnp.arange(tokens, dtype=jnp.int32)
    counted = jnp.sum((places[:, None] >= starts[None, :]).astype(jnp.int32), axis=-1) - 1
    segment = jnp.where(places < row_length, counted, span_count)
    same = segment[:, None] == segment[None, :]
    valid = (places < row_length).astype(F32)[:, None]
    picker = (starts[:, None] == places[None, :]).astype(F32)
    first = jnp.sum(picker, axis=0)[:, None] > 0

    vec0, vec1 = vectors(0), vectors(1)
    backbone, kept0 = layer_forward(x.astype(F32), same, attn_w0, ffn_w0, vec0)
    cls = mm(picker.astype(BF), backbone.astype(BF), 1, 0).astype(BF)
    anchors = lax.all_gather(cls, ("dp", "span", "tensor"), axis=0, tiled=False)
    dp_count = lax.axis_size("dp")
    pair_count = lax.axis_size("span")
    anchors = anchors.reshape(dp_count, pair_count, tensor_count * span_count, width)
    anchors = jnp.swapaxes(anchors, 0, 1).reshape(pair_count, dp_count * tensor_count * span_count, width)

    head_in = jnp.where(first, backbone, skip.astype(F32))
    head, kept1 = layer_forward(head_in, same, attn_w1, ffn_w1, vec1)

    vector_count = anchors.shape[1]
    root = math.sqrt(width)
    logits = mm(anchors[0], anchors[1], 1, 1) / root
    columns = jnp.arange(vector_count, dtype=jnp.int32)
    target = (pair_index[:, None] == columns[None, :]).astype(F32)
    lse_rows = jax.nn.logsumexp(logits, axis=1)
    lse_cols = jax.nn.logsumexp(logits, axis=0)
    dlogits = LOSS_WEIGHT * (
        jnp.exp(logits - lse_rows[:, None]) + jnp.exp(logits - lse_cols[None, :]) - 2.0 * target
    )
    span_loss = (jnp.sum(lse_rows) + jnp.sum(lse_cols) - 2.0 * jnp.sum(target * logits)) / (
        2 * vector_count
    )
    own = (lax.axis_index("dp") * tensor_count + mine) * span_count
    wanted = jnp.where(side == 0, dlogits, dlogits.T)
    wanted = lax.dynamic_slice(wanted, (own, 0), (span_count, vector_count))
    other = lax.dynamic_index_in_dim(anchors, 1 - side, 0, keepdims=False).astype(F32)
    dcls = jnp.dot(wanted, other, precision=HIGHEST) / root

    du, dattn1, dffn1, small1 = layer_backward(
        head_cot.astype(F32) * valid, same, attn_w1, ffn_w1, vec1, kept1
    )
    grad_skip = jnp.where(first, 0.0, du).astype(BF)
    seed = backbone_cot.astype(F32) * valid + jnp.where(first, du, 0.0)
    seed = seed + jnp.dot(picker.T, dcls, precision=HIGHEST)
    dx, dattn0, dffn0, small0 = layer_backward(seed, same, attn_w0, ffn_w0, vec0, kept0)

    def reduce_attn(grads):
        packed = jnp.stack([g.reshape(tensor_count, head_cols, width) for g in grads])
        packed = packed.reshape(2, 2, tensor_count, head_cols, width)
        packed = jnp.swapaxes(packed, 1, 2).reshape(2 * tensor_count, 2, head_cols, width)
        part = lax.psum_scatter(packed, BOTH, scatter_dimension=0, tiled=False)
        part = lax.psum(part, "dp")
        got = lax.all_gather(part, "span", axis=0, tiled=False).astype(F32)
        heads = jnp.stack([got[0, 0], got[0, 1], got[1, 0]])
        return jnp.swapaxes(heads, 1, 2), got[1, 1]

    def reduce_ffn(grads):
        packed = jnp.stack(grads).reshape(2 * tensor_count, width, ff_cols)
        part = lax.psum_scatter(packed, BOTH, scatter_dimension=0, tiled=False)
        part = lax.psum(part, "dp")
        got = lax.all_gather(part, "span", axis=0, tiled=False).astype(F32)
        return got[0], got[1]

    ge1, gs1 = reduce_ffn(dffn1)
    gh1, gp1 = reduce_attn(dattn1)
    ge0, gs0 = reduce_ffn(dffn0)
    gh0, gp0 = reduce_attn(dattn0)

    flat = jnp.concatenate([small[k] for small in (small0, small1) for k in SMALL])
    flat = lax.psum(flat, ("dp", "span", "tensor"))
    sizes = [small0[k].shape[0] for k in SMALL] * 2
    cuts = []
    at = 0
    for size in sizes:
        cuts.append(flat[at : at + size])
        at += size
    s0 = dict(zip(SMALL, cuts[: len(SMALL)]))
    s1 = dict(zip(SMALL, cuts[len(SMALL) :]))

    def local(values, size):
        return lax.dynamic_slice(values, (mine * size,), (size,))

    hb = jnp.stack(
        [jnp.stack([local(s["qb"], head_cols), local(s["vb"], head_cols)]) for s in (s0, s1)]
    )
    eb = jnp.stack([local(s["eb"], ff_cols) for s in (s0, s1)])
    return (
        to_places((backbone * valid).astype(BF))[None],
        to_places((head * valid).astype(BF))[None],
        span_loss,
        to_places(dx.astype(BF))[None],
        to_places(grad_skip)[None],
        jnp.stack([gh0, gh1]),
        hb,
        jnp.stack([gp0, gp1]),
        jnp.stack([s0["pb"], s1["pb"]]),
        jnp.stack([jnp.stack([s["g0"], s["g1"]]) for s in (s0, s1)]),
        jnp.stack([jnp.stack([s["s0"], s["s1"]]) for s in (s0, s1)]),
        jnp.stack([ge0, ge1]),
        eb,
        jnp.stack([gs0, gs1]),
        jnp.stack([s0["sb"], s1["sb"]]),
    )


def solution(mesh):
    rows = P("span", "dp", "tensor", None)
    in_specs = (
        rows, rows, rows, rows, P("span", "dp", None), P(),
        P(None, None, None, "tensor"), P(None, None, "tensor"), P(None, "tensor", None),
        P(), P(), P(), P(None, None, "tensor"), P(None, "tensor"), P(None, "tensor", None), P(),
    )
    out_specs = (
        rows, rows, P(), rows, rows,
        P(None, None, None, "tensor"), P(None, None, "tensor"), P(None, "tensor", None),
        P(), P(), P(), P(None, None, "tensor"), P(None, "tensor"), P(None, "tensor", None), P(),
    )
    return jax.shard_map(shards, mesh=mesh, in_specs=in_specs, out_specs=out_specs, check_vma=False)
```

time: 1530 us -> 992 us (0.65)
  waiting for transfers between devices: 1000 us -> 462 us
  blocking collectives: 145 us -> 85.4 us
  starting transfers between devices: 2.71 us -> 34.9 us
  local copies, waits for them, and re-layouts: 72.2 us -> 102 us
    reduce_scatter x8 -> x4, waiting for transfers between devices: 484 us -> 139 us  [the longest x2 139 us: reduce_ffn(): part = lax.psum_scatter(packed, BOTH, scatter_dimension=0, tiled=False)]
    all_gather x8, waiting for transfers between devices: 323 us -> 106 us  [the longest x2 56.6 us: gather_ffn(): lax.all_gather(jnp.where(side == 0, w_expand[l], w_shrink[l]), BOTH, axis...]
    psum x2 -> x0, blocking collectives: 70.9 us -> none  [the longest x1 41.6 us: shards(): lax.psum((backbone_vectors[0], backbone_vectors[1], backbone_vectors[2],...]
    dynamic_slice x64 -> x7, local copies, waits for them, and re-layouts: 38.4 us -> 0.46 us  [the longest x6 0.46 us: local(): return lax.dynamic_slice(values, (mine * size,), (size,))]
    all_to_all x0 -> x8, starting transfers between devices: none -> 33.2 us  [the longest x4 17.5 us: to_rows(): lax.all_to_all(values, 'tensor', split_axis=0, concat_axis=1, tiled=True)[0]]
    reshape x1 -> x11, local copies, waits for them, and re-layouts: 0.02 us -> 31.7 us  [the longest x2 26.1 us: reduce_ffn(): packed = jnp.stack(grads).reshape(2 * tensor_count, width, ff_cols)]
    unnamed x0 -> x8, other arithmetic: none -> 23.5 us
    convert_element_type x20 -> x9, other arithmetic: 44.9 us -> 21.8 us  [the longest x2 14.2 us: attend_backward(): grad_scores = (attention * (grad_weights - inner)).astype(BF)]
  transfers between devices with their start and end apart: 17 -> 22, of which waited for: 17 -> 10; matrix products, arithmetic and copies ran while one was open for 4% -> 36% of each run, Pallas kernels for 0% -> 0%
where the time goes in v1:
time: 992 us; the launch traced here: 986 us
  waiting for transfers between devices  462 us (47%)
  matrix products  180 us (18%)
  local copies, waits for them, and re-layouts  102 us (10%)
  other arithmetic  102 us (10%)
  blocking collectives  85.4 us (9%)
  starting transfers between devices  34.9 us (4%)
  between operations  19.5 us (2%)
    reduce_scatter x2, waiting for transfers between devices, reduce_ffn(): part = lax.psum_scatter(packed, BOTH, scatter_dimension=0, tiled=False)  139 us
    psum x1, waiting for transfers between devices, reduce_attn(): part = lax.psum(part, 'dp')  135 us
    psum x1, waiting for transfers between devices, shards(): flat = lax.psum(flat, ('dp', 'span', 'tensor'))  71.1 us
    all_gather x1, blocking collectives, shards(): anchors = lax.all_gather(cls, ('dp', 'span', 'tensor'), axis=0, tiled=False)  69.3 us
    all_gather x2, waiting for transfers between devices, gather_ffn(): lax.all_gather(jnp.where(side == 0, w_expand[l], w_shrink[l]), BOTH, axis...  56.6 us
    dot_general x26, matrix products, mm(): lax.dot_general(a, b, (((ca,), (cb,)), ((), ())), preferred_element_type=...  43.4 us
    all_gather x2, waiting for transfers between devices, gather_attn(): lax.all_gather(jnp.where(side == 0, zero, one), BOTH, axis=0, tiled=False)  41.2 us
    unnamed x265, local copies, waits for them, and re-layouts  32.2 us
  transfers between devices with their start and end apart: 22, of which 10 were waited for; matrix products, arithmetic and copies ran while one was open for 36% of the time, Pallas kernels for 0%

profile of v1, /device:TPU:0, one launch (start us, length us, event | category | flops | bytes accessed | tf_op | source)
XLA Modules:
  0.0 985.8 jit_solution(689958023518793474)
XLA Ops:
  16.1 5.3 all-to-all-start.5
  25.8 16.1 %all-gather.4 = bf16[4,1,2304]{2,1,0:T(2,128)(2,1)S(1)} all-gather(bf16[1,1,2304]{2,1,0:T(2,128)(2,1)S(1)} %reshape.546), channel_id=3, replica_groups=mesh['dp'=4,'span'=2,'tensor'=4] {'tensor'}, dimensions={0}, use_global_device_ids=true | all-gather | bytes 23040 | tf_op jit(solution)/shard_map/all_gather | solution.py:173
  44.3 3.5 all-to-all-start
  49.3 20.0 %all-gather.27.cloned.1.call-done = bf16[16,192,768]{2,1,0:T(8,128)(2,1)} async-done(((bf16[2,192,768]{2,1,0:T(8,128)(2,1)}), bf16[16,192,768]{2,1,0:T(8,128)(2,1)}) %all-gather.27.cloned.1.call-update) | async-done | bytes 4718608 | tf_op jit(solution)/shard_map/all_gather | solution.py:159
  69.3 4.2 fusion.150
  73.5 4.4 all-to-all-start.2
  90.9 3.6 fusion.69
  96.6 21.1 %all-gather.29.cloned.1.call-done = bf16[16,192,768]{2,1,0:T(8,128)(2,1)} async-done(((bf16[2,192,768]{2,1,0:T(8,128)(2,1)}), bf16[16,192,768]{2,1,0:T(8,128)(2,1)}) %all-gather.29.cloned.1.call-update) | async-done | bytes 4718608 | tf_op jit(solution)/shard_map/all_gather | solution.py:159
  117.7 4.6 fusion.149
  122.4 56.6 %all-gather.15.cloned.1.call-done = bf16[8,768,768]{2,1,0:T(8,128)(2,1)} async-done(((bf16[1,768,768]{2,1,0:T(8,128)(2,1)}), bf16[8,768,768]{2,1,0:T(8,128)(2,1)}) %all-gather.15.cloned.1.call-update) | async-done | bytes 9437200 | tf_op jit(solution)/shard_map/all_gather | solution.py:166
  178.9 7.4 fusion.25
  189.9 69.3 %all-gather.5 = bf16[32,4,768]{2,1,0:T(4,128)(2,1)S(1)} all-gather(bf16[1,4,768]{2,1,0:T(4,128)(2,1)S(1)} %fusion.74), channel_id=5, replica_groups=mesh['dp'=4,'span'=2,'tensor'=4] {'dp','span','tensor'}, dimensions={0}, use_global_device_ids=true | all-gather | bytes 202752 | tf_op jit(solution)/shard_map/all_gather | solution.py:212
  260.0 4.2 all-to-all-start.4
  287.6 3.8 fusion.68
  295.3 5.5 fusion.21
  308.3 4.9 fusion.36
  313.2 9.8 multiply_reduce_fusion.3
  331.5 9.6 convert_reduce_fusion
  341.1 9.7 multiply_reduce_fusion.1
  350.7 7.1 multiply_convert_fusion.1
  377.4 4.7 add_add_fusion
  382.1 4.0 multiply_reduce_fusion.4
  386.9 8.0 fusion.38
  404.0 8.3 convert_reduce_fusion.2
  414.0 11.2 %multiply_reduce_fusion = (f32[12,512]{1,0:T(8,128)S(1)}, f32[12,512,512]{1,2,0:T(8,128)}) fusion(f32[12,512]{1,0:T(8,128)S(1)} %copy-done.66, f32[12,512,512]{1,2,0:T(8,128)} %copy-done, pred[512,512]{0,1:T(8,128)(4,1)S(1)} %broadcast_compare_fusion, bf16[512,12,64]{0,2,1:T(8,128)(2,1)S(1)} %bitcast.409, bf16[512,12,64]{0,2,1:T(8,128)(2,1)S(1)} %bitcast.439), kind=kOutput, calls=%fused_computation.1 | convolution fusion | flops 418375680 | bytes 27049984 | tf_op jit(solution)/shard_map/qhd,khd->hqk/dot_general | solution.py:59
  425.5 7.1 multiply_convert_fusion
  443.1 7.4 convert_bitcast_fusion
  450.5 8.4 convert_bitcast_fusion.1
  458.9 8.4 pad_maximum_fusion.1
  467.3 12.7 %copy.209 = bf16[8,768,768]{2,1,0:T(8,128)(2,1)} copy(bf16[8,768,768]{1,2,0:T(8,128)(2,1)} %bitcast.378) | data formatting | bytes 18874368 | tf_op jit(solution)/shard_map/reshape | solution.py:259
  480.5 7.3 convert_bitcast_fusion.2
  487.9 7.7 convert_bitcast_fusion.3
  495.6 8.3 pad_maximum_fusion
  503.9 13.5 %copy.205 = bf16[8,768,768]{2,1,0:T(8,128)(2,1)} copy(bf16[8,768,768]{1,2,0:T(8,128)(2,1)} %bitcast.379) | data formatting | bytes 18874368 | tf_op jit(solution)/shard_map/reshape | solution.py:259
  517.5 58.3 %reduce-scatter.11.cloned.1.call-done = bf16[1,768,768]{2,1,0:T(8,128)(2,1)} async-done(((bf16[8,768,768]{2,1,0:T(8,128)(2,1)}), bf16[1,768,768]{2,1,0:T(8,128)(2,1)}) %reduce-scatter.11.cloned.1.call-update) | async-done | bytes 1179664 | tf_op jit(solution)/shard_map/reduce_scatter | solution.py:260
  575.7 80.3 %reduce-scatter.9.cloned.1.call-done = bf16[1,768,768]{2,1,0:T(8,128)(2,1)} async-done(((bf16[8,768,768]{2,1,0:T(8,128)(2,1)}), bf16[1,768,768]{2,1,0:T(8,128)(2,1)}) %reduce-scatter.9.cloned.1.call-update) | async-done | bytes 1179664 | tf_op jit(solution)/shard_map/reduce_scatter | solution.py:260
  658.1 134.5 %all-reduce.6.cloned.1.call-done = (bf16[1,2,192,768]{3,2,1,0:T(8,128)(2,1)}, bf16[1,2,192,768]{3,2,1,0:T(8,128)(2,1)}, bf16[1,768,768]{2,1,0:T(8,128)(2,1)}, bf16[1,768,768]{2,1,0:T(8,128)(2,1)}) async-done(((bf16[1,2,192,768]{3,2,1,0:T(8,128)(2,1)}, bf16[1,2,192,768]{3,2,1,0:T(8,128)(2,1)}, bf16[1,768,768]{2,1,0:T(8,128)(2,1)}, bf16[1,768,768]{2,1,0:T(8,128)(2,1)}), (bf16[1,2,192,768]{3,2,1,0:T(8,128)(2,1)}, ...) | async-done | bytes 3538960 | tf_op jit(solution)/shard_map/psum | solution.py:253
  796.1 6.3 reduce.44
  804.3 4.2 all-to-all-start.1
  811.1 6.3 reduce.45
  823.6 4.6 all-to-all-start.3
  830.3 5.4 reduce.47
  838.2 5.4 reduce.46
  847.2 71.1 %all-reduce.4.cloned.1.call-done = f32[18432]{0:T(1024)} async-done(((f32[18432]{0:T(1024)}), f32[18432]{0:T(1024)}) %all-reduce.4.cloned.1.call-update) | async-done | bytes 73744 | tf_op jit(solution)/shard_map/psum | solution.py:271
  920.0 3.5 all-to-all-start.7
  925.2 10.3 %all-to-all-done.7 = bf16[4,2,49152]{2,1,0:T(2,128)(2,1)S(1)} async-done(((bf16[4,2,49152]{2,1,0:T(2,128)(2,1)}), bf16[4,2,49152]{2,1,0:T(2,128)(2,1)S(1)}, u32[]{:S(2)}, u32[]{:S(2)}) %all-to-all-start.7) | async-done | bytes 786464 | tf_op jit(solution)/shard_map/all_to_all | solution.py:140
  935.5 3.5 all-to-all-start.6
  962.3 8.0 all-gather.25.cloned.1.call-done
  (486 shorter events, 177.1 us)
Async XLA Ops:
  7.2 62.2 %all-gather.27.cloned.1.call-start = ((), (), s32[]{:S(2)}) async-start(), calls=%async_computation.23 | async-start | bytes 5308416 | tf_op jit(solution)/shard_map/all_gather | solution.py:159
  10.8 106.9 %all-gather.29.cloned.1.call-start = ((), (), s32[]{:S(2)}) async-start(), calls=%async_computation.24 | async-start | bytes 5308416 | tf_op jit(solution)/shard_map/all_gather | solution.py:159
  11.8 167.1 %all-gather.15.cloned.1.call-start = ((), (), s32[]{:S(2)}) async-start(), calls=%async_computation.12 | async-start | bytes 10616832 | tf_op jit(solution)/shard_map/all_gather | solution.py:166
  16.1 9.7 copy-start.69
  16.1 26.7 %copy-start.70 = (bf16[2,2,768]{2,1,0:T(2,128)(2,1)S(1)}, bf16[2,2,768]{2,1,0:T(2,128)(2,1)}, u32[]{:S(2)}) copy-start(bf16[2,2,768]{2,1,0:T(2,128)(2,1)} %param.27) | copy-start | bytes 18436
  16.1 28.2 %all-to-all-start.5 = ((bf16[4,128,768]{2,1,0:T(8,128)(2,1)}), bf16[4,128,768]{2,1,0:T(8,128)(2,1)S(1)}, u32[]{:S(2)}, u32[]{:S(2)}) async-start(bf16[4,128,768]{2,1,0:T(8,128)(2,1)} %bitcast.446), calls=%async_computation.5 | async-start | bytes 1572864 | tf_op jit(solution)/shard_map/all_to_all | solution.py:136
  21.4 273.8 %all-gather.17.cloned.1.call-start = ((), (), s32[]{:S(2)}) async-start(), calls=%async_computation.13 | async-start | bytes 10616832 | tf_op jit(solution)/shard_map/all_gather | solution.py:166
  22.8 166.7 %copy-start.88 = (s32[4]{0:T(128)}, s32[4]{0:T(128)S(1)}, u32[]{:S(2)}) copy-start(s32[4]{0:T(128)S(1)} %bitcast_subtract_fusion) | copy-start | bytes 52
  23.7 267.7 %copy-start.94 = (pred[512]{0:T(512)(128)(4,1)}, pred[512]{0:T(512)(128)(4,1)S(1)}, u32[]{:S(2)}) copy-start(pred[512]{0:T(512)(128)(4,1)S(1)} %broadcast_compare_fusion.1) | copy-start | bytes 1540
  43.4 142.9 %copy-start.77 = (f32[768]{0:T(1024)}, f32[768]{0:T(1024)S(1)}, u32[]{:S(2)}) copy-start(f32[768]{0:T(1024)S(1)} %get-tuple-element.45) | copy-start | bytes 9220
  44.0 134.9 %copy-start.84 = (f32[4,768]{1,0:T(4,128)}, f32[4,768]{1,0:T(4,128)S(1)}, u32[]{:S(2)}) copy-start(f32[4,768]{1,0:T(4,128)S(1)} %get-tuple-element.121) | copy-start | bytes 36868
  44.3 29.3 %copy-start.6 = (bf16[4,128,768]{2,1,0:T(8,128)(2,1)}, bf16[4,128,768]{2,1,0:T(8,128)(2,1)S(1)}, u32[]{:S(2)}) copy-start(bf16[4,128,768]{2,1,0:T(8,128)(2,1)S(1)} %all-to-all-done.5) | copy-start | bytes 2359300
  44.3 29.3 %all-to-all-start = ((bf16[4,128,768]{2,1,0:T(8,128)(2,1)}), bf16[4,128,768]{2,1,0:T(8,128)(2,1)S(1)}, u32[]{:S(2)}, u32[]{:S(2)}) async-start(bf16[4,128,768]{2,1,0:T(8,128)(2,1)} %bitcast), calls=%async_computation | async-start | bytes 1572864 | tf_op jit(solution)/shard_map/all_to_all | solution.py:136
  73.5 186.5 %all-to-all-start.2 = ((bf16[4,128,768]{2,1,0:T(8,128)(2,1)}), bf16[4,128,768]{2,1,0:T(8,128)(2,1)}, u32[]{:S(2)}, u32[]{:S(2)}) async-start(bf16[4,128,768]{2,1,0:T(8,128)(2,1)} %bitcast.29), calls=%async_computation.2 | async-start | bytes 1572864 | tf_op jit(solution)/shard_map/all_to_all | solution.py:136
  95.5 90.8 %copy-start.2 = (f32[512,768]{1,0:T(8,128)}, f32[512,768]{1,0:T(8,128)S(1)}, u32[]{:S(2)}) copy-start(f32[512,768]{1,0:T(8,128)S(1)} %get-tuple-element.127) | copy-start | bytes 4718596
  260.0 122.0 %all-to-all-start.4 = ((bf16[4,128,768]{2,1,0:T(8,128)(2,1)}), bf16[4,128,768]{2,1,0:T(8,128)(2,1)}, u32[]{:S(2)}, u32[]{:S(2)}) async-start(bf16[4,128,768]{2,1,0:T(8,128)(2,1)} %bitcast.54), calls=%async_computation.4 | async-start | bytes 1572864 | tf_op jit(solution)/shard_map/all_to_all | solution.py:136
  264.3 253.2 %reduce-scatter.7.cloned.1.call-start = ((), (), s32[]{:S(2)}) async-start(), calls=%async_computation.16 | async-start | bytes 5308416 | tf_op jit(solution)/shard_map/reduce_scatter | solution.py:252
  270.9 10.1 %copy-start.11 = (bf16[512,768]{0,1:T(8,128)(2,1)}, bf16[512,768]{0,1:T(8,128)(2,1)S(1)}, u32[]{:S(2)}) copy-start(bf16[512,768]{0,1:T(8,128)(2,1)S(1)} %copy.183) | copy-start | bytes 2359300
  280.8 14.3 %copy-start.48 = (f32[64,64]{1,0:T(8,128)}, f32[64,64]{1,0:T(8,128)S(1)}, u32[]{:S(2)}) copy-start(f32[64,64]{1,0:T(8,128)S(1)} %get-tuple-element.140) | copy-start | bytes 49156
  293.9 19.3 %copy-start.4 = (f32[512,768]{1,0:T(8,128)}, f32[512,768]{1,0:T(8,128)S(1)}, u32[]{:S(2)}) copy-start(f32[512,768]{1,0:T(8,128)S(1)} %get-tuple-element.135) | copy-start | bytes 4718596
  295.0 28.0 %copy-start.71 = (f32[512]{0:T(512)}, f32[512]{0:T(512)S(1)}, u32[]{:S(2)}) copy-start(f32[512]{0:T(512)S(1)} %add_rsqrt_fusion.1) | copy-start | bytes 6148
  313.2 9.8 copy-start.15
  313.2 9.8 copy-start.27
  331.5 9.6 copy-start.22
  331.5 9.6 copy-start.24
  331.5 19.2 %slice-start.3 = ((s8[12582912]{0:T(1024)(128)(4,1)}), s8[4194304]{0:T(1024)(128)(4,1)S(1)}, s32[]{:S(2)}) async-start(s8[12582912]{0:T(1024)(128)(4,1)} %bitcast.376), calls=%async_computation.29 | async-start | bytes 8388608
  331.5 19.2 %slice-start.4 = ((s8[12582912]{0:T(1024)(128)(4,1)}), s8[4194304]{0:T(1024)(128)(4,1)S(1)}, s32[]{:S(2)}) async-start(s8[12582912]{0:T(1024)(128)(4,1)} %bitcast.376), calls=%async_computation.30 | async-start | bytes 8388608
  341.1 9.7 slice-start.5
  375.5 142.0 %reduce-scatter.5.cloned.1.call-start = ((), (), s32[]{:S(2)}) async-start(), calls=%async_computation.14 | async-start | bytes 5308416 | tf_op jit(solution)/shard_map/reduce_scatter | solution.py:252
  382.1 12.8 %slice-start.6 = ((s8[9437184]{0:T(1024)(128)(4,1)}), s8[4194304]{0:T(1024)(128)(4,1)S(1)}, s32[]{:S(2)}) async-start(s8[9437184]{0:T(1024)(128)(4,1)} %bitcast.475), calls=%async_computation.32 | async-start | bytes 8388608
  404.0 9.2 copy-start.61
  404.0 10.0 %copy-start.23 = (bf16[512,768]{0,1:T(8,128)(2,1)S(1)}, bf16[512,768]{0,1:T(8,128)(2,1)}, u32[]{:S(2)}) copy-start(bf16[512,768]{0,1:T(8,128)(2,1)} %copy.194) | copy-start | bytes 2359300
  404.0 10.0 %copy-start.51 = (bf16[768,512]{1,0:T(8,128)(2,1)S(1)}, bf16[768,512]{1,0:T(8,128)(2,1)}, u32[]{:S(2)}) copy-start(bf16[768,512]{1,0:T(8,128)(2,1)} %add_convert_fusion.4) | copy-start | bytes 2359300
  413.2 12.0 %slice-start = ((s8[12582912]{0:T(1024)(128)(4,1)}), s8[4194304]{0:T(1024)(128)(4,1)S(1)}, s32[]{:S(2)}) async-start(s8[12582912]{0:T(1024)(128)(4,1)} %bitcast.374), calls=%async_computation.26 | async-start | bytes 8388608
  414.0 11.2 %slice-start.1 = ((s8[12582912]{0:T(1024)(128)(4,1)}), s8[4194304]{0:T(1024)(128)(4,1)S(1)}, s32[]{:S(2)}) async-start(s8[12582912]{0:T(1024)(128)(4,1)} %bitcast.374), calls=%async_computation.27 | async-start | bytes 8388608
  414.0 11.5 %slice-start.2 = ((s8[12582912]{0:T(1024)(128)(4,1)}), s8[4194304]{0:T(1024)(128)(4,1)S(1)}, s32[]{:S(2)}) async-start(s8[12582912]{0:T(1024)(128)(4,1)} %bitcast.374), calls=%async_computation.28 | async-start | bytes 8388608
  442.7 133.0 %reduce-scatter.11.cloned.1.call-start = ((), (), s32[]{:S(2)}) async-start(), calls=%async_computation.21 | async-start | bytes 10616832 | tf_op jit(solution)/shard_map/reduce_scatter | solution.py:260
  480.0 176.1 %reduce-scatter.9.cloned.1.call-start = ((), (), s32[]{:S(2)}) async-start(), calls=%async_computation.19 | async-start | bytes 10616832 | tf_op jit(solution)/shard_map/reduce_scatter | solution.py:260
  517.4 275.2 %all-reduce.6.cloned.1.call-start = ((), (), s32[]{:S(2)}) async-start(), calls=%async_computation.25 | async-start | bytes 7077888 | tf_op jit(solution)/shard_map/psum | solution.py:253
  656.2 262.2 %all-reduce.4.cloned.1.call-start = ((), (), s32[]{:S(2)}) async-start(), calls=%async_computation.18 | async-start | bytes 147456 | tf_op jit(solution)/shard_map/psum | solution.py:271
  658.0 294.1 %all-gather.19.cloned.1.call-start = ((), (), s32[]{:S(2)}) async-start(), calls=%async_computation.15 | async-start | bytes 1769472 | tf_op jit(solution)/shard_map/all_gather | solution.py:254
  792.6 161.1 %all-gather.21.cloned.1.call-start = ((), (), s32[]{:S(2)}) async-start(), calls=%async_computation.17 | async-start | bytes 1769472 | tf_op jit(solution)/shard_map/all_gather | solution.py:254
  804.3 19.2 %all-to-all-start.1 = ((bf16[4,2,49152]{2,1,0:T(2,128)(2,1)}), bf16[4,2,49152]{2,1,0:T(2,128)(2,1)}, u32[]{:S(2)}, u32[]{:S(2)}) async-start(bf16[4,2,49152]{2,1,0:T(2,128)(2,1)} %reshape.577), calls=%async_computation.1 | async-start | bytes 1572864 | tf_op jit(solution)/shard_map/all_to_all | solution.py:140
  808.5 150.4 %all-gather.23.cloned.1.call-start = ((), (), s32[]{:S(2)}) async-start(), calls=%async_computation.20 | async-start | bytes 3538944 | tf_op jit(solution)/shard_map/all_gather | solution.py:262
  823.6 96.4 %all-to-all-start.3 = ((bf16[4,2,49152]{2,1,0:T(2,128)(2,1)}), bf16[4,2,49152]{2,1,0:T(2,128)(2,1)}, u32[]{:S(2)}, u32[]{:S(2)}) async-start(bf16[4,2,49152]{2,1,0:T(2,128)(2,1)} %reshape.579), calls=%async_computation.3 | async-start | bytes 1572864 | tf_op jit(solution)/shard_map/all_to_all | solution.py:140
  920.0 15.5 %all-to-all-start.7 = ((bf16[4,2,49152]{2,1,0:T(2,128)(2,1)}), bf16[4,2,49152]{2,1,0:T(2,128)(2,1)S(1)}, u32[]{:S(2)}, u32[]{:S(2)}) async-start(bf16[4,2,49152]{2,1,0:T(2,128)(2,1)} %reshape.583), calls=%async_computation.7 | async-start | bytes 1572864 | tf_op jit(solution)/shard_map/all_to_all | solution.py:140
  923.5 46.8 %all-gather.25.cloned.1.call-start = ((), (), s32[]{:S(2)}) async-start(), calls=%async_computation.22 | async-start | bytes 3538944 | tf_op jit(solution)/shard_map/all_gather | solution.py:262
  935.5 14.9 %all-to-all-start.6 = ((bf16[4,2,49152]{2,1,0:T(2,128)(2,1)}), bf16[4,2,49152]{2,1,0:T(2,128)(2,1)S(1)}, u32[]{:S(2)}, u32[]{:S(2)}) async-start(bf16[4,2,49152]{2,1,0:T(2,128)(2,1)} %reshape.581), calls=%async_computation.6 | async-start | bytes 1572864 | tf_op jit(solution)/shard_map/all_to_all | solution.py:140
  (90 other events, 341.5 us)
Sparse Core Ops, SparseCore 0:
  11.0 58.3 all-gather.26
  71.8 45.9 all-gather.28
  120.2 58.6 all-gather.14
  181.2 60.4 all-gather.16
  375.6 52.3 reduce-scatter.6
  442.8 52.5 reduce-scatter.4
  498.9 76.8 reduce-scatter.10
  579.2 76.8 reduce-scatter.8
  658.7 133.8 all-reduce.5
  798.6 119.6 all-reduce.3
  919.9 11.2 all-gather.18
  932.6 10.3 all-gather.20
  944.6 12.1 all-gather.22
  958.1 12.1 all-gather.24

commit v2 on v1

v2 whole, which is shorter than its diff:
```python
import math

import jax
import jax.numpy as jnp
from jax import lax
from jax.experimental import pallas as pl
from jax.experimental.pallas import tpu as pltpu
from jax.sharding import PartitionSpec as P

HEAD_DIM = 64
EPSILON = 1e-12
LOSS_WEIGHT = 8.0
HIGHEST = lax.Precision.HIGHEST
MASKED = -1e30
BF = jnp.bfloat16
F32 = jnp.float32
PLANE = ("span", "tensor")
MESH = pl.DeviceIdType.MESH
TENSORS = 4
MAIN, DIAG, SWAP = "main", "diag", "swap"


def mm(a, b, ca, cb):
    return lax.dot_general(a, b, (((ca,), (cb,)), ((), ())), preferred_element_type=F32)


def normal_parts(values):
    centred = values - jnp.mean(values, axis=-1, keepdims=True)
    spread = jnp.mean(centred * centred, axis=-1, keepdims=True)
    scale = lax.rsqrt(spread + EPSILON)
    return centred * scale, scale


def normal_back(upward, normed, scale, gain):
    weighted = upward * gain
    first = jnp.mean(weighted, axis=-1, keepdims=True)
    second = jnp.mean(weighted * normed, axis=-1, keepdims=True)
    return (weighted - first - normed * second) * scale


def gelu_parts(hidden):
    phi = 0.5 * (1.0 + lax.erf(hidden * math.sqrt(0.5)))
    slope = phi + hidden * jnp.exp(-0.5 * hidden * hidden) * (1.0 / math.sqrt(2.0 * math.pi))
    return hidden * phi, slope


def to_rows(values):
    return lax.all_to_all(values, "tensor", split_axis=0, concat_axis=1, tiled=True)[0]


def to_places(values):
    return lax.all_to_all(values[None], "tensor", split_axis=1, concat_axis=0, tiled=True)


def plane_pairs(kind):
    pairs = []
    for side in range(2):
        for t in range(TENSORS):
            if kind == SWAP:
                target = (1 - side, t)
            elif kind == MAIN:
                target = (side, t ^ (1 + side))
            else:
                target = (side, t ^ (2 - side))
            pairs.append((side * TENSORS + t, target[0] * TENSORS + target[1]))
    return pairs


def send(values, kind):
    return lax.ppermute(values, PLANE, plane_pairs(kind))


def plus(*terms):
    total = terms[0].astype(F32)
    for term in terms[1:]:
        total = total + term.astype(F32)
    return total.astype(BF)


def gather_part(part, side):
    half = part.shape[0] // 2
    got = send(part, MAIN)
    piece = lax.dynamic_slice(got, (side * half, 0), (half, part.shape[1]))
    across = send(piece, DIAG)
    other = send(got, SWAP)
    rest = send(across, SWAP)
    lower = jnp.where(side == 0, across, rest)
    upper = jnp.where(side == 0, rest, across)
    return [part, got, other, jnp.concatenate([lower, upper], axis=0)], across


def sum_over_dp(values):
    count = lax.axis_size("dp")
    place = lax.axis_index("dp")
    width = values.shape[1]
    bits = []
    bit = 1
    while bit < count:
        pairs = [(d, d ^ bit) for d in range(count)]
        half = values.shape[0] // 2
        up = (place // bit) % 2
        away = lax.dynamic_slice(values, ((1 - up) * half, 0), (half, width))
        kept = lax.dynamic_slice(values, (up * half, 0), (half, width))
        values = plus(kept, lax.ppermute(away, "dp", pairs))
        bits.append((pairs, up))
        bit *= 2
    for pairs, up in reversed(bits):
        got = lax.ppermute(values, "dp", pairs)
        values = jnp.concatenate(
            [jnp.where(up == 0, values, got), jnp.where(up == 0, got, values)], axis=0
        )
    return values


def reduce_part(own, rest):
    outgoing = jnp.stack([own[2], rest[2], rest[3], rest[0]])
    got = send(outgoing, SWAP)
    main_rest = plus(rest[1], got[0])
    main_own = plus(own[1], got[1])
    across = plus(own[3], got[2])
    mine = plus(own[0], got[3])
    from_rest = send(main_rest, MAIN)
    main_own = plus(main_own, send(across, DIAG))
    from_own = send(main_own, MAIN)
    return plus(mine, from_own, send(from_rest, SWAP))


def finish_part(mine, side):
    mine = sum_over_dp(mine)
    other = send(mine, SWAP)
    low = jnp.where(side == 0, mine, other).astype(F32)
    high = jnp.where(side == 0, other, mine).astype(F32)
    return low, high


Q_ROWS = 128


def attend_forward_kernel(qkv_ref, down_ref, across_ref, o_ref, lse_ref):
    tokens, width = o_ref.shape

    def step(i, carry):
        rows = pl.ds(pl.multiple_of(i * Q_ROWS, Q_ROWS), Q_ROWS)
        same = down_ref[rows, :] == across_ref[...]
        for h in range(width // HEAD_DIM):
            at = h * HEAD_DIM
            q = qkv_ref[rows, at : at + HEAD_DIM]
            k = qkv_ref[:, width + at : width + at + HEAD_DIM]
            v = qkv_ref[:, 2 * width + at : 2 * width + at + HEAD_DIM]
            s = mm(q, k, 1, 1) * 0.125
            s = jnp.where(same, s, MASKED)
            top = jnp.max(s, axis=-1, keepdims=True)
            raised = jnp.exp(s - top)
            total = jnp.sum(raised, axis=-1, keepdims=True)
            weights = (raised * (1.0 / total)).astype(BF)
            o_ref[rows, at : at + HEAD_DIM] = mm(weights, v, 1, 0).astype(BF)
            lse_ref[rows, h : h + 1] = top + jnp.log(total)
        return carry

    lax.fori_loop(0, tokens // Q_ROWS, step, 0)


def attend_backward_kernel(qkv_ref, do_ref, lse_ref, down_ref, across_ref, d_ref, dk_ref, dv_ref):
    tokens, width = do_ref.shape
    dk_ref[...] = jnp.zeros_like(dk_ref)
    dv_ref[...] = jnp.zeros_like(dv_ref)

    def step(i, carry):
        rows = pl.ds(pl.multiple_of(i * Q_ROWS, Q_ROWS), Q_ROWS)
        same = down_ref[rows, :] == across_ref[...]
        for h in range(width // HEAD_DIM):
            at = h * HEAD_DIM
            q = qkv_ref[rows, at : at + HEAD_DIM]
            k = qkv_ref[:, width + at : width + at + HEAD_DIM]
            v = qkv_ref[:, 2 * width + at : 2 * width + at + HEAD_DIM]
            up = do_ref[rows, at : at + HEAD_DIM]
            s = mm(q, k, 1, 1) * 0.125
            s = jnp.where(same, s, MASKED)
            pr = jnp.exp(s - lse_ref[rows, h : h + 1])
            dp = mm(up, v, 1, 1)
            inner = jnp.sum(pr * dp, axis=-1, keepdims=True)
            ds = (pr * (dp - inner)).astype(BF)
            d_ref[rows, at : at + HEAD_DIM] = (mm(ds, k, 1, 0) * 0.125).astype(BF)
            dk_ref[:, at : at + HEAD_DIM] += mm(ds, q, 0, 0)
            dv_ref[:, at : at + HEAD_DIM] += mm(pr.astype(BF), up, 0, 0)
        return carry

    lax.fori_loop(0, tokens // Q_ROWS, step, 0)
    d_ref[:, width : 2 * width] = (dk_ref[...] * 0.125).astype(BF)
    d_ref[:, 2 * width :] = dv_ref[...].astype(BF)


def attend_cost(tokens, width, products):
    heads = width // HEAD_DIM
    return pl.CostEstimate(
        flops=2 * products * tokens * tokens * width,
        bytes_accessed=2 * 8 * tokens * width,
        transcendentals=heads * tokens * tokens,
    )


def attend_forward(qkv, down, across):
    tokens = qkv.shape[0]
    width = qkv.shape[1] // 3
    return pl.pallas_call(
        attend_forward_kernel,
        name="attend_forward",
        out_shape=(
            jax.ShapeDtypeStruct((tokens, width), BF),
            jax.ShapeDtypeStruct((tokens, width // HEAD_DIM), F32),
        ),
        compiler_params=pltpu.CompilerParams(vmem_limit_bytes=24 << 20),
        cost_estimate=attend_cost(tokens, width, 2),
    )(qkv, down, across)


def attend_backward(qkv, do, lse, down, across):
    tokens, width = do.shape
    return pl.pallas_call(
        attend_backward_kernel,
        name="attend_backward",
        out_shape=jax.ShapeDtypeStruct(qkv.shape, BF),
        scratch_shapes=[pltpu.VMEM((tokens, width), F32), pltpu.VMEM((tokens, width), F32)],
        compiler_params=pltpu.CompilerParams(vmem_limit_bytes=24 << 20),
        cost_estimate=attend_cost(tokens, width, 5),
    )(qkv, do, lse, down, across)


def anchors_kernel(dps, planes, x_ref, out_ref, near_send, near_recv, far_send, far_recv, own_sem):
    dp = lax.axis_index("dp")
    me = lax.axis_index("span") * TENSORS + lax.axis_index("tensor")

    def near(k):
        peer = lax.rem(me + k, planes)
        return {"span": peer // TENSORS, "tensor": lax.rem(peer, TENSORS)}

    def far(k):
        return {"dp": lax.rem(dp + k, dps)}

    barrier = pltpu.get_barrier_semaphore()
    for k in range(1, planes):
        pl.semaphore_signal(barrier, inc=1, device_id=near(k), device_id_type=MESH)
    for k in range(1, dps):
        pl.semaphore_signal(barrier, inc=1, device_id=far(k), device_id_type=MESH)
    pl.semaphore_wait(barrier, planes + dps - 2)

    own = pltpu.make_async_copy(x_ref, out_ref.at[dp, me], own_sem)
    own.start()

    def near_copy(k):
        return pltpu.make_async_remote_copy(
            src_ref=x_ref, dst_ref=out_ref.at[dp, me], send_sem=near_send.at[k],
            recv_sem=near_recv.at[k], device_id=near(k), device_id_type=MESH,
        )

    def far_copy(k):
        return pltpu.make_async_remote_copy(
            src_ref=out_ref.at[dp], dst_ref=out_ref.at[dp], send_sem=far_send.at[k],
            recv_sem=far_recv.at[k], device_id=far(k), device_id_type=MESH,
        )

    for k in range(1, planes):
        near_copy(k).start()
    own.wait()
    for k in range(1, planes):
        near_copy(k).wait()
    for k in range(1, dps):
        far_copy(k).start()
    for k in range(1, dps):
        far_copy(k).wait()


def gather_anchors(values):
    dps = lax.axis_size("dp")
    planes = lax.axis_size("span") * lax.axis_size("tensor")
    dma = pltpu.SemaphoreType.DMA
    vmem = pl.BlockSpec(memory_space=pltpu.VMEM)

    def body(*refs):
        anchors_kernel(dps, planes, *refs)

    return pl.pallas_call(
        body,
        name="gather_anchors",
        out_shape=jax.ShapeDtypeStruct((dps, planes) + values.shape, values.dtype),
        in_specs=[vmem],
        out_specs=vmem,
        scratch_shapes=[dma((planes,)), dma((planes,)), dma((dps,)), dma((dps,)), dma],
        compiler_params=pltpu.CompilerParams(collective_id=0, has_side_effects=True),
    )(values)


def total_kernel(
    dps, planes, x_ref, out_ref, parts, sums, one_send, one_recv, two_send, two_recv, three_send, three_recv
):
    dp = lax.axis_index("dp")
    me = lax.axis_index("span") * TENSORS + lax.axis_index("tensor")

    def near_peer(k):
        return lax.rem(me + k, planes)

    def near(k):
        peer = near_peer(k)
        return {"span": peer // TENSORS, "tensor": lax.rem(peer, TENSORS)}

    def far(k):
        return {"dp": lax.rem(dp + k, dps)}

    barrier = pltpu.get_barrier_semaphore()
    for k in range(1, planes):
        pl.semaphore_signal(barrier, inc=1, device_id=near(k), device_id_type=MESH)
    for k in range(1, dps):
        pl.semaphore_signal(barrier, inc=1, device_id=far(k), device_id_type=MESH)
    pl.semaphore_wait(barrier, planes + dps - 2)

    def one(k):
        return pltpu.make_async_remote_copy(
            src_ref=x_ref.at[near_peer(k)], dst_ref=parts.at[k], send_sem=one_send.at[k],
            recv_sem=one_recv.at[k], device_id=near(k), device_id_type=MESH,
        )

    def two(k):
        return pltpu.make_async_remote_copy(
            src_ref=sums.at[dp], dst_ref=sums.at[dp], send_sem=two_send.at[k],
            recv_sem=two_recv.at[k], device_id=far(k), device_id_type=MESH,
        )

    def three(k):
        return pltpu.make_async_remote_copy(
            src_ref=out_ref.at[me], dst_ref=out_ref.at[me], send_sem=three_send.at[k],
            recv_sem=three_recv.at[k], device_id=near(k), device_id_type=MESH,
        )

    for k in range(1, planes):
        one(k).start()
    for k in range(1, planes):
        one(k).wait()
    total = x_ref[me]
    for k in range(1, planes):
        total = total + parts[k]
    sums[dp] = total
    for k in range(1, dps):
        two(k).start()
    for k in range(1, dps):
        two(k).wait()
    total = sums[0]
    for k in range(1, dps):
        total = total + sums[k]
    out_ref[me] = total
    for k in range(1, planes):
        three(k).start()
    for k in range(1, planes):
        three(k).wait()


def total_over_all(flat):
    dps = lax.axis_size("dp")
    planes = lax.axis_size("span") * lax.axis_size("tensor")
    lanes = 128
    unit = planes * 8 * lanes
    size = flat.shape[0]
    padded = -(-size // unit) * unit
    flat = jnp.pad(flat, (0, padded - size)).reshape(planes, padded // (planes * lanes), lanes)
    dma = pltpu.SemaphoreType.DMA
    vmem = pl.BlockSpec(memory_space=pltpu.VMEM)

    def body(*refs):
        total_kernel(dps, planes, *refs)

    out = pl.pallas_call(
        body,
        name="total_over_all",
        out_shape=jax.ShapeDtypeStruct(flat.shape, F32),
        in_specs=[vmem],
        out_specs=vmem,
        scratch_shapes=[
            pltpu.VMEM(flat.shape, F32),
            pltpu.VMEM((dps,) + flat.shape[1:], F32),
            dma((planes,)), dma((planes,)), dma((dps,)), dma((dps,)), dma((planes,)), dma((planes,)),
        ],
        compiler_params=pltpu.CompilerParams(collective_id=1, has_side_effects=True),
    )(flat)
    return out.reshape(-1)[:size]


def layer_forward(x, seg, attn_w, ffn_w, vec):
    down, across = seg
    xb = x.astype(BF)
    cols = vec["heads"][0].shape[0]
    qkv, o, lse = [], [], []
    z1 = x + vec["pb"]
    for w, bias in zip(attn_w, vec["heads"]):
        qkv.append((mm(xb, w[:cols], 1, 1) + bias).astype(BF))
        mixed, total = attend_forward(qkv[-1], down, across)
        o.append(mixed)
        lse.append(total)
        z1 = z1 + mm(mixed, w[cols : cols + cols // 3], 1, 0)
    n1, r1 = normal_parts(z1)
    y = n1 * vec["g0"] + vec["s0"]
    yb = y.astype(BF)
    width = x.shape[1]
    act, slope = [], []
    z2 = y + vec["sb"]
    for w, bias in zip(ffn_w, vec["eb"]):
        hid = mm(yb, w[:width], 1, 0) + bias
        a, b = gelu_parts(hid)
        act.append(a.astype(BF))
        slope.append(b.astype(BF))
        z2 = z2 + mm(act[-1], w[width:], 1, 0)
    n2, r2 = normal_parts(z2)
    out = n2 * vec["g1"] + vec["s1"]
    return out, (xb, qkv, o, lse, n1, r1, yb, act, slope, n2, r2)


def halves(values, side):
    half = values.shape[1] // 2
    rows = values.shape[0]
    own = lax.dynamic_slice(values, (0, side * half), (rows, half))
    rest = lax.dynamic_slice(values, (0, (1 - side) * half), (rows, half))
    return own, rest


def ffn_backward(dout, ffn_w, vec, kept, side):
    xb, qkv, o, lse, n1, r1, yb, act, slope, n2, r2 = kept
    width = yb.shape[1]
    dz2 = normal_back(dout, n2, r2, vec["g1"])
    dgain1 = jnp.sum(dout * n2, axis=0)
    dshift1 = jnp.sum(dout, axis=0)
    dsb = jnp.sum(dz2, axis=0)
    dzb = dz2.astype(BF)
    yb_halves = halves(yb, side)
    parts = ([], [])
    dy = dz2
    deb = []
    for w, a, b in zip(ffn_w, act, slope):
        dhid = mm(dzb, w[width:], 1, 1) * b.astype(F32)
        deb.append(jnp.sum(dhid, axis=0))
        dhb = dhid.astype(BF)
        dy = dy + mm(dhb, w[:width], 1, 1)
        for part, y_half, a_half in zip(parts, yb_halves, halves(a, side)):
            part.append((mm(y_half, dhb, 0, 0).astype(BF), mm(a_half, dzb, 0, 0).astype(BF)))
    return dy, parts, {"g1": dgain1, "s1": dshift1, "sb": dsb, "eb": jnp.stack(deb)}


def attn_backward(dy, seg, attn_w, vec, kept, side):
    xb, qkv, o, lse, n1, r1, yb, act, slope, n2, r2 = kept
    down, across = seg
    cols = vec["heads"][0].shape[0]
    dz1 = normal_back(dy, n1, r1, vec["g0"])
    dgain0 = jnp.sum(dy * n1, axis=0)
    dshift0 = jnp.sum(dy, axis=0)
    dpb = jnp.sum(dz1, axis=0)
    da = dz1.astype(BF)
    x_halves = halves(xb, side)
    da_halves = halves(da, side)
    parts = ([], [])
    dhead = []
    dx = dz1
    for w, qkv_j, o_j, lse_j in zip(attn_w, qkv, o, lse):
        do = mm(da, w[cols : cols + cols // 3], 1, 1).astype(BF)
        d = attend_backward(qkv_j, do, lse_j, down, across)
        dx = dx + mm(d, w[:cols], 1, 0)
        dhead.append(jnp.sum(d.astype(F32), axis=0))
        for part, x_half, da_half in zip(parts, x_halves, da_halves):
            top = mm(d, x_half, 0, 0).astype(BF)
            low = mm(o_j, da_half, 0, 0).astype(BF)
            part.append((top, low))
    small = {"g0": dgain0, "s0": dshift0, "pb": dpb, "heads": jnp.stack(dhead)}
    return dx, parts, small


def pack_ffn(parts):
    return [[jnp.concatenate([e, s], axis=0) for e, s in part] for part in parts]


def pack_attn(parts):
    packed = []
    for part in parts:
        rows = []
        for top, low in part:
            whole = jnp.concatenate([top, low], axis=0)
            half = whole.shape[0] // 2
            rows.append(jnp.concatenate([whole[:half], whole[half:]], axis=1))
        packed.append(rows)
    return packed


def unpack_ffn(low, high):
    rows = low.shape[0] // 2
    expand = jnp.concatenate([low[:rows], high[:rows]], axis=0)
    shrink = jnp.concatenate([low[rows:], high[rows:]], axis=0)
    return expand, shrink


def unpack_attn(low, high):
    half = low.shape[1] // 2
    upper = jnp.concatenate([low[:, :half], high[:, :half]], axis=1)
    lower = jnp.concatenate([low[:, half:], high[:, half:]], axis=1)
    cols = low.shape[0] // 2
    heads = jnp.stack([upper[:cols], upper[cols:], lower[:cols]])
    return jnp.swapaxes(heads, 1, 2), lower[cols:]


VECTORS = ("pb", "g0", "g1", "s0", "s1", "sb")


def shards(
    layer_input, skip_tokens, backbone_cotangent, head_cotangent, segment_lengths, pair_index,
    w_heads, heads_bias, w_project, project_bias, norm_gain, norm_shift,
    w_expand, expand_bias, w_shrink, shrink_bias,
):
    side = lax.axis_index("span")
    mine = lax.axis_index("tensor")
    width = layer_input.shape[-1]
    head_cols = w_heads.shape[-1]
    ff_cols = w_expand.shape[-1]

    def attn_rows(l):
        heads = jnp.swapaxes(w_heads[l], 1, 2).reshape(3 * head_cols, width)
        return jnp.concatenate([heads, w_project[l]], axis=0)

    def ffn_rows(l):
        return jnp.concatenate([w_expand[l], w_shrink[l]], axis=0)

    bias_rows = jnp.concatenate([heads_bias.reshape(1, 4 * head_cols), expand_bias], axis=0)
    bias_rows = jnp.pad(bias_rows, ((0, 32 - bias_rows.shape[0]), (0, 0)))
    attn_rows_count = 4 * head_cols

    attn_w0, mark = gather_part(jnp.concatenate([attn_rows(0), bias_rows], axis=0), side)
    x = to_rows(layer_input[0])
    payload, mark = lax.optimization_barrier((ffn_rows(0), mark))
    ffn_w0, mark = gather_part(payload, side)
    payload, mark = lax.optimization_barrier(
        (jnp.concatenate([attn_rows(1), ffn_rows(1)], axis=0), mark)
    )
    w1, mark = gather_part(payload, side)
    attn_w1 = [w[:attn_rows_count] for w in w1]
    ffn_w1 = [w[attn_rows_count:] for w in w1]

    skip = to_rows(skip_tokens[0])
    backbone_cot = to_rows(backbone_cotangent[0])
    head_cot = to_rows(head_cotangent[0])
    tokens = x.shape[0]

    biases = [w[attn_rows_count : attn_rows_count + 3].astype(F32) for w in attn_w0]

    def vectors(l):
        heads = []
        for b in biases:
            own = b[0].reshape(2, 2, head_cols)[l]
            heads.append(jnp.concatenate([own[0], jnp.zeros_like(own[0]), own[1]]))
        return {
            "heads": heads, "eb": [b[1 + l] for b in biases], "pb": project_bias[l].astype(F32),
            "g0": norm_gain[l, 0].astype(F32), "g1": norm_gain[l, 1].astype(F32),
            "s0": norm_shift[l, 0].astype(F32), "s1": norm_shift[l, 1].astype(F32),
            "sb": shrink_bias[l].astype(F32),
        }

    lengths = lax.dynamic_index_in_dim(segment_lengths[0], mine, 0, keepdims=False)
    span_count = lengths.shape[0]
    starts = jnp.cumsum(lengths) - lengths
    row_length = jnp.sum(lengths)
    places = jnp.arange(tokens, dtype=jnp.int32)
    counted = jnp.sum((places[:, None] >= starts[None, :]).astype(jnp.int32), axis=-1) - 1
    segment = jnp.where(places < row_length, counted, span_count)
    seg = (segment[:, None], segment[None, :])
    valid = (places < row_length).astype(F32)[:, None]
    picker = (starts[:, None] == places[None, :]).astype(F32)
    first = jnp.sum(picker, axis=0)[:, None] > 0

    vec0, vec1 = vectors(0), vectors(1)
    backbone, kept0 = layer_forward(x.astype(F32), seg, attn_w0, ffn_w0, vec0)
    cls = mm(picker.astype(BF), backbone.astype(BF), 1, 0).astype(BF)
    anchors = gather_anchors(cls)
    dp_count = lax.axis_size("dp")
    pair_count = lax.axis_size("span")
    vector_count = dp_count * TENSORS * span_count
    anchors = anchors.reshape(dp_count, pair_count, TENSORS * span_count, width)
    anchors = jnp.swapaxes(anchors, 0, 1).reshape(pair_count, vector_count, width)

    head_in = jnp.where(first, backbone, skip.astype(F32))
    head, kept1 = layer_forward(head_in, seg, attn_w1, ffn_w1, vec1)

    root = math.sqrt(width)
    logits = mm(anchors[0], anchors[1], 1, 1) / root
    columns = jnp.arange(vector_count, dtype=jnp.int32)
    target = (pair_index[:, None] == columns[None, :]).astype(F32)
    lse_rows = jax.nn.logsumexp(logits, axis=1)
    lse_cols = jax.nn.logsumexp(logits, axis=0)
    dlogits = LOSS_WEIGHT * (
        jnp.exp(logits - lse_rows[:, None]) + jnp.exp(logits - lse_cols[None, :]) - 2.0 * target
    )
    span_loss = (jnp.sum(lse_rows) + jnp.sum(lse_cols) - 2.0 * jnp.sum(target * logits)) / (
        2 * vector_count
    )
    own = (lax.axis_index("dp") * TENSORS + mine) * span_count
    wanted = jnp.where(side == 0, dlogits, dlogits.T)
    wanted = lax.dynamic_slice(wanted, (own, 0), (span_count, vector_count))
    other = lax.dynamic_index_in_dim(anchors, 1 - side, 0, keepdims=False).astype(F32)
    dcls = jnp.dot(wanted, other, precision=HIGHEST) / root

    dy1, ffn_parts1, small1 = ffn_backward(head_cot.astype(F32) * valid, ffn_w1, vec1, kept1, side)
    du, attn_parts1, more1 = attn_backward(dy1, seg, attn_w1, vec1, kept1, side)
    small1.update(more1)
    grad_skip = jnp.where(first, 0.0, du).astype(BF)
    attn_packed = pack_attn(attn_parts1)
    ffn_packed = pack_ffn(ffn_parts1)
    packed1 = [
        [jnp.concatenate([a, f], axis=0) for a, f in zip(a_part, f_part)]
        for a_part, f_part in zip(attn_packed, ffn_packed)
    ]
    sum1 = reduce_part(*packed1)

    seed = backbone_cot.astype(F32) * valid + jnp.where(first, du, 0.0)
    seed = seed + jnp.dot(picker.T, dcls, precision=HIGHEST)
    dy0, ffn_parts0, small0 = ffn_backward(seed, ffn_w0, vec0, kept0, side)
    ffn_sum0 = reduce_part(*pack_ffn(ffn_parts0))
    dx, attn_parts0, more0 = attn_backward(dy0, seg, attn_w0, vec0, kept0, side)
    small0.update(more0)
    attn_sum0 = reduce_part(*pack_attn(attn_parts0))

    order = jnp.where(
        side == 0,
        jnp.stack([mine, mine ^ 1, mine ^ 2, mine ^ 3]),
        jnp.stack([mine, mine ^ 2, mine ^ 1, mine ^ 3]),
    )
    chosen = (order[None, :] == jnp.arange(TENSORS, dtype=order.dtype)[:, None]).astype(F32)

    def placed(values):
        return jnp.sum(chosen[:, :, None] * values[None], axis=1)

    flat = []
    for small in (small0, small1):
        flat += [small[k] for k in VECTORS]
        flat += [placed(small["heads"]).reshape(-1), placed(small["eb"]).reshape(-1)]
    sizes = [f.shape[0] for f in flat]
    total = total_over_all(jnp.concatenate(flat))
    cuts = []
    at = 0
    for size in sizes:
        cuts.append(total[at : at + size])
        at += size
    count = len(VECTORS) + 2
    sums = [dict(zip(VECTORS + ("heads", "eb"), cuts[l * count : (l + 1) * count])) for l in range(2)]

    def local(values):
        size = values.shape[0] // TENSORS
        return lax.dynamic_slice(values, (mine * size,), (size,))

    hb, eb = [], []
    for s in sums:
        h = local(s["heads"]).reshape(3, head_cols)
        hb.append(jnp.stack([h[0], h[2]]))
        eb.append(local(s["eb"]))

    low1, high1 = finish_part(sum1, side)
    half_rows = attn_rows_count // 2
    gh1, gp1 = unpack_attn(low1[:half_rows], high1[:half_rows])
    ge1, gs1 = unpack_ffn(low1[half_rows:], high1[half_rows:])
    ge0, gs0 = unpack_ffn(*finish_part(ffn_sum0, side))
    gh0, gp0 = unpack_attn(*finish_part(attn_sum0, side))

    return (
        to_places((backbone * valid).astype(BF))[None],
        to_places((head * valid).astype(BF))[None],
        span_loss,
        to_places(dx.astype(BF))[None],
        to_places(grad_skip)[None],
        jnp.stack([gh0, gh1]),
        jnp.stack(hb),
        jnp.stack([gp0, gp1]),
        jnp.stack([s["pb"] for s in sums]),
        jnp.stack([jnp.stack([s["g0"], s["g1"]]) for s in sums]),
        jnp.stack([jnp.stack([s["s0"], s["s1"]]) for s in sums]),
        jnp.stack([ge0, ge1]),
        jnp.stack(eb),
        jnp.stack([gs0, gs1]),
        jnp.stack([s["sb"] for s in sums]),
    )


def solution(mesh):
    rows = P("span", "dp", "tensor", None)
    in_specs = (
        rows, rows, rows, rows, P("span", "dp", None), P(),
        P(None, None, None, "tensor"), P(None, None, "tensor"), P(None, "tensor", None),
        P(), P(), P(), P(None, None, "tensor"), P(None, "tensor"), P(None, "tensor", None), P(),
    )
    out_specs = (
        rows, rows, P(), rows, rows,
        P(None, None, None, "tensor"), P(None, None, "tensor"), P(None, "tensor", None),
        P(), P(), P(), P(None, None, "tensor"), P(None, "tensor"), P(None, "tensor", None), P(),
    )
    return jax.shard_map(shards, mesh=mesh, in_specs=in_specs, out_specs=out_specs, check_vma=False)
```

time: 992 us -> 848 us (0.85)
  waiting for transfers between devices: 462 us -> 205 us
  Pallas kernels: 0 us -> 127 us
  blocking collectives: 85.4 us -> 0 us
  local copies, waits for them, and re-layouts: 102 us -> 137 us
  starting transfers between devices: 34.9 us -> 67.1 us
  between operations: 19.5 us -> 7.89 us
    psum x2 -> x0, waiting for transfers between devices: 206 us -> none  [the longest x1 135 us: reduce_attn(): part = lax.psum(part, 'dp')]
    ppermute x0 -> x42, waiting for transfers between devices: none -> 202 us  [the longest x30 116 us: send(): return lax.ppermute(values, PLANE, plane_pairs(kind))]
    reduce_scatter x4 -> x0, waiting for transfers between devices: 139 us -> none  [the longest x2 139 us: reduce_ffn(): part = lax.psum_scatter(packed, BOTH, scatter_dimension=0, tiled=False)]
    dot_general x26 -> x130, matrix products: 43.4 us -> 181 us  [mm(): lax.dot_general(a, b, (((ca,), (cb,)), ((), ())), preferred_element_type=...]
    dot_general x24 -> x0, matrix products: 132 us -> none  [the longest x2 20.8 us: attend_backward(): jnp.einsum('qhd,khd->hqk', uh, vh, preferred_element_type=F32)]
    pallas_call x0 -> x18, Pallas kernels: none -> 127 us  [the longest x8 50.5 us: attend_backward(): pl.pallas_call(attend_backward_kernel, name='attend_backward', out_shape=...]
    all_gather x8 -> x0, waiting for transfers between devices: 106 us -> none  [the longest x2 56.6 us: gather_ffn(): lax.all_gather(jnp.where(side == 0, w_expand[l], w_shrink[l]), BOTH, axis...]
    all_gather x2 -> x0, blocking collectives: 85.4 us -> none  [the longest x1 69.3 us: shards(): anchors = lax.all_gather(cls, ('dp', 'span', 'tensor'), axis=0, tiled=False)]
  transfers between devices with their start and end apart: 22 -> 50, of which waited for: 10 -> 20; matrix products, arithmetic and copies ran while one was open for 36% -> 29% of each run, Pallas kernels for 0% -> 10%
where the time goes in v2:
time: 848 us; the launch traced here: 836 us
  waiting for transfers between devices  205 us (24%)
  matrix products  187 us (22%)
  local copies, waits for them, and re-layouts  137 us (16%)
  Pallas kernels  127 us (15%)
  other arithmetic  105 us (12%)
  starting transfers between devices  67.1 us (8%)
    dot_general x130, matrix products, mm(): lax.dot_general(a, b, (((ca,), (cb,)), ((), ())), preferred_element_type=...  181 us
    ppermute x30, waiting for transfers between devices, send(): return lax.ppermute(values, PLANE, plane_pairs(kind))  116 us
    unnamed x635, local copies, waits for them, and re-layouts  82 us
    ppermute x6, waiting for transfers between devices, sum_over_dp(): got = lax.ppermute(values, 'dp', pairs)  61.1 us
    pallas_call x8, Pallas kernels, attend_backward(): pl.pallas_call(attend_backward_kernel, name='attend_backward', out_shape=...  50.5 us
    pallas_call x8, Pallas kernels, attend_forward(): pl.pallas_call(attend_forward_kernel, name='attend_forward', out_shape=(j...  41.6 us
    unnamed x5, other arithmetic  26.8 us
    ppermute x30, starting transfers between devices, send(): return lax.ppermute(values, PLANE, plane_pairs(kind))  25.1 us
  transfers between devices with their start and end apart: 50, of which 20 were waited for; matrix products, arithmetic and copies ran while one was open for 29% of the time, Pallas kernels for 10%

profile of v2, /device:TPU:0, one launch (start us, length us, event | category | flops | bytes accessed | tf_op | source)
XLA Modules:
  0.0 836.0 jit_solution(6675525143449882541)
XLA Ops:
  9.2 3.5 all-to-all-start.5
  35.4 3.5 all-to-all-start
  39.8 6.9 collective-permute-done.2
  54.4 5.2 all-to-all-start.2
  61.7 5.2 attend_forward.11
  67.8 5.2 attend_forward.10
  75.8 5.2 attend_forward.9
  82.0 5.3 attend_forward.8
  95.8 11.4 %collective-permute-done.6 = bf16[768,768]{1,0:T(8,128)(2,1)S(1)} collective-permute-done((bf16[768,768]{1,0:T(8,128)(2,1)S(1)}, bf16[768,768]{1,0:T(8,128)(2,1)S(1)}, u32[]{:S(2)}, u32[]{:S(2)}) %collective-permute-start.6) | collective-permute-done | bytes 1179680 | tf_op jit(solution)/shard_map/ppermute | solution.py:70
  124.6 24.0 %collective-permute-done.8 = bf16[2304,768]{1,0:T(8,128)(2,1)S(1)} collective-permute-done((bf16[2304,768]{1,0:T(8,128)(2,1)S(1)}, bf16[2304,768]{1,0:T(8,128)(2,1)S(1)}, u32[]{:S(2)}, u32[]{:S(2)}) %collective-permute-start.8) | collective-permute-done | bytes 3538976 | tf_op jit(solution)/shard_map/ppermute | solution.py:70
  158.1 6.8 reduce.48
  166.0 4.2 all-to-all-start.1
  171.3 19.5 %gather_anchors.1 = bf16[4,8,4,768]{3,2,1,0:T(4,128)(2,1)} custom-call(bf16[4,768]{1,0:T(4,128)(2,1)} %convolution_convert_fusion.72.refs_0_), custom_call_target="tpu_custom_call" | custom-call | tf_op jit(solution)/shard_map/gather_anchors/pallas_call | solution.py:282
  198.5 5.2 attend_forward.12
  207.2 4.2 all-to-all-start.4
  217.3 5.2 attend_forward.13
  226.8 5.2 attend_forward.15
  234.8 5.2 attend_forward.14
  281.7 6.2 attend_backward.8
  291.2 6.3 attend_backward.10
  297.5 6.3 attend_backward.9
  315.3 6.3 attend_backward.11
  321.6 4.8 add_add_fusion.1
  326.5 4.9 multiply_reduce_fusion.2
  391.0 6.3 attend_backward.14
  405.7 6.2 attend_backward.15
  419.6 6.7 attend_backward.12
  448.7 6.3 attend_backward.13
  484.4 15.1 %total_over_all.1 = f32[8,24,128]{2,1,0:T(8,128)} custom-call(f32[8,24,128]{2,1,0:T(8,128)} %bitcast.426), custom_call_target="tpu_custom_call" | custom-call | tf_op jit(solution)/shard_map/total_over_all/pallas_call | solution.py:370
  505.8 7.3 reduce.49
  515.1 4.3 all-to-all-start.3
  574.0 21.1 %collective-permute-done.13 = bf16[384,768]{1,0:T(8,128)(2,1)S(1)} collective-permute-done((bf16[384,768]{1,0:T(8,128)(2,1)S(1)}, bf16[384,768]{1,0:T(8,128)(2,1)S(1)}, u32[]{:S(2)}, u32[]{:S(2)}) %collective-permute-start.13) | collective-permute-done | bytes 589856 | tf_op jit(solution)/shard_map/ppermute | solution.py:70
  605.9 6.8 collective-permute-done.15
  612.8 15.1 %collective-permute-done.33 = bf16[768,768]{1,0:T(8,128)(2,1)S(1)} collective-permute-done((bf16[768,768]{1,0:T(8,128)(2,1)S(1)}, bf16[768,768]{1,0:T(8,128)(2,1)S(1)}, u32[]{:S(2)}, u32[]{:S(2)}) %collective-permute-start.33) | collective-permute-done | bytes 1179680 | tf_op jit(solution)/shard_map/ppermute | solution.py:70
  630.9 13.7 %collective-permute-done.14 = bf16[384,768]{1,0:T(8,128)(2,1)S(1)} collective-permute-done((bf16[384,768]{1,0:T(8,128)(2,1)}, bf16[384,768]{1,0:T(8,128)(2,1)S(1)}, u32[]{:S(2)}, u32[]{:S(2)}) %collective-permute-start.14) | collective-permute-done | bytes 589856 | tf_op jit(solution)/shard_map/ppermute | solution.py:70
  648.7 8.6 %collective-permute-done.35 = bf16[768,768]{1,0:T(8,128)(2,1)S(1)} collective-permute-done((bf16[768,768]{1,0:T(8,128)(2,1)S(1)}, bf16[768,768]{1,0:T(8,128)(2,1)S(1)}, u32[]{:S(2)}, u32[]{:S(2)}) %collective-permute-start.35) | collective-permute-done | bytes 1179680 | tf_op jit(solution)/shard_map/ppermute | solution.py:70
  662.0 7.7 collective-permute-done.18
  670.5 8.6 %collective-permute-done.19 = bf16[96,768]{1,0:T(8,128)(2,1)S(1)} collective-permute-done((bf16[96,768]{1,0:T(8,128)(2,1)S(1)}, bf16[96,768]{1,0:T(8,128)(2,1)S(1)}, u32[]{:S(2)}, u32[]{:S(2)}) %collective-permute-start.19) | collective-permute-done | bytes 147488 | tf_op jit(solution)/shard_map/ppermute | solution.py:108
  683.5 5.4 collective-permute-done.24
  693.7 6.3 reduce.50
  704.8 6.3 reduce.51
  714.3 4.2 all-to-all-start.6
  728.6 3.7 all-to-all-start.7
  749.8 14.7 %collective-permute-done.28 = bf16[288,768]{1,0:T(8,128)(2,1)} collective-permute-done((bf16[288,768]{1,0:T(8,128)(2,1)}, bf16[288,768]{1,0:T(8,128)(2,1)}, u32[]{:S(2)}, u32[]{:S(2)}) %collective-permute-start.28) | collective-permute-done | bytes 442400 | tf_op jit(solution)/shard_map/ppermute | solution.py:104
  767.0 13.2 %collective-permute-done.39 = bf16[192,768]{1,0:T(8,128)(2,1)S(1)} collective-permute-done((bf16[192,768]{1,0:T(8,128)(2,1)S(1)}, bf16[192,768]{1,0:T(8,128)(2,1)S(1)}, u32[]{:S(2)}, u32[]{:S(2)}) %collective-permute-start.39) | collective-permute-done | bytes 294944 | tf_op jit(solution)/shard_map/ppermute | solution.py:108
  780.4 8.5 %collective-permute-done.29 = bf16[288,768]{1,0:T(8,128)(2,1)S(1)} collective-permute-done((bf16[288,768]{1,0:T(8,128)(2,1)S(1)}, bf16[288,768]{1,0:T(8,128)(2,1)S(1)}, u32[]{:S(2)}, u32[]{:S(2)}) %collective-permute-start.29) | collective-permute-done | bytes 442400 | tf_op jit(solution)/shard_map/ppermute | solution.py:108
  789.2 12.3 %collective-permute-done.40 = bf16[384,768]{1,0:T(8,128)(2,1)S(1)} collective-permute-done((bf16[384,768]{1,0:T(8,128)(2,1)S(1)}, bf16[384,768]{1,0:T(8,128)(2,1)S(1)}, u32[]{:S(2)}, u32[]{:S(2)}) %collective-permute-start.40) | collective-permute-done | bytes 589856 | tf_op jit(solution)/shard_map/ppermute | solution.py:108
  802.0 18.4 %collective-permute-done.30 = bf16[576,768]{1,0:T(8,128)(2,1)S(1)} collective-permute-done((bf16[576,768]{1,0:T(8,128)(2,1)S(1)}, bf16[576,768]{1,0:T(8,128)(2,1)S(1)}, u32[]{:S(2)}, u32[]{:S(2)}) %collective-permute-start.30) | collective-permute-done | bytes 884768 | tf_op jit(solution)/shard_map/ppermute | solution.py:108
  (1122 shorter events, 435.8 us)
Async XLA Ops:
  6.2 22.2 %collective-permute-start = (bf16[800,768]{1,0:T(8,128)(2,1)}, bf16[800,768]{1,0:T(8,128)(2,1)}, u32[]{:S(2)}, u32[]{:S(2)}) collective-permute-start(bf16[800,768]{1,0:T(8,128)(2,1)} %fusion.94), channel_id=1, source_target_pairs={{0,1},{1,0},{2,3},{3,2},{4,6},{5,7},{6,4},{7,5},{8,9},{9,8},{10,11... | collective-permute-start | bytes 3686408 | tf_op jit(solution)/shard_map/ppermute | solution.py:70
  9.2 26.2 %all-to-all-start.5 = ((bf16[4,128,768]{2,1,0:T(8,128)(2,1)}), bf16[4,128,768]{2,1,0:T(8,128)(2,1)S(1)}, u32[]{:S(2)}, u32[]{:S(2)}) async-start(bf16[4,128,768]{2,1,0:T(8,128)(2,1)} %bitcast.49), calls=%async_computation.5 | async-start | bytes 1572864 | tf_op jit(solution)/shard_map/all_to_all | solution.py:48
  30.3 16.4 %collective-permute-start.2 = (bf16[400,768]{1,0:T(8,128)(2,1)}, bf16[400,768]{1,0:T(8,128)(2,1)}, u32[]{:S(2)}, u32[]{:S(2)}) collective-permute-start(bf16[400,768]{1,0:T(8,128)(2,1)} %constant_dynamic-slice_fusion.9), channel_id=1, source_target_pairs={{0,2},{1,3},{2,0},{3,1},{4,5},{5,4},{6,7},{7,6},{8,10},{9,11},{10,... | collective-permute-start | bytes 1843208 | tf_op jit(solution)/shard_map/ppermute | solution.py:70
  35.4 18.1 %all-to-all-start = ((bf16[4,128,768]{2,1,0:T(8,128)(2,1)}), bf16[4,128,768]{2,1,0:T(8,128)(2,1)S(1)}, u32[]{:S(2)}, u32[]{:S(2)}) async-start(bf16[4,128,768]{2,1,0:T(8,128)(2,1)} %bitcast.415), calls=%async_computation | async-start | bytes 1572864 | tf_op jit(solution)/shard_map/all_to_all | solution.py:48
  47.3 4.5 collective-permute-start.1
  49.2 40.3 %collective-permute-start.4 = (bf16[1536,768]{1,0:T(8,128)(2,1)}, bf16[1536,768]{1,0:T(8,128)(2,1)}, u32[]{:S(2)}, u32[]{:S(2)}) collective-permute-start(bf16[1536,768]{1,0:T(8,128)(2,1)} %pad_maximum_fusion.6), channel_id=1, source_target_pairs={{0,1},{1,0},{2,3},{3,2},{4,6},{5,7},{6,4},{7,5},{8,9},{9,8},{10,11... | collective-permute-start | bytes 7077896 | tf_op jit(solution)/shard_map/ppermute | solution.py:70
  54.4 98.6 %all-to-all-start.2 = ((bf16[4,128,768]{2,1,0:T(8,128)(2,1)}), bf16[4,128,768]{2,1,0:T(8,128)(2,1)S(1)}, u32[]{:S(2)}, u32[]{:S(2)}) async-start(bf16[4,128,768]{2,1,0:T(8,128)(2,1)} %bitcast.416), calls=%async_computation.2 | async-start | bytes 1572864 | tf_op jit(solution)/shard_map/all_to_all | solution.py:48
  90.9 16.3 %collective-permute-start.6 = (bf16[768,768]{1,0:T(8,128)(2,1)S(1)}, bf16[768,768]{1,0:T(8,128)(2,1)S(1)}, u32[]{:S(2)}, u32[]{:S(2)}) collective-permute-start(bf16[768,768]{1,0:T(8,128)(2,1)S(1)} %constant_dynamic-slice_fusion.8), channel_id=1, source_target_pairs={{0,2},{1,3},{2,0},{3,1},{4,5},{5,4},{6,7},{7,6},{8,10},{9,11},{10,... | collective-permute-start | bytes 3538952 | tf_op jit(solution)/shard_map/ppermute | solution.py:70
  94.8 23.1 %collective-permute-start.5 = (bf16[1536,768]{1,0:T(8,128)(2,1)}, bf16[1536,768]{1,0:T(8,128)(2,1)S(1)}, u32[]{:S(2)}, u32[]{:S(2)}) collective-permute-start(bf16[1536,768]{1,0:T(8,128)(2,1)} %collective-permute-done.4), channel_id=1, source_target_pairs={{0,4},{1,5},{2,6},{3,7},{4,0},{5,1},{6,2},{7,3},{8,12},{9,13},{10,... | collective-permute-start | bytes 7077896 | tf_op jit(solution)/shard_map/ppermute | solution.py:70
  107.1 41.5 %collective-permute-start.8 = (bf16[2304,768]{1,0:T(8,128)(2,1)S(1)}, bf16[2304,768]{1,0:T(8,128)(2,1)S(1)}, u32[]{:S(2)}, u32[]{:S(2)}) collective-permute-start(bf16[2304,768]{1,0:T(8,128)(2,1)S(1)} %copy-done.73), channel_id=1, source_target_pairs={{0,1},{1,0},{2,3},{3,2},{4,6},{5,7},{6,4},{7,5},{8,9},{9,8},{10,11... | collective-permute-start | bytes 10616840 | tf_op jit(solution)/shard_map/ppermute | solution.py:70
  112.1 8.6 %collective-permute-start.7 = (bf16[768,768]{1,0:T(8,128)(2,1)S(1)}, bf16[768,768]{1,0:T(8,128)(2,1)S(1)}, u32[]{:S(2)}, u32[]{:S(2)}) collective-permute-start(bf16[768,768]{1,0:T(8,128)(2,1)S(1)} %collective-permute-done.6), channel_id=1, source_target_pairs={{0,4},{1,5},{2,6},{3,7},{4,0},{5,1},{6,2},{7,3},{8,12},{9,13},{10,... | collective-permute-start | bytes 3538952 | tf_op jit(solution)/shard_map/ppermute | solution.py:70
  151.0 42.1 %collective-permute-start.10 = (bf16[1152,768]{1,0:T(8,128)(2,1)}, bf16[1152,768]{1,0:T(8,128)(2,1)}, u32[]{:S(2)}, u32[]{:S(2)}) collective-permute-start(bf16[1152,768]{1,0:T(8,128)(2,1)} %constant_dynamic-slice_fusion.7), channel_id=1, source_target_pairs={{0,2},{1,3},{2,0},{3,1},{4,5},{5,4},{6,7},{7,6},{8,10},{9,11},{10,... | collective-permute-start | bytes 5308424 | tf_op jit(solution)/shard_map/ppermute | solution.py:70
  166.0 41.2 %all-to-all-start.1 = ((bf16[4,2,49152]{2,1,0:T(2,128)(2,1)}), bf16[4,2,49152]{2,1,0:T(2,128)(2,1)}, u32[]{:S(2)}, u32[]{:S(2)}) async-start(bf16[4,2,49152]{2,1,0:T(2,128)(2,1)} %reshape.608), calls=%async_computation.1 | async-start | bytes 1572864 | tf_op jit(solution)/shard_map/all_to_all | solution.py:52
  192.1 40.6 %collective-permute-start.9 = (bf16[2304,768]{1,0:T(8,128)(2,1)}, bf16[2304,768]{1,0:T(8,128)(2,1)}, u32[]{:S(2)}, u32[]{:S(2)}) collective-permute-start(bf16[2304,768]{1,0:T(8,128)(2,1)} %copy-done.101), channel_id=1, source_target_pairs={{0,4},{1,5},{2,6},{3,7},{4,0},{5,1},{6,2},{7,3},{8,12},{9,13},{10,... | collective-permute-start | bytes 10616840 | tf_op jit(solution)/shard_map/ppermute | solution.py:70
  193.1 30.5 %collective-permute-start.11 = (bf16[1152,768]{1,0:T(8,128)(2,1)}, bf16[1152,768]{1,0:T(8,128)(2,1)}, u32[]{:S(2)}, u32[]{:S(2)}) collective-permute-start(bf16[1152,768]{1,0:T(8,128)(2,1)} %collective-permute-done.10), channel_id=1, source_target_pairs={{0,4},{1,5},{2,6},{3,7},{4,0},{5,1},{6,2},{7,3},{8,12},{9,13},{10,... | collective-permute-start | bytes 5308424 | tf_op jit(solution)/shard_map/ppermute | solution.py:70
  207.2 119.3 %all-to-all-start.4 = ((bf16[4,128,768]{2,1,0:T(8,128)(2,1)}), bf16[4,128,768]{2,1,0:T(8,128)(2,1)}, u32[]{:S(2)}, u32[]{:S(2)}) async-start(bf16[4,128,768]{2,1,0:T(8,128)(2,1)} %bitcast.47), calls=%async_computation.4 | async-start | bytes 1572864 | tf_op jit(solution)/shard_map/all_to_all | solution.py:48
  515.1 199.3 %all-to-all-start.3 = ((bf16[4,2,49152]{2,1,0:T(2,128)(2,1)}), bf16[4,2,49152]{2,1,0:T(2,128)(2,1)}, u32[]{:S(2)}, u32[]{:S(2)}) async-start(bf16[4,2,49152]{2,1,0:T(2,128)(2,1)} %reshape.610), calls=%async_computation.3 | async-start | bytes 1572864 | tf_op jit(solution)/shard_map/all_to_all | solution.py:52
  526.4 38.1 %collective-permute-start.22 = (bf16[4,1152,768]{2,1,0:T(8,128)(2,1)S(1)}, bf16[4,1152,768]{2,1,0:T(8,128)(2,1)S(1)}, u32[]{:S(2)}, u32[]{:S(2)}) collective-permute-start(bf16[4,1152,768]{2,1,0:T(8,128)(2,1)S(1)} %pad_maximum_fusion), channel_id=1, source_target_pairs={{0,4},{1,5},{2,6},{3,7},{4,0},{5,1},{6,2},{7,3},{8,12},{9,13},{10,... | collective-permute-start | bytes 21233672 | tf_op jit(solution)/shard_map/ppermute | solution.py:70
  529.6 40.1 %collective-permute-start.12 = (bf16[4,384,768]{2,1,0:T(8,128)(2,1)S(1)}, bf16[4,384,768]{2,1,0:T(8,128)(2,1)S(1)}, u32[]{:S(2)}, u32[]{:S(2)}) collective-permute-start(bf16[4,384,768]{2,1,0:T(8,128)(2,1)S(1)} %pad_maximum_fusion.7), channel_id=1, source_target_pairs={{0,4},{1,5},{2,6},{3,7},{4,0},{5,1},{6,2},{7,3},{8,12},{9,13},{10,... | collective-permute-start | bytes 7077896 | tf_op jit(solution)/shard_map/ppermute | solution.py:70
  535.3 63.3 %collective-permute-start.32 = (bf16[4,768,768]{2,1,0:T(8,128)(2,1)S(1)}, bf16[4,768,768]{2,1,0:T(8,128)(2,1)S(1)}, u32[]{:S(2)}, u32[]{:S(2)}) collective-permute-start(bf16[4,768,768]{2,1,0:T(8,128)(2,1)S(1)} %pad_maximum_fusion.1), channel_id=1, source_target_pairs={{0,4},{1,5},{2,6},{3,7},{4,0},{5,1},{6,2},{7,3},{8,12},{9,13},{10,... | collective-permute-start | bytes 14155784 | tf_op jit(solution)/shard_map/ppermute | solution.py:70
  566.1 34.4 %collective-permute-start.23 = (bf16[1152,768]{1,0:T(8,128)(2,1)S(1)}, bf16[1152,768]{1,0:T(8,128)(2,1)S(1)}, u32[]{:S(2)}, u32[]{:S(2)}) collective-permute-start(bf16[1152,768]{1,0:T(8,128)(2,1)S(1)} %fusion.1), channel_id=1, source_target_pairs={{0,2},{1,3},{2,0},{3,1},{4,5},{5,4},{6,7},{7,6},{8,10},{9,11},{10,... | collective-permute-start | bytes 5308424 | tf_op jit(solution)/shard_map/ppermute | solution.py:70
  570.1 24.9 %collective-permute-start.13 = (bf16[384,768]{1,0:T(8,128)(2,1)S(1)}, bf16[384,768]{1,0:T(8,128)(2,1)S(1)}, u32[]{:S(2)}, u32[]{:S(2)}) collective-permute-start(bf16[384,768]{1,0:T(8,128)(2,1)S(1)} %fusion.97), channel_id=1, source_target_pairs={{0,2},{1,3},{2,0},{3,1},{4,5},{5,4},{6,7},{7,6},{8,10},{9,11},{10,... | collective-permute-start | bytes 1769480 | tf_op jit(solution)/shard_map/ppermute | solution.py:70
  596.5 16.2 %collective-permute-start.15 = (bf16[384,768]{1,0:T(8,128)(2,1)}, bf16[384,768]{1,0:T(8,128)(2,1)}, u32[]{:S(2)}, u32[]{:S(2)}) collective-permute-start(bf16[384,768]{1,0:T(8,128)(2,1)} %get-tuple-element.130), channel_id=1, source_target_pairs={{0,1},{1,0},{2,3},{3,2},{4,6},{5,7},{6,4},{7,5},{8,9},{9,8},{10,11... | collective-permute-start | bytes 1769480 | tf_op jit(solution)/shard_map/ppermute | solution.py:70
  598.9 28.9 %collective-permute-start.33 = (bf16[768,768]{1,0:T(8,128)(2,1)S(1)}, bf16[768,768]{1,0:T(8,128)(2,1)S(1)}, u32[]{:S(2)}, u32[]{:S(2)}) collective-permute-start(bf16[768,768]{1,0:T(8,128)(2,1)S(1)} %fusion.6), channel_id=1, source_target_pairs={{0,2},{1,3},{2,0},{3,1},{4,5},{5,4},{6,7},{7,6},{8,10},{9,11},{10,... | collective-permute-start | bytes 3538952 | tf_op jit(solution)/shard_map/ppermute | solution.py:70
  603.7 55.5 %collective-permute-start.25 = (bf16[1152,768]{1,0:T(8,128)(2,1)S(1)}, bf16[1152,768]{1,0:T(8,128)(2,1)}, u32[]{:S(2)}, u32[]{:S(2)}) collective-permute-start(bf16[1152,768]{1,0:T(8,128)(2,1)S(1)} %get-tuple-element.108), channel_id=1, source_target_pairs={{0,1},{1,0},{2,3},{3,2},{4,6},{5,7},{6,4},{7,5},{8,9},{9,8},{10,11... | collective-permute-start | bytes 5308424 | tf_op jit(solution)/shard_map/ppermute | solution.py:70
  604.4 40.2 %collective-permute-start.14 = (bf16[384,768]{1,0:T(8,128)(2,1)}, bf16[384,768]{1,0:T(8,128)(2,1)S(1)}, u32[]{:S(2)}, u32[]{:S(2)}) collective-permute-start(bf16[384,768]{1,0:T(8,128)(2,1)} %get-tuple-element.129), channel_id=1, source_target_pairs={{0,1},{1,0},{2,3},{3,2},{4,6},{5,7},{6,4},{7,5},{8,9},{9,8},{10,11... | collective-permute-start | bytes 1769480 | tf_op jit(solution)/shard_map/ppermute | solution.py:70
  612.8 31.9 %collective-permute-start.16 = (bf16[384,768]{1,0:T(8,128)(2,1)}, bf16[384,768]{1,0:T(8,128)(2,1)S(1)}, u32[]{:S(2)}, u32[]{:S(2)}) collective-permute-start(bf16[384,768]{1,0:T(8,128)(2,1)} %collective-permute-done.15), channel_id=1, source_target_pairs={{0,4},{1,5},{2,6},{3,7},{4,0},{5,1},{6,2},{7,3},{8,12},{9,13},{10,... | collective-permute-start | bytes 1769480 | tf_op jit(solution)/shard_map/ppermute | solution.py:70
  629.9 27.3 %collective-permute-start.35 = (bf16[768,768]{1,0:T(8,128)(2,1)S(1)}, bf16[768,768]{1,0:T(8,128)(2,1)S(1)}, u32[]{:S(2)}, u32[]{:S(2)}) collective-permute-start(bf16[768,768]{1,0:T(8,128)(2,1)S(1)} %get-tuple-element.110), channel_id=1, source_target_pairs={{0,1},{1,0},{2,3},{3,2},{4,6},{5,7},{6,4},{7,5},{8,9},{9,8},{10,11... | collective-permute-start | bytes 3538952 | tf_op jit(solution)/shard_map/ppermute | solution.py:70
  645.0 14.2 %collective-permute-start.17 = (bf16[192,768]{1,0:T(8,128)(2,1)S(1)}, bf16[192,768]{1,0:T(8,128)(2,1)S(1)}, u32[]{:S(2)}, u32[]{:S(2)}) collective-permute-start(bf16[192,768]{1,0:T(8,128)(2,1)S(1)} %constant_dynamic-slice_fusion.6), channel_id=1, source_target_pairs={{0,8},{8,0},{16,24},{24,16},{1,9},{9,1},{17,25},{25,17},{2,10},{10... | collective-permute-start | bytes 884744 | tf_op jit(solution)/shard_map/ppermute | solution.py:104
  646.8 33.1 %collective-permute-start.34 = (bf16[768,768]{1,0:T(8,128)(2,1)S(1)}, bf16[768,768]{1,0:T(8,128)(2,1)S(1)}, u32[]{:S(2)}, u32[]{:S(2)}) collective-permute-start(bf16[768,768]{1,0:T(8,128)(2,1)S(1)} %get-tuple-element.109), channel_id=1, source_target_pairs={{0,1},{1,0},{2,3},{3,2},{4,6},{5,7},{6,4},{7,5},{8,9},{9,8},{10,11... | collective-permute-start | bytes 3538952 | tf_op jit(solution)/shard_map/ppermute | solution.py:70
  657.3 22.7 %collective-permute-start.36 = (bf16[768,768]{1,0:T(8,128)(2,1)S(1)}, bf16[768,768]{1,0:T(8,128)(2,1)S(1)}, u32[]{:S(2)}, u32[]{:S(2)}) collective-permute-start(bf16[768,768]{1,0:T(8,128)(2,1)S(1)} %collective-permute-done.35), channel_id=1, source_target_pairs={{0,4},{1,5},{2,6},{3,7},{4,0},{5,1},{6,2},{7,3},{8,12},{9,13},{10,... | collective-permute-start | bytes 3538952 | tf_op jit(solution)/shard_map/ppermute | solution.py:70
  657.3 31.6 %collective-permute-start.24 = (bf16[1152,768]{1,0:T(8,128)(2,1)S(1)}, bf16[1152,768]{1,0:T(8,128)(2,1)S(1)}, u32[]{:S(2)}, u32[]{:S(2)}) collective-permute-start(bf16[1152,768]{1,0:T(8,128)(2,1)S(1)} %get-tuple-element.107), channel_id=1, source_target_pairs={{0,1},{1,0},{2,3},{3,2},{4,6},{5,7},{6,4},{7,5},{8,9},{9,8},{10,11... | collective-permute-start | bytes 5308424 | tf_op jit(solution)/shard_map/ppermute | solution.py:70
  659.2 29.7 %collective-permute-start.26 = (bf16[1152,768]{1,0:T(8,128)(2,1)}, bf16[1152,768]{1,0:T(8,128)(2,1)S(1)}, u32[]{:S(2)}, u32[]{:S(2)}) collective-permute-start(bf16[1152,768]{1,0:T(8,128)(2,1)} %collective-permute-done.25), channel_id=1, source_target_pairs={{0,4},{1,5},{2,6},{3,7},{4,0},{5,1},{6,2},{7,3},{8,12},{9,13},{10,... | collective-permute-start | bytes 5308424 | tf_op jit(solution)/shard_map/ppermute | solution.py:70
  659.3 10.4 %collective-permute-start.18 = (bf16[96,768]{1,0:T(8,128)(2,1)S(1)}, bf16[96,768]{1,0:T(8,128)(2,1)S(1)}, u32[]{:S(2)}, u32[]{:S(2)}) collective-permute-start(bf16[96,768]{1,0:T(8,128)(2,1)S(1)} %constant_dynamic-slice_fusion.5), channel_id=1, source_target_pairs={{0,16},{8,24},{16,0},{24,8},{1,17},{9,25},{17,1},{25,9},{2,18},{10... | collective-permute-start | bytes 442376 | tf_op jit(solution)/shard_map/ppermute | solution.py:104
  669.7 9.4 %collective-permute-start.19 = (bf16[96,768]{1,0:T(8,128)(2,1)S(1)}, bf16[96,768]{1,0:T(8,128)(2,1)S(1)}, u32[]{:S(2)}, u32[]{:S(2)}) collective-permute-start(bf16[96,768]{1,0:T(8,128)(2,1)S(1)} %add_convert_fusion.12), channel_id=1, source_target_pairs={{0,16},{8,24},{16,0},{24,8},{1,17},{9,25},{17,1},{25,9},{2,18},{10... | collective-permute-start | bytes 442376 | tf_op jit(solution)/shard_map/ppermute | solution.py:108
  679.9 38.6 %collective-permute-start.20 = (bf16[192,768]{1,0:T(8,128)(2,1)}, bf16[192,768]{1,0:T(8,128)(2,1)}, u32[]{:S(2)}, u32[]{:S(2)}) collective-permute-start(bf16[192,768]{1,0:T(8,128)(2,1)} %pad_maximum_fusion.40), channel_id=1, source_target_pairs={{0,8},{8,0},{16,24},{24,16},{1,9},{9,1},{17,25},{25,17},{2,10},{10... | collective-permute-start | bytes 884744 | tf_op jit(solution)/shard_map/ppermute | solution.py:108
  681.5 39.0 %collective-permute-start.37 = (bf16[384,768]{1,0:T(8,128)(2,1)}, bf16[384,768]{1,0:T(8,128)(2,1)}, u32[]{:S(2)}, u32[]{:S(2)}) collective-permute-start(bf16[384,768]{1,0:T(8,128)(2,1)} %constant_dynamic-slice_fusion.2), channel_id=1, source_target_pairs={{0,8},{8,0},{16,24},{24,16},{1,9},{9,1},{17,25},{25,17},{2,10},{10... | collective-permute-start | bytes 1769480 | tf_op jit(solution)/shard_map/ppermute | solution.py:104
  691.7 40.5 %collective-permute-start.27 = (bf16[576,768]{1,0:T(8,128)(2,1)}, bf16[576,768]{1,0:T(8,128)(2,1)}, u32[]{:S(2)}, u32[]{:S(2)}) collective-permute-start(bf16[576,768]{1,0:T(8,128)(2,1)} %constant_dynamic-slice_fusion.4), channel_id=1, source_target_pairs={{0,8},{8,0},{16,24},{24,16},{1,9},{9,1},{17,25},{25,17},{2,10},{10... | collective-permute-start | bytes 2654216 | tf_op jit(solution)/shard_map/ppermute | solution.py:104
  714.3 14.2 %all-to-all-start.6 = ((bf16[4,2,49152]{2,1,0:T(2,128)(2,1)}), bf16[4,2,49152]{2,1,0:T(2,128)(2,1)}, u32[]{:S(2)}, u32[]{:S(2)}) async-start(bf16[4,2,49152]{2,1,0:T(2,128)(2,1)} %reshape.612), calls=%async_computation.6 | async-start | bytes 1572864 | tf_op jit(solution)/shard_map/all_to_all | solution.py:52
  723.2 25.5 %collective-permute-start.38 = (bf16[192,768]{1,0:T(8,128)(2,1)}, bf16[192,768]{1,0:T(8,128)(2,1)}, u32[]{:S(2)}, u32[]{:S(2)}) collective-permute-start(bf16[192,768]{1,0:T(8,128)(2,1)} %constant_dynamic-slice_fusion.1), channel_id=1, source_target_pairs={{0,16},{8,24},{16,0},{24,8},{1,17},{9,25},{17,1},{25,9},{2,18},{10... | collective-permute-start | bytes 884744 | tf_op jit(solution)/shard_map/ppermute | solution.py:104
  728.6 16.3 %all-to-all-start.7 = ((bf16[4,2,49152]{2,1,0:T(2,128)(2,1)}), bf16[4,2,49152]{2,1,0:T(2,128)(2,1)S(1)}, u32[]{:S(2)}, u32[]{:S(2)}) async-start(bf16[4,2,49152]{2,1,0:T(2,128)(2,1)} %reshape.614), calls=%async_computation.7 | async-start | bytes 1572864 | tf_op jit(solution)/shard_map/all_to_all | solution.py:52
  734.5 30.0 %collective-permute-start.28 = (bf16[288,768]{1,0:T(8,128)(2,1)}, bf16[288,768]{1,0:T(8,128)(2,1)}, u32[]{:S(2)}, u32[]{:S(2)}) collective-permute-start(bf16[288,768]{1,0:T(8,128)(2,1)} %constant_dynamic-slice_fusion.3), channel_id=1, source_target_pairs={{0,16},{8,24},{16,0},{24,8},{1,17},{9,25},{17,1},{25,9},{2,18},{10... | collective-permute-start | bytes 1327112 | tf_op jit(solution)/shard_map/ppermute | solution.py:104
  737.4 28.3 %collective-permute-start.21 = (bf16[384,768]{1,0:T(8,128)(2,1)}, bf16[384,768]{1,0:T(8,128)(2,1)}, u32[]{:S(2)}, u32[]{:S(2)}) collective-permute-start(bf16[384,768]{1,0:T(8,128)(2,1)} %pad_maximum_fusion.34), channel_id=1, source_target_pairs={{0,4},{1,5},{2,6},{3,7},{4,0},{5,1},{6,2},{7,3},{8,12},{9,13},{10,... | collective-permute-start | bytes 1769480 | tf_op jit(solution)/shard_map/ppermute | solution.py:70
  749.7 30.5 %collective-permute-start.39 = (bf16[192,768]{1,0:T(8,128)(2,1)S(1)}, bf16[192,768]{1,0:T(8,128)(2,1)S(1)}, u32[]{:S(2)}, u32[]{:S(2)}) collective-permute-start(bf16[192,768]{1,0:T(8,128)(2,1)S(1)} %add_convert_fusion.10), channel_id=1, source_target_pairs={{0,16},{8,24},{16,0},{24,8},{1,17},{9,25},{17,1},{25,9},{2,18},{10... | collective-permute-start | bytes 884744 | tf_op jit(solution)/shard_map/ppermute | solution.py:108
  765.6 23.3 %collective-permute-start.29 = (bf16[288,768]{1,0:T(8,128)(2,1)S(1)}, bf16[288,768]{1,0:T(8,128)(2,1)S(1)}, u32[]{:S(2)}, u32[]{:S(2)}) collective-permute-start(bf16[288,768]{1,0:T(8,128)(2,1)S(1)} %add_convert_fusion.9), channel_id=1, source_target_pairs={{0,16},{8,24},{16,0},{24,8},{1,17},{9,25},{17,1},{25,9},{2,18},{10... | collective-permute-start | bytes 1327112 | tf_op jit(solution)/shard_map/ppermute | solution.py:108
  780.3 21.2 %collective-permute-start.40 = (bf16[384,768]{1,0:T(8,128)(2,1)S(1)}, bf16[384,768]{1,0:T(8,128)(2,1)S(1)}, u32[]{:S(2)}, u32[]{:S(2)}) collective-permute-start(bf16[384,768]{1,0:T(8,128)(2,1)S(1)} %pad_maximum_fusion.35), channel_id=1, source_target_pairs={{0,8},{8,0},{16,24},{24,16},{1,9},{9,1},{17,25},{25,17},{2,10},{10... | collective-permute-start | bytes 1769480 | tf_op jit(solution)/shard_map/ppermute | solution.py:108
  789.0 31.4 %collective-permute-start.30 = (bf16[576,768]{1,0:T(8,128)(2,1)S(1)}, bf16[576,768]{1,0:T(8,128)(2,1)S(1)}, u32[]{:S(2)}, u32[]{:S(2)}) collective-permute-start(bf16[576,768]{1,0:T(8,128)(2,1)S(1)} %pad_maximum_fusion.21), channel_id=1, source_target_pairs={{0,8},{8,0},{16,24},{24,16},{1,9},{9,1},{17,25},{25,17},{2,10},{10... | collective-permute-start | bytes 2654216 | tf_op jit(solution)/shard_map/ppermute | solution.py:108
  801.8 19.4 %collective-permute-start.41 = (bf16[768,768]{1,0:T(8,128)(2,1)S(1)}, bf16[768,768]{1,0:T(8,128)(2,1)S(1)}, u32[]{:S(2)}, u32[]{:S(2)}) collective-permute-start(bf16[768,768]{1,0:T(8,128)(2,1)S(1)} %pad_maximum_fusion.19), channel_id=1, source_target_pairs={{0,4},{1,5},{2,6},{3,7},{4,0},{5,1},{6,2},{7,3},{8,12},{9,13},{10,... | collective-permute-start | bytes 3538952 | tf_op jit(solution)/shard_map/ppermute | solution.py:70
  (321 other events, 3241.8 us)

commit v3 on v2

v3 whole, which is shorter than its diff:
```python
import math

import jax
import jax.numpy as jnp
from jax import lax
from jax.experimental import pallas as pl
from jax.experimental.pallas import tpu as pltpu
from jax.sharding import PartitionSpec as P

HEAD_DIM = 64
EPSILON = 1e-12
LOSS_WEIGHT = 8.0
HIGHEST = lax.Precision.HIGHEST
MASKED = -1e30
BF = jnp.bfloat16
F32 = jnp.float32
PLANE = ("span", "tensor")
MESH = pl.DeviceIdType.MESH
TENSORS = 4
MAIN, DIAG, SWAP = "main", "diag", "swap"


def mm(a, b, ca, cb):
    return lax.dot_general(a, b, (((ca,), (cb,)), ((), ())), preferred_element_type=F32)


def normal_parts(values):
    centred = values - jnp.mean(values, axis=-1, keepdims=True)
    spread = jnp.mean(centred * centred, axis=-1, keepdims=True)
    scale = lax.rsqrt(spread + EPSILON)
    return centred * scale, scale


def normal_back(upward, normed, scale, gain):
    weighted = upward * gain
    first = jnp.mean(weighted, axis=-1, keepdims=True)
    second = jnp.mean(weighted * normed, axis=-1, keepdims=True)
    return (weighted - first - normed * second) * scale


def gelu_parts(hidden):
    phi = 0.5 * (1.0 + lax.erf(hidden * math.sqrt(0.5)))
    slope = phi + hidden * jnp.exp(-0.5 * hidden * hidden) * (1.0 / math.sqrt(2.0 * math.pi))
    return hidden * phi, slope


def plane_pairs(kind):
    pairs = []
    for side in range(2):
        for t in range(TENSORS):
            if kind == SWAP:
                target = (1 - side, t)
            elif kind == MAIN:
                target = (side, t ^ (1 + side))
            else:
                target = (side, t ^ (2 - side))
            pairs.append((side * TENSORS + t, target[0] * TENSORS + target[1]))
    return pairs


def send(values, kind):
    return lax.ppermute(values, PLANE, plane_pairs(kind))


def plus(*terms):
    total = terms[0].astype(F32)
    for term in terms[1:]:
        total = total + term.astype(F32)
    return total.astype(BF)


def pick(side, zero, one):
    return jnp.where(side == 0, zero, one)


def tie(*values):
    return lax.optimization_barrier(values)


def gather_part(first, second, side):
    got_first, got_second = send(first, MAIN), send(second, MAIN)
    across = send(pick(side, got_first, got_second), DIAG)
    other_first, other_second = send(got_first, SWAP), send(got_second, SWAP)
    rest = send(across, SWAP)
    blocks = [
        (first, second), (got_first, got_second), (other_first, other_second),
        (pick(side, across, rest), pick(side, rest, across)),
    ]
    return blocks, across


def reduce_outgoing(blocks, side):
    return (
        blocks[2][0], blocks[2][1], pick(side, blocks[3][1], blocks[3][0]), pick(side, blocks[0][1], blocks[0][0])
    )


def reduce_swapped(blocks, outgoing, side):
    got = [send(o, SWAP) for o in outgoing]
    first = plus(blocks[1][0], got[0])
    second = plus(blocks[1][1], got[1])
    main_rest = pick(side, second, first)
    main_own = pick(side, first, second)
    across = plus(pick(side, blocks[3][0], blocks[3][1]), got[2])
    mine = plus(pick(side, blocks[0][0], blocks[0][1]), got[3])
    return main_rest, main_own, across, mine


def reduce_across(main_own, across):
    return plus(main_own, send(across, DIAG))


def finish_part(mine, side):
    other = send(mine, SWAP)
    return pick(side, mine, other).astype(F32), pick(side, other, mine).astype(F32)


Q_ROWS = 128


def attend_forward_kernel(qk_ref, v_ref, down_ref, across_ref, o_ref, lse_ref):
    tokens, width = o_ref.shape

    def step(i, carry):
        rows = pl.ds(pl.multiple_of(i * Q_ROWS, Q_ROWS), Q_ROWS)
        same = down_ref[rows, :] == across_ref[...]
        for h in range(width // HEAD_DIM):
            at = h * HEAD_DIM
            q = qk_ref[rows, at : at + HEAD_DIM]
            k = qk_ref[:, width + at : width + at + HEAD_DIM]
            v = v_ref[:, at : at + HEAD_DIM]
            s = mm(q, k, 1, 1) * 0.125
            s = jnp.where(same, s, MASKED)
            top = jnp.max(s, axis=-1, keepdims=True)
            raised = jnp.exp(s - top)
            total = jnp.sum(raised, axis=-1, keepdims=True)
            weights = (raised * (1.0 / total)).astype(BF)
            o_ref[rows, at : at + HEAD_DIM] = mm(weights, v, 1, 0).astype(BF)
            lse_ref[rows, h : h + 1] = top + jnp.log(total)
        return carry

    lax.fori_loop(0, tokens // Q_ROWS, step, 0)


def attend_backward_kernel(
    qk_ref, v_ref, do_ref, lse_ref, down_ref, across_ref, dqk_ref, dv_out_ref, dk_ref, dv_ref
):
    tokens, width = do_ref.shape
    dk_ref[...] = jnp.zeros_like(dk_ref)
    dv_ref[...] = jnp.zeros_like(dv_ref)

    def step(i, carry):
        rows = pl.ds(pl.multiple_of(i * Q_ROWS, Q_ROWS), Q_ROWS)
        same = down_ref[rows, :] == across_ref[...]
        for h in range(width // HEAD_DIM):
            at = h * HEAD_DIM
            q = qk_ref[rows, at : at + HEAD_DIM]
            k = qk_ref[:, width + at : width + at + HEAD_DIM]
            v = v_ref[:, at : at + HEAD_DIM]
            up = do_ref[rows, at : at + HEAD_DIM]
            s = mm(q, k, 1, 1) * 0.125
            s = jnp.where(same, s, MASKED)
            pr = jnp.exp(s - lse_ref[rows, h : h + 1])
            dp = mm(up, v, 1, 1)
            inner = jnp.sum(pr * dp, axis=-1, keepdims=True)
            ds = (pr * (dp - inner)).astype(BF)
            dqk_ref[rows, at : at + HEAD_DIM] = (mm(ds, k, 1, 0) * 0.125).astype(BF)
            dk_ref[:, at : at + HEAD_DIM] += mm(ds, q, 0, 0)
            dv_ref[:, at : at + HEAD_DIM] += mm(pr.astype(BF), up, 0, 0)
        return carry

    lax.fori_loop(0, tokens // Q_ROWS, step, 0)
    dqk_ref[:, width:] = (dk_ref[...] * 0.125).astype(BF)
    dv_out_ref[...] = dv_ref[...].astype(BF)


def attend_cost(tokens, width, products):
    heads = width // HEAD_DIM
    return pl.CostEstimate(
        flops=2 * products * tokens * tokens * width,
        bytes_accessed=2 * 8 * tokens * width,
        transcendentals=heads * tokens * tokens,
    )


def attend_forward(qk, v, down, across):
    tokens, width = v.shape
    return pl.pallas_call(
        attend_forward_kernel,
        name="attend_forward",
        out_shape=(
            jax.ShapeDtypeStruct((tokens, width), BF),
            jax.ShapeDtypeStruct((tokens, width // HEAD_DIM), F32),
        ),
        compiler_params=pltpu.CompilerParams(vmem_limit_bytes=24 << 20),
        cost_estimate=attend_cost(tokens, width, 2),
    )(qk, v, down, across)


def attend_backward(qk, v, do, lse, down, across):
    tokens, width = do.shape
    return pl.pallas_call(
        attend_backward_kernel,
        name="attend_backward",
        out_shape=(jax.ShapeDtypeStruct(qk.shape, BF), jax.ShapeDtypeStruct(v.shape, BF)),
        scratch_shapes=[pltpu.VMEM((tokens, width), F32), pltpu.VMEM((tokens, width), F32)],
        compiler_params=pltpu.CompilerParams(vmem_limit_bytes=24 << 20),
        cost_estimate=attend_cost(tokens, width, 5),
    )(qk, v, do, lse, down, across)


def anchors_kernel(dps, planes, x_ref, out_ref, near_send, near_recv, far_send, far_recv, own_sem):
    dp = lax.axis_index("dp")
    me = lax.axis_index("span") * TENSORS + lax.axis_index("tensor")

    def near(k):
        peer = lax.rem(me + k, planes)
        return {"span": peer // TENSORS, "tensor": lax.rem(peer, TENSORS)}

    def far(k):
        return {"dp": lax.rem(dp + k, dps)}

    barrier = pltpu.get_barrier_semaphore()
    for k in range(1, planes):
        pl.semaphore_signal(barrier, inc=1, device_id=near(k), device_id_type=MESH)
    for k in range(1, dps):
        pl.semaphore_signal(barrier, inc=1, device_id=far(k), device_id_type=MESH)
    pl.semaphore_wait(barrier, planes + dps - 2)

    own = pltpu.make_async_copy(x_ref, out_ref.at[dp, me], own_sem)
    own.start()

    def near_copy(k):
        return pltpu.make_async_remote_copy(
            src_ref=x_ref, dst_ref=out_ref.at[dp, me], send_sem=near_send.at[k],
            recv_sem=near_recv.at[k], device_id=near(k), device_id_type=MESH,
        )

    def far_copy(k):
        return pltpu.make_async_remote_copy(
            src_ref=out_ref.at[dp], dst_ref=out_ref.at[dp], send_sem=far_send.at[k],
            recv_sem=far_recv.at[k], device_id=far(k), device_id_type=MESH,
        )

    for k in range(1, planes):
        near_copy(k).start()
    own.wait()
    for k in range(1, planes):
        near_copy(k).wait()
    for k in range(1, dps):
        far_copy(k).start()
    for k in range(1, dps):
        far_copy(k).wait()


def gather_anchors(values):
    dps = lax.axis_size("dp")
    planes = lax.axis_size("span") * lax.axis_size("tensor")
    dma = pltpu.SemaphoreType.DMA
    vmem = pl.BlockSpec(memory_space=pltpu.VMEM)

    def body(*refs):
        anchors_kernel(dps, planes, *refs)

    return pl.pallas_call(
        body,
        name="gather_anchors",
        out_shape=jax.ShapeDtypeStruct((dps, planes) + values.shape, values.dtype),
        in_specs=[vmem],
        out_specs=vmem,
        scratch_shapes=[dma((planes,)), dma((planes,)), dma((dps,)), dma((dps,)), dma],
        compiler_params=pltpu.CompilerParams(collective_id=0, has_side_effects=True),
    )(values)


VECTORS = ("pb", "g0", "g1", "s0", "s1", "sb")
ROWS_PER_CHUNK = 4
CHUNKS_PER_LAYER = 4
FAR_LANE = 256


def total_kernel(dps, planes, inputs, out_ref, x_ref, parts, sums, sems):
    one_send, one_recv, two_send, two_recv, three_send, three_recv = sems
    dp = lax.axis_index("dp")
    side = lax.axis_index("span")
    tensor = lax.axis_index("tensor")
    me = side * TENSORS + tensor
    flip_one = tensor + 1 - 2 * lax.rem(tensor, 2)
    flip_two = tensor + 2 - 4 * (tensor // 2)
    order = (
        tensor, flip_one + side * (flip_two - flip_one), flip_two + side * (flip_one - flip_two),
        TENSORS - 1 - tensor,
    )

    x_ref[...] = jnp.zeros_like(x_ref)
    for l, (vectors, eb, dq, dv) in enumerate(inputs):
        base = l * CHUNKS_PER_LAYER
        for j in range(TENSORS):
            row = pl.ds(order[j], 1)
            cols = dq[j].shape[1]
            x_ref[base, row, :] = eb[j][...]
            x_ref[base + 1, row, :cols] = dq[j][...]
            x_ref[base + 1, row, FAR_LANE : FAR_LANE + cols] = dv[j][...]
        for i, vector in enumerate(vectors):
            at = 2 * ROWS_PER_CHUNK + i
            x_ref[base + at // ROWS_PER_CHUNK, pl.ds(at % ROWS_PER_CHUNK, 1), :] = vector[...]

    def near_peer(k):
        return lax.rem(me + k, planes)

    def near(k):
        peer = near_peer(k)
        return {"span": peer // TENSORS, "tensor": lax.rem(peer, TENSORS)}

    def far(k):
        return {"dp": lax.rem(dp + k, dps)}

    barrier = pltpu.get_barrier_semaphore()
    for k in range(1, planes):
        pl.semaphore_signal(barrier, inc=1, device_id=near(k), device_id_type=MESH)
    for k in range(1, dps):
        pl.semaphore_signal(barrier, inc=1, device_id=far(k), device_id_type=MESH)
    pl.semaphore_wait(barrier, planes + dps - 2)

    def one(k):
        return pltpu.make_async_remote_copy(
            src_ref=x_ref.at[near_peer(k)], dst_ref=parts.at[k], send_sem=one_send.at[k],
            recv_sem=one_recv.at[k], device_id=near(k), device_id_type=MESH,
        )

    def two(k):
        return pltpu.make_async_remote_copy(
            src_ref=sums.at[dp], dst_ref=sums.at[dp], send_sem=two_send.at[k],
            recv_sem=two_recv.at[k], device_id=far(k), device_id_type=MESH,
        )

    def three(k):
        return pltpu.make_async_remote_copy(
            src_ref=out_ref.at[me], dst_ref=out_ref.at[me], send_sem=three_send.at[k],
            recv_sem=three_recv.at[k], device_id=near(k), device_id_type=MESH,
        )

    for k in range(1, planes):
        one(k).start()
    for k in range(1, planes):
        one(k).wait()
    total = x_ref[me]
    for k in range(1, planes):
        total = total + parts[k]
    sums[dp] = total
    for k in range(1, dps):
        two(k).start()
    for k in range(1, dps):
        two(k).wait()
    total = sums[0]
    for k in range(1, dps):
        total = total + sums[k]
    out_ref[me] = total
    for k in range(1, planes):
        three(k).start()
    for k in range(1, planes):
        three(k).wait()


def total_over_all(layers):
    dps = lax.axis_size("dp")
    planes = lax.axis_size("span") * lax.axis_size("tensor")
    flat, tree = jax.tree.flatten(layers)
    width = layers[0][0][0].shape[1]
    shape = (planes, ROWS_PER_CHUNK, width)
    dma = pltpu.SemaphoreType.DMA
    vmem = pl.BlockSpec(memory_space=pltpu.VMEM)

    def body(*refs):
        inputs = jax.tree.unflatten(tree, refs[: len(flat)])
        out_ref, x_ref, parts, sums = refs[len(flat) : len(flat) + 4]
        total_kernel(dps, planes, inputs, out_ref, x_ref, parts, sums, refs[len(flat) + 4 :])

    return pl.pallas_call(
        body,
        name="total_over_all",
        out_shape=jax.ShapeDtypeStruct(shape, F32),
        in_specs=[vmem] * len(flat),
        out_specs=vmem,
        scratch_shapes=[
            pltpu.VMEM(shape, F32),
            pltpu.VMEM(shape, F32),
            pltpu.VMEM((dps,) + shape[1:], F32),
            dma((planes,)), dma((planes,)), dma((dps,)), dma((dps,)), dma((planes,)), dma((planes,)),
        ],
        compiler_params=pltpu.CompilerParams(collective_id=1, has_side_effects=True),
    )(*flat)


def to_rows(values):
    return lax.all_to_all(values, "tensor", split_axis=0, concat_axis=0, tiled=True).reshape(
        -1, values.shape[-1]
    )


def to_places(values):
    blocks = values.reshape(TENSORS, -1, values.shape[-1])
    return lax.all_to_all(blocks, "tensor", split_axis=0, concat_axis=0, tiled=True)


def layer_forward(x, seg, attn_w, ffn_w, vec):
    down, across = seg
    xb = x.astype(BF)
    cols = vec["qb"][0].shape[0]
    q_k, v, o, lse = [], [], [], []
    z1 = x + vec["pb"]
    for (first, second), qb, vb in zip(attn_w, vec["qb"], vec["vb"]):
        bias = jnp.concatenate([qb, jnp.zeros_like(qb)])
        q_k.append((mm(xb, first[: 2 * cols], 1, 1) + bias).astype(BF))
        v.append((mm(xb, second[:cols], 1, 1) + vb).astype(BF))
        mixed, total = attend_forward(q_k[-1], v[-1], down, across)
        o.append(mixed)
        lse.append(total)
        z1 = z1 + mm(mixed, second[cols : 2 * cols], 1, 0)
    n1, r1 = normal_parts(z1)
    y = n1 * vec["g0"] + vec["s0"]
    yb = y.astype(BF)
    act, slope = [], []
    z2 = y + vec["sb"]
    for (first, second), bias in zip(ffn_w, vec["eb"]):
        a, b = gelu_parts(mm(yb, first, 1, 0) + bias)
        act.append(a.astype(BF))
        slope.append(b.astype(BF))
        z2 = z2 + mm(act[-1], second, 1, 0)
    n2, r2 = normal_parts(z2)
    out = n2 * vec["g1"] + vec["s1"]
    return out, (xb, q_k, v, o, lse, n1, r1, yb, act, slope, n2, r2)


def total_rows(values):
    return jnp.sum(values.astype(F32), axis=0, keepdims=True)


def ffn_backward(dout, ffn_w, vec, kept, hook):
    xb, q_k, v, o, lse, n1, r1, yb, act, slope, n2, r2 = kept
    dz2 = normal_back(dout, n2, r2, vec["g1"])
    small = {"g1": total_rows(dout * n2), "s1": total_rows(dout), "sb": total_rows(dz2), "eb": []}
    dz2 = hook("seeded", dz2)
    dzb = dz2.astype(BF)
    dy = dz2
    hidden = []
    for (first, second), b in zip(ffn_w, slope):
        dhid = mm(dzb, second, 1, 1) * b.astype(F32)
        small["eb"].append(total_rows(dhid))
        hidden.append(dhid.astype(BF))
        dy = dy + mm(hidden[-1], first, 1, 1)
    dy = hook("hidden", dy)
    blocks = [(mm(yb, h, 0, 0).astype(BF), mm(a, dzb, 0, 0).astype(BF)) for h, a in zip(hidden, act)]
    return dy, blocks, small


def attn_backward(dy, seg, attn_w, vec, kept, hook):
    xb, q_k, v, o, lse, n1, r1, yb, act, slope, n2, r2 = kept
    down, across = seg
    cols = vec["qb"][0].shape[0]
    dz1 = normal_back(dy, n1, r1, vec["g0"])
    small = {"g0": total_rows(dy * n1), "s0": total_rows(dy), "pb": total_rows(dz1), "dq": [], "dv": []}
    dz1 = hook("normed", dz1)
    da = dz1.astype(BF)
    dx = dz1
    grads = []
    for j, (first, second) in enumerate(attn_w):
        do = mm(da, second[cols : 2 * cols], 1, 1).astype(BF)
        dqk, dv = attend_backward(q_k[j], v[j], do, lse[j], down, across)
        dx = dx + mm(dqk, first[: 2 * cols], 1, 0) + mm(dv, second[:cols], 1, 0)
        small["dq"].append(total_rows(dqk[:, :cols]))
        small["dv"].append(total_rows(dv))
        grads.append((dqk, dv))
        if j == 2:
            da, dx = hook("three", (da, dx))
    blocks = [
        (
            mm(dqk, xb, 0, 0).astype(BF),
            jnp.concatenate([mm(dv, xb, 0, 0), mm(o_j, da, 0, 0)], axis=0).astype(BF),
        )
        for (dqk, dv), o_j in zip(grads, o)
    ]
    return dx, blocks, small


def attn_unpack(first, second):
    cols = first.shape[0] // 2
    heads = jnp.stack([first[:cols], first[cols:], second[:cols]])
    return jnp.swapaxes(heads, 1, 2), second[cols:]


class Reduction:
    def __init__(self, side):
        self.side = side

    def start(self, value, blocks):
        self.blocks = blocks
        value, *self.outgoing = tie(value, *reduce_outgoing(blocks, self.side))
        return value

    def swapped(self, value):
        value, self.main_rest, self.main_own, self.across, self.mine = tie(
            value, *reduce_swapped(self.blocks, self.outgoing, self.side)
        )
        self.from_rest = send(self.main_rest, MAIN)
        return value

    def crossed(self, value):
        value, self.main_own = tie(value, reduce_across(self.main_own, self.across))
        self.from_own = send(self.main_own, MAIN)
        self.from_peer = send(self.from_rest, SWAP)
        return value

    def summed(self, value):
        value, self.total = tie(value, plus(self.mine, self.from_own, self.from_peer))
        return value


def shards(
    layer_input, skip_tokens, backbone_cotangent, head_cotangent, segment_lengths, pair_index,
    w_heads, heads_bias, w_project, project_bias, norm_gain, norm_shift,
    w_expand, expand_bias, w_shrink, shrink_bias,
):
    side = lax.axis_index("span")
    mine = lax.axis_index("tensor")
    width = layer_input.shape[-1]
    head_cols = w_heads.shape[-1]
    ff_cols = w_expand.shape[-1]

    extra = 16
    bias_rows = jnp.concatenate([heads_bias.reshape(1, 4 * head_cols), expand_bias], axis=0)
    bias_rows = jnp.pad(bias_rows, ((0, extra - bias_rows.shape[0]), (0, 0)))

    def attn_rows(l):
        heads = jnp.swapaxes(w_heads[l], 1, 2)
        first = heads[:2].reshape(2 * head_cols, width)
        return first, jnp.concatenate([heads[2], w_project[l]], axis=0)

    first, second = attn_rows(0)
    first = jnp.concatenate([first, bias_rows], axis=0)
    second = jnp.pad(second, ((0, extra), (0, 0)))
    attn_w0, mark = gather_part(first, second, side)
    x = to_rows(layer_input[0])
    first, second, mark = tie(w_expand[0], w_shrink[0], mark)
    ffn_w0, mark = gather_part(first, second, side)
    first, second, mark = tie(*attn_rows(1), mark)
    attn_w1, mark = gather_part(first, second, side)
    later_skip, mark = tie(skip_tokens[0], mark)
    skip = to_rows(later_skip)
    first, second, mark = tie(w_expand[1], w_shrink[1], mark)
    ffn_w1, mark = gather_part(first, second, side)
    later_head, later_backbone, mark = tie(head_cotangent[0], backbone_cotangent[0], mark)
    head_cot = to_rows(later_head)
    backbone_cot = to_rows(later_backbone)
    tokens = x.shape[0]

    biases = [first[2 * head_cols : 2 * head_cols + 3].astype(F32) for first, second in attn_w0]

    def vectors(l):
        heads = [b[0].reshape(2, 2, head_cols)[l] for b in biases]
        return {
            "qb": [h[0] for h in heads], "vb": [h[1] for h in heads],
            "eb": [b[1 + l] for b in biases], "pb": project_bias[l].astype(F32),
            "g0": norm_gain[l, 0].astype(F32), "g1": norm_gain[l, 1].astype(F32),
            "s0": norm_shift[l, 0].astype(F32), "s1": norm_shift[l, 1].astype(F32),
            "sb": shrink_bias[l].astype(F32),
        }

    lengths = lax.dynamic_index_in_dim(segment_lengths[0], mine, 0, keepdims=False)
    span_count = lengths.shape[0]
    starts = jnp.cumsum(lengths) - lengths
    row_length = jnp.sum(lengths)
    places = jnp.arange(tokens, dtype=jnp.int32)
    counted = jnp.sum((places[:, None] >= starts[None, :]).astype(jnp.int32), axis=-1) - 1
    segment = jnp.where(places < row_length, counted, span_count)
    seg = (segment[:, None], segment[None, :])
    valid = (places < row_length).astype(F32)[:, None]
    picker = (starts[:, None] == places[None, :]).astype(F32)
    first_place = jnp.sum(picker, axis=0)[:, None] > 0

    vec0, vec1 = vectors(0), vectors(1)
    backbone, kept0 = layer_forward(x.astype(F32), seg, attn_w0, ffn_w0, vec0)
    cls = mm(picker.astype(BF), backbone.astype(BF), 1, 0).astype(BF)
    anchors = gather_anchors(cls)
    dp_count = lax.axis_size("dp")
    pair_count = lax.axis_size("span")
    vector_count = dp_count * TENSORS * span_count
    anchors = anchors.reshape(dp_count, pair_count, TENSORS * span_count, width)
    anchors = jnp.swapaxes(anchors, 0, 1).reshape(pair_count, vector_count, width)

    head_in = jnp.where(first_place, backbone, skip.astype(F32))
    head, kept1 = layer_forward(head_in, seg, attn_w1, ffn_w1, vec1)

    root = math.sqrt(width)
    logits = mm(anchors[0], anchors[1], 1, 1) / root
    columns = jnp.arange(vector_count, dtype=jnp.int32)
    target = (pair_index[:, None] == columns[None, :]).astype(F32)
    lse_rows = jax.nn.logsumexp(logits, axis=1)
    lse_cols = jax.nn.logsumexp(logits, axis=0)
    dlogits = LOSS_WEIGHT * (
        jnp.exp(logits - lse_rows[:, None]) + jnp.exp(logits - lse_cols[None, :]) - 2.0 * target
    )
    span_loss = (jnp.sum(lse_rows) + jnp.sum(lse_cols) - 2.0 * jnp.sum(target * logits)) / (
        2 * vector_count
    )
    own = (lax.axis_index("dp") * TENSORS + mine) * span_count
    wanted = jnp.where(side == 0, dlogits, dlogits.T)
    wanted = lax.dynamic_slice(wanted, (own, 0), (span_count, vector_count))
    other = lax.dynamic_index_in_dim(anchors, 1 - side, 0, keepdims=False).astype(F32)
    dcls = jnp.dot(wanted, other, precision=HIGHEST) / root

    ffn1, attn1, ffn0, attn0 = (Reduction(side) for _ in range(4))

    def plain(name, value):
        return value

    dy, blocks, small1 = ffn_backward(head_cot.astype(F32) * valid, ffn_w1, vec1, kept1, plain)
    dy = ffn1.start(dy, blocks)

    def during_attn1(name, value):
        if name == "normed":
            return ffn1.swapped(value)
        return ffn1.crossed(value)

    du, blocks, more = attn_backward(dy, seg, attn_w1, vec1, kept1, during_attn1)
    small1.update(more)
    du = attn1.start(du, blocks)
    du = ffn1.summed(du)
    grad_skip = jnp.where(first_place, 0.0, du).astype(BF)

    seed = backbone_cot.astype(F32) * valid + jnp.where(first_place, du, 0.0)
    seed = seed + jnp.dot(picker.T, dcls, precision=HIGHEST)

    def during_ffn0(name, value):
        if name == "seeded":
            return attn1.swapped(value)
        return attn1.crossed(value)

    dy, blocks, small0 = ffn_backward(seed, ffn_w0, vec0, kept0, during_ffn0)
    dy = ffn0.start(dy, blocks)
    dy = attn1.summed(dy)
    ffn_total1, attn_total1 = lax.psum((ffn1.total, attn1.total), "dp")

    def during_attn0(name, value):
        if name == "normed":
            return ffn0.swapped(value)
        return ffn0.crossed(value)

    dx, blocks, more = attn_backward(dy, seg, attn_w0, vec0, kept0, during_attn0)
    small0.update(more)
    dx = attn0.start(dx, blocks)
    dx = ffn0.summed(dx)
    ffn_total0, ffn_total1, attn_total1 = tie(ffn0.total, ffn_total1, attn_total1)
    ffn_total0 = lax.psum(ffn_total0, "dp")

    rows0, rows1 = (
        ([small[k] for k in VECTORS], small["eb"], small["dq"], small["dv"]) for small in (small0, small1)
    )
    last = attn0.swapped(rows0[0][0])
    rows0[0][0] = last
    total = total_over_all((rows0, rows1))
    total = attn0.crossed(total)
    total = attn0.summed(total)
    attn_total0, ffn_total0 = tie(attn0.total, ffn_total0)
    attn_total0 = lax.psum(attn_total0, "dp")

    hb, eb, vector_sums = [], [], []
    for l in range(2):
        base = l * CHUNKS_PER_LAYER
        own = lax.dynamic_slice(total[base : base + 2], (0, mine, 0), (2, 1, width))[:, 0]
        eb.append(own[0])
        hb.append(jnp.stack([own[1, :head_cols], own[1, FAR_LANE : FAR_LANE + head_cols]]))
        rows = total[base + 2 : base + CHUNKS_PER_LAYER].reshape(-1, width)
        vector_sums.append({k: rows[i] for i, k in enumerate(VECTORS)})
    sums = vector_sums

    ge1, gs1 = finish_part(ffn_total1, side)
    gh1, gp1 = attn_unpack(*finish_part(attn_total1, side))
    ge0, gs0 = finish_part(ffn_total0, side)
    gh0, gp0 = attn_unpack(*finish_part(attn_total0, side))

    return (
        to_places((backbone * valid).astype(BF))[None],
        to_places((head * valid).astype(BF))[None],
        span_loss,
        to_places(dx.astype(BF))[None],
        to_places(grad_skip)[None],
        jnp.stack([gh0, gh1]),
        jnp.stack(hb),
        jnp.stack([gp0, gp1]),
        jnp.stack([s["pb"] for s in sums]),
        jnp.stack([jnp.stack([s["g0"], s["g1"]]) for s in sums]),
        jnp.stack([jnp.stack([s["s0"], s["s1"]]) for s in sums]),
        jnp.stack([ge0, ge1]),
        jnp.stack(eb),
        jnp.stack([gs0, gs1]),
        jnp.stack([s["sb"] for s in sums]),
    )


def solution(mesh):
    rows = P("span", "dp", "tensor", None)
    in_specs = (
        rows, rows, rows, rows, P("span", "dp", None), P(),
        P(None, None, None, "tensor"), P(None, None, "tensor"), P(None, "tensor", None),
        P(), P(), P(), P(None, None, "tensor"), P(None, "tensor"), P(None, "tensor", None), P(),
    )
    out_specs = (
        rows, rows, P(), rows, rows,
        P(None, None, None, "tensor"), P(None, None, "tensor"), P(None, "tensor", None),
        P(), P(), P(), P(None, None, "tensor"), P(None, "tensor"), P(None, "tensor", None), P(),
    )
    return jax.shard_map(shards, mesh=mesh, in_specs=in_specs, out_specs=out_specs, check_vma=False)
```

time: 848 us -> 744 us (0.88)
  local copies, waits for them, and re-layouts: 137 us -> 60.8 us
  waiting for transfers between devices: 205 us -> 166 us
  other arithmetic: 105 us -> 87.8 us
  between operations: 7.89 us -> 20.6 us
  starting transfers between devices: 67.1 us -> 76.8 us
    psum x0 -> x3, waiting for transfers between devices: none -> 90.4 us  [the longest x1 50.3 us: shards(): ffn_total0 = lax.psum(ffn_total0, 'dp')]
    ppermute x12 -> x0, waiting for transfers between devices: 85.5 us -> none  [the longest x6 61.1 us: sum_over_dp(): got = lax.ppermute(values, 'dp', pairs)]
    ppermute x30 -> x60, waiting for transfers between devices: 116 us -> 60.8 us  [send(): return lax.ppermute(values, PLANE, plane_pairs(kind))]
    unnamed x635 -> x445, local copies, waits for them, and re-layouts: 82 us -> 28.6 us
    unnamed x5 -> x0, other arithmetic: 26.8 us -> none
    ppermute x30 -> x60, starting transfers between devices: 25.1 us -> 44.4 us  [send(): return lax.ppermute(values, PLANE, plane_pairs(kind))]
    all_to_all x8, waiting for transfers between devices: 3.29 us -> 15 us  [the longest x4 14.6 us: to_places(): lax.all_to_all(blocks, 'tensor', split_axis=0, concat_axis=0, tiled=True)]
    convert_element_type x15 -> x16, other arithmetic: 16.2 us -> 25.6 us  [plus(): return total.astype(BF)]
  transfers between devices with their start and end apart: 50 -> 71, of which waited for: 20 -> 14; matrix products, arithmetic and copies ran while one was open for 29% -> 42% of each run, Pallas kernels for 10% -> 17%
where the time goes in v3:
time: 744 us; the launch traced here: 732 us
  matrix products  192 us (26%)
  waiting for transfers between devices  166 us (22%)
  Pallas kernels  127 us (17%)
  other arithmetic  87.8 us (12%)
  starting transfers between devices  76.8 us (10%)
  local copies, waits for them, and re-layouts  60.8 us (8%)
  between operations  20.6 us (3%)
    dot_general x122, matrix products, mm(): lax.dot_general(a, b, (((ca,), (cb,)), ((), ())), preferred_element_type=...  187 us
    ppermute x60, waiting for transfers between devices, send(): return lax.ppermute(values, PLANE, plane_pairs(kind))  60.8 us
    psum x1, waiting for transfers between devices, shards(): ffn_total0 = lax.psum(ffn_total0, 'dp')  50.3 us
    pallas_call x8, Pallas kernels, attend_backward(): pl.pallas_call(attend_backward_kernel, name='attend_backward', out_shape=...  50.3 us
    ppermute x60, starting transfers between devices, send(): return lax.ppermute(values, PLANE, plane_pairs(kind))  44.4 us
    pallas_call x8, Pallas kernels, attend_forward(): pl.pallas_call(attend_forward_kernel, name='attend_forward', out_shape=(j...  41.6 us
    psum x1, waiting for transfers between devices, shards(): attn_total0 = lax.psum(attn_total0, 'dp')  40 us
    unnamed x445, local copies, waits for them, and re-layouts  28.6 us
  transfers between devices with their start and end apart: 71, of which 14 were waited for; matrix products, arithmetic and copies ran while one was open for 42% of the time, Pallas kernels for 17%

profile of v3, /device:TPU:0, one launch (start us, length us, event | category | flops | bytes accessed | tf_op | source)
XLA Modules:
  0.0 731.7 jit_solution(7192036991129429191)
XLA Ops:
  9.8 3.0 collective-permute-start
  14.9 3.8 all-to-all-start
  18.7 4.6 slice_bitcast_fusion
  37.7 5.2 attend_forward.8
  52.8 5.2 attend_forward.9
  59.6 8.6 %collective-permute-done.19 = bf16[768,768]{1,0:T(8,128)(2,1)} collective-permute-done((bf16[768,768]{1,0:T(8,128)(2,1)}, bf16[768,768]{1,0:T(8,128)(2,1)}, u32[]{:S(2)}, u32[]{:S(2)}) %collective-permute-start.19) | collective-permute-done | bytes 1179680 | tf_op jit(solution)/shard_map/ppermute | solution.py:62
  76.1 5.2 attend_forward.10
  83.7 5.2 attend_forward.11
  90.0 6.8 collective-permute-done.6
  96.8 12.6 %collective-permute-done.7 = bf16[768,768]{1,0:T(8,128)(2,1)S(1)} collective-permute-done((bf16[768,768]{1,0:T(8,128)(2,1)S(1)}, bf16[768,768]{1,0:T(8,128)(2,1)S(1)}, u32[]{:S(2)}, u32[]{:S(2)}) %collective-permute-start.7) | collective-permute-done | bytes 1179680 | tf_op jit(solution)/shard_map/ppermute | solution.py:62
  117.7 4.0 all-to-all-start.5
  122.2 3.6 multiply_convert_fusion.8
  125.9 7.3 collective-permute-done.10
  139.2 4.1 collective-permute-done.12
  143.4 6.3 collective-permute-done.13
  153.6 3.3 multiply_convert_fusion.7
  157.0 3.4 fusion.233
  161.6 3.5 all-to-all-start.2
  173.5 14.3 %gather_anchors.1 = bf16[4,8,4,768]{3,2,1,0:T(4,128)(2,1)} custom-call(bf16[4,768]{1,0:T(4,128)(2,1)} %convolution_convert_fusion.48.refs_0_), custom_call_target="tpu_custom_call" | custom-call | tf_op jit(solution)/shard_map/gather_anchors/pallas_call | solution.py:265
  192.3 4.2 all-to-all-start.4
  205.8 5.2 attend_forward.15
  211.0 5.1 attend_forward.12
  220.5 5.2 attend_forward.14
  228.9 5.3 attend_forward.13
  301.9 6.2 attend_backward.8
  317.7 6.2 attend_backward.10
  338.0 6.3 attend_backward.9
  362.0 6.4 attend_backward.11
  374.7 3.6 collective-permute-start.29
  384.0 8.5 %collective-permute-done.29 = bf16[768,768]{1,0:T(8,128)(2,1)S(1)} collective-permute-done((bf16[768,768]{1,0:T(8,128)(2,1)S(1)}, bf16[768,768]{1,0:T(8,128)(2,1)S(1)}, u32[]{:S(2)}, u32[]{:S(2)}) %collective-permute-start.29) | collective-permute-done | bytes 1179680 | tf_op jit(solution)/shard_map/ppermute | solution.py:62
  394.0 4.3 all-to-all-start.1
  398.5 3.9 multiply_reduce_fusion.2
  424.9 3.4 add_add_fusion.2
  442.3 3.0 collective-permute-done.37
  454.5 3.0 add_convert_fusion.3
  457.5 3.9 broadcast_select_fusion
  466.2 6.2 attend_backward.12
  482.6 6.3 attend_backward.14
  493.1 6.4 attend_backward.13
  515.8 6.3 attend_backward.15
  537.0 3.5 all-to-all-start.3
  548.9 14.5 %all-to-all-done.3 = bf16[4,128,768]{2,1,0:T(8,128)(2,1)S(1)} async-done(((bf16[4,128,768]{2,1,0:T(8,128)(2,1)}), bf16[4,128,768]{2,1,0:T(8,128)(2,1)S(1)}, u32[]{:S(2)}, u32[]{:S(2)}) %all-to-all-start.3) | async-done | bytes 786464 | tf_op jit(solution)/shard_map/all_to_all | solution.py:403
  563.4 4.4 all-to-all-start.7
  568.5 21.2 %total_over_all.1 = f32[8,4,768]{2,1,0:T(4,128)} custom-call(f32[1,768]{1,0:T(1,128)} %broadcast_in_dim.214.refs_0_, f32[1,768]{1,0:T(1,128)} %broadcast_in_dim.215.refs_1_, f32[1,768]{1,0:T(1,128)} %broadcast_in_dim.216.refs_2_, f32[1,768]{1,0:T(1,128)} %broadcast_in_dim.217.refs_3_, f32[1,768]{1,0:T(1,128)} %broadcast_in_dim.218.refs_4_, ...), custom_call_target="tpu_custom_call" | custom-call | tf_op jit(solution)/shard_map/total_over_all/pallas_call | solution.py:379
  594.6 3.1 add_convert_fusion
  597.7 4.3 all-to-all-start.6
  610.6 50.3 %all-reduce.15.cloned.1.call-done = bf16[768,768]{1,0:T(8,128)(2,1)} async-done(((bf16[768,768]{1,0:T(8,128)(2,1)}), bf16[768,768]{1,0:T(8,128)(2,1)}) %all-reduce.15.cloned.1.call-update) | async-done | bytes 1179664 | tf_op jit(solution)/shard_map/psum | solution.py:654
  663.0 40.0 %all-reduce.17.cloned.1.call-done = bf16[384,768]{1,0:T(8,128)(2,1)} async-done(((bf16[384,768]{1,0:T(8,128)(2,1)}), bf16[384,768]{1,0:T(8,128)(2,1)}) %all-reduce.17.cloned.1.call-update) | async-done | bytes 589840 | tf_op jit(solution)/shard_map/psum | solution.py:665
  (883 shorter events, 350.7 us)
Async XLA Ops:
  9.8 33.5 %collective-permute-start = (bf16[400,768]{1,0:T(8,128)(2,1)}, bf16[400,768]{1,0:T(8,128)(2,1)}, u32[]{:S(2)}, u32[]{:S(2)}) collective-permute-start(bf16[400,768]{1,0:T(8,128)(2,1)} %fusion.78), channel_id=1, source_target_pairs={{0,1},{1,0},{2,3},{3,2},{4,6},{5,7},{6,4},{7,5},{8,9},{9,8},{10,11... | collective-permute-start | bytes 1843208 | tf_op jit(solution)/shard_map/ppermute | solution.py:62
  14.4 28.9 %collective-permute-start.1 = (bf16[400,768]{1,0:T(8,128)(2,1)}, bf16[400,768]{1,0:T(8,128)(2,1)}, u32[]{:S(2)}, u32[]{:S(2)}) collective-permute-start(bf16[400,768]{1,0:T(8,128)(2,1)} %fusion.79), channel_id=1, source_target_pairs={{0,1},{1,0},{2,3},{3,2},{4,6},{5,7},{6,4},{7,5},{8,9},{9,8},{10,11... | collective-permute-start | bytes 1843208 | tf_op jit(solution)/shard_map/ppermute | solution.py:62
  14.9 21.8 %all-to-all-start = ((bf16[4,128,768]{2,1,0:T(8,128)(2,1)}), bf16[4,128,768]{2,1,0:T(8,128)(2,1)S(1)}, u32[]{:S(2)}, u32[]{:S(2)}) async-start(bf16[4,128,768]{2,1,0:T(8,128)(2,1)} %bitcast.395), calls=%async_computation | async-start | bytes 1572864 | tf_op jit(solution)/shard_map/all_to_all | solution.py:396
  23.3 36.3 %collective-permute-start.18 = (bf16[768,768]{1,0:T(8,128)(2,1)}, bf16[768,768]{1,0:T(8,128)(2,1)}, u32[]{:S(2)}, u32[]{:S(2)}) collective-permute-start(bf16[768,768]{1,0:T(8,128)(2,1)} %get-tuple-element.132), channel_id=1, source_target_pairs={{0,1},{1,0},{2,3},{3,2},{4,6},{5,7},{6,4},{7,5},{8,9},{9,8},{10,11... | collective-permute-start | bytes 3538952 | tf_op jit(solution)/shard_map/ppermute | solution.py:62
  25.4 42.8 %collective-permute-start.19 = (bf16[768,768]{1,0:T(8,128)(2,1)}, bf16[768,768]{1,0:T(8,128)(2,1)}, u32[]{:S(2)}, u32[]{:S(2)}) collective-permute-start(bf16[768,768]{1,0:T(8,128)(2,1)} %get-tuple-element.133), channel_id=1, source_target_pairs={{0,1},{1,0},{2,3},{3,2},{4,6},{5,7},{6,4},{7,5},{8,9},{9,8},{10,11... | collective-permute-start | bytes 3538952 | tf_op jit(solution)/shard_map/ppermute | solution.py:62
  44.5 27.2 %collective-permute-start.4 = (bf16[400,768]{1,0:T(8,128)(2,1)S(1)}, bf16[400,768]{1,0:T(8,128)(2,1)S(1)}, u32[]{:S(2)}, u32[]{:S(2)}) collective-permute-start(bf16[400,768]{1,0:T(8,128)(2,1)S(1)} %broadcast_select_fusion.16), channel_id=1, source_target_pairs={{0,2},{1,3},{2,0},{3,1},{4,5},{5,4},{6,7},{7,6},{8,10},{9,11},{10,... | collective-permute-start | bytes 1843208 | tf_op jit(solution)/shard_map/ppermute | solution.py:62
  48.5 25.2 %collective-permute-start.2 = (bf16[400,768]{1,0:T(8,128)(2,1)}, bf16[400,768]{1,0:T(8,128)(2,1)S(1)}, u32[]{:S(2)}, u32[]{:S(2)}) collective-permute-start(bf16[400,768]{1,0:T(8,128)(2,1)} %collective-permute-done), channel_id=1, source_target_pairs={{0,4},{1,5},{2,6},{3,7},{4,0},{5,1},{6,2},{7,3},{8,12},{9,13},{10,... | collective-permute-start | bytes 1843208 | tf_op jit(solution)/shard_map/ppermute | solution.py:62
  48.5 27.1 %collective-permute-start.3 = (bf16[400,768]{1,0:T(8,128)(2,1)}, bf16[400,768]{1,0:T(8,128)(2,1)S(1)}, u32[]{:S(2)}, u32[]{:S(2)}) collective-permute-start(bf16[400,768]{1,0:T(8,128)(2,1)} %collective-permute-done.1), channel_id=1, source_target_pairs={{0,4},{1,5},{2,6},{3,7},{4,0},{5,1},{6,2},{7,3},{8,12},{9,13},{10,... | collective-permute-start | bytes 1843208 | tf_op jit(solution)/shard_map/ppermute | solution.py:62
  69.6 48.1 %collective-permute-start.22 = (bf16[768,768]{1,0:T(8,128)(2,1)S(1)}, bf16[768,768]{1,0:T(8,128)(2,1)}, u32[]{:S(2)}, u32[]{:S(2)}) collective-permute-start(bf16[768,768]{1,0:T(8,128)(2,1)S(1)} %broadcast_select_fusion.10), channel_id=1, source_target_pairs={{0,2},{1,3},{2,0},{3,1},{4,5},{5,4},{6,7},{7,6},{8,10},{9,11},{10,... | collective-permute-start | bytes 3538952 | tf_op jit(solution)/shard_map/ppermute | solution.py:62
  71.7 25.1 %collective-permute-start.6 = (bf16[768,768]{1,0:T(8,128)(2,1)S(1)}, bf16[768,768]{1,0:T(8,128)(2,1)S(1)}, u32[]{:S(2)}, u32[]{:S(2)}) collective-permute-start(bf16[768,768]{1,0:T(8,128)(2,1)S(1)} %copy-done.111), channel_id=1, source_target_pairs={{0,1},{1,0},{2,3},{3,2},{4,6},{5,7},{6,4},{7,5},{8,9},{9,8},{10,11... | collective-permute-start | bytes 3538952 | tf_op jit(solution)/shard_map/ppermute | solution.py:62
  73.2 36.2 %collective-permute-start.7 = (bf16[768,768]{1,0:T(8,128)(2,1)S(1)}, bf16[768,768]{1,0:T(8,128)(2,1)S(1)}, u32[]{:S(2)}, u32[]{:S(2)}) collective-permute-start(bf16[768,768]{1,0:T(8,128)(2,1)S(1)} %copy-done.113), channel_id=1, source_target_pairs={{0,1},{1,0},{2,3},{3,2},{4,6},{5,7},{6,4},{7,5},{8,9},{9,8},{10,11... | collective-permute-start | bytes 3538952 | tf_op jit(solution)/shard_map/ppermute | solution.py:62
  110.9 22.3 %collective-permute-start.10 = (bf16[768,768]{1,0:T(8,128)(2,1)}, bf16[768,768]{1,0:T(8,128)(2,1)}, u32[]{:S(2)}, u32[]{:S(2)}) collective-permute-start(bf16[768,768]{1,0:T(8,128)(2,1)} %broadcast_select_fusion.13), channel_id=1, source_target_pairs={{0,2},{1,3},{2,0},{3,1},{4,5},{5,4},{6,7},{7,6},{8,10},{9,11},{10,... | collective-permute-start | bytes 3538952 | tf_op jit(solution)/shard_map/ppermute | solution.py:62
  117.7 19.9 %all-to-all-start.5 = ((bf16[4,128,768]{2,1,0:T(8,128)(2,1)}), bf16[4,128,768]{2,1,0:T(8,128)(2,1)S(1)}, u32[]{:S(2)}, u32[]{:S(2)}) async-start(bf16[4,128,768]{2,1,0:T(8,128)(2,1)} %bitcast.396), calls=%async_computation.5 | async-start | bytes 1572864 | tf_op jit(solution)/shard_map/all_to_all | solution.py:396
  121.7 29.2 %collective-permute-start.8 = (bf16[768,768]{1,0:T(8,128)(2,1)}, bf16[768,768]{1,0:T(8,128)(2,1)}, u32[]{:S(2)}, u32[]{:S(2)}) collective-permute-start(bf16[768,768]{1,0:T(8,128)(2,1)} %copy-done.133), channel_id=1, source_target_pairs={{0,4},{1,5},{2,6},{3,7},{4,0},{5,1},{6,2},{7,3},{8,12},{9,13},{10,... | collective-permute-start | bytes 3538952 | tf_op jit(solution)/shard_map/ppermute | solution.py:62
  121.7 35.2 %collective-permute-start.9 = (bf16[768,768]{1,0:T(8,128)(2,1)}, bf16[768,768]{1,0:T(8,128)(2,1)}, u32[]{:S(2)}, u32[]{:S(2)}) collective-permute-start(bf16[768,768]{1,0:T(8,128)(2,1)} %copy-done.135), channel_id=1, source_target_pairs={{0,4},{1,5},{2,6},{3,7},{4,0},{5,1},{6,2},{7,3},{8,12},{9,13},{10,... | collective-permute-start | bytes 3538952 | tf_op jit(solution)/shard_map/ppermute | solution.py:62
  133.2 16.5 %collective-permute-start.13 = (bf16[384,768]{1,0:T(8,128)(2,1)}, bf16[384,768]{1,0:T(8,128)(2,1)}, u32[]{:S(2)}, u32[]{:S(2)}) collective-permute-start(bf16[384,768]{1,0:T(8,128)(2,1)} %pad_maximum_fusion.2), channel_id=1, source_target_pairs={{0,1},{1,0},{2,3},{3,2},{4,6},{5,7},{6,4},{7,5},{8,9},{9,8},{10,11... | collective-permute-start | bytes 1769480 | tf_op jit(solution)/shard_map/ppermute | solution.py:62
  137.1 28.0 %collective-permute-start.11 = (bf16[768,768]{1,0:T(8,128)(2,1)}, bf16[768,768]{1,0:T(8,128)(2,1)}, u32[]{:S(2)}, u32[]{:S(2)}) collective-permute-start(bf16[768,768]{1,0:T(8,128)(2,1)} %collective-permute-done.10), channel_id=1, source_target_pairs={{0,4},{1,5},{2,6},{3,7},{4,0},{5,1},{6,2},{7,3},{8,12},{9,13},{10,... | collective-permute-start | bytes 3538952 | tf_op jit(solution)/shard_map/ppermute | solution.py:62
  143.4 104.2 %collective-permute-start.20 = (bf16[768,768]{1,0:T(8,128)(2,1)}, bf16[768,768]{1,0:T(8,128)(2,1)}, u32[]{:S(2)}, u32[]{:S(2)}) collective-permute-start(bf16[768,768]{1,0:T(8,128)(2,1)} %collective-permute-done.18), channel_id=1, source_target_pairs={{0,4},{1,5},{2,6},{3,7},{4,0},{5,1},{6,2},{7,3},{8,12},{9,13},{10,... | collective-permute-start | bytes 3538952 | tf_op jit(solution)/shard_map/ppermute | solution.py:62
  149.7 102.2 %collective-permute-start.21 = (bf16[768,768]{1,0:T(8,128)(2,1)}, bf16[768,768]{1,0:T(8,128)(2,1)}, u32[]{:S(2)}, u32[]{:S(2)}) collective-permute-start(bf16[768,768]{1,0:T(8,128)(2,1)} %collective-permute-done.19), channel_id=1, source_target_pairs={{0,4},{1,5},{2,6},{3,7},{4,0},{5,1},{6,2},{7,3},{8,12},{9,13},{10,... | collective-permute-start | bytes 3538952 | tf_op jit(solution)/shard_map/ppermute | solution.py:62
  156.9 92.8 %collective-permute-start.23 = (bf16[768,768]{1,0:T(8,128)(2,1)}, bf16[768,768]{1,0:T(8,128)(2,1)}, u32[]{:S(2)}, u32[]{:S(2)}) collective-permute-start(bf16[768,768]{1,0:T(8,128)(2,1)} %collective-permute-done.22), channel_id=1, source_target_pairs={{0,4},{1,5},{2,6},{3,7},{4,0},{5,1},{6,2},{7,3},{8,12},{9,13},{10,... | collective-permute-start | bytes 3538952 | tf_op jit(solution)/shard_map/ppermute | solution.py:62
  161.6 55.3 %collective-permute-start.15 = (bf16[384,768]{1,0:T(8,128)(2,1)}, bf16[384,768]{1,0:T(8,128)(2,1)}, u32[]{:S(2)}, u32[]{:S(2)}) collective-permute-start(bf16[384,768]{1,0:T(8,128)(2,1)} %collective-permute-done.12), channel_id=1, source_target_pairs={{0,4},{1,5},{2,6},{3,7},{4,0},{5,1},{6,2},{7,3},{8,12},{9,13},{10,... | collective-permute-start | bytes 1769480 | tf_op jit(solution)/shard_map/ppermute | solution.py:62
  161.6 30.7 %all-to-all-start.2 = ((bf16[4,128,768]{2,1,0:T(8,128)(2,1)}), bf16[4,128,768]{2,1,0:T(8,128)(2,1)S(1)}, u32[]{:S(2)}, u32[]{:S(2)}) async-start(bf16[4,128,768]{2,1,0:T(8,128)(2,1)} %bitcast.397), calls=%async_computation.2 | async-start | bytes 1572864 | tf_op jit(solution)/shard_map/all_to_all | solution.py:396
  165.1 35.4 %collective-permute-start.17 = (bf16[384,768]{1,0:T(8,128)(2,1)}, bf16[384,768]{1,0:T(8,128)(2,1)}, u32[]{:S(2)}, u32[]{:S(2)}) collective-permute-start(bf16[384,768]{1,0:T(8,128)(2,1)} %collective-permute-done.14), channel_id=1, source_target_pairs={{0,4},{1,5},{2,6},{3,7},{4,0},{5,1},{6,2},{7,3},{8,12},{9,13},{10,... | collective-permute-start | bytes 1769480 | tf_op jit(solution)/shard_map/ppermute | solution.py:62
  192.3 201.8 %all-to-all-start.4 = ((bf16[4,128,768]{2,1,0:T(8,128)(2,1)}), bf16[4,128,768]{2,1,0:T(8,128)(2,1)}, u32[]{:S(2)}, u32[]{:S(2)}) async-start(bf16[4,128,768]{2,1,0:T(8,128)(2,1)} %bitcast.398), calls=%async_computation.4 | async-start | bytes 1572864 | tf_op jit(solution)/shard_map/all_to_all | solution.py:396
  200.5 19.5 %collective-permute-start.16 = (bf16[384,768]{1,0:T(8,128)(2,1)}, bf16[384,768]{1,0:T(8,128)(2,1)S(1)}, u32[]{:S(2)}, u32[]{:S(2)}) collective-permute-start(bf16[384,768]{1,0:T(8,128)(2,1)} %collective-permute-done.13), channel_id=1, source_target_pairs={{0,4},{1,5},{2,6},{3,7},{4,0},{5,1},{6,2},{7,3},{8,12},{9,13},{10,... | collective-permute-start | bytes 1769480 | tf_op jit(solution)/shard_map/ppermute | solution.py:62
  329.4 25.8 %collective-permute-start.28 = (bf16[768,768]{1,0:T(8,128)(2,1)}, bf16[768,768]{1,0:T(8,128)(2,1)S(1)}, u32[]{:S(2)}, u32[]{:S(2)}) collective-permute-start(bf16[768,768]{1,0:T(8,128)(2,1)} %add_convert_fusion.9), channel_id=1, source_target_pairs={{0,2},{1,3},{2,0},{3,1},{4,5},{5,4},{6,7},{7,6},{8,10},{9,11},{10,... | collective-permute-start | bytes 3538952 | tf_op jit(solution)/shard_map/ppermute | solution.py:62
  333.6 45.2 %collective-permute-start.30 = (bf16[768,768]{1,0:T(8,128)(2,1)}, bf16[768,768]{1,0:T(8,128)(2,1)}, u32[]{:S(2)}, u32[]{:S(2)}) collective-permute-start(bf16[768,768]{1,0:T(8,128)(2,1)} %get-tuple-element.161), channel_id=1, source_target_pairs={{0,1},{1,0},{2,3},{3,2},{4,6},{5,7},{6,4},{7,5},{8,9},{9,8},{10,11... | collective-permute-start | bytes 3538952 | tf_op jit(solution)/shard_map/ppermute | solution.py:62
  374.7 17.8 %collective-permute-start.29 = (bf16[768,768]{1,0:T(8,128)(2,1)S(1)}, bf16[768,768]{1,0:T(8,128)(2,1)S(1)}, u32[]{:S(2)}, u32[]{:S(2)}) collective-permute-start(bf16[768,768]{1,0:T(8,128)(2,1)S(1)} %copy-done.120), channel_id=1, source_target_pairs={{0,1},{1,0},{2,3},{3,2},{4,6},{5,7},{6,4},{7,5},{8,9},{9,8},{10,11... | collective-permute-start | bytes 3538952 | tf_op jit(solution)/shard_map/ppermute | solution.py:62
  394.0 142.9 %all-to-all-start.1 = ((bf16[4,128,768]{2,1,0:T(8,128)(2,1)}), bf16[4,128,768]{2,1,0:T(8,128)(2,1)}, u32[]{:S(2)}, u32[]{:S(2)}) async-start(bf16[4,128,768]{2,1,0:T(8,128)(2,1)} %bitcast.29), calls=%async_computation.1 | async-start | bytes 1572864 | tf_op jit(solution)/shard_map/all_to_all | solution.py:403
  398.4 203.7 %all-reduce.19.cloned.1.call-start = ((), (), s32[]{:S(2)}) async-start(), calls=%async_computation.10 | async-start | bytes 3538944 | tf_op jit(solution)/shard_map/psum | solution.py:642
  408.1 27.0 %collective-permute-start.36 = (bf16[384,768]{1,0:T(8,128)(2,1)S(1)}, bf16[384,768]{1,0:T(8,128)(2,1)S(1)}, u32[]{:S(2)}, u32[]{:S(2)}) collective-permute-start(bf16[384,768]{1,0:T(8,128)(2,1)S(1)} %copy-done.152), channel_id=1, source_target_pairs={{0,2},{1,3},{2,0},{3,1},{4,5},{5,4},{6,7},{7,6},{8,10},{9,11},{10,... | collective-permute-start | bytes 1769480 | tf_op jit(solution)/shard_map/ppermute | solution.py:62
  416.5 19.6 %collective-permute-start.38 = (bf16[384,768]{1,0:T(8,128)(2,1)S(1)}, bf16[384,768]{1,0:T(8,128)(2,1)S(1)}, u32[]{:S(2)}, u32[]{:S(2)}) collective-permute-start(bf16[384,768]{1,0:T(8,128)(2,1)S(1)} %copy-done.205), channel_id=1, source_target_pairs={{0,1},{1,0},{2,3},{3,2},{4,6},{5,7},{6,4},{7,5},{8,9},{9,8},{10,11... | collective-permute-start | bytes 1769480 | tf_op jit(solution)/shard_map/ppermute | solution.py:62
  441.3 16.1 %collective-permute-start.41 = (bf16[768,768]{1,0:T(8,128)(2,1)}, bf16[768,768]{1,0:T(8,128)(2,1)}, u32[]{:S(2)}, u32[]{:S(2)}) collective-permute-start(bf16[768,768]{1,0:T(8,128)(2,1)} %convolution_convert_fusion.7), channel_id=1, source_target_pairs={{0,4},{1,5},{2,6},{3,7},{4,0},{5,1},{6,2},{7,3},{8,12},{9,13},{10,... | collective-permute-start | bytes 3538952 | tf_op jit(solution)/shard_map/ppermute | solution.py:62
  441.8 12.6 %collective-permute-start.42 = (bf16[768,768]{1,0:T(8,128)(2,1)}, bf16[768,768]{1,0:T(8,128)(2,1)}, u32[]{:S(2)}, u32[]{:S(2)}) collective-permute-start(bf16[768,768]{1,0:T(8,128)(2,1)} %get-tuple-element.178), channel_id=1, source_target_pairs={{0,4},{1,5},{2,6},{3,7},{4,0},{5,1},{6,2},{7,3},{8,12},{9,13},{10,... | collective-permute-start | bytes 3538952 | tf_op jit(solution)/shard_map/ppermute | solution.py:62
  441.9 19.4 %collective-permute-start.43 = (bf16[768,768]{1,0:T(8,128)(2,1)}, bf16[768,768]{1,0:T(8,128)(2,1)}, u32[]{:S(2)}, u32[]{:S(2)}) collective-permute-start(bf16[768,768]{1,0:T(8,128)(2,1)} %get-tuple-element.179), channel_id=1, source_target_pairs={{0,4},{1,5},{2,6},{3,7},{4,0},{5,1},{6,2},{7,3},{8,12},{9,13},{10,... | collective-permute-start | bytes 3538952 | tf_op jit(solution)/shard_map/ppermute | solution.py:62
  481.8 25.3 %collective-permute-start.44 = (bf16[768,768]{1,0:T(8,128)(2,1)}, bf16[768,768]{1,0:T(8,128)(2,1)S(1)}, u32[]{:S(2)}, u32[]{:S(2)}) collective-permute-start(bf16[768,768]{1,0:T(8,128)(2,1)} %add_convert_fusion.3), channel_id=1, source_target_pairs={{0,2},{1,3},{2,0},{3,1},{4,5},{5,4},{6,7},{7,6},{8,10},{9,11},{10,... | collective-permute-start | bytes 3538952 | tf_op jit(solution)/shard_map/ppermute | solution.py:62
  492.4 40.4 %collective-permute-start.46 = (bf16[768,768]{1,0:T(8,128)(2,1)}, bf16[768,768]{1,0:T(8,128)(2,1)}, u32[]{:S(2)}, u32[]{:S(2)}) collective-permute-start(bf16[768,768]{1,0:T(8,128)(2,1)} %get-tuple-element.200), channel_id=1, source_target_pairs={{0,1},{1,0},{2,3},{3,2},{4,6},{5,7},{6,4},{7,5},{8,9},{9,8},{10,11... | collective-permute-start | bytes 3538952 | tf_op jit(solution)/shard_map/ppermute | solution.py:62
  532.9 61.7 %collective-permute-start.45 = (bf16[768,768]{1,0:T(8,128)(2,1)}, bf16[768,768]{1,0:T(8,128)(2,1)}, u32[]{:S(2)}, u32[]{:S(2)}) collective-permute-start(bf16[768,768]{1,0:T(8,128)(2,1)} %add_convert_fusion.1), channel_id=1, source_target_pairs={{0,1},{1,0},{2,3},{3,2},{4,6},{5,7},{6,4},{7,5},{8,9},{9,8},{10,11... | collective-permute-start | bytes 3538952 | tf_op jit(solution)/shard_map/ppermute | solution.py:62
  534.3 60.3 %collective-permute-start.47 = (bf16[768,768]{1,0:T(8,128)(2,1)}, bf16[768,768]{1,0:T(8,128)(2,1)}, u32[]{:S(2)}, u32[]{:S(2)}) collective-permute-start(bf16[768,768]{1,0:T(8,128)(2,1)} %collective-permute-done.46), channel_id=1, source_target_pairs={{0,4},{1,5},{2,6},{3,7},{4,0},{5,1},{6,2},{7,3},{8,12},{9,13},{10,... | collective-permute-start | bytes 3538952 | tf_op jit(solution)/shard_map/ppermute | solution.py:62
  537.0 26.4 %all-to-all-start.3 = ((bf16[4,128,768]{2,1,0:T(8,128)(2,1)}), bf16[4,128,768]{2,1,0:T(8,128)(2,1)S(1)}, u32[]{:S(2)}, u32[]{:S(2)}) async-start(bf16[4,128,768]{2,1,0:T(8,128)(2,1)} %bitcast.49), calls=%async_computation.3 | async-start | bytes 1572864 | tf_op jit(solution)/shard_map/all_to_all | solution.py:403
  542.8 47.0 %collective-permute-start.52 = (bf16[384,768]{1,0:T(8,128)(2,1)}, bf16[384,768]{1,0:T(8,128)(2,1)}, u32[]{:S(2)}, u32[]{:S(2)}) collective-permute-start(bf16[384,768]{1,0:T(8,128)(2,1)} %add_convert_fusion.15), channel_id=1, source_target_pairs={{0,2},{1,3},{2,0},{3,1},{4,5},{5,4},{6,7},{7,6},{8,10},{9,11},{10,... | collective-permute-start | bytes 1769480 | tf_op jit(solution)/shard_map/ppermute | solution.py:62
  546.1 45.1 %collective-permute-start.54 = (bf16[384,768]{1,0:T(8,128)(2,1)}, bf16[384,768]{1,0:T(8,128)(2,1)}, u32[]{:S(2)}, u32[]{:S(2)}) collective-permute-start(bf16[384,768]{1,0:T(8,128)(2,1)} %get-tuple-element.212), channel_id=1, source_target_pairs={{0,1},{1,0},{2,3},{3,2},{4,6},{5,7},{6,4},{7,5},{8,9},{9,8},{10,11... | collective-permute-start | bytes 1769480 | tf_op jit(solution)/shard_map/ppermute | solution.py:62
  563.4 31.2 %all-to-all-start.7 = ((bf16[4,128,768]{2,1,0:T(8,128)(2,1)}), bf16[4,128,768]{2,1,0:T(8,128)(2,1)}, u32[]{:S(2)}, u32[]{:S(2)}) async-start(bf16[4,128,768]{2,1,0:T(8,128)(2,1)} %bitcast.64), calls=%async_computation.7 | async-start | bytes 1572864 | tf_op jit(solution)/shard_map/all_to_all | solution.py:403
  591.2 12.5 %collective-permute-start.55 = (bf16[384,768]{1,0:T(8,128)(2,1)}, bf16[384,768]{1,0:T(8,128)(2,1)}, u32[]{:S(2)}, u32[]{:S(2)}) collective-permute-start(bf16[384,768]{1,0:T(8,128)(2,1)} %collective-permute-done.54), channel_id=1, source_target_pairs={{0,4},{1,5},{2,6},{3,7},{4,0},{5,1},{6,2},{7,3},{8,12},{9,13},{10,... | collective-permute-start | bytes 1769480 | tf_op jit(solution)/shard_map/ppermute | solution.py:62
  597.7 63.3 %all-to-all-start.6 = ((bf16[4,128,768]{2,1,0:T(8,128)(2,1)}), bf16[4,128,768]{2,1,0:T(8,128)(2,1)}, u32[]{:S(2)}, u32[]{:S(2)}) async-start(bf16[4,128,768]{2,1,0:T(8,128)(2,1)} %bitcast.392), calls=%async_computation.6 | async-start | bytes 1572864 | tf_op jit(solution)/shard_map/all_to_all | solution.py:403
  602.0 59.0 %all-reduce.15.cloned.1.call-start = ((), (), s32[]{:S(2)}) async-start(), calls=%async_computation.8 | async-start | bytes 2359296 | tf_op jit(solution)/shard_map/psum | solution.py:654
  602.8 100.3 %all-reduce.17.cloned.1.call-start = ((), (), s32[]{:S(2)}) async-start(), calls=%async_computation.9 | async-start | bytes 1179648 | tf_op jit(solution)/shard_map/psum | solution.py:665
  603.0 102.6 %collective-permute-start.59 = (bf16[768,768]{1,0:T(8,128)(2,1)}, bf16[768,768]{1,0:T(8,128)(2,1)}, u32[]{:S(2)}, u32[]{:S(2)}) collective-permute-start(bf16[768,768]{1,0:T(8,128)(2,1)} %get-tuple-element.222), channel_id=1, source_target_pairs={{0,4},{1,5},{2,6},{3,7},{4,0},{5,1},{6,2},{7,3},{8,12},{9,13},{10,... | collective-permute-start | bytes 3538952 | tf_op jit(solution)/shard_map/ppermute | solution.py:62
  (242 other events, 2156.5 us)
Sparse Core Ops, SparseCore 0:
  452.2 74.1 all-reduce.18
  605.8 55.1 all-reduce.14
  663.9 39.0 all-reduce.16

commit v4 on v3

--- a/solution.py
+++ b/solution.py
@@ -118,34 +118,43 @@
 Q_ROWS = 128
 
 
-def attend_forward_kernel(qk_ref, v_ref, down_ref, across_ref, o_ref, lse_ref):
-    tokens, width = o_ref.shape
+def attend_forward_kernel(
+    layer, x_ref, first_ref, second_ref, bias_ref, z_ref, down_ref, across_ref,
+    q_ref, k_ref, v_ref, o_ref, lse_ref, out_ref
+):
+    tokens, width = q_ref.shape
+    at = 2 * layer * width
+    x = x_ref[...]
+    q_ref[...] = (mm(x, first_ref[:width, :], 1, 1) + bias_ref[:, at : at + width]).astype(BF)
+    k_ref[...] = mm(x, first_ref[width : 2 * width, :], 1, 1).astype(BF)
+    v_ref[...] = (mm(x, second_ref[:width, :], 1, 1) + bias_ref[:, at + width : at + 2 * width]).astype(BF)
 
     def step(i, carry):
         rows = pl.ds(pl.multiple_of(i * Q_ROWS, Q_ROWS), Q_ROWS)
         same = down_ref[rows, :] == across_ref[...]
         for h in range(width // HEAD_DIM):
-            at = h * HEAD_DIM
-            q = qk_ref[rows, at : at + HEAD_DIM]
-            k = qk_ref[:, width + at : width + at + HEAD_DIM]
-            v = v_ref[:, at : at + HEAD_DIM]
-            s = mm(q, k, 1, 1) * 0.125
+            head = slice(h * HEAD_DIM, (h + 1) * HEAD_DIM)
+            s = mm(q_ref[rows, head], k_ref[:, head], 1, 1) * 0.125
             s = jnp.where(same, s, MASKED)
             top = jnp.max(s, axis=-1, keepdims=True)
             raised = jnp.exp(s - top)
             total = jnp.sum(raised, axis=-1, keepdims=True)
             weights = (raised * (1.0 / total)).astype(BF)
-            o_ref[rows, at : at + HEAD_DIM] = mm(weights, v, 1, 0).astype(BF)
+            o_ref[rows, head] = mm(weights, v_ref[:, head], 1, 0).astype(BF)
             lse_ref[rows, h : h + 1] = top + jnp.log(total)
+        out_ref[rows, :] = z_ref[rows, :] + mm(o_ref[rows, :], second_ref[width : 2 * width, :], 1, 0)
         return carry
 
     lax.fori_loop(0, tokens // Q_ROWS, step, 0)
 
 
 def attend_backward_kernel(
-    qk_ref, v_ref, do_ref, lse_ref, down_ref, across_ref, dqk_ref, dv_out_ref, dk_ref, dv_ref
+    da_ref, x_ref, first_ref, second_ref, q_ref, k_ref, v_ref, o_ref, lse_ref, dx_ref, down_ref, across_ref,
+    dfirst_ref, dsecond_ref, sums_ref, out_ref, do_ref, dq_ref, dk_ref, dv_ref
 ):
-    tokens, width = do_ref.shape
+    tokens, width = q_ref.shape
+    da = da_ref[...]
+    do_ref[...] = mm(da, second_ref[width : 2 * width, :], 1, 1).astype(BF)
     dk_ref[...] = jnp.zeros_like(dk_ref)
     dv_ref[...] = jnp.zeros_like(dv_ref)
 
@@ -153,60 +162,85 @@
         rows = pl.ds(pl.multiple_of(i * Q_ROWS, Q_ROWS), Q_ROWS)
         same = down_ref[rows, :] == across_ref[...]
         for h in range(width // HEAD_DIM):
-            at = h * HEAD_DIM
-            q = qk_ref[rows, at : at + HEAD_DIM]
-            k = qk_ref[:, width + at : width + at + HEAD_DIM]
-            v = v_ref[:, at : at + HEAD_DIM]
-            up = do_ref[rows, at : at + HEAD_DIM]
+            head = slice(h * HEAD_DIM, (h + 1) * HEAD_DIM)
+            q, k, up = q_ref[rows, head], k_ref[:, head], do_ref[rows, head]
             s = mm(q, k, 1, 1) * 0.125
             s = jnp.where(same, s, MASKED)
             pr = jnp.exp(s - lse_ref[rows, h : h + 1])
-            dp = mm(up, v, 1, 1)
+            dp = mm(up, v_ref[:, head], 1, 1)
             inner = jnp.sum(pr * dp, axis=-1, keepdims=True)
             ds = (pr * (dp - inner)).astype(BF)
-            dqk_ref[rows, at : at + HEAD_DIM] = (mm(ds, k, 1, 0) * 0.125).astype(BF)
-            dk_ref[:, at : at + HEAD_DIM] += mm(ds, q, 0, 0)
-            dv_ref[:, at : at + HEAD_DIM] += mm(pr.astype(BF), up, 0, 0)
+            dq_ref[rows, head] = (mm(ds, k, 1, 0) * 0.125).astype(BF)
+            dk_ref[:, head] += mm(ds, q, 0, 0)
+            dv_ref[:, head] += mm(pr.astype(BF), up, 0, 0)
         return carry
 
     lax.fori_loop(0, tokens // Q_ROWS, step, 0)
-    dqk_ref[:, width:] = (dk_ref[...] * 0.125).astype(BF)
-    dv_out_ref[...] = dv_ref[...].astype(BF)
-
-
-def attend_cost(tokens, width, products):
+    x = x_ref[...]
+    dq = dq_ref[...]
+    dk = (dk_ref[...] * 0.125).astype(BF)
+    dv = dv_ref[...].astype(BF)
+    out_ref[...] = (
+        dx_ref[...]
+        + mm(dq, first_ref[:width, :], 1, 0)
+        + mm(dk, first_ref[width : 2 * width, :], 1, 0)
+        + mm(dv, second_ref[:width, :], 1, 0)
+    )
+    dfirst_ref[:width, :] = mm(dq, x, 0, 0).astype(BF)
+    dfirst_ref[width:, :] = mm(dk, x, 0, 0).astype(BF)
+    dsecond_ref[:width, :] = mm(dv, x, 0, 0).astype(BF)
+    dsecond_ref[width:, :] = mm(o_ref[...], da, 0, 0).astype(BF)
+    sums_ref[:, :width] = jnp.sum(dq.astype(F32), axis=0, keepdims=True)
+    sums_ref[:, width:] = jnp.sum(dv.astype(F32), axis=0, keepdims=True)
+
+
+def attend_cost(tokens, width, model, products, mats):
     heads = width // HEAD_DIM
     return pl.CostEstimate(
-        flops=2 * products * tokens * tokens * width,
-        bytes_accessed=2 * 8 * tokens * width,
+        flops=2 * tokens * width * (products * tokens + mats * model),
+        bytes_accessed=8 << 20,
         transcendentals=heads * tokens * tokens,
     )
 
 
-def attend_forward(qk, v, down, across):
-    tokens, width = v.shape
+def attend_forward(layer, cols, x, first, second, bias, z, seg):
+    tokens, model = x.shape
+    narrow = jax.ShapeDtypeStruct((tokens, cols), BF)
+
+    def body(*refs):
+        attend_forward_kernel(layer, *refs)
+
     return pl.pallas_call(
-        attend_forward_kernel,
+        body,
         name="attend_forward",
         out_shape=(
-            jax.ShapeDtypeStruct((tokens, width), BF),
-            jax.ShapeDtypeStruct((tokens, width // HEAD_DIM), F32),
+            narrow, narrow, narrow, narrow,
+            jax.ShapeDtypeStruct((tokens, cols // HEAD_DIM), F32),
+            jax.ShapeDtypeStruct(z.shape, F32),
         ),
         compiler_params=pltpu.CompilerParams(vmem_limit_bytes=24 << 20),
-        cost_estimate=attend_cost(tokens, width, 2),
-    )(qk, v, down, across)
-
-
-def attend_backward(qk, v, do, lse, down, across):
-    tokens, width = do.shape
+        cost_estimate=attend_cost(tokens, cols, model, 2, 4),
+    )(x, first, second, bias, z, *seg)
+
+
+def attend_backward(cols, da, x, first, second, kept, dx, seg):
+    tokens, model = x.shape
     return pl.pallas_call(
         attend_backward_kernel,
         name="attend_backward",
-        out_shape=(jax.ShapeDtypeStruct(qk.shape, BF), jax.ShapeDtypeStruct(v.shape, BF)),
-        scratch_shapes=[pltpu.VMEM((tokens, width), F32), pltpu.VMEM((tokens, width), F32)],
+        out_shape=(
+            jax.ShapeDtypeStruct((2 * cols, model), BF),
+            jax.ShapeDtypeStruct((2 * cols, model), BF),
+            jax.ShapeDtypeStruct((1, 2 * cols), F32),
+            jax.ShapeDtypeStruct(dx.shape, F32),
+        ),
+        scratch_shapes=[
+            pltpu.VMEM((tokens, cols), BF), pltpu.VMEM((tokens, cols), BF),
+            pltpu.VMEM((tokens, cols), F32), pltpu.VMEM((tokens, cols), F32),
+        ],
         compiler_params=pltpu.CompilerParams(vmem_limit_bytes=24 << 20),
-        cost_estimate=attend_cost(tokens, width, 5),
-    )(qk, v, do, lse, down, across)
+        cost_estimate=attend_cost(tokens, cols, model, 5, 8),
+    )(da, x, first, second, *kept, dx, *seg)
 
 
 def anchors_kernel(dps, planes, x_ref, out_ref, near_send, near_recv, far_send, far_recv, own_sem):
@@ -276,34 +310,27 @@
 VECTORS = ("pb", "g0", "g1", "s0", "s1", "sb")
 ROWS_PER_CHUNK = 4
 CHUNKS_PER_LAYER = 4
-FAR_LANE = 256
-
-
-def total_kernel(dps, planes, inputs, out_ref, x_ref, parts, sums, sems):
+
+
+def block_order(side, tensor):
+    flip_one = tensor + 1 - 2 * lax.rem(tensor, 2)
+    flip_two = tensor + 2 - 4 * (tensor // 2)
+    swing = side * (flip_two - flip_one)
+    return tensor, flip_one + swing, flip_two - swing, TENSORS - 1 - tensor
+
+
+def total_kernel(dps, planes, rows_ref, heads, out_ref, x_ref, parts, sums, sems):
     one_send, one_recv, two_send, two_recv, three_send, three_recv = sems
     dp = lax.axis_index("dp")
     side = lax.axis_index("span")
     tensor = lax.axis_index("tensor")
     me = side * TENSORS + tensor
-    flip_one = tensor + 1 - 2 * lax.rem(tensor, 2)
-    flip_two = tensor + 2 - 4 * (tensor // 2)
-    order = (
-        tensor, flip_one + side * (flip_two - flip_one), flip_two + side * (flip_one - flip_two),
-        TENSORS - 1 - tensor,
-    )
-
-    x_ref[...] = jnp.zeros_like(x_ref)
-    for l, (vectors, eb, dq, dv) in enumerate(inputs):
-        base = l * CHUNKS_PER_LAYER
+    order = block_order(side, tensor)
+    x_ref[...] = rows_ref[...]
+    for l in range(2):
         for j in range(TENSORS):
-            row = pl.ds(order[j], 1)
-            cols = dq[j].shape[1]
-            x_ref[base, row, :] = eb[j][...]
-            x_ref[base + 1, row, :cols] = dq[j][...]
-            x_ref[base + 1, row, FAR_LANE : FAR_LANE + cols] = dv[j][...]
-        for i, vector in enumerate(vectors):
-            at = 2 * ROWS_PER_CHUNK + i
-            x_ref[base + at // ROWS_PER_CHUNK, pl.ds(at % ROWS_PER_CHUNK, 1), :] = vector[...]
+            columns = heads[l][j].shape[1]
+            x_ref[l * CHUNKS_PER_LAYER + 1, pl.ds(order[j], 1), :columns] = heads[l][j][...]
 
     def near_peer(k):
         return lax.rem(me + k, planes)
@@ -362,25 +389,24 @@
         three(k).wait()
 
 
-def total_over_all(layers):
+def total_over_all(rows, heads):
     dps = lax.axis_size("dp")
     planes = lax.axis_size("span") * lax.axis_size("tensor")
-    flat, tree = jax.tree.flatten(layers)
-    width = layers[0][0][0].shape[1]
-    shape = (planes, ROWS_PER_CHUNK, width)
+    flat, tree = jax.tree.flatten(heads)
+    shape = rows.shape
     dma = pltpu.SemaphoreType.DMA
     vmem = pl.BlockSpec(memory_space=pltpu.VMEM)
 
-    def body(*refs):
+    def body(rows_ref, *refs):
         inputs = jax.tree.unflatten(tree, refs[: len(flat)])
         out_ref, x_ref, parts, sums = refs[len(flat) : len(flat) + 4]
-        total_kernel(dps, planes, inputs, out_ref, x_ref, parts, sums, refs[len(flat) + 4 :])
+        total_kernel(dps, planes, rows_ref, inputs, out_ref, x_ref, parts, sums, refs[len(flat) + 4 :])
 
     return pl.pallas_call(
         body,
         name="total_over_all",
         out_shape=jax.ShapeDtypeStruct(shape, F32),
-        in_specs=[vmem] * len(flat),
+        in_specs=[vmem] * (1 + len(flat)),
         out_specs=vmem,
         scratch_shapes=[
             pltpu.VMEM(shape, F32),
@@ -389,7 +415,7 @@
             dma((planes,)), dma((planes,)), dma((dps,)), dma((dps,)), dma((planes,)), dma((planes,)),
         ],
         compiler_params=pltpu.CompilerParams(collective_id=1, has_side_effects=True),
-    )(*flat)
+    )(rows, *flat)
 
 
 def to_rows(values):
@@ -403,20 +429,13 @@
     return lax.all_to_all(blocks, "tensor", split_axis=0, concat_axis=0, tiled=True)
 
 
-def layer_forward(x, seg, attn_w, ffn_w, vec):
-    down, across = seg
+def layer_forward(l, x, seg, attn_w, ffn_w, vec):
     xb = x.astype(BF)
-    cols = vec["qb"][0].shape[0]
-    q_k, v, o, lse = [], [], [], []
+    kept = []
     z1 = x + vec["pb"]
-    for (first, second), qb, vb in zip(attn_w, vec["qb"], vec["vb"]):
-        bias = jnp.concatenate([qb, jnp.zeros_like(qb)])
-        q_k.append((mm(xb, first[: 2 * cols], 1, 1) + bias).astype(BF))
-        v.append((mm(xb, second[:cols], 1, 1) + vb).astype(BF))
-        mixed, total = attend_forward(q_k[-1], v[-1], down, across)
-        o.append(mixed)
-        lse.append(total)
-        z1 = z1 + mm(mixed, second[cols : 2 * cols], 1, 0)
+    for (first, second), bias in zip(attn_w, vec["heads"]):
+        *saved, z1 = attend_forward(l, vec["cols"], xb, first, second, bias, z1, seg)
+        kept.append(saved)
     n1, r1 = normal_parts(z1)
     y = n1 * vec["g0"] + vec["s0"]
     yb = y.astype(BF)
@@ -429,15 +448,15 @@
         z2 = z2 + mm(act[-1], second, 1, 0)
     n2, r2 = normal_parts(z2)
     out = n2 * vec["g1"] + vec["s1"]
-    return out, (xb, q_k, v, o, lse, n1, r1, yb, act, slope, n2, r2)
+    return out, (xb, kept, n1, r1, yb, act, slope, n2, r2)
 
 
 def total_rows(values):
-    return jnp.sum(values.astype(F32), axis=0, keepdims=True)
+    return jnp.sum(values, axis=0)
 
 
 def ffn_backward(dout, ffn_w, vec, kept, hook):
-    xb, q_k, v, o, lse, n1, r1, yb, act, slope, n2, r2 = kept
+    xb, saved, n1, r1, yb, act, slope, n2, r2 = kept
     dz2 = normal_back(dout, n2, r2, vec["g1"])
     small = {"g1": total_rows(dout * n2), "s1": total_rows(dout), "sb": total_rows(dz2), "eb": []}
     dz2 = hook("seeded", dz2)
@@ -455,31 +474,19 @@
 
 
 def attn_backward(dy, seg, attn_w, vec, kept, hook):
-    xb, q_k, v, o, lse, n1, r1, yb, act, slope, n2, r2 = kept
-    down, across = seg
-    cols = vec["qb"][0].shape[0]
+    xb, saved, n1, r1, yb, act, slope, n2, r2 = kept
     dz1 = normal_back(dy, n1, r1, vec["g0"])
-    small = {"g0": total_rows(dy * n1), "s0": total_rows(dy), "pb": total_rows(dz1), "dq": [], "dv": []}
+    small = {"g0": total_rows(dy * n1), "s0": total_rows(dy), "pb": total_rows(dz1), "heads": []}
     dz1 = hook("normed", dz1)
     da = dz1.astype(BF)
     dx = dz1
-    grads = []
+    blocks = []
     for j, (first, second) in enumerate(attn_w):
-        do = mm(da, second[cols : 2 * cols], 1, 1).astype(BF)
-        dqk, dv = attend_backward(q_k[j], v[j], do, lse[j], down, across)
-        dx = dx + mm(dqk, first[: 2 * cols], 1, 0) + mm(dv, second[:cols], 1, 0)
-        small["dq"].append(total_rows(dqk[:, :cols]))
-        small["dv"].append(total_rows(dv))
-        grads.append((dqk, dv))
+        dfirst, dsecond, sums, dx = attend_backward(vec["cols"], da, xb, first, second, saved[j], dx, seg)
+        small["heads"].append(sums)
+        blocks.append((dfirst, dsecond))
         if j == 2:
             da, dx = hook("three", (da, dx))
-    blocks = [
-        (
-            mm(dqk, xb, 0, 0).astype(BF),
-            jnp.concatenate([mm(dv, xb, 0, 0), mm(o_j, da, 0, 0)], axis=0).astype(BF),
-        )
-        for (dqk, dv), o_j in zip(grads, o)
-    ]
     return dx, blocks, small
 
 
@@ -541,14 +548,15 @@
     second = jnp.pad(second, ((0, extra), (0, 0)))
     attn_w0, mark = gather_part(first, second, side)
     x = to_rows(layer_input[0])
-    first, second, mark = tie(w_expand[0], w_shrink[0], mark)
-    ffn_w0, mark = gather_part(first, second, side)
-    first, second, mark = tie(*attn_rows(1), mark)
-    attn_w1, mark = gather_part(first, second, side)
+    expand, shrink, first = tie(w_expand[0], w_shrink[0], first)
+    ffn_w0, mark = gather_part(expand, shrink, side)
+    first, second, expand = tie(*attn_rows(1), expand)
+    attn_w1, attn_mark = gather_part(first, second, side)
+    expand, shrink, first = tie(w_expand[1], w_shrink[1], first)
+    ffn_w1, ffn_mark = gather_part(expand, shrink, side)
     later_skip, mark = tie(skip_tokens[0], mark)
     skip = to_rows(later_skip)
-    first, second, mark = tie(w_expand[1], w_shrink[1], mark)
-    ffn_w1, mark = gather_part(first, second, side)
+    mark = attn_mark
     later_head, later_backbone, mark = tie(head_cotangent[0], backbone_cotangent[0], mark)
     head_cot = to_rows(later_head)
     backbone_cot = to_rows(later_backbone)
@@ -557,9 +565,8 @@
     biases = [first[2 * head_cols : 2 * head_cols + 3].astype(F32) for first, second in attn_w0]
 
     def vectors(l):
-        heads = [b[0].reshape(2, 2, head_cols)[l] for b in biases]
         return {
-            "qb": [h[0] for h in heads], "vb": [h[1] for h in heads],
+            "cols": head_cols, "heads": [b[:1] for b in biases],
             "eb": [b[1 + l] for b in biases], "pb": project_bias[l].astype(F32),
             "g0": norm_gain[l, 0].astype(F32), "g1": norm_gain[l, 1].astype(F32),
             "s0": norm_shift[l, 0].astype(F32), "s1": norm_shift[l, 1].astype(F32),
@@ -579,7 +586,7 @@
     first_place = jnp.sum(picker, axis=0)[:, None] > 0
 
     vec0, vec1 = vectors(0), vectors(1)
-    backbone, kept0 = layer_forward(x.astype(F32), seg, attn_w0, ffn_w0, vec0)
+    backbone, kept0 = layer_forward(0, x.astype(F32), seg, attn_w0, ffn_w0, vec0)
     cls = mm(picker.astype(BF), backbone.astype(BF), 1, 0).astype(BF)
     anchors = gather_anchors(cls)
     dp_count = lax.axis_size("dp")
@@ -589,7 +596,7 @@
     anchors = jnp.swapaxes(anchors, 0, 1).reshape(pair_count, vector_count, width)
 
     head_in = jnp.where(first_place, backbone, skip.astype(F32))
-    head, kept1 = layer_forward(head_in, seg, attn_w1, ffn_w1, vec1)
+    head, kept1 = layer_forward(1, head_in, seg, attn_w1, ffn_w1, vec1)
 
     root = math.sqrt(width)
     logits = mm(anchors[0], anchors[1], 1, 1) / root
@@ -650,15 +657,21 @@
     small0.update(more)
     dx = attn0.start(dx, blocks)
     dx = ffn0.summed(dx)
-    ffn_total0, ffn_total1, attn_total1 = tie(ffn0.total, ffn_total1, attn_total1)
-    ffn_total0 = lax.psum(ffn_total0, "dp")
-
-    rows0, rows1 = (
-        ([small[k] for k in VECTORS], small["eb"], small["dq"], small["dv"]) for small in (small0, small1)
-    )
-    last = attn0.swapped(rows0[0][0])
-    rows0[0][0] = last
-    total = total_over_all((rows0, rows1))
+    late, ffn_total1, attn_total1 = tie(ffn0.total, ffn_total1, attn_total1)
+    ffn_total0 = lax.psum(late, "dp")
+
+    order = block_order(side, mine)
+    place = lax.broadcasted_iota(jnp.int32, (2 * CHUNKS_PER_LAYER * ROWS_PER_CHUNK, 1), 0)
+    rows = jnp.zeros((place.shape[0], width), F32)
+    for l, small in enumerate((small0, small1)):
+        base = l * CHUNKS_PER_LAYER * ROWS_PER_CHUNK
+        for j in range(TENSORS):
+            rows = rows + jnp.where(place == base + order[j], small["eb"][j][None], 0.0)
+        for i, k in enumerate(VECTORS):
+            rows = rows + jnp.where(place == base + 2 * ROWS_PER_CHUNK + i, small[k][None], 0.0)
+    rows, mark = tie(rows.reshape(2 * CHUNKS_PER_LAYER, ROWS_PER_CHUNK, width), ffn0.total)
+    rows = attn0.swapped(rows)
+    total = total_over_all(rows, (small0["heads"], small1["heads"]))
     total = attn0.crossed(total)
     total = attn0.summed(total)
     attn_total0, ffn_total0 = tie(attn0.total, ffn_total0)
@@ -669,7 +682,7 @@
         base = l * CHUNKS_PER_LAYER
         own = lax.dynamic_slice(total[base : base + 2], (0, mine, 0), (2, 1, width))[:, 0]
         eb.append(own[0])
-        hb.append(jnp.stack([own[1, :head_cols], own[1, FAR_LANE : FAR_LANE + head_cols]]))
+        hb.append(jnp.stack([own[1, :head_cols], own[1, head_cols : 2 * head_cols]]))
         rows = total[base + 2 : base + CHUNKS_PER_LAYER].reshape(-1, width)
         vector_sums.append({k: rows[i] for i, k in enumerate(VECTORS)})
     sums = vector_sums

time: 744 us -> 722 us (0.970)
  matrix products: 192 us -> 116 us
  Pallas kernels: 127 us -> 157 us
  waiting for transfers between devices: 166 us -> 185 us
    dot_general x122 -> x50, matrix products: 187 us -> 111 us  [mm(): lax.dot_general(a, b, (((ca,), (cb,)), ((), ())), preferred_element_type=...]
    psum x1, waiting for transfers between devices: 0.02 us -> 37.3 us  [shards(): ffn_total1, attn_total1 = lax.psum((ffn1.total, attn1.total), 'dp')]
    psum x1, waiting for transfers between devices: 50.3 us -> 25.6 us  [shards(): ffn_total0 = lax.psum(late, 'dp')]
    pallas_call x8, Pallas kernels: 50.3 us -> 67.7 us  [attend_backward(): pl.pallas_call(attend_backward_kernel, name='attend_backward', out_shape=...]
    unnamed x445 -> x441, local copies, waits for them, and re-layouts: 28.6 us -> 45.6 us
    select_n x6 -> x12, other arithmetic: 6.17 us -> 20.5 us  [pick(): return jnp.where(side == 0, zero, one)]
    pallas_call x8, Pallas kernels: 41.6 us -> 54.9 us  [attend_forward(): pl.pallas_call(body, name='attend_forward', out_shape=(narrow, narrow, na...]
    broadcast_in_dim x20 -> x0, local copies, waits for them, and re-layouts: 11.8 us -> none  [total_rows(): return jnp.sum(values.astype(F32), axis=0, keepdims=True)]
  transfers between devices with their start and end apart: 71 -> 71, of which waited for: 14 -> 15; matrix products, arithmetic and copies ran while one was open for 42% -> 29% of each run, Pallas kernels for 17% -> 22%
where the time goes in v4:
time: 722 us; the launch traced here: 708 us
  waiting for transfers between devices  185 us (26%)
  Pallas kernels  157 us (22%)
  matrix products  116 us (16%)
  other arithmetic  95.2 us (13%)
  starting transfers between devices  73.5 us (10%)
  local copies, waits for them, and re-layouts  61.1 us (8%)
  between operations  19.9 us (3%)
    dot_general x50, matrix products, mm(): lax.dot_general(a, b, (((ca,), (cb,)), ((), ())), preferred_element_type=...  111 us
    pallas_call x8, Pallas kernels, attend_backward(): pl.pallas_call(attend_backward_kernel, name='attend_backward', out_shape=...  67.7 us
    ppermute x60, waiting for transfers between devices, send(): return lax.ppermute(values, PLANE, plane_pairs(kind))  65.3 us
    pallas_call x8, Pallas kernels, attend_forward(): pl.pallas_call(body, name='attend_forward', out_shape=(narrow, narrow, na...  54.9 us
    unnamed x441, local copies, waits for them, and re-layouts  45.6 us
    ppermute x60, starting transfers between devices, send(): return lax.ppermute(values, PLANE, plane_pairs(kind))  40.5 us
    psum x1, waiting for transfers between devices, shards(): attn_total0 = lax.psum(attn_total0, 'dp')  40.4 us
    psum x1, waiting for transfers between devices, shards(): ffn_total1, attn_total1 = lax.psum((ffn1.total, attn1.total), 'dp')  37.3 us
  transfers between devices with their start and end apart: 71, of which 15 were waited for; matrix products, arithmetic and copies ran while one was open for 29% of the time, Pallas kernels for 22%

profile of v4, /device:TPU:0, one launch (start us, length us, event | category | flops | bytes accessed | tf_op | source)
XLA Modules:
  0.0 707.5 jit_solution(15757011442528136707)
XLA Ops:
  18.1 3.9 all-to-all-start
  33.9 28.1 %collective-permute-done.12.refs_1_.first_ref = bf16[384,768]{1,0:T(8,128)(2,1)} collective-permute-done((bf16[384,768]{1,0:T(8,128)(2,1)}, bf16[384,768]{1,0:T(8,128)(2,1)}, u32[]{:S(2)}, u32[]{:S(2)}) %collective-permute-start.12) | collective-permute-done | bytes 589856 | tf_op jit(solution)/shard_map/ppermute | solution.py:62
  64.1 4.3 collective-permute-done.13.refs_2_.second_ref
  72.6 6.4 attend_forward.8
  84.6 7.5 %attend_forward.9 = (bf16[512,192]{1,0:T(8,128)(2,1)S(1)}, bf16[512,192]{1,0:T(8,128)(2,1)S(1)}, bf16[512,192]{1,0:T(8,128)(2,1)S(1)}, bf16[512,192]{1,0:T(8,128...) custom-call(bf16[512,768]{1,0:T(8,128)(2,1)S(1)} %bitcast.221, ...), custom_call_target="tpu_custom_call" | custom-call | flops 805306368 | bytes 8388608 | tf_op jit(solution)/shard_map/attend_forward/pallas_call | solution.py:213
  94.3 4.6 collective-permute-done.14
  98.9 4.4 all-to-all-start.5
  112.1 9.9 %collective-permute-done.2 = bf16[400,768]{1,0:T(8,128)(2,1)} collective-permute-done((bf16[400,768]{1,0:T(8,128)(2,1)}, bf16[400,768]{1,0:T(8,128)(2,1)}, u32[]{:S(2)}, u32[]{:S(2)}) %collective-permute-start.2) | collective-permute-done | bytes 614432 | tf_op jit(solution)/shard_map/ppermute | solution.py:62
  123.4 6.4 attend_forward.10
  142.1 6.4 attend_forward.11
  152.9 3.6 multiply_convert_fusion.9
  156.5 3.6 multiply_convert_fusion.8
  160.4 3.2 fusion.156
  163.6 3.2 fusion.157
  166.8 4.2 all-to-all-start.2
  171.3 3.5 multiply_convert_fusion.7
  180.1 3.2 fusion.146
  184.8 4.6 all-to-all-start.4
  192.5 7.9 %attend_forward.12 = (bf16[512,192]{1,0:T(8,128)(2,1)S(1)}, bf16[512,192]{1,0:T(8,128)(2,1)S(1)}, bf16[512,192]{1,0:T(8,128)(2,1)S(1)}, bf16[512,192]{1,0:T(8,12...) custom-call(bf16[512,768]{1,0:T(8,128)(2,1)S(1)} %get-tuple-element.376.refs_0_.x_ref, ...), custom_call_target="tpu_custom_call" | custom-call | flops 805306368 | bytes 8388608 | tf_op jit(solution)/shard_map/attend_forward/pallas_call | solution.py:213
  203.9 7.6 %attend_forward.13 = (bf16[512,192]{1,0:T(8,128)(2,1)S(1)}, bf16[512,192]{1,0:T(8,128)(2,1)S(1)}, bf16[512,192]{1,0:T(8,128)(2,1)S(1)}, bf16[512,192]{1,0:T(8,12...) custom-call(bf16[512,768]{1,0:T(8,128)(2,1)S(1)} %get-tuple-element.376.refs_0_.x_ref, ...), custom_call_target="tpu_custom_call" | custom-call | flops 805306368 | bytes 8388608 | tf_op jit(solution)/shard_map/attend_forward/pallas_call | solution.py:213
  212.3 6.4 attend_forward.14
  218.8 6.4 attend_forward.15
  231.4 3.6 multiply_convert_fusion.3
  240.5 3.3 multiply_convert_fusion.2
  264.5 14.7 %gather_anchors.1 = bf16[4,8,4,768]{3,2,1,0:T(4,128)(2,1)} custom-call(bf16[4,768]{1,0:T(4,128)(2,1)} %convolution_convert_fusion.16.refs_0_), custom_call_target="tpu_custom_call" | custom-call | tf_op jit(solution)/shard_map/gather_anchors/pallas_call | solution.py:299
  282.5 3.2 fusion.149
  317.5 9.0 %attend_backward.8 = (bf16[384,768]{1,0:T(8,128)(2,1)S(1)}, bf16[384,768]{1,0:T(8,128)(2,1)S(1)}, f32[1,384]{1,0:T(1,128)S(1)}, f32[512,768]{1,0:T(8,128)S(1)}) custom-call(bf16[512,768]{1,0:T(8,128)(2,1)S(1)} %convert_element_type.659.da_ref, bf16[512,768]{1,0:T(8,128)(2,1)S(1)} %copy-done.3, bf16[384,768]{1,0:T(8,128)(2,1)} %bitcast.21.refs_1_.first_ref, ...), custom_call_target="tpu_custom_call" | custom-call | flops 1711276032 | bytes 8388608 | tf_op jit(solution)/shard_map/attend_backward/pallas_call | solution.py:228
  327.2 9.4 %attend_backward.9 = (bf16[384,768]{1,0:T(8,128)(2,1)S(1)}, bf16[384,768]{1,0:T(8,128)(2,1)S(1)}, f32[1,384]{1,0:T(1,128)S(1)}, f32[512,768]{1,0:T(8,128)S(1)}) custom-call(bf16[512,768]{1,0:T(8,128)(2,1)S(1)} %convert_element_type.659.da_ref, bf16[512,768]{1,0:T(8,128)(2,1)S(1)} %copy-done.3, bf16[384,768]{1,0:T(8,128)(2,1)} %collective-permute-done.12.refs_1_.first_ref, ...), custom_call_target="tpu_custom_call" | custom-call | flops 1711276032 | bytes 8388608 | tf_op jit(solution)/shard_map/attend_backward/pallas_call | solution.py:228
  338.2 8.5 %attend_backward.10 = (bf16[384,768]{1,0:T(8,128)(2,1)}, bf16[384,768]{1,0:T(8,128)(2,1)}, f32[1,384]{1,0:T(1,128)S(1)}, f32[512,768]{1,0:T(8,128)S(1)}) custom-call(bf16[512,768]{1,0:T(8,128)(2,1)S(1)} %convert_element_type.659.da_ref, bf16[512,768]{1,0:T(8,128)(2,1)S(1)} %copy-done.3, bf16[384,768]{1,0:T(8,128)(2,1)S(1)} %copy-done.35, ...), custom_call_target="tpu_custom_call" | custom-call | flops 1711276032 | bytes 8388608 | tf_op jit(solution)/shard_map/attend_backward/pallas_call | solution.py:228
  349.7 7.7 %attend_backward.11 = (bf16[384,768]{1,0:T(8,128)(2,1)S(1)}, bf16[384,768]{1,0:T(8,128)(2,1)S(1)}, f32[1,384]{1,0:T(1,128)S(1)}, f32[512,768]{1,0:T(8,128)S(1)}) custom-call(bf16[512,768]{1,0:T(8,128)(2,1)S(1)} %convert_element_type.659.da_ref, bf16[512,768]{1,0:T(8,128)(2,1)S(1)} %copy-done.3, bf16[384,768]{1,0:T(8,128)(2,1)S(1)} %copy-done.17, ...), custom_call_target="tpu_custom_call" | custom-call | flops 1711276032 | bytes 8388608 | tf_op jit(solution)/shard_map/attend_backward/pallas_call | solution.py:228
  367.9 8.3 %collective-permute-done.29 = bf16[768,768]{1,0:T(8,128)(2,1)} collective-permute-done((bf16[768,768]{1,0:T(8,128)(2,1)}, bf16[768,768]{1,0:T(8,128)(2,1)}, u32[]{:S(2)}, u32[]{:S(2)}) %collective-permute-start.29) | collective-permute-done | bytes 1179680 | tf_op jit(solution)/shard_map/ppermute | solution.py:62
  379.3 4.4 multiply_reduce_fusion.2
  421.3 4.6 collective-permute-done.37
  433.2 3.5 broadcast_select_fusion
  442.3 7.7 %attend_backward.12 = (bf16[384,768]{1,0:T(8,128)(2,1)S(1)}, bf16[384,768]{1,0:T(8,128)(2,1)S(1)}, f32[1,384]{1,0:T(1,128)S(1)}, f32[512,768]{1,0:T(8,128)S(1)}) custom-call(bf16[512,768]{1,0:T(8,128)(2,1)S(1)} %convert_element_type.719.da_ref, bf16[512,768]{1,0:T(8,128)(2,1)S(1)} %bitcast.224, bf16[400,768]{1,0:T(8,128)(2,1)S(1)} %copy-done.9, ...), custom_call_target="tpu_custom_call" | custom-call | flops 1711276032 | bytes 8388608 | tf_op jit(solution)/shard_map/attend_backward/pallas_call | solution.py:228
  450.6 8.8 %attend_backward.13 = (bf16[384,768]{1,0:T(8,128)(2,1)S(1)}, bf16[384,768]{1,0:T(8,128)(2,1)S(1)}, f32[1,384]{1,0:T(1,128)S(1)}, f32[512,768]{1,0:T(8,128)S(1)}) custom-call(bf16[512,768]{1,0:T(8,128)(2,1)S(1)} %convert_element_type.719.da_ref, bf16[512,768]{1,0:T(8,128)(2,1)S(1)} %bitcast.225, bf16[400,768]{1,0:T(8,128)(2,1)S(1)} %copy-done.5, ...), custom_call_target="tpu_custom_call" | custom-call | flops 1711276032 | bytes 8388608 | tf_op jit(solution)/shard_map/attend_backward/pallas_call | solution.py:228
  462.5 8.9 %attend_backward.14 = (bf16[384,768]{1,0:T(8,128)(2,1)}, bf16[384,768]{1,0:T(8,128)(2,1)}, f32[1,384]{1,0:T(1,128)S(1)}, f32[512,768]{1,0:T(8,128)S(1)}) custom-call(bf16[512,768]{1,0:T(8,128)(2,1)S(1)} %convert_element_type.719.da_ref, bf16[512,768]{1,0:T(8,128)(2,1)S(1)} %bitcast.226, bf16[400,768]{1,0:T(8,128)(2,1)S(1)} %copy-done.31, ...), custom_call_target="tpu_custom_call" | custom-call | flops 1711276032 | bytes 8388608 | tf_op jit(solution)/shard_map/attend_backward/pallas_call | solution.py:228
  473.5 7.7 %attend_backward.15 = (bf16[384,768]{1,0:T(8,128)(2,1)S(1)}, bf16[384,768]{1,0:T(8,128)(2,1)S(1)}, f32[1,384]{1,0:T(1,128)S(1)}, f32[512,768]{1,0:T(8,128)S(1)}) custom-call(bf16[512,768]{1,0:T(8,128)(2,1)S(1)} %convert_element_type.719.da_ref, bf16[512,768]{1,0:T(8,128)(2,1)S(1)} %bitcast.227, bf16[400,768]{1,0:T(8,128)(2,1)S(1)} %copy-done.7, ...), custom_call_target="tpu_custom_call" | custom-call | flops 1711276032 | bytes 8388608 | tf_op jit(solution)/shard_map/attend_backward/pallas_call | solution.py:228
  483.2 4.2 all-to-all-start.1
  499.7 3.5 all-to-all-start.3
  508.1 12.2 %all-to-all-done.3 = bf16[4,128,768]{2,1,0:T(8,128)(2,1)S(1)} async-done(((bf16[4,128,768]{2,1,0:T(8,128)(2,1)}), bf16[4,128,768]{2,1,0:T(8,128)(2,1)S(1)}, u32[]{:S(2)}, u32[]{:S(2)}) %all-to-all-start.3) | async-done | bytes 786464 | tf_op jit(solution)/shard_map/all_to_all | solution.py:429
  520.3 4.2 all-to-all-start.7
  524.6 3.2 add_convert_fusion
  529.7 37.3 %all-reduce.11.cloned.1.call-done = (bf16[768,768]{1,0:T(8,128)(2,1)}, bf16[384,768]{1,0:T(8,128)(2,1)}) async-done(((bf16[768,768]{1,0:T(8,128)(2,1)}, bf16[384,768]{1,0:T(8,128)(2,1)}), (bf16[768,768]{1,0:T(8,128)(2,1)}, bf16[384,768]{1,0:T(8,128)(2,1)})) %all-reduce.11.cloned.1.call-update) | async-done | bytes 1769488 | tf_op jit(solution)/shard_map/psum | solution.py:649
  572.9 3.6 all-to-all-start.6
  577.9 19.9 %total_over_all.1 = f32[8,4,768]{2,1,0:T(4,128)} custom-call(f32[8,4,768]{2,1,0:T(4,128)} %select_add_fusion.rows_ref, f32[1,384]{1,0:T(1,128)} %copy-done.48, f32[1,384]{1,0:T(1,128)} %copy-done.49, f32[1,384]{1,0:T(1,128)} %copy-done.50, f32[1,384]{1,0:T(1,128)} %copy-done.51, f32[1,384]{1,0:T(1,128)} %copy-done.44, f32[1,384]{1,0:T(1,128)} %copy-done.45, ...), custom_call_target="tpu_custom_call" | custom-call | tf_op jit(solution)/shard_map/total_over_all/pallas_call | solution.py:405
  611.3 25.6 %all-reduce.7.cloned.1.call-done = bf16[768,768]{1,0:T(8,128)(2,1)} async-done(((bf16[768,768]{1,0:T(8,128)(2,1)}), bf16[768,768]{1,0:T(8,128)(2,1)}) %all-reduce.7.cloned.1.call-update) | async-done | bytes 1179664 | tf_op jit(solution)/shard_map/psum | solution.py:661
  638.5 40.4 %all-reduce.9.cloned.1.call-done = bf16[384,768]{1,0:T(8,128)(2,1)} async-done(((bf16[384,768]{1,0:T(8,128)(2,1)}), bf16[384,768]{1,0:T(8,128)(2,1)}) %all-reduce.9.cloned.1.call-update) | async-done | bytes 589840 | tf_op jit(solution)/shard_map/psum | solution.py:678
  (771 shorter events, 280.9 us)
Async XLA Ops:
  10.7 61.8 %collective-permute-start = (bf16[400,768]{1,0:T(8,128)(2,1)S(1)}, bf16[400,768]{1,0:T(8,128)(2,1)S(1)}, u32[]{:S(2)}, u32[]{:S(2)}) collective-permute-start(bf16[400,768]{1,0:T(8,128)(2,1)S(1)} %fusion.55.refs_1_.first_ref), channel_id=1, source_target_pairs={{0,1},{1,0},{2,3},{3,2},{4,6},{5,7},{6,4},{7,5},{8,9},{9,8},{10,11... | collective-permute-start | bytes 1843208 | tf_op jit(solution)/shard_map/ppermute | solution.py:62
  16.1 87.2 %collective-permute-start.6 = (bf16[768,768]{1,0:T(8,128)(2,1)}, bf16[768,768]{1,0:T(8,128)(2,1)}, u32[]{:S(2)}, u32[]{:S(2)}) collective-permute-start(bf16[768,768]{1,0:T(8,128)(2,1)} %get-tuple-element.172), channel_id=1, source_target_pairs={{0,1},{1,0},{2,3},{3,2},{4,6},{5,7},{6,4},{7,5},{8,9},{9,8},{10,11... | collective-permute-start | bytes 3538952 | tf_op jit(solution)/shard_map/ppermute | solution.py:62
  17.8 87.6 %collective-permute-start.7 = (bf16[768,768]{1,0:T(8,128)(2,1)}, bf16[768,768]{1,0:T(8,128)(2,1)}, u32[]{:S(2)}, u32[]{:S(2)}) collective-permute-start(bf16[768,768]{1,0:T(8,128)(2,1)} %get-tuple-element.173), channel_id=1, source_target_pairs={{0,1},{1,0},{2,3},{3,2},{4,6},{5,7},{6,4},{7,5},{8,9},{9,8},{10,11... | collective-permute-start | bytes 3538952 | tf_op jit(solution)/shard_map/ppermute | solution.py:62
  18.1 54.2 %all-to-all-start = ((bf16[4,128,768]{2,1,0:T(8,128)(2,1)}), bf16[4,128,768]{2,1,0:T(8,128)(2,1)S(1)}, u32[]{:S(2)}, u32[]{:S(2)}) async-start(bf16[4,128,768]{2,1,0:T(8,128)(2,1)} %bitcast.235), calls=%async_computation | async-start | bytes 1572864 | tf_op jit(solution)/shard_map/all_to_all | solution.py:422
  26.7 35.4 %collective-permute-start.12 = (bf16[384,768]{1,0:T(8,128)(2,1)}, bf16[384,768]{1,0:T(8,128)(2,1)}, u32[]{:S(2)}, u32[]{:S(2)}) collective-permute-start(bf16[384,768]{1,0:T(8,128)(2,1)} %bitcast.21.refs_1_.first_ref), channel_id=1, source_target_pairs={{0,1},{1,0},{2,3},{3,2},{4,6},{5,7},{6,4},{7,5},{8,9},{9,8},{10,11... | collective-permute-start | bytes 1769480 | tf_op jit(solution)/shard_map/ppermute | solution.py:62
  28.7 39.7 %collective-permute-start.13 = (bf16[384,768]{1,0:T(8,128)(2,1)}, bf16[384,768]{1,0:T(8,128)(2,1)}, u32[]{:S(2)}, u32[]{:S(2)}) collective-permute-start(bf16[384,768]{1,0:T(8,128)(2,1)} %pad_maximum_fusion.2.refs_2_.second_ref), channel_id=1, source_target_pairs={{0,1},{1,0},{2,3},{3,2},{4,6},{5,7},{6,4},{7,5},{8,9},{9,8},{10,11... | collective-permute-start | bytes 1769480 | tf_op jit(solution)/shard_map/ppermute | solution.py:62
  62.0 20.5 %collective-permute-start.1 = (bf16[400,768]{1,0:T(8,128)(2,1)S(1)}, bf16[400,768]{1,0:T(8,128)(2,1)}, u32[]{:S(2)}, u32[]{:S(2)}) collective-permute-start(bf16[400,768]{1,0:T(8,128)(2,1)S(1)} %fusion.56.refs_2_.second_ref), channel_id=1, source_target_pairs={{0,1},{1,0},{2,3},{3,2},{4,6},{5,7},{6,4},{7,5},{8,9},{9,8},{10,11... | collective-permute-start | bytes 1843208 | tf_op jit(solution)/shard_map/ppermute | solution.py:62
  68.4 39.6 %collective-permute-start.18 = (bf16[768,768]{1,0:T(8,128)(2,1)}, bf16[768,768]{1,0:T(8,128)(2,1)}, u32[]{:S(2)}, u32[]{:S(2)}) collective-permute-start(bf16[768,768]{1,0:T(8,128)(2,1)} %get-tuple-element.181), channel_id=1, source_target_pairs={{0,1},{1,0},{2,3},{3,2},{4,6},{5,7},{6,4},{7,5},{8,9},{9,8},{10,11... | collective-permute-start | bytes 3538952 | tf_op jit(solution)/shard_map/ppermute | solution.py:62
  72.5 35.8 %collective-permute-start.19 = (bf16[768,768]{1,0:T(8,128)(2,1)}, bf16[768,768]{1,0:T(8,128)(2,1)}, u32[]{:S(2)}, u32[]{:S(2)}) collective-permute-start(bf16[768,768]{1,0:T(8,128)(2,1)} %get-tuple-element.182), channel_id=1, source_target_pairs={{0,1},{1,0},{2,3},{3,2},{4,6},{5,7},{6,4},{7,5},{8,9},{9,8},{10,11... | collective-permute-start | bytes 3538952 | tf_op jit(solution)/shard_map/ppermute | solution.py:62
  82.6 16.3 %collective-permute-start.14 = (bf16[384,768]{1,0:T(8,128)(2,1)S(1)}, bf16[384,768]{1,0:T(8,128)(2,1)}, u32[]{:S(2)}, u32[]{:S(2)}) collective-permute-start(bf16[384,768]{1,0:T(8,128)(2,1)S(1)} %copy-done.182), channel_id=1, source_target_pairs={{0,2},{1,3},{2,0},{3,1},{4,5},{5,4},{6,7},{7,6},{8,10},{9,11},{10,... | collective-permute-start | bytes 1769480 | tf_op jit(solution)/shard_map/ppermute | solution.py:62
  98.9 113.4 %collective-permute-start.16 = (bf16[384,768]{1,0:T(8,128)(2,1)}, bf16[384,768]{1,0:T(8,128)(2,1)S(1)}, u32[]{:S(2)}, u32[]{:S(2)}) collective-permute-start(bf16[384,768]{1,0:T(8,128)(2,1)} %collective-permute-done.12.refs_1_.first_ref), channel_id=1, source_target_pairs={{0,4},{1,5},{2,6},{3,7},{4,0},{5,1},{6,2},{7,3},{8,12},{9,13},{10,... | collective-permute-start | bytes 1769480 | tf_op jit(solution)/shard_map/ppermute | solution.py:62
  98.9 37.3 %all-to-all-start.5 = ((bf16[4,128,768]{2,1,0:T(8,128)(2,1)}), bf16[4,128,768]{2,1,0:T(8,128)(2,1)}, u32[]{:S(2)}, u32[]{:S(2)}) async-start(bf16[4,128,768]{2,1,0:T(8,128)(2,1)} %bitcast.236), calls=%async_computation.5 | async-start | bytes 1572864 | tf_op jit(solution)/shard_map/all_to_all | solution.py:422
  103.3 18.6 %collective-permute-start.2 = (bf16[400,768]{1,0:T(8,128)(2,1)}, bf16[400,768]{1,0:T(8,128)(2,1)}, u32[]{:S(2)}, u32[]{:S(2)}) collective-permute-start(bf16[400,768]{1,0:T(8,128)(2,1)} %broadcast_select_fusion.16), channel_id=1, source_target_pairs={{0,2},{1,3},{2,0},{3,1},{4,5},{5,4},{6,7},{7,6},{8,10},{9,11},{10,... | collective-permute-start | bytes 1843208 | tf_op jit(solution)/shard_map/ppermute | solution.py:62
  108.3 51.7 %collective-permute-start.10 = (bf16[768,768]{1,0:T(8,128)(2,1)}, bf16[768,768]{1,0:T(8,128)(2,1)}, u32[]{:S(2)}, u32[]{:S(2)}) collective-permute-start(bf16[768,768]{1,0:T(8,128)(2,1)} %broadcast_select_fusion.13), channel_id=1, source_target_pairs={{0,2},{1,3},{2,0},{3,1},{4,5},{5,4},{6,7},{7,6},{8,10},{9,11},{10,... | collective-permute-start | bytes 3538952 | tf_op jit(solution)/shard_map/ppermute | solution.py:62
  112.0 25.8 %collective-permute-start.15 = (bf16[384,768]{1,0:T(8,128)(2,1)}, bf16[384,768]{1,0:T(8,128)(2,1)}, u32[]{:S(2)}, u32[]{:S(2)}) collective-permute-start(bf16[384,768]{1,0:T(8,128)(2,1)} %collective-permute-done.14), channel_id=1, source_target_pairs={{0,4},{1,5},{2,6},{3,7},{4,0},{5,1},{6,2},{7,3},{8,12},{9,13},{10,... | collective-permute-start | bytes 1769480 | tf_op jit(solution)/shard_map/ppermute | solution.py:62
  121.9 55.3 %collective-permute-start.22 = (bf16[768,768]{1,0:T(8,128)(2,1)}, bf16[768,768]{1,0:T(8,128)(2,1)}, u32[]{:S(2)}, u32[]{:S(2)}) collective-permute-start(bf16[768,768]{1,0:T(8,128)(2,1)} %broadcast_select_fusion.10), channel_id=1, source_target_pairs={{0,2},{1,3},{2,0},{3,1},{4,5},{5,4},{6,7},{7,6},{8,10},{9,11},{10,... | collective-permute-start | bytes 3538952 | tf_op jit(solution)/shard_map/ppermute | solution.py:62
  122.4 17.8 %collective-permute-start.3 = (bf16[400,768]{1,0:T(8,128)(2,1)}, bf16[400,768]{1,0:T(8,128)(2,1)}, u32[]{:S(2)}, u32[]{:S(2)}) collective-permute-start(bf16[400,768]{1,0:T(8,128)(2,1)} %collective-permute-done.2), channel_id=1, source_target_pairs={{0,4},{1,5},{2,6},{3,7},{4,0},{5,1},{6,2},{7,3},{8,12},{9,13},{10,... | collective-permute-start | bytes 1843208 | tf_op jit(solution)/shard_map/ppermute | solution.py:62
  137.8 33.2 %collective-permute-start.8 = (bf16[768,768]{1,0:T(8,128)(2,1)}, bf16[768,768]{1,0:T(8,128)(2,1)}, u32[]{:S(2)}, u32[]{:S(2)}) collective-permute-start(bf16[768,768]{1,0:T(8,128)(2,1)} %collective-permute-done.6), channel_id=1, source_target_pairs={{0,4},{1,5},{2,6},{3,7},{4,0},{5,1},{6,2},{7,3},{8,12},{9,13},{10,... | collective-permute-start | bytes 3538952 | tf_op jit(solution)/shard_map/ppermute | solution.py:62
  140.2 34.7 %collective-permute-start.9 = (bf16[768,768]{1,0:T(8,128)(2,1)}, bf16[768,768]{1,0:T(8,128)(2,1)}, u32[]{:S(2)}, u32[]{:S(2)}) collective-permute-start(bf16[768,768]{1,0:T(8,128)(2,1)} %collective-permute-done.7), channel_id=1, source_target_pairs={{0,4},{1,5},{2,6},{3,7},{4,0},{5,1},{6,2},{7,3},{8,12},{9,13},{10,... | collective-permute-start | bytes 3538952 | tf_op jit(solution)/shard_map/ppermute | solution.py:62
  160.0 17.6 %collective-permute-start.11 = (bf16[768,768]{1,0:T(8,128)(2,1)}, bf16[768,768]{1,0:T(8,128)(2,1)}, u32[]{:S(2)}, u32[]{:S(2)}) collective-permute-start(bf16[768,768]{1,0:T(8,128)(2,1)} %collective-permute-done.10), channel_id=1, source_target_pairs={{0,4},{1,5},{2,6},{3,7},{4,0},{5,1},{6,2},{7,3},{8,12},{9,13},{10,... | collective-permute-start | bytes 3538952 | tf_op jit(solution)/shard_map/ppermute | solution.py:62
  166.8 18.0 %all-to-all-start.2 = ((bf16[4,128,768]{2,1,0:T(8,128)(2,1)}), bf16[4,128,768]{2,1,0:T(8,128)(2,1)}, u32[]{:S(2)}, u32[]{:S(2)}) async-start(bf16[4,128,768]{2,1,0:T(8,128)(2,1)} %bitcast.17), calls=%async_computation.2 | async-start | bytes 1572864 | tf_op jit(solution)/shard_map/all_to_all | solution.py:422
  171.0 41.3 %collective-permute-start.17 = (bf16[384,768]{1,0:T(8,128)(2,1)}, bf16[384,768]{1,0:T(8,128)(2,1)S(1)}, u32[]{:S(2)}, u32[]{:S(2)}) collective-permute-start(bf16[384,768]{1,0:T(8,128)(2,1)} %collective-permute-done.13.refs_2_.second_ref), channel_id=1, source_target_pairs={{0,4},{1,5},{2,6},{3,7},{4,0},{5,1},{6,2},{7,3},{8,12},{9,13},{10,... | collective-permute-start | bytes 1769480 | tf_op jit(solution)/shard_map/ppermute | solution.py:62
  174.9 65.6 %collective-permute-start.20 = (bf16[768,768]{1,0:T(8,128)(2,1)}, bf16[768,768]{1,0:T(8,128)(2,1)}, u32[]{:S(2)}, u32[]{:S(2)}) collective-permute-start(bf16[768,768]{1,0:T(8,128)(2,1)} %collective-permute-done.18), channel_id=1, source_target_pairs={{0,4},{1,5},{2,6},{3,7},{4,0},{5,1},{6,2},{7,3},{8,12},{9,13},{10,... | collective-permute-start | bytes 3538952 | tf_op jit(solution)/shard_map/ppermute | solution.py:62
  177.3 68.7 %collective-permute-start.21 = (bf16[768,768]{1,0:T(8,128)(2,1)}, bf16[768,768]{1,0:T(8,128)(2,1)}, u32[]{:S(2)}, u32[]{:S(2)}) collective-permute-start(bf16[768,768]{1,0:T(8,128)(2,1)} %collective-permute-done.19), channel_id=1, source_target_pairs={{0,4},{1,5},{2,6},{3,7},{4,0},{5,1},{6,2},{7,3},{8,12},{9,13},{10,... | collective-permute-start | bytes 3538952 | tf_op jit(solution)/shard_map/ppermute | solution.py:62
  177.6 66.3 %collective-permute-start.23 = (bf16[768,768]{1,0:T(8,128)(2,1)}, bf16[768,768]{1,0:T(8,128)(2,1)}, u32[]{:S(2)}, u32[]{:S(2)}) collective-permute-start(bf16[768,768]{1,0:T(8,128)(2,1)} %collective-permute-done.22), channel_id=1, source_target_pairs={{0,4},{1,5},{2,6},{3,7},{4,0},{5,1},{6,2},{7,3},{8,12},{9,13},{10,... | collective-permute-start | bytes 3538952 | tf_op jit(solution)/shard_map/ppermute | solution.py:62
  184.8 194.5 %all-to-all-start.4 = ((bf16[4,128,768]{2,1,0:T(8,128)(2,1)}), bf16[4,128,768]{2,1,0:T(8,128)(2,1)}, u32[]{:S(2)}, u32[]{:S(2)}) async-start(bf16[4,128,768]{2,1,0:T(8,128)(2,1)} %bitcast.237), calls=%async_computation.4 | async-start | bytes 1572864 | tf_op jit(solution)/shard_map/all_to_all | solution.py:422
  313.7 34.1 %collective-permute-start.28 = (bf16[768,768]{1,0:T(8,128)(2,1)S(1)}, bf16[768,768]{1,0:T(8,128)(2,1)S(1)}, u32[]{:S(2)}, u32[]{:S(2)}) collective-permute-start(bf16[768,768]{1,0:T(8,128)(2,1)S(1)} %add_convert_fusion.9), channel_id=1, source_target_pairs={{0,2},{1,3},{2,0},{3,1},{4,5},{5,4},{6,7},{7,6},{8,10},{9,11},{10,... | collective-permute-start | bytes 3538952 | tf_op jit(solution)/shard_map/ppermute | solution.py:62
  316.0 44.9 %collective-permute-start.30 = (bf16[768,768]{1,0:T(8,128)(2,1)S(1)}, bf16[768,768]{1,0:T(8,128)(2,1)}, u32[]{:S(2)}, u32[]{:S(2)}) collective-permute-start(bf16[768,768]{1,0:T(8,128)(2,1)S(1)} %get-tuple-element.228), channel_id=1, source_target_pairs={{0,1},{1,0},{2,3},{3,2},{4,6},{5,7},{6,4},{7,5},{8,9},{9,8},{10,11... | collective-permute-start | bytes 3538952 | tf_op jit(solution)/shard_map/ppermute | solution.py:62
  359.6 16.6 %collective-permute-start.29 = (bf16[768,768]{1,0:T(8,128)(2,1)}, bf16[768,768]{1,0:T(8,128)(2,1)}, u32[]{:S(2)}, u32[]{:S(2)}) collective-permute-start(bf16[768,768]{1,0:T(8,128)(2,1)} %add_convert_fusion.7), channel_id=1, source_target_pairs={{0,1},{1,0},{2,3},{3,2},{4,6},{5,7},{6,4},{7,5},{8,9},{9,8},{10,11... | collective-permute-start | bytes 3538952 | tf_op jit(solution)/shard_map/ppermute | solution.py:62
  392.2 23.6 %collective-permute-start.36 = (bf16[384,768]{1,0:T(8,128)(2,1)S(1)}, bf16[384,768]{1,0:T(8,128)(2,1)S(1)}, u32[]{:S(2)}, u32[]{:S(2)}) collective-permute-start(bf16[384,768]{1,0:T(8,128)(2,1)S(1)} %copy-done.180), channel_id=1, source_target_pairs={{0,2},{1,3},{2,0},{3,1},{4,5},{5,4},{6,7},{7,6},{8,10},{9,11},{10,... | collective-permute-start | bytes 1769480 | tf_op jit(solution)/shard_map/ppermute | solution.py:62
  395.1 21.8 %collective-permute-start.38 = (bf16[384,768]{1,0:T(8,128)(2,1)S(1)}, bf16[384,768]{1,0:T(8,128)(2,1)S(1)}, u32[]{:S(2)}, u32[]{:S(2)}) collective-permute-start(bf16[384,768]{1,0:T(8,128)(2,1)S(1)} %copy-done.184), channel_id=1, source_target_pairs={{0,1},{1,0},{2,3},{3,2},{4,6},{5,7},{6,4},{7,5},{8,9},{9,8},{10,11... | collective-permute-start | bytes 1769480 | tf_op jit(solution)/shard_map/ppermute | solution.py:62
  421.3 15.4 %collective-permute-start.43 = (bf16[768,768]{1,0:T(8,128)(2,1)}, bf16[768,768]{1,0:T(8,128)(2,1)}, u32[]{:S(2)}, u32[]{:S(2)}) collective-permute-start(bf16[768,768]{1,0:T(8,128)(2,1)} %get-tuple-element.248), channel_id=1, source_target_pairs={{0,4},{1,5},{2,6},{3,7},{4,0},{5,1},{6,2},{7,3},{8,12},{9,13},{10,... | collective-permute-start | bytes 3538952 | tf_op jit(solution)/shard_map/ppermute | solution.py:62
  439.6 31.8 %collective-permute-start.44 = (bf16[768,768]{1,0:T(8,128)(2,1)S(1)}, bf16[768,768]{1,0:T(8,128)(2,1)S(1)}, u32[]{:S(2)}, u32[]{:S(2)}) collective-permute-start(bf16[768,768]{1,0:T(8,128)(2,1)S(1)} %add_convert_fusion.3), channel_id=1, source_target_pairs={{0,2},{1,3},{2,0},{3,1},{4,5},{5,4},{6,7},{7,6},{8,10},{9,11},{10,... | collective-permute-start | bytes 3538952 | tf_op jit(solution)/shard_map/ppermute | solution.py:62
  440.8 49.6 %collective-permute-start.46 = (bf16[768,768]{1,0:T(8,128)(2,1)}, bf16[768,768]{1,0:T(8,128)(2,1)}, u32[]{:S(2)}, u32[]{:S(2)}) collective-permute-start(bf16[768,768]{1,0:T(8,128)(2,1)} %get-tuple-element.287), channel_id=1, source_target_pairs={{0,1},{1,0},{2,3},{3,2},{4,6},{5,7},{6,4},{7,5},{8,9},{9,8},{10,11... | collective-permute-start | bytes 3538952 | tf_op jit(solution)/shard_map/ppermute | solution.py:62
  483.2 16.5 %all-to-all-start.1 = ((bf16[4,128,768]{2,1,0:T(8,128)(2,1)}), bf16[4,128,768]{2,1,0:T(8,128)(2,1)}, u32[]{:S(2)}, u32[]{:S(2)}) async-start(bf16[4,128,768]{2,1,0:T(8,128)(2,1)} %bitcast.231), calls=%async_computation.1 | async-start | bytes 1572864 | tf_op jit(solution)/shard_map/all_to_all | solution.py:429
  487.5 79.5 %all-reduce.11.cloned.1.call-start = ((), (), s32[]{:S(2)}) async-start(), calls=%async_computation.10 | async-start | bytes 3538944 | tf_op jit(solution)/shard_map/psum | solution.py:649
  488.3 36.2 %collective-permute-start.45 = (bf16[768,768]{1,0:T(8,128)(2,1)}, bf16[768,768]{1,0:T(8,128)(2,1)}, u32[]{:S(2)}, u32[]{:S(2)}) collective-permute-start(bf16[768,768]{1,0:T(8,128)(2,1)} %add_convert_fusion.1), channel_id=1, source_target_pairs={{0,1},{1,0},{2,3},{3,2},{4,6},{5,7},{6,4},{7,5},{8,9},{9,8},{10,11... | collective-permute-start | bytes 3538952 | tf_op jit(solution)/shard_map/ppermute | solution.py:62
  490.3 34.2 %collective-permute-start.47 = (bf16[768,768]{1,0:T(8,128)(2,1)}, bf16[768,768]{1,0:T(8,128)(2,1)}, u32[]{:S(2)}, u32[]{:S(2)}) collective-permute-start(bf16[768,768]{1,0:T(8,128)(2,1)} %collective-permute-done.46), channel_id=1, source_target_pairs={{0,4},{1,5},{2,6},{3,7},{4,0},{5,1},{6,2},{7,3},{8,12},{9,13},{10,... | collective-permute-start | bytes 3538952 | tf_op jit(solution)/shard_map/ppermute | solution.py:62
  499.7 20.6 %all-to-all-start.3 = ((bf16[4,128,768]{2,1,0:T(8,128)(2,1)}), bf16[4,128,768]{2,1,0:T(8,128)(2,1)S(1)}, u32[]{:S(2)}, u32[]{:S(2)}) async-start(bf16[4,128,768]{2,1,0:T(8,128)(2,1)} %bitcast.228), calls=%async_computation.3 | async-start | bytes 1572864 | tf_op jit(solution)/shard_map/all_to_all | solution.py:429
  520.3 51.7 %all-to-all-start.7 = ((bf16[4,128,768]{2,1,0:T(8,128)(2,1)}), bf16[4,128,768]{2,1,0:T(8,128)(2,1)}, u32[]{:S(2)}, u32[]{:S(2)}) async-start(bf16[4,128,768]{2,1,0:T(8,128)(2,1)} %bitcast.42), calls=%async_computation.7 | async-start | bytes 1572864 | tf_op jit(solution)/shard_map/all_to_all | solution.py:429
  527.8 70.0 %collective-permute-start.52 = (bf16[384,768]{1,0:T(8,128)(2,1)}, bf16[384,768]{1,0:T(8,128)(2,1)S(1)}, u32[]{:S(2)}, u32[]{:S(2)}) collective-permute-start(bf16[384,768]{1,0:T(8,128)(2,1)} %add_convert_fusion.15), channel_id=1, source_target_pairs={{0,2},{1,3},{2,0},{3,1},{4,5},{5,4},{6,7},{7,6},{8,10},{9,11},{10,... | collective-permute-start | bytes 1769480 | tf_op jit(solution)/shard_map/ppermute | solution.py:62
  567.0 33.2 %collective-permute-start.57 = (bf16[384,768]{1,0:T(8,128)(2,1)}, bf16[384,768]{1,0:T(8,128)(2,1)S(1)}, u32[]{:S(2)}, u32[]{:S(2)}) collective-permute-start(bf16[384,768]{1,0:T(8,128)(2,1)} %get-tuple-element.317), channel_id=1, source_target_pairs={{0,4},{1,5},{2,6},{3,7},{4,0},{5,1},{6,2},{7,3},{8,12},{9,13},{10,... | collective-permute-start | bytes 1769480 | tf_op jit(solution)/shard_map/ppermute | solution.py:62
  567.9 32.6 %collective-permute-start.54 = (bf16[384,768]{1,0:T(8,128)(2,1)}, bf16[384,768]{1,0:T(8,128)(2,1)}, u32[]{:S(2)}, u32[]{:S(2)}) collective-permute-start(bf16[384,768]{1,0:T(8,128)(2,1)} %get-tuple-element.311), channel_id=1, source_target_pairs={{0,1},{1,0},{2,3},{3,2},{4,6},{5,7},{6,4},{7,5},{8,9},{9,8},{10,11... | collective-permute-start | bytes 1769480 | tf_op jit(solution)/shard_map/ppermute | solution.py:62
  572.9 29.6 %all-to-all-start.6 = ((bf16[4,128,768]{2,1,0:T(8,128)(2,1)}), bf16[4,128,768]{2,1,0:T(8,128)(2,1)S(1)}, u32[]{:S(2)}, u32[]{:S(2)}) async-start(bf16[4,128,768]{2,1,0:T(8,128)(2,1)} %bitcast.40), calls=%async_computation.6 | async-start | bytes 1572864 | tf_op jit(solution)/shard_map/all_to_all | solution.py:429
  576.6 60.3 %all-reduce.7.cloned.1.call-start = ((), (), s32[]{:S(2)}) async-start(), calls=%async_computation.8 | async-start | bytes 2359296 | tf_op jit(solution)/shard_map/psum | solution.py:661
  577.3 101.6 %all-reduce.9.cloned.1.call-start = ((), (), s32[]{:S(2)}) async-start(), calls=%async_computation.9 | async-start | bytes 1179648 | tf_op jit(solution)/shard_map/psum | solution.py:678
  577.6 26.6 %collective-permute-start.59 = (bf16[768,768]{1,0:T(8,128)(2,1)}, bf16[768,768]{1,0:T(8,128)(2,1)}, u32[]{:S(2)}, u32[]{:S(2)}) collective-permute-start(bf16[768,768]{1,0:T(8,128)(2,1)} %get-tuple-element.320), channel_id=1, source_target_pairs={{0,4},{1,5},{2,6},{3,7},{4,0},{5,1},{6,2},{7,3},{8,12},{9,13},{10,... | collective-permute-start | bytes 3538952 | tf_op jit(solution)/shard_map/ppermute | solution.py:62
  637.2 49.8 %collective-permute-start.58 = (bf16[768,768]{1,0:T(8,128)(2,1)}, bf16[768,768]{1,0:T(8,128)(2,1)}, u32[]{:S(2)}, u32[]{:S(2)}) collective-permute-start(bf16[768,768]{1,0:T(8,128)(2,1)} %all-reduce.7.cloned.1.call-done), channel_id=1, source_target_pairs={{0,4},{1,5},{2,6},{3,7},{4,0},{5,1},{6,2},{7,3},{8,12},{9,13},{10,... | collective-permute-start | bytes 3538952 | tf_op jit(solution)/shard_map/ppermute | solution.py:62
  (240 other events, 1444.5 us)
Sparse Core Ops, SparseCore 0:
  491.3 75.6 all-reduce.10
  580.4 56.4 all-reduce.6
  639.8 39.0 all-reduce.8

commit v5 on v4

--- a/solution.py
+++ b/solution.py
@@ -89,21 +89,15 @@
     return blocks, across
 
 
-def reduce_outgoing(blocks, side):
+def reduce_outgoing(blocks):
+    return blocks[2][0], blocks[2][1], blocks[3][1], blocks[0][1]
+
+
+def reduce_swapped(blocks, outgoing):
+    got = [send(o, SWAP) for o in outgoing]
     return (
-        blocks[2][0], blocks[2][1], pick(side, blocks[3][1], blocks[3][0]), pick(side, blocks[0][1], blocks[0][0])
-    )
-
-
-def reduce_swapped(blocks, outgoing, side):
-    got = [send(o, SWAP) for o in outgoing]
-    first = plus(blocks[1][0], got[0])
-    second = plus(blocks[1][1], got[1])
-    main_rest = pick(side, second, first)
-    main_own = pick(side, first, second)
-    across = plus(pick(side, blocks[3][0], blocks[3][1]), got[2])
-    mine = plus(pick(side, blocks[0][0], blocks[0][1]), got[3])
-    return main_rest, main_own, across, mine
+        plus(blocks[1][1], got[0]), plus(blocks[1][0], got[1]), plus(blocks[3][0], got[2]), plus(blocks[0][0], got[3])
+    )
 
 
 def reduce_across(main_own, across):
@@ -150,7 +144,7 @@
 
 def attend_backward_kernel(
     da_ref, x_ref, first_ref, second_ref, q_ref, k_ref, v_ref, o_ref, lse_ref, dx_ref, down_ref, across_ref,
-    dfirst_ref, dsecond_ref, sums_ref, out_ref, do_ref, dq_ref, dk_ref, dv_ref
+    own_ref, rest_ref, sums_ref, out_ref, do_ref, dq_ref, dk_ref, dv_ref
 ):
     tokens, width = q_ref.shape
     da = da_ref[...]
@@ -186,21 +180,79 @@
         + mm(dk, first_ref[width : 2 * width, :], 1, 0)
         + mm(dv, second_ref[:width, :], 1, 0)
     )
-    dfirst_ref[:width, :] = mm(dq, x, 0, 0).astype(BF)
-    dfirst_ref[width:, :] = mm(dk, x, 0, 0).astype(BF)
-    dsecond_ref[:width, :] = mm(dv, x, 0, 0).astype(BF)
-    dsecond_ref[width:, :] = mm(o_ref[...], da, 0, 0).astype(BF)
+    side = lax.axis_index("span")
+    store_both(
+        side, own_ref, rest_ref, slice(0, width), mm(dq, x, 0, 0).astype(BF), mm(dv, x, 0, 0).astype(BF)
+    )
+    store_both(
+        side, own_ref, rest_ref, slice(width, 2 * width),
+        mm(dk, x, 0, 0).astype(BF), mm(o_ref[...], da, 0, 0).astype(BF),
+    )
     sums_ref[:, :width] = jnp.sum(dq.astype(F32), axis=0, keepdims=True)
     sums_ref[:, width:] = jnp.sum(dv.astype(F32), axis=0, keepdims=True)
 
 
-def attend_cost(tokens, width, model, products, mats):
-    heads = width // HEAD_DIM
-    return pl.CostEstimate(
-        flops=2 * tokens * width * (products * tokens + mats * model),
-        bytes_accessed=8 << 20,
-        transcendentals=heads * tokens * tokens,
-    )
+def small_cost():
+    return pl.CostEstimate(flops=1 << 20, bytes_accessed=1 << 10, transcendentals=0)
+
+
+def kernel_params():
+    return pltpu.CompilerParams(vmem_limit_bytes=24 << 20)
+
+
+def store_both(side, own_ref, rest_ref, rows, first, second):
+    @pl.when(side == 0)
+    def _():
+        own_ref[rows, :] = first
+        rest_ref[rows, :] = second
+
+    @pl.when(side != 0)
+    def _():
+        own_ref[rows, :] = second
+        rest_ref[rows, :] = first
+
+
+def ffn_backward_kernel(
+    dz_ref, y_ref, act_ref, slope_ref, first_ref, second_ref, dy_ref, own_ref, rest_ref, sums_ref, out_ref, dh_ref
+):
+    tokens, model = dz_ref.shape
+    side = lax.axis_index("span")
+    sums_ref[...] = jnp.zeros_like(sums_ref)
+
+    def data(i, carry):
+        rows = pl.ds(pl.multiple_of(i * Q_ROWS, Q_ROWS), Q_ROWS)
+        dhid = mm(dz_ref[rows, :], second_ref[...], 1, 1) * slope_ref[rows, :].astype(F32)
+        sums_ref[...] += jnp.sum(dhid, axis=0, keepdims=True)
+        dhb = dhid.astype(BF)
+        dh_ref[rows, :] = dhb
+        out_ref[rows, :] = dy_ref[rows, :] + mm(dhb, first_ref[...], 1, 1)
+        return carry
+
+    def weights(i, carry):
+        rows = pl.ds(pl.multiple_of(i * Q_ROWS, Q_ROWS), Q_ROWS)
+        first = mm(y_ref[:, rows], dh_ref[...], 0, 0).astype(BF)
+        second = mm(act_ref[:, rows], dz_ref[...], 0, 0).astype(BF)
+        store_both(side, own_ref, rest_ref, rows, first, second)
+        return carry
+
+    lax.fori_loop(0, tokens // Q_ROWS, data, 0)
+    lax.fori_loop(0, model // Q_ROWS, weights, 0)
+
+
+def ffn_block_backward(dzb, yb, act, slope, first, second, dy):
+    return pl.pallas_call(
+        ffn_backward_kernel,
+        name="ffn_backward",
+        out_shape=(
+            jax.ShapeDtypeStruct(first.shape, BF),
+            jax.ShapeDtypeStruct(first.shape, BF),
+            jax.ShapeDtypeStruct((1, act.shape[1]), F32),
+            jax.ShapeDtypeStruct(dy.shape, F32),
+        ),
+        scratch_shapes=[pltpu.VMEM(act.shape, BF)],
+        compiler_params=kernel_params(),
+        cost_estimate=small_cost(),
+    )(dzb, yb, act, slope, first, second, dy)
 
 
 def attend_forward(layer, cols, x, first, second, bias, z, seg):
@@ -218,8 +270,8 @@
             jax.ShapeDtypeStruct((tokens, cols // HEAD_DIM), F32),
             jax.ShapeDtypeStruct(z.shape, F32),
         ),
-        compiler_params=pltpu.CompilerParams(vmem_limit_bytes=24 << 20),
-        cost_estimate=attend_cost(tokens, cols, model, 2, 4),
+        compiler_params=kernel_params(),
+        cost_estimate=small_cost(),
     )(x, first, second, bias, z, *seg)
 
 
@@ -238,8 +290,8 @@
             pltpu.VMEM((tokens, cols), BF), pltpu.VMEM((tokens, cols), BF),
             pltpu.VMEM((tokens, cols), F32), pltpu.VMEM((tokens, cols), F32),
         ],
-        compiler_params=pltpu.CompilerParams(vmem_limit_bytes=24 << 20),
-        cost_estimate=attend_cost(tokens, cols, model, 5, 8),
+        compiler_params=kernel_params(),
+        cost_estimate=small_cost(),
     )(da, x, first, second, *kept, dx, *seg)
 
 
@@ -319,7 +371,7 @@
     return tensor, flip_one + swing, flip_two - swing, TENSORS - 1 - tensor
 
 
-def total_kernel(dps, planes, rows_ref, heads, out_ref, x_ref, parts, sums, sems):
+def total_kernel(dps, planes, rows_ref, blocks, out_ref, x_ref, parts, sums, sems):
     one_send, one_recv, two_send, two_recv, three_send, three_recv = sems
     dp = lax.axis_index("dp")
     side = lax.axis_index("span")
@@ -329,8 +381,9 @@
     x_ref[...] = rows_ref[...]
     for l in range(2):
         for j in range(TENSORS):
-            columns = heads[l][j].shape[1]
-            x_ref[l * CHUNKS_PER_LAYER + 1, pl.ds(order[j], 1), :columns] = heads[l][j][...]
+            for k in range(2):
+                columns = blocks[l][k][j].shape[1]
+                x_ref[l * CHUNKS_PER_LAYER + k, pl.ds(order[j], 1), :columns] = blocks[l][k][j][...]
 
     def near_peer(k):
         return lax.rem(me + k, planes)
@@ -389,10 +442,10 @@
         three(k).wait()
 
 
-def total_over_all(rows, heads):
+def total_over_all(rows, blocks):
     dps = lax.axis_size("dp")
     planes = lax.axis_size("span") * lax.axis_size("tensor")
-    flat, tree = jax.tree.flatten(heads)
+    flat, tree = jax.tree.flatten(blocks)
     shape = rows.shape
     dma = pltpu.SemaphoreType.DMA
     vmem = pl.BlockSpec(memory_space=pltpu.VMEM)
@@ -429,13 +482,14 @@
     return lax.all_to_all(blocks, "tensor", split_axis=0, concat_axis=0, tiled=True)
 
 
-def layer_forward(l, x, seg, attn_w, ffn_w, vec):
+def layer_forward(l, x, seg, attn_w, ffn_w, vec, hook):
     xb = x.astype(BF)
     kept = []
     z1 = x + vec["pb"]
-    for (first, second), bias in zip(attn_w, vec["heads"]):
+    for j, ((first, second), bias) in enumerate(zip(attn_w, vec["heads"])):
         *saved, z1 = attend_forward(l, vec["cols"], xb, first, second, bias, z1, seg)
         kept.append(saved)
+        z1 = hook(j, z1)
     n1, r1 = normal_parts(z1)
     y = n1 * vec["g0"] + vec["s0"]
     yb = y.astype(BF)
@@ -462,14 +516,13 @@
     dz2 = hook("seeded", dz2)
     dzb = dz2.astype(BF)
     dy = dz2
-    hidden = []
-    for (first, second), b in zip(ffn_w, slope):
-        dhid = mm(dzb, second, 1, 1) * b.astype(F32)
-        small["eb"].append(total_rows(dhid))
-        hidden.append(dhid.astype(BF))
-        dy = dy + mm(hidden[-1], first, 1, 1)
-    dy = hook("hidden", dy)
-    blocks = [(mm(yb, h, 0, 0).astype(BF), mm(a, dzb, 0, 0).astype(BF)) for h, a in zip(hidden, act)]
+    blocks = []
+    for j, (first, second) in enumerate(ffn_w):
+        own, rest, sums, dy = ffn_block_backward(dzb, yb, act[j], slope[j], first, second, dy)
+        small["eb"].append(sums)
+        blocks.append((own, rest))
+        if j == 2:
+            dzb, dy = hook("three", (dzb, dy))
     return dy, blocks, small
 
 
@@ -497,17 +550,14 @@
 
 
 class Reduction:
-    def __init__(self, side):
-        self.side = side
-
     def start(self, value, blocks):
         self.blocks = blocks
-        value, *self.outgoing = tie(value, *reduce_outgoing(blocks, self.side))
+        value, *self.outgoing = tie(value, *reduce_outgoing(blocks))
         return value
 
     def swapped(self, value):
         value, self.main_rest, self.main_own, self.across, self.mine = tie(
-            value, *reduce_swapped(self.blocks, self.outgoing, self.side)
+            value, *reduce_swapped(self.blocks, self.outgoing)
         )
         self.from_rest = send(self.main_rest, MAIN)
         return value
@@ -550,16 +600,21 @@
     x = to_rows(layer_input[0])
     expand, shrink, first = tie(w_expand[0], w_shrink[0], first)
     ffn_w0, mark = gather_part(expand, shrink, side)
-    first, second, expand = tie(*attn_rows(1), expand)
-    attn_w1, attn_mark = gather_part(first, second, side)
-    expand, shrink, first = tie(w_expand[1], w_shrink[1], first)
-    ffn_w1, ffn_mark = gather_part(expand, shrink, side)
-    later_skip, mark = tie(skip_tokens[0], mark)
-    skip = to_rows(later_skip)
-    mark = attn_mark
-    later_head, later_backbone, mark = tie(head_cotangent[0], backbone_cotangent[0], mark)
-    head_cot = to_rows(later_head)
-    backbone_cot = to_rows(later_backbone)
+    later = {}
+
+    def during_forward0(j, value):
+        if j == 1:
+            first, second, value = tie(*attn_rows(1), value)
+            later["attn"], mark = gather_part(first, second, side)
+        if j == 3:
+            first, second, skip, value = tie(w_expand[1], w_shrink[1], skip_tokens[0], value)
+            later["ffn"], mark = gather_part(first, second, side)
+            later["skip"] = to_rows(skip)
+        return value
+
+    def plain(name, value):
+        return value
+
     tokens = x.shape[0]
 
     biases = [first[2 * head_cols : 2 * head_cols + 3].astype(F32) for first, second in attn_w0]
@@ -586,7 +641,11 @@
     first_place = jnp.sum(picker, axis=0)[:, None] > 0
 
     vec0, vec1 = vectors(0), vectors(1)
-    backbone, kept0 = layer_forward(0, x.astype(F32), seg, attn_w0, ffn_w0, vec0)
+    backbone, kept0 = layer_forward(0, x.astype(F32), seg, attn_w0, ffn_w0, vec0, during_forward0)
+    attn_w1, ffn_w1, skip = later["attn"], later["ffn"], later["skip"]
+    later_head, later_backbone, backbone = tie(head_cotangent[0], backbone_cotangent[0], backbone)
+    head_cot = to_rows(later_head)
+    backbone_cot = to_rows(later_backbone)
     cls = mm(picker.astype(BF), backbone.astype(BF), 1, 0).astype(BF)
     anchors = gather_anchors(cls)
     dp_count = lax.axis_size("dp")
@@ -596,7 +655,7 @@
     anchors = jnp.swapaxes(anchors, 0, 1).reshape(pair_count, vector_count, width)
 
     head_in = jnp.where(first_place, backbone, skip.astype(F32))
-    head, kept1 = layer_forward(1, head_in, seg, attn_w1, ffn_w1, vec1)
+    head, kept1 = layer_forward(1, head_in, seg, attn_w1, ffn_w1, vec1, plain)
 
     root = math.sqrt(width)
     logits = mm(anchors[0], anchors[1], 1, 1) / root
@@ -616,10 +675,7 @@
     other = lax.dynamic_index_in_dim(anchors, 1 - side, 0, keepdims=False).astype(F32)
     dcls = jnp.dot(wanted, other, precision=HIGHEST) / root
 
-    ffn1, attn1, ffn0, attn0 = (Reduction(side) for _ in range(4))
-
-    def plain(name, value):
-        return value
+    ffn1, attn1, ffn0, attn0 = (Reduction() for _ in range(4))
 
     dy, blocks, small1 = ffn_backward(head_cot.astype(F32) * valid, ffn_w1, vec1, kept1, plain)
     dy = ffn1.start(dy, blocks)
@@ -633,6 +689,7 @@
     small1.update(more)
     du = attn1.start(du, blocks)
     du = ffn1.summed(du)
+    ffn_total1 = lax.psum(ffn1.total, "dp")
     grad_skip = jnp.where(first_place, 0.0, du).astype(BF)
 
     seed = backbone_cot.astype(F32) * valid + jnp.where(first_place, du, 0.0)
@@ -646,32 +703,31 @@
     dy, blocks, small0 = ffn_backward(seed, ffn_w0, vec0, kept0, during_ffn0)
     dy = ffn0.start(dy, blocks)
     dy = attn1.summed(dy)
-    ffn_total1, attn_total1 = lax.psum((ffn1.total, attn1.total), "dp")
 
     def during_attn0(name, value):
         if name == "normed":
             return ffn0.swapped(value)
         return ffn0.crossed(value)
 
+    dy, ffn_total1, attn_total1 = tie(dy, ffn_total1, attn1.total)
+    attn_total1 = lax.psum(attn_total1, "dp")
+
     dx, blocks, more = attn_backward(dy, seg, attn_w0, vec0, kept0, during_attn0)
     small0.update(more)
     dx = attn0.start(dx, blocks)
     dx = ffn0.summed(dx)
-    late, ffn_total1, attn_total1 = tie(ffn0.total, ffn_total1, attn_total1)
+    dx, late, attn_total1 = tie(dx, ffn0.total, attn_total1)
     ffn_total0 = lax.psum(late, "dp")
 
-    order = block_order(side, mine)
     place = lax.broadcasted_iota(jnp.int32, (2 * CHUNKS_PER_LAYER * ROWS_PER_CHUNK, 1), 0)
     rows = jnp.zeros((place.shape[0], width), F32)
     for l, small in enumerate((small0, small1)):
         base = l * CHUNKS_PER_LAYER * ROWS_PER_CHUNK
-        for j in range(TENSORS):
-            rows = rows + jnp.where(place == base + order[j], small["eb"][j][None], 0.0)
         for i, k in enumerate(VECTORS):
             rows = rows + jnp.where(place == base + 2 * ROWS_PER_CHUNK + i, small[k][None], 0.0)
-    rows, mark = tie(rows.reshape(2 * CHUNKS_PER_LAYER, ROWS_PER_CHUNK, width), ffn0.total)
+    rows, mark = tie(rows.reshape(2 * CHUNKS_PER_LAYER, ROWS_PER_CHUNK, width), late)
     rows = attn0.swapped(rows)
-    total = total_over_all(rows, (small0["heads"], small1["heads"]))
+    total = total_over_all(rows, [(small["eb"], small["heads"]) for small in (small0, small1)])
     total = attn0.crossed(total)
     total = attn0.summed(total)
     attn_total0, ffn_total0 = tie(attn0.total, ffn_total0)

time: 722 us -> 732 us (1.014)
  Pallas kernels: 157 us -> 236 us
  matrix products: 116 us -> 46 us
  waiting for transfers between devices: 185 us -> 128 us
  other arithmetic: 95.2 us -> 127 us
  local copies, waits for them, and re-layouts: 61.1 us -> 88.5 us
    dot_general x50 -> x18, matrix products: 111 us -> 41.1 us  [mm(): lax.dot_general(a, b, (((ca,), (cb,)), ((), ())), preferred_element_type=...]
    pallas_call x0 -> x8, Pallas kernels: none -> 65.2 us  [ffn_block_backward(): pl.pallas_call(ffn_backward_kernel, name='ffn_backward', out_shape=(jax.S...]
    psum x1 -> x2, waiting for transfers between devices: 37.3 us -> 10.6 us  [the longest x1 5.38 us: shards(): ffn_total1 = lax.psum(ffn1.total, 'dp')]
    convert_element_type x16 -> x24, other arithmetic: 27.6 us -> 45 us  [plus(): return total.astype(BF)]
    unnamed x441 -> x557, local copies, waits for them, and re-layouts: 45.6 us -> 62.2 us
    psum x1, waiting for transfers between devices: 25.6 us -> 9.2 us  [shards(): ffn_total0 = lax.psum(late, 'dp')]
    reduce_sum x8, other arithmetic: 9.31 us -> 19.5 us  [total_rows(): return jnp.sum(values, axis=0)]
    select_n x12 -> x8, other arithmetic: 20.5 us -> 12.4 us  [pick(): return jnp.where(side == 0, zero, one)]
  transfers between devices with their start and end apart: 71 -> 72, of which waited for: 15 -> 13; matrix products, arithmetic and copies ran while one was open for 29% -> 24% of each run, Pallas kernels for 22% -> 28%
where the time goes in v5:
time: 732 us; the launch traced here: 722 us
  Pallas kernels  236 us (32%)
  waiting for transfers between devices  128 us (17%)
  other arithmetic  127 us (17%)
  local copies, waits for them, and re-layouts  88.5 us (12%)
  starting transfers between devices  76.9 us (11%)
  matrix products  46 us (6%)
  between operations  20.1 us (3%)
    pallas_call x8, Pallas kernels, attend_backward(): pl.pallas_call(attend_backward_kernel, name='attend_backward', out_shape=...  70.3 us
    pallas_call x8, Pallas kernels, ffn_block_backward(): pl.pallas_call(ffn_backward_kernel, name='ffn_backward', out_shape=(jax.S...  65.2 us
    pallas_call x8, Pallas kernels, attend_forward(): pl.pallas_call(body, name='attend_forward', out_shape=(narrow, narrow, na...  62.4 us
    unnamed x557, local copies, waits for them, and re-layouts  62.2 us
    ppermute x60, waiting for transfers between devices, send(): return lax.ppermute(values, PLANE, plane_pairs(kind))  59.3 us
    convert_element_type x24, other arithmetic, plus(): return total.astype(BF)  45 us
    ppermute x60, starting transfers between devices, send(): return lax.ppermute(values, PLANE, plane_pairs(kind))  44.5 us
    dot_general x18, matrix products, mm(): lax.dot_general(a, b, (((ca,), (cb,)), ((), ())), preferred_element_type=...  41.1 us
  transfers between devices with their start and end apart: 72, of which 13 were waited for; matrix products, arithmetic and copies ran while one was open for 24% of the time, Pallas kernels for 28%

profile of v5, /device:TPU:0, one launch (start us, length us, event | category | flops | bytes accessed | tf_op | source)
XLA Modules:
  0.0 721.9 jit_solution(11457507692340105487)
XLA Ops:
  37.9 6.4 attend_forward.8
  46.1 6.4 attend_forward.9
  56.7 12.0 %collective-permute-done.7.second_ref = bf16[768,768]{1,0:T(8,128)(2,1)} collective-permute-done((bf16[768,768]{1,0:T(8,128)(2,1)}, bf16[768,768]{1,0:T(8,128)(2,1)}, u32[]{:S(2)}, u32[]{:S(2)}) %collective-permute-start.7) | collective-permute-done | bytes 1179680 | tf_op jit(solution)/shard_map/ppermute | solution.py:62
  71.1 3.9 collective-permute-done.12.refs_1_.first_ref
  77.1 8.4 %collective-permute-done.13.refs_2_.second_ref = bf16[384,768]{1,0:T(8,128)(2,1)} collective-permute-done((bf16[384,768]{1,0:T(8,128)(2,1)S(1)}, bf16[384,768]{1,0:T(8,128)(2,1)}, u32[]{:S(2)}, u32[]{:S(2)}) %collective-permute-start.13) | collective-permute-done | bytes 589856 | tf_op jit(solution)/shard_map/ppermute | solution.py:62
  90.4 6.4 attend_forward.10
  97.9 6.4 attend_forward.11
  108.3 3.8 all-to-all-start.2
  114.5 3.6 fusion.34
  136.3 12.6 %collective-permute-done.19.second_ref = bf16[768,768]{1,0:T(8,128)(2,1)} collective-permute-done((bf16[768,768]{1,0:T(8,128)(2,1)S(1)}, bf16[768,768]{1,0:T(8,128)(2,1)}, u32[]{:S(2)}, u32[]{:S(2)}) %collective-permute-start.19) | collective-permute-done | bytes 1179680 | tf_op jit(solution)/shard_map/ppermute | solution.py:62
  161.3 4.2 all-to-all-start.5
  169.8 6.4 attend_forward.12
  179.7 7.6 %attend_forward.13 = (bf16[512,192]{1,0:T(8,128)(2,1)S(1)}, bf16[512,192]{1,0:T(8,128)(2,1)S(1)}, bf16[512,192]{1,0:T(8,128)(2,1)S(1)}, bf16[512,192]{1,0:T(8,12...) custom-call(bf16[512,768]{1,0:T(8,128)(2,1)S(1)} %fusion.50.refs_0_.x_ref, ...), custom_call_target="tpu_custom_call" | custom-call | flops 1048576 | bytes 1024 | tf_op jit(solution)/shard_map/attend_forward/pallas_call | solution.py:265
  190.9 7.7 %attend_forward.14 = (bf16[512,192]{1,0:T(8,128)(2,1)S(1)}, bf16[512,192]{1,0:T(8,128)(2,1)S(1)}, bf16[512,192]{1,0:T(8,128)(2,1)S(1)}, bf16[512,192]{1,0:T(8,12...) custom-call(bf16[512,768]{1,0:T(8,128)(2,1)S(1)} %fusion.50.refs_0_.x_ref, ...), custom_call_target="tpu_custom_call" | custom-call | flops 1048576 | bytes 1024 | tf_op jit(solution)/shard_map/attend_forward/pallas_call | solution.py:265
  199.4 15.1 %attend_forward.15 = (bf16[512,192]{1,0:T(8,128)(2,1)S(1)}, bf16[512,192]{1,0:T(8,128)(2,1)S(1)}, bf16[512,192]{1,0:T(8,128)(2,1)S(1)}, bf16[512,192]{1,0:T(8,12...) custom-call(bf16[512,768]{1,0:T(8,128)(2,1)S(1)} %fusion.50.refs_0_.x_ref, bf16[384,768]{1,0:T(8,128)(2,1)S(1)} %copy-done.30, ...), custom_call_target="tpu_custom_call" | custom-call | flops 1048576 | bytes 1024 | tf_op jit(solution)/shard_map/attend_forward/pallas_call | solution.py:265
  226.0 3.7 fusion.14
  255.1 6.5 ffn_backward.8
  264.2 8.3 %ffn_backward.9 = (bf16[768,768]{1,0:T(8,128)(2,1)S(1)}, bf16[768,768]{1,0:T(8,128)(2,1)S(1)}, f32[1,768]{1,0:T(1,128)S(1)}, f32[512,768]{1,0:T(8,128)S(1)}) custom-call(bf16[512,768]{1,0:T(8,128)(2,1)S(1)} %convert_element_type.530.dz_ref, bf16[512,768]{1,0:T(8,128)(2,1)S(1)} %copy-done.7, bf16[512,768]{1,0:T(8,128)(2,1)S(1)} %copy-done.81, ...), custom_call_target="tpu_custom_call" | custom-call | flops 1048576 | bytes 1024 | tf_op jit(solution)/shard_map/ffn_backward/pallas_call | solution.py:243
  274.6 9.1 %ffn_backward.10 = (bf16[768,768]{1,0:T(8,128)(2,1)}, bf16[768,768]{1,0:T(8,128)(2,1)S(1)}, f32[1,768]{1,0:T(1,128)S(1)}, f32[512,768]{1,0:T(8,128)S(1)}) custom-call(bf16[512,768]{1,0:T(8,128)(2,1)S(1)} %convert_element_type.530.dz_ref, bf16[512,768]{1,0:T(8,128)(2,1)S(1)} %copy-done.7, bf16[512,768]{1,0:T(8,128)(2,1)S(1)} %get-tuple-element.483.act_ref, ...), custom_call_target="tpu_custom_call" | custom-call | flops 1048576 | bytes 1024 | tf_op jit(solution)/shard_map/ffn_backward/pallas_call | solution.py:243
  284.8 6.5 ffn_backward.11
  297.8 14.6 %gather_anchors.1 = bf16[4,8,4,768]{3,2,1,0:T(4,128)(2,1)} custom-call(bf16[4,768]{1,0:T(4,128)(2,1)} %convolution_convert_fusion.refs_0_), custom_call_target="tpu_custom_call" | custom-call | tf_op jit(solution)/shard_map/gather_anchors/pallas_call | solution.py:351
  315.6 3.5 multiply_reduce_fusion.1
  331.3 8.2 %attend_backward.8 = (bf16[384,768]{1,0:T(8,128)(2,1)S(1)}, bf16[384,768]{1,0:T(8,128)(2,1)S(1)}, f32[1,384]{1,0:T(1,128)S(1)}, f32[512,768]{1,0:T(8,128)S(1)}) custom-call(bf16[512,768]{1,0:T(8,128)(2,1)S(1)} %convert_element_type.547.da_ref, bf16[512,768]{1,0:T(8,128)(2,1)S(1)} %fusion.50.refs_0_.x_ref, bf16[384,768]{1,0:T(8,128)(2,1)S(1)} %bitcast.177, ...), custom_call_target="tpu_custom_call" | custom-call | flops 1048576 | bytes 1024 | tf_op jit(solution)/shard_map/attend_backward/pallas_call | solution.py:280
  341.2 9.9 %attend_backward.9 = (bf16[384,768]{1,0:T(8,128)(2,1)S(1)}, bf16[384,768]{1,0:T(8,128)(2,1)S(1)}, f32[1,384]{1,0:T(1,128)S(1)}, f32[512,768]{1,0:T(8,128)S(1)}) custom-call(bf16[512,768]{1,0:T(8,128)(2,1)S(1)} %convert_element_type.547.da_ref, bf16[512,768]{1,0:T(8,128)(2,1)S(1)} %fusion.50.refs_0_.x_ref, ...), custom_call_target="tpu_custom_call" | custom-call | flops 1048576 | bytes 1024 | tf_op jit(solution)/shard_map/attend_backward/pallas_call | solution.py:280
  352.8 10.3 %attend_backward.10 = (bf16[384,768]{1,0:T(8,128)(2,1)}, bf16[384,768]{1,0:T(8,128)(2,1)}, f32[1,384]{1,0:T(1,128)S(1)}, f32[512,768]{1,0:T(8,128)S(1)}) custom-call(bf16[512,768]{1,0:T(8,128)(2,1)S(1)} %convert_element_type.547.da_ref, bf16[512,768]{1,0:T(8,128)(2,1)S(1)} %fusion.50.refs_0_.x_ref, ...), custom_call_target="tpu_custom_call" | custom-call | flops 1048576 | bytes 1024 | tf_op jit(solution)/shard_map/attend_backward/pallas_call | solution.py:280
  365.1 8.2 %attend_backward.11 = (bf16[384,768]{1,0:T(8,128)(2,1)S(1)}, bf16[384,768]{1,0:T(8,128)(2,1)S(1)}, f32[1,384]{1,0:T(1,128)S(1)}, f32[512,768]{1,0:T(8,128)S(1)}) custom-call(bf16[512,768]{1,0:T(8,128)(2,1)S(1)} %convert_element_type.547.da_ref, bf16[512,768]{1,0:T(8,128)(2,1)S(1)} %fusion.50.refs_0_.x_ref, bf16[384,768]{1,0:T(8,128)(2,1)S(1)} %copy-done.31, ...), custom_call_target="tpu_custom_call" | custom-call | flops 1048576 | bytes 1024 | tf_op jit(solution)/shard_map/attend_backward/pallas_call | solution.py:280
  377.6 4.2 all-to-all-start.4
  391.2 14.4 %collective-permute-done.29 = bf16[768,768]{1,0:T(8,128)(2,1)S(1)} collective-permute-done((bf16[768,768]{1,0:T(8,128)(2,1)}, bf16[768,768]{1,0:T(8,128)(2,1)S(1)}, u32[]{:S(2)}, u32[]{:S(2)}) %collective-permute-start.29) | collective-permute-done | bytes 1179680 | tf_op jit(solution)/shard_map/ppermute | solution.py:62
  407.2 4.5 multiply_reduce_fusion.2
  418.7 9.4 %ffn_backward.12 = (bf16[768,768]{1,0:T(8,128)(2,1)S(1)}, bf16[768,768]{1,0:T(8,128)(2,1)}, f32[1,768]{1,0:T(1,128)S(1)}, f32[512,768]{1,0:T(8,128)S(1)}) custom-call(bf16[512,768]{1,0:T(8,128)(2,1)S(1)} %convert_element_type.567.dz_ref, bf16[512,768]{1,0:T(8,128)(2,1)S(1)} %copy-done.5, bf16[512,768]{1,0:T(8,128)(2,1)S(1)} %copy-done.74, ...), custom_call_target="tpu_custom_call" | custom-call | flops 1048576 | bytes 1024 | tf_op jit(solution)/shard_map/ffn_backward/pallas_call | solution.py:243
  429.8 8.3 %ffn_backward.13 = (bf16[768,768]{1,0:T(8,128)(2,1)S(1)}, bf16[768,768]{1,0:T(8,128)(2,1)S(1)}, f32[1,768]{1,0:T(1,128)S(1)}, f32[512,768]{1,0:T(8,128)S(1)}) custom-call(bf16[512,768]{1,0:T(8,128)(2,1)S(1)} %convert_element_type.567.dz_ref, bf16[512,768]{1,0:T(8,128)(2,1)S(1)} %copy-done.5, bf16[512,768]{1,0:T(8,128)(2,1)S(1)} %copy-done.71, ...), custom_call_target="tpu_custom_call" | custom-call | flops 1048576 | bytes 1024 | tf_op jit(solution)/shard_map/ffn_backward/pallas_call | solution.py:243
  440.7 9.6 %ffn_backward.14 = (bf16[768,768]{1,0:T(8,128)(2,1)}, bf16[768,768]{1,0:T(8,128)(2,1)}, f32[1,768]{1,0:T(1,128)S(1)}, f32[512,768]{1,0:T(8,128)S(1)}) custom-call(bf16[512,768]{1,0:T(8,128)(2,1)S(1)} %convert_element_type.567.dz_ref, bf16[512,768]{1,0:T(8,128)(2,1)S(1)} %copy-done.5, bf16[512,768]{1,0:T(8,128)(2,1)S(1)} %copy-done.77, ...), custom_call_target="tpu_custom_call" | custom-call | flops 1048576 | bytes 1024 | tf_op jit(solution)/shard_map/ffn_backward/pallas_call | solution.py:243
  453.3 7.5 %ffn_backward.15 = (bf16[768,768]{1,0:T(8,128)(2,1)S(1)}, bf16[768,768]{1,0:T(8,128)(2,1)}, f32[1,768]{1,0:T(1,128)S(1)}, f32[512,768]{1,0:T(8,128)S(1)}) custom-call(bf16[512,768]{1,0:T(8,128)(2,1)S(1)} %convert_element_type.567.dz_ref, bf16[512,768]{1,0:T(8,128)(2,1)S(1)} %copy-done.5, bf16[512,768]{1,0:T(8,128)(2,1)S(1)} %copy-done.46, ...), custom_call_target="tpu_custom_call" | custom-call | flops 1048576 | bytes 1024 | tf_op jit(solution)/shard_map/ffn_backward/pallas_call | solution.py:243
  465.0 5.4 all-reduce.7.cloned.1.call-done
  491.6 4.2 all-to-all-start.1
  498.5 8.1 %attend_backward.12 = (bf16[384,768]{1,0:T(8,128)(2,1)S(1)}, bf16[384,768]{1,0:T(8,128)(2,1)S(1)}, f32[1,384]{1,0:T(1,128)S(1)}, f32[512,768]{1,0:T(8,128)S(1)}) custom-call(bf16[512,768]{1,0:T(8,128)(2,1)S(1)} %convert_element_type.591.da_ref, bf16[512,768]{1,0:T(8,128)(2,1)S(1)} %bitcast.171, bf16[400,768]{1,0:T(8,128)(2,1)S(1)} %copy-done.21, ...), custom_call_target="tpu_custom_call" | custom-call | flops 1048576 | bytes 1024 | tf_op jit(solution)/shard_map/attend_backward/pallas_call | solution.py:280
  507.6 8.2 %attend_backward.13 = (bf16[384,768]{1,0:T(8,128)(2,1)S(1)}, bf16[384,768]{1,0:T(8,128)(2,1)S(1)}, f32[1,384]{1,0:T(1,128)S(1)}, f32[512,768]{1,0:T(8,128)S(1)}) custom-call(bf16[512,768]{1,0:T(8,128)(2,1)S(1)} %convert_element_type.591.da_ref, bf16[512,768]{1,0:T(8,128)(2,1)S(1)} %bitcast.172, bf16[400,768]{1,0:T(8,128)(2,1)S(1)} %copy-done.17, ...), custom_call_target="tpu_custom_call" | custom-call | flops 1048576 | bytes 1024 | tf_op jit(solution)/shard_map/attend_backward/pallas_call | solution.py:280
  517.2 9.3 %attend_backward.14 = (bf16[384,768]{1,0:T(8,128)(2,1)}, bf16[384,768]{1,0:T(8,128)(2,1)}, f32[1,384]{1,0:T(1,128)S(1)}, f32[512,768]{1,0:T(8,128)S(1)}) custom-call(bf16[512,768]{1,0:T(8,128)(2,1)S(1)} %convert_element_type.591.da_ref, bf16[512,768]{1,0:T(8,128)(2,1)S(1)} %bitcast.173, bf16[400,768]{1,0:T(8,128)(2,1)S(1)} %copy-done.48, ...), custom_call_target="tpu_custom_call" | custom-call | flops 1048576 | bytes 1024 | tf_op jit(solution)/shard_map/attend_backward/pallas_call | solution.py:280
  529.4 8.2 %attend_backward.15 = (bf16[384,768]{1,0:T(8,128)(2,1)S(1)}, bf16[384,768]{1,0:T(8,128)(2,1)S(1)}, f32[1,384]{1,0:T(1,128)S(1)}, f32[512,768]{1,0:T(8,128)S(1)}) custom-call(bf16[512,768]{1,0:T(8,128)(2,1)S(1)} %convert_element_type.591.da_ref, bf16[512,768]{1,0:T(8,128)(2,1)S(1)} %bitcast.174, bf16[400,768]{1,0:T(8,128)(2,1)S(1)} %copy-done.19, ...), custom_call_target="tpu_custom_call" | custom-call | flops 1048576 | bytes 1024 | tf_op jit(solution)/shard_map/attend_backward/pallas_call | solution.py:280
  544.6 4.2 all-to-all-start.3
  555.6 10.5 %all-to-all-done.3 = bf16[4,128,768]{2,1,0:T(8,128)(2,1)} async-done(((bf16[4,128,768]{2,1,0:T(8,128)(2,1)}), bf16[4,128,768]{2,1,0:T(8,128)(2,1)}, u32[]{:S(2)}, u32[]{:S(2)}) %all-to-all-start.3) | async-done | bytes 786464 | tf_op jit(solution)/shard_map/all_to_all | solution.py:482
  566.1 4.1 all-to-all-start.7
  575.5 5.3 all-reduce.9.cloned.1.call-done
  581.7 3.6 all-to-all-start.6
  594.4 23.4 %total_over_all.1 = f32[8,4,768]{2,1,0:T(4,128)} custom-call(f32[8,4,768]{2,1,0:T(4,128)} %select_add_fusion.rows_ref, f32[1,768]{1,0:T(1,128)} %copy-done.182, f32[1,768]{1,0:T(1,128)} %copy-done.183, f32[1,768]{1,0:T(1,128)} %copy-done.184, f32[1,768]{1,0:T(1,128)} %copy-done.185, f32[1,384]{1,0:T(1,128)} %copy-done.190, f32[1,384]{1,0:T(1,128)} %copy-done.191, ...), custom_call_target="tpu_custom_call" | custom-call | tf_op jit(solution)/shard_map/total_over_all/pallas_call | solution.py:458
  624.6 4.7 collective-permute-done.53
  640.6 9.2 %all-reduce.11.cloned.1.call-done = bf16[768,768]{1,0:T(8,128)(2,1)} async-done(((bf16[768,768]{1,0:T(8,128)(2,1)}), bf16[768,768]{1,0:T(8,128)(2,1)}) %all-reduce.11.cloned.1.call-update) | async-done | bytes 1179664 | tf_op jit(solution)/shard_map/psum | solution.py:720
  653.9 37.9 %all-reduce.13.cloned.1.call-done = bf16[384,768]{1,0:T(8,128)(2,1)} async-done(((bf16[384,768]{1,0:T(8,128)(2,1)}), bf16[384,768]{1,0:T(8,128)(2,1)}) %all-reduce.13.cloned.1.call-update) | async-done | bytes 589840 | tf_op jit(solution)/shard_map/psum | solution.py:734
  (867 shorter events, 298.1 us)
Async XLA Ops:
  10.6 33.8 %collective-permute-start = (bf16[400,768]{1,0:T(8,128)(2,1)S(1)}, bf16[400,768]{1,0:T(8,128)(2,1)S(1)}, u32[]{:S(2)}, u32[]{:S(2)}) collective-permute-start(bf16[400,768]{1,0:T(8,128)(2,1)S(1)} %fusion.52.refs_1_.first_ref), channel_id=1, source_target_pairs={{0,1},{1,0},{2,3},{3,2},{4,6},{5,7},{6,4},{7,5},{8,9},{9,8},{10,11... | collective-permute-start | bytes 1843208 | tf_op jit(solution)/shard_map/ppermute | solution.py:62
  13.6 24.1 %all-to-all-start = ((bf16[4,128,768]{2,1,0:T(8,128)(2,1)}), bf16[4,128,768]{2,1,0:T(8,128)(2,1)S(1)}, u32[]{:S(2)}, u32[]{:S(2)}) async-start(bf16[4,128,768]{2,1,0:T(8,128)(2,1)} %bitcast.185), calls=%async_computation | async-start | bytes 1572864 | tf_op jit(solution)/shard_map/all_to_all | solution.py:475
  19.2 25.2 %collective-permute-start.1 = (bf16[400,768]{1,0:T(8,128)(2,1)S(1)}, bf16[400,768]{1,0:T(8,128)(2,1)S(1)}, u32[]{:S(2)}, u32[]{:S(2)}) collective-permute-start(bf16[400,768]{1,0:T(8,128)(2,1)S(1)} %fusion.53.refs_2_.second_ref), channel_id=1, source_target_pairs={{0,1},{1,0},{2,3},{3,2},{4,6},{5,7},{6,4},{7,5},{8,9},{9,8},{10,11... | collective-permute-start | bytes 1843208 | tf_op jit(solution)/shard_map/ppermute | solution.py:62
  24.4 31.5 %collective-permute-start.6 = (bf16[768,768]{1,0:T(8,128)(2,1)}, bf16[768,768]{1,0:T(8,128)(2,1)}, u32[]{:S(2)}, u32[]{:S(2)}) collective-permute-start(bf16[768,768]{1,0:T(8,128)(2,1)} %get-tuple-element.213.first_ref), channel_id=1, source_target_pairs={{0,1},{1,0},{2,3},{3,2},{4,6},{5,7},{6,4},{7,5},{8,9},{9,8},{10,11... | collective-permute-start | bytes 3538952 | tf_op jit(solution)/shard_map/ppermute | solution.py:62
  25.5 43.2 %collective-permute-start.7 = (bf16[768,768]{1,0:T(8,128)(2,1)}, bf16[768,768]{1,0:T(8,128)(2,1)}, u32[]{:S(2)}, u32[]{:S(2)}) collective-permute-start(bf16[768,768]{1,0:T(8,128)(2,1)} %get-tuple-element.214.second_ref), channel_id=1, source_target_pairs={{0,1},{1,0},{2,3},{3,2},{4,6},{5,7},{6,4},{7,5},{8,9},{9,8},{10,11... | collective-permute-start | bytes 3538952 | tf_op jit(solution)/shard_map/ppermute | solution.py:62
  44.4 41.0 %collective-permute-start.2 = (bf16[400,768]{1,0:T(8,128)(2,1)S(1)}, bf16[400,768]{1,0:T(8,128)(2,1)S(1)}, u32[]{:S(2)}, u32[]{:S(2)}) collective-permute-start(bf16[400,768]{1,0:T(8,128)(2,1)S(1)} %broadcast_select_fusion.8), channel_id=1, source_target_pairs={{0,2},{1,3},{2,0},{3,1},{4,5},{5,4},{6,7},{7,6},{8,10},{9,11},{10,... | collective-permute-start | bytes 1843208 | tf_op jit(solution)/shard_map/ppermute | solution.py:62
  52.5 22.5 %collective-permute-start.12 = (bf16[384,768]{1,0:T(8,128)(2,1)S(1)}, bf16[384,768]{1,0:T(8,128)(2,1)}, u32[]{:S(2)}, u32[]{:S(2)}) collective-permute-start(bf16[384,768]{1,0:T(8,128)(2,1)S(1)} %bitcast.175), channel_id=1, source_target_pairs={{0,1},{1,0},{2,3},{3,2},{4,6},{5,7},{6,4},{7,5},{8,9},{9,8},{10,11... | collective-permute-start | bytes 1769480 | tf_op jit(solution)/shard_map/ppermute | solution.py:62
  53.2 32.3 %collective-permute-start.13 = (bf16[384,768]{1,0:T(8,128)(2,1)S(1)}, bf16[384,768]{1,0:T(8,128)(2,1)}, u32[]{:S(2)}, u32[]{:S(2)}) collective-permute-start(bf16[384,768]{1,0:T(8,128)(2,1)S(1)} %copy-done.32), channel_id=1, source_target_pairs={{0,1},{1,0},{2,3},{3,2},{4,6},{5,7},{6,4},{7,5},{8,9},{9,8},{10,11... | collective-permute-start | bytes 1769480 | tf_op jit(solution)/shard_map/ppermute | solution.py:62
  55.9 32.0 %collective-permute-start.4 = (bf16[400,768]{1,0:T(8,128)(2,1)S(1)}, bf16[400,768]{1,0:T(8,128)(2,1)S(1)}, u32[]{:S(2)}, u32[]{:S(2)}) collective-permute-start(bf16[400,768]{1,0:T(8,128)(2,1)S(1)} %collective-permute-done.refs_1_.first_ref), channel_id=1, source_target_pairs={{0,4},{1,5},{2,6},{3,7},{4,0},{5,1},{6,2},{7,3},{8,12},{9,13},{10,... | collective-permute-start | bytes 1843208 | tf_op jit(solution)/shard_map/ppermute | solution.py:62
  75.0 51.4 %collective-permute-start.10 = (bf16[768,768]{1,0:T(8,128)(2,1)}, bf16[768,768]{1,0:T(8,128)(2,1)}, u32[]{:S(2)}, u32[]{:S(2)}) collective-permute-start(bf16[768,768]{1,0:T(8,128)(2,1)} %broadcast_select_fusion.5), channel_id=1, source_target_pairs={{0,2},{1,3},{2,0},{3,1},{4,5},{5,4},{6,7},{7,6},{8,10},{9,11},{10,... | collective-permute-start | bytes 3538952 | tf_op jit(solution)/shard_map/ppermute | solution.py:62
  85.4 40.9 %collective-permute-start.8 = (bf16[768,768]{1,0:T(8,128)(2,1)}, bf16[768,768]{1,0:T(8,128)(2,1)}, u32[]{:S(2)}, u32[]{:S(2)}) collective-permute-start(bf16[768,768]{1,0:T(8,128)(2,1)} %collective-permute-done.6.first_ref), channel_id=1, source_target_pairs={{0,4},{1,5},{2,6},{3,7},{4,0},{5,1},{6,2},{7,3},{8,12},{9,13},{10,... | collective-permute-start | bytes 3538952 | tf_op jit(solution)/shard_map/ppermute | solution.py:62
  87.9 42.4 %collective-permute-start.9 = (bf16[768,768]{1,0:T(8,128)(2,1)}, bf16[768,768]{1,0:T(8,128)(2,1)}, u32[]{:S(2)}, u32[]{:S(2)}) collective-permute-start(bf16[768,768]{1,0:T(8,128)(2,1)} %collective-permute-done.7.second_ref), channel_id=1, source_target_pairs={{0,4},{1,5},{2,6},{3,7},{4,0},{5,1},{6,2},{7,3},{8,12},{9,13},{10,... | collective-permute-start | bytes 3538952 | tf_op jit(solution)/shard_map/ppermute | solution.py:62
  88.0 36.0 %collective-permute-start.14 = (bf16[384,768]{1,0:T(8,128)(2,1)}, bf16[384,768]{1,0:T(8,128)(2,1)}, u32[]{:S(2)}, u32[]{:S(2)}) collective-permute-start(bf16[384,768]{1,0:T(8,128)(2,1)} %broadcast_select_fusion.11), channel_id=1, source_target_pairs={{0,2},{1,3},{2,0},{3,1},{4,5},{5,4},{6,7},{7,6},{8,10},{9,11},{10,... | collective-permute-start | bytes 1769480 | tf_op jit(solution)/shard_map/ppermute | solution.py:62
  108.3 52.1 %all-to-all-start.2 = ((bf16[4,128,768]{2,1,0:T(8,128)(2,1)}), bf16[4,128,768]{2,1,0:T(8,128)(2,1)S(1)}, u32[]{:S(2)}, u32[]{:S(2)}) async-start(bf16[4,128,768]{2,1,0:T(8,128)(2,1)} %bitcast.186), calls=%async_computation.2 | async-start | bytes 1572864 | tf_op jit(solution)/shard_map/all_to_all | solution.py:475
  112.1 24.2 %collective-permute-start.18 = (bf16[768,768]{1,0:T(8,128)(2,1)}, bf16[768,768]{1,0:T(8,128)(2,1)}, u32[]{:S(2)}, u32[]{:S(2)}) collective-permute-start(bf16[768,768]{1,0:T(8,128)(2,1)} %get-tuple-element.223.first_ref), channel_id=1, source_target_pairs={{0,1},{1,0},{2,3},{3,2},{4,6},{5,7},{6,4},{7,5},{8,9},{9,8},{10,11... | collective-permute-start | bytes 3538952 | tf_op jit(solution)/shard_map/ppermute | solution.py:62
  124.0 25.0 %collective-permute-start.19 = (bf16[768,768]{1,0:T(8,128)(2,1)S(1)}, bf16[768,768]{1,0:T(8,128)(2,1)}, u32[]{:S(2)}, u32[]{:S(2)}) collective-permute-start(bf16[768,768]{1,0:T(8,128)(2,1)S(1)} %copy-done.42), channel_id=1, source_target_pairs={{0,1},{1,0},{2,3},{3,2},{4,6},{5,7},{6,4},{7,5},{8,9},{9,8},{10,11... | collective-permute-start | bytes 3538952 | tf_op jit(solution)/shard_map/ppermute | solution.py:62
  126.4 26.4 %collective-permute-start.11 = (bf16[768,768]{1,0:T(8,128)(2,1)}, bf16[768,768]{1,0:T(8,128)(2,1)S(1)}, u32[]{:S(2)}, u32[]{:S(2)}) collective-permute-start(bf16[768,768]{1,0:T(8,128)(2,1)} %collective-permute-done.10), channel_id=1, source_target_pairs={{0,4},{1,5},{2,6},{3,7},{4,0},{5,1},{6,2},{7,3},{8,12},{9,13},{10,... | collective-permute-start | bytes 3538952 | tf_op jit(solution)/shard_map/ppermute | solution.py:62
  130.3 60.6 %collective-permute-start.16 = (bf16[384,768]{1,0:T(8,128)(2,1)}, bf16[384,768]{1,0:T(8,128)(2,1)}, u32[]{:S(2)}, u32[]{:S(2)}) collective-permute-start(bf16[384,768]{1,0:T(8,128)(2,1)} %collective-permute-done.12.refs_1_.first_ref), channel_id=1, source_target_pairs={{0,4},{1,5},{2,6},{3,7},{4,0},{5,1},{6,2},{7,3},{8,12},{9,13},{10,... | collective-permute-start | bytes 1769480 | tf_op jit(solution)/shard_map/ppermute | solution.py:62
  132.6 58.3 %collective-permute-start.17 = (bf16[384,768]{1,0:T(8,128)(2,1)}, bf16[384,768]{1,0:T(8,128)(2,1)}, u32[]{:S(2)}, u32[]{:S(2)}) collective-permute-start(bf16[384,768]{1,0:T(8,128)(2,1)} %collective-permute-done.13.refs_2_.second_ref), channel_id=1, source_target_pairs={{0,4},{1,5},{2,6},{3,7},{4,0},{5,1},{6,2},{7,3},{8,12},{9,13},{10,... | collective-permute-start | bytes 1769480 | tf_op jit(solution)/shard_map/ppermute | solution.py:62
  151.4 80.2 %collective-permute-start.22 = (bf16[768,768]{1,0:T(8,128)(2,1)}, bf16[768,768]{1,0:T(8,128)(2,1)}, u32[]{:S(2)}, u32[]{:S(2)}) collective-permute-start(bf16[768,768]{1,0:T(8,128)(2,1)} %broadcast_select_fusion.2), channel_id=1, source_target_pairs={{0,2},{1,3},{2,0},{3,1},{4,5},{5,4},{6,7},{7,6},{8,10},{9,11},{10,... | collective-permute-start | bytes 3538952 | tf_op jit(solution)/shard_map/ppermute | solution.py:62
  152.9 84.1 %collective-permute-start.20 = (bf16[768,768]{1,0:T(8,128)(2,1)}, bf16[768,768]{1,0:T(8,128)(2,1)}, u32[]{:S(2)}, u32[]{:S(2)}) collective-permute-start(bf16[768,768]{1,0:T(8,128)(2,1)} %collective-permute-done.18.first_ref), channel_id=1, source_target_pairs={{0,4},{1,5},{2,6},{3,7},{4,0},{5,1},{6,2},{7,3},{8,12},{9,13},{10,... | collective-permute-start | bytes 3538952 | tf_op jit(solution)/shard_map/ppermute | solution.py:62
  152.9 86.8 %collective-permute-start.21 = (bf16[768,768]{1,0:T(8,128)(2,1)}, bf16[768,768]{1,0:T(8,128)(2,1)}, u32[]{:S(2)}, u32[]{:S(2)}) collective-permute-start(bf16[768,768]{1,0:T(8,128)(2,1)} %collective-permute-done.19.second_ref), channel_id=1, source_target_pairs={{0,4},{1,5},{2,6},{3,7},{4,0},{5,1},{6,2},{7,3},{8,12},{9,13},{10,... | collective-permute-start | bytes 3538952 | tf_op jit(solution)/shard_map/ppermute | solution.py:62
  161.3 73.5 %all-to-all-start.5 = ((bf16[4,128,768]{2,1,0:T(8,128)(2,1)}), bf16[4,128,768]{2,1,0:T(8,128)(2,1)}, u32[]{:S(2)}, u32[]{:S(2)}) async-start(bf16[4,128,768]{2,1,0:T(8,128)(2,1)} %bitcast.187), calls=%async_computation.5 | async-start | bytes 1572864 | tf_op jit(solution)/shard_map/all_to_all | solution.py:475
  294.5 25.8 %collective-permute-start.24 = (bf16[768,768]{1,0:T(8,128)(2,1)}, bf16[768,768]{1,0:T(8,128)(2,1)}, u32[]{:S(2)}, u32[]{:S(2)}) collective-permute-start(bf16[768,768]{1,0:T(8,128)(2,1)} %get-tuple-element.237), channel_id=1, source_target_pairs={{0,4},{1,5},{2,6},{3,7},{4,0},{5,1},{6,2},{7,3},{8,12},{9,13},{10,... | collective-permute-start | bytes 3538952 | tf_op jit(solution)/shard_map/ppermute | solution.py:62
  295.5 27.7 %collective-permute-start.25 = (bf16[768,768]{1,0:T(8,128)(2,1)}, bf16[768,768]{1,0:T(8,128)(2,1)}, u32[]{:S(2)}, u32[]{:S(2)}) collective-permute-start(bf16[768,768]{1,0:T(8,128)(2,1)} %copy-done.195), channel_id=1, source_target_pairs={{0,4},{1,5},{2,6},{3,7},{4,0},{5,1},{6,2},{7,3},{8,12},{9,13},{10,... | collective-permute-start | bytes 3538952 | tf_op jit(solution)/shard_map/ppermute | solution.py:62
  327.6 35.5 %collective-permute-start.28 = (bf16[768,768]{1,0:T(8,128)(2,1)S(1)}, bf16[768,768]{1,0:T(8,128)(2,1)S(1)}, u32[]{:S(2)}, u32[]{:S(2)}) collective-permute-start(bf16[768,768]{1,0:T(8,128)(2,1)S(1)} %add_convert_fusion.9), channel_id=1, source_target_pairs={{0,2},{1,3},{2,0},{3,1},{4,5},{5,4},{6,7},{7,6},{8,10},{9,11},{10,... | collective-permute-start | bytes 3538952 | tf_op jit(solution)/shard_map/ppermute | solution.py:62
  328.8 55.3 %collective-permute-start.30 = (bf16[768,768]{1,0:T(8,128)(2,1)}, bf16[768,768]{1,0:T(8,128)(2,1)}, u32[]{:S(2)}, u32[]{:S(2)}) collective-permute-start(bf16[768,768]{1,0:T(8,128)(2,1)} %add_convert_fusion.11), channel_id=1, source_target_pairs={{0,1},{1,0},{2,3},{3,2},{4,6},{5,7},{6,4},{7,5},{8,9},{9,8},{10,11... | collective-permute-start | bytes 3538952 | tf_op jit(solution)/shard_map/ppermute | solution.py:62
  377.6 29.6 %all-to-all-start.4 = ((bf16[4,128,768]{2,1,0:T(8,128)(2,1)}), bf16[4,128,768]{2,1,0:T(8,128)(2,1)}, u32[]{:S(2)}, u32[]{:S(2)}) async-start(bf16[4,128,768]{2,1,0:T(8,128)(2,1)} %bitcast.188), calls=%async_computation.4 | async-start | bytes 1572864 | tf_op jit(solution)/shard_map/all_to_all | solution.py:475
  381.8 88.6 %all-reduce.7.cloned.1.call-start = ((), (), s32[]{:S(2)}) async-start(), calls=%async_computation.8 | async-start | bytes 2359296 | tf_op jit(solution)/shard_map/psum | solution.py:692
  382.0 23.7 %collective-permute-start.29 = (bf16[768,768]{1,0:T(8,128)(2,1)}, bf16[768,768]{1,0:T(8,128)(2,1)S(1)}, u32[]{:S(2)}, u32[]{:S(2)}) collective-permute-start(bf16[768,768]{1,0:T(8,128)(2,1)} %add_convert_fusion.7), channel_id=1, source_target_pairs={{0,1},{1,0},{2,3},{3,2},{4,6},{5,7},{6,4},{7,5},{8,9},{9,8},{10,11... | collective-permute-start | bytes 3538952 | tf_op jit(solution)/shard_map/ppermute | solution.py:62
  413.4 36.9 %collective-permute-start.36 = (bf16[384,768]{1,0:T(8,128)(2,1)}, bf16[384,768]{1,0:T(8,128)(2,1)}, u32[]{:S(2)}, u32[]{:S(2)}) collective-permute-start(bf16[384,768]{1,0:T(8,128)(2,1)} %add_convert_fusion.21), channel_id=1, source_target_pairs={{0,2},{1,3},{2,0},{3,1},{4,5},{5,4},{6,7},{7,6},{8,10},{9,11},{10,... | collective-permute-start | bytes 1769480 | tf_op jit(solution)/shard_map/ppermute | solution.py:62
  414.9 36.8 %collective-permute-start.38 = (bf16[384,768]{1,0:T(8,128)(2,1)}, bf16[384,768]{1,0:T(8,128)(2,1)}, u32[]{:S(2)}, u32[]{:S(2)}) collective-permute-start(bf16[384,768]{1,0:T(8,128)(2,1)} %add_convert_fusion.23), channel_id=1, source_target_pairs={{0,1},{1,0},{2,3},{3,2},{4,6},{5,7},{6,4},{7,5},{8,9},{9,8},{10,11... | collective-permute-start | bytes 1769480 | tf_op jit(solution)/shard_map/ppermute | solution.py:62
  463.5 20.2 %collective-permute-start.43 = (bf16[768,768]{1,0:T(8,128)(2,1)}, bf16[768,768]{1,0:T(8,128)(2,1)}, u32[]{:S(2)}, u32[]{:S(2)}) collective-permute-start(bf16[768,768]{1,0:T(8,128)(2,1)} %get-tuple-element.318), channel_id=1, source_target_pairs={{0,4},{1,5},{2,6},{3,7},{4,0},{5,1},{6,2},{7,3},{8,12},{9,13},{10,... | collective-permute-start | bytes 3538952 | tf_op jit(solution)/shard_map/ppermute | solution.py:62
  486.3 40.2 %collective-permute-start.44 = (bf16[768,768]{1,0:T(8,128)(2,1)}, bf16[768,768]{1,0:T(8,128)(2,1)}, u32[]{:S(2)}, u32[]{:S(2)}) collective-permute-start(bf16[768,768]{1,0:T(8,128)(2,1)} %add_convert_fusion.3), channel_id=1, source_target_pairs={{0,2},{1,3},{2,0},{3,1},{4,5},{5,4},{6,7},{7,6},{8,10},{9,11},{10,... | collective-permute-start | bytes 3538952 | tf_op jit(solution)/shard_map/ppermute | solution.py:62
  487.8 55.3 %collective-permute-start.46 = (bf16[768,768]{1,0:T(8,128)(2,1)}, bf16[768,768]{1,0:T(8,128)(2,1)}, u32[]{:S(2)}, u32[]{:S(2)}) collective-permute-start(bf16[768,768]{1,0:T(8,128)(2,1)} %add_convert_fusion.5), channel_id=1, source_target_pairs={{0,1},{1,0},{2,3},{3,2},{4,6},{5,7},{6,4},{7,5},{8,9},{9,8},{10,11... | collective-permute-start | bytes 3538952 | tf_op jit(solution)/shard_map/ppermute | solution.py:62
  491.6 53.0 %all-to-all-start.1 = ((bf16[4,128,768]{2,1,0:T(8,128)(2,1)}), bf16[4,128,768]{2,1,0:T(8,128)(2,1)}, u32[]{:S(2)}, u32[]{:S(2)}) async-start(bf16[4,128,768]{2,1,0:T(8,128)(2,1)} %bitcast.26), calls=%async_computation.1 | async-start | bytes 1572864 | tf_op jit(solution)/shard_map/all_to_all | solution.py:482
  495.8 84.9 %all-reduce.9.cloned.1.call-start = ((), (), s32[]{:S(2)}) async-start(), calls=%async_computation.9 | async-start | bytes 1179648 | tf_op jit(solution)/shard_map/psum | solution.py:713
  541.0 31.3 %collective-permute-start.45 = (bf16[768,768]{1,0:T(8,128)(2,1)}, bf16[768,768]{1,0:T(8,128)(2,1)}, u32[]{:S(2)}, u32[]{:S(2)}) collective-permute-start(bf16[768,768]{1,0:T(8,128)(2,1)} %add_convert_fusion.1), channel_id=1, source_target_pairs={{0,1},{1,0},{2,3},{3,2},{4,6},{5,7},{6,4},{7,5},{8,9},{9,8},{10,11... | collective-permute-start | bytes 3538952 | tf_op jit(solution)/shard_map/ppermute | solution.py:62
  543.1 29.3 %collective-permute-start.47 = (bf16[768,768]{1,0:T(8,128)(2,1)}, bf16[768,768]{1,0:T(8,128)(2,1)}, u32[]{:S(2)}, u32[]{:S(2)}) collective-permute-start(bf16[768,768]{1,0:T(8,128)(2,1)} %collective-permute-done.46), channel_id=1, source_target_pairs={{0,4},{1,5},{2,6},{3,7},{4,0},{5,1},{6,2},{7,3},{8,12},{9,13},{10,... | collective-permute-start | bytes 3538952 | tf_op jit(solution)/shard_map/ppermute | solution.py:62
  544.6 21.5 %all-to-all-start.3 = ((bf16[4,128,768]{2,1,0:T(8,128)(2,1)}), bf16[4,128,768]{2,1,0:T(8,128)(2,1)}, u32[]{:S(2)}, u32[]{:S(2)}) async-start(bf16[4,128,768]{2,1,0:T(8,128)(2,1)} %bitcast.178), calls=%async_computation.3 | async-start | bytes 1572864 | tf_op jit(solution)/shard_map/all_to_all | solution.py:482
  548.8 21.4 %collective-permute-start.51 = (bf16[384,768]{1,0:T(8,128)(2,1)}, bf16[384,768]{1,0:T(8,128)(2,1)}, u32[]{:S(2)}, u32[]{:S(2)}) collective-permute-start(bf16[384,768]{1,0:T(8,128)(2,1)} %copy-done.197), channel_id=1, source_target_pairs={{0,4},{1,5},{2,6},{3,7},{4,0},{5,1},{6,2},{7,3},{8,12},{9,13},{10,... | collective-permute-start | bytes 1769480 | tf_op jit(solution)/shard_map/ppermute | solution.py:62
  551.0 40.6 %collective-permute-start.59 = (bf16[768,768]{1,0:T(8,128)(2,1)}, bf16[768,768]{1,0:T(8,128)(2,1)}, u32[]{:S(2)}, u32[]{:S(2)}) collective-permute-start(bf16[768,768]{1,0:T(8,128)(2,1)} %all-reduce.7.cloned.1.call-done), channel_id=1, source_target_pairs={{0,4},{1,5},{2,6},{3,7},{4,0},{5,1},{6,2},{7,3},{8,12},{9,13},{10,... | collective-permute-start | bytes 3538952 | tf_op jit(solution)/shard_map/ppermute | solution.py:62
  581.7 36.1 %all-to-all-start.6 = ((bf16[4,128,768]{2,1,0:T(8,128)(2,1)}), bf16[4,128,768]{2,1,0:T(8,128)(2,1)S(1)}, u32[]{:S(2)}, u32[]{:S(2)}) async-start(bf16[4,128,768]{2,1,0:T(8,128)(2,1)} %bitcast.181), calls=%async_computation.6 | async-start | bytes 1572864 | tf_op jit(solution)/shard_map/all_to_all | solution.py:482
  585.3 64.5 %all-reduce.11.cloned.1.call-start = ((), (), s32[]{:S(2)}) async-start(), calls=%async_computation.10 | async-start | bytes 2359296 | tf_op jit(solution)/shard_map/psum | solution.py:720
  585.3 32.5 %collective-permute-start.52 = (bf16[384,768]{1,0:T(8,128)(2,1)}, bf16[384,768]{1,0:T(8,128)(2,1)}, u32[]{:S(2)}, u32[]{:S(2)}) collective-permute-start(bf16[384,768]{1,0:T(8,128)(2,1)} %add_convert_fusion.15), channel_id=1, source_target_pairs={{0,2},{1,3},{2,0},{3,1},{4,5},{5,4},{6,7},{7,6},{8,10},{9,11},{10,... | collective-permute-start | bytes 1769480 | tf_op jit(solution)/shard_map/ppermute | solution.py:62
  589.9 31.0 %collective-permute-start.57 = (bf16[384,768]{1,0:T(8,128)(2,1)}, bf16[384,768]{1,0:T(8,128)(2,1)}, u32[]{:S(2)}, u32[]{:S(2)}) collective-permute-start(bf16[384,768]{1,0:T(8,128)(2,1)} %all-reduce.9.cloned.1.call-done), channel_id=1, source_target_pairs={{0,4},{1,5},{2,6},{3,7},{4,0},{5,1},{6,2},{7,3},{8,12},{9,13},{10,... | collective-permute-start | bytes 1769480 | tf_op jit(solution)/shard_map/ppermute | solution.py:62
  590.0 32.3 %collective-permute-start.54 = (bf16[384,768]{1,0:T(8,128)(2,1)}, bf16[384,768]{1,0:T(8,128)(2,1)}, u32[]{:S(2)}, u32[]{:S(2)}) collective-permute-start(bf16[384,768]{1,0:T(8,128)(2,1)} %add_convert_fusion.17), channel_id=1, source_target_pairs={{0,1},{1,0},{2,3},{3,2},{4,6},{5,7},{6,4},{7,5},{8,9},{9,8},{10,11... | collective-permute-start | bytes 1769480 | tf_op jit(solution)/shard_map/ppermute | solution.py:62
  594.4 97.4 %all-reduce.13.cloned.1.call-start = ((), (), s32[]{:S(2)}) async-start(), calls=%async_computation.11 | async-start | bytes 1179648 | tf_op jit(solution)/shard_map/psum | solution.py:734
  (299 other events, 1835.8 us)
Sparse Core Ops, SparseCore 0:
  415.6 54.7 all-reduce.6
  541.1 39.5 all-reduce.8
  594.5 55.3 all-reduce.10
  652.6 39.0 all-reduce.12

commit v6 on v5

--- a/solution.py
+++ b/solution.py
@@ -77,16 +77,27 @@
     return lax.optimization_barrier(values)
 
 
-def gather_part(first, second, side):
-    got_first, got_second = send(first, MAIN), send(second, MAIN)
-    across = send(pick(side, got_first, got_second), DIAG)
-    other_first, other_second = send(got_first, SWAP), send(got_second, SWAP)
-    rest = send(across, SWAP)
-    blocks = [
-        (first, second), (got_first, got_second), (other_first, other_second),
-        (pick(side, across, rest), pick(side, rest, across)),
-    ]
-    return blocks, across
+class Gathering:
+    def __init__(self, side):
+        self.side = side
+
+    def start(self, value, first, second):
+        value, first, second = tie(value, first, second)
+        self.got = (send(first, MAIN), send(second, MAIN))
+        self.blocks = [(first, second)]
+        return value
+
+    def arrived(self, value):
+        value, *got = tie(value, *self.got)
+        self.across = send(pick(self.side, *got), DIAG)
+        self.blocks += [tuple(got), tuple(send(g, SWAP) for g in got)]
+        return value
+
+    def crossed(self, value):
+        value, across = tie(value, self.across)
+        rest = send(across, SWAP)
+        self.blocks.append((pick(self.side, across, rest), pick(self.side, rest, across)))
+        return value
 
 
 def reduce_outgoing(blocks):
@@ -482,24 +493,27 @@
     return lax.all_to_all(blocks, "tensor", split_axis=0, concat_axis=0, tiled=True)
 
 
-def layer_forward(l, x, seg, attn_w, ffn_w, vec, hook):
+def layer_forward(l, x, seg, attn, ffn, vec, hook):
     xb = x.astype(BF)
     kept = []
     z1 = x + vec["pb"]
-    for j, ((first, second), bias) in enumerate(zip(attn_w, vec["heads"])):
-        *saved, z1 = attend_forward(l, vec["cols"], xb, first, second, bias, z1, seg)
+    for j in range(TENSORS):
+        first, second = attn.blocks[j]
+        *saved, z1 = attend_forward(l, vec["cols"], xb, first, second, vec["heads"](j), z1, seg)
         kept.append(saved)
-        z1 = hook(j, z1)
+        z1 = hook("attn", j, z1)
     n1, r1 = normal_parts(z1)
     y = n1 * vec["g0"] + vec["s0"]
     yb = y.astype(BF)
     act, slope = [], []
     z2 = y + vec["sb"]
-    for (first, second), bias in zip(ffn_w, vec["eb"]):
-        a, b = gelu_parts(mm(yb, first, 1, 0) + bias)
+    for j in range(TENSORS):
+        first, second = ffn.blocks[j]
+        a, b = gelu_parts(mm(yb, first, 1, 0) + vec["eb"](j))
         act.append(a.astype(BF))
         slope.append(b.astype(BF))
         z2 = z2 + mm(act[-1], second, 1, 0)
+        z2 = hook("ffn", j, z2)
     n2, r2 = normal_parts(z2)
     out = n2 * vec["g1"] + vec["s1"]
     return out, (xb, kept, n1, r1, yb, act, slope, n2, r2)
@@ -596,33 +610,62 @@
     first, second = attn_rows(0)
     first = jnp.concatenate([first, bias_rows], axis=0)
     second = jnp.pad(second, ((0, extra), (0, 0)))
-    attn_w0, mark = gather_part(first, second, side)
+    gather_attn0, gather_ffn0, gather_attn1, gather_ffn1 = (Gathering(side) for _ in range(4))
     x = to_rows(layer_input[0])
-    expand, shrink, first = tie(w_expand[0], w_shrink[0], first)
-    ffn_w0, mark = gather_part(expand, shrink, side)
+    mark = gather_attn0.start(layer_input[0, 0, 0], first, second)
+    mark = gather_ffn0.start(mark, w_expand[0], w_shrink[0])
     later = {}
 
-    def during_forward0(j, value):
-        if j == 1:
-            first, second, value = tie(*attn_rows(1), value)
-            later["attn"], mark = gather_part(first, second, side)
-        if j == 3:
-            first, second, skip, value = tie(w_expand[1], w_shrink[1], skip_tokens[0], value)
-            later["ffn"], mark = gather_part(first, second, side)
-            later["skip"] = to_rows(skip)
-        return value
-
-    def plain(name, value):
+    def during_forward0(kind, j, value):
+        if kind == "attn":
+            if j == 0:
+                value = gather_attn0.arrived(value)
+            if j == 1:
+                value = gather_attn1.start(value, *attn_rows(1))
+            if j == 2:
+                value = gather_attn0.crossed(value)
+            if j == 3:
+                value = gather_ffn0.arrived(value)
+                value = gather_ffn1.start(value, w_expand[1], w_shrink[1])
+        else:
+            if j == 0:
+                skip, value = tie(skip_tokens[0], value)
+                later["skip"] = to_rows(skip)
+            if j == 1:
+                value = gather_attn1.arrived(value)
+            if j == 2:
+                value = gather_ffn0.crossed(value)
+        return value
+
+    def during_forward1(kind, j, value):
+        if kind == "attn":
+            if j == 0:
+                head_cot, value = tie(head_cotangent[0], value)
+                later["head"] = to_rows(head_cot)
+            if j == 1:
+                value = gather_attn1.crossed(value)
+            if j == 2:
+                value, later["backbone_out"] = tie(value, later["backbone_out"])
+            if j == 3:
+                value = gather_ffn1.arrived(value)
+        else:
+            if j == 0:
+                backbone_cot, value = tie(backbone_cotangent[0], value)
+                later["backbone"] = to_rows(backbone_cot)
+            if j == 2:
+                value = gather_ffn1.crossed(value)
         return value
 
     tokens = x.shape[0]
 
-    biases = [first[2 * head_cols : 2 * head_cols + 3].astype(F32) for first, second in attn_w0]
+    def bias_row(j, i):
+        first, second = gather_attn0.blocks[j]
+        return first[2 * head_cols + i : 2 * head_cols + i + 1].astype(F32)
 
     def vectors(l):
         return {
-            "cols": head_cols, "heads": [b[:1] for b in biases],
-            "eb": [b[1 + l] for b in biases], "pb": project_bias[l].astype(F32),
+            "cols": head_cols, "heads": lambda j: bias_row(j, 0),
+            "eb": lambda j: bias_row(j, 1 + l), "pb": project_bias[l].astype(F32),
             "g0": norm_gain[l, 0].astype(F32), "g1": norm_gain[l, 1].astype(F32),
             "s0": norm_shift[l, 0].astype(F32), "s1": norm_shift[l, 1].astype(F32),
             "sb": shrink_bias[l].astype(F32),
@@ -641,11 +684,9 @@
     first_place = jnp.sum(picker, axis=0)[:, None] > 0
 
     vec0, vec1 = vectors(0), vectors(1)
-    backbone, kept0 = layer_forward(0, x.astype(F32), seg, attn_w0, ffn_w0, vec0, during_forward0)
-    attn_w1, ffn_w1, skip = later["attn"], later["ffn"], later["skip"]
-    later_head, later_backbone, backbone = tie(head_cotangent[0], backbone_cotangent[0], backbone)
-    head_cot = to_rows(later_head)
-    backbone_cot = to_rows(later_backbone)
+    backbone, kept0 = layer_forward(0, x.astype(F32), seg, gather_attn0, gather_ffn0, vec0, during_forward0)
+    attn_w0, ffn_w0 = gather_attn0.blocks, gather_ffn0.blocks
+    later["backbone_out"] = to_places((backbone * valid).astype(BF))
     cls = mm(picker.astype(BF), backbone.astype(BF), 1, 0).astype(BF)
     anchors = gather_anchors(cls)
     dp_count = lax.axis_size("dp")
@@ -654,8 +695,11 @@
     anchors = anchors.reshape(dp_count, pair_count, TENSORS * span_count, width)
     anchors = jnp.swapaxes(anchors, 0, 1).reshape(pair_count, vector_count, width)
 
-    head_in = jnp.where(first_place, backbone, skip.astype(F32))
-    head, kept1 = layer_forward(1, head_in, seg, attn_w1, ffn_w1, vec1, plain)
+    head_in = jnp.where(first_place, backbone, later["skip"].astype(F32))
+    head, kept1 = layer_forward(1, head_in, seg, gather_attn1, gather_ffn1, vec1, during_forward1)
+    attn_w1, ffn_w1 = gather_attn1.blocks, gather_ffn1.blocks
+    head_cot, backbone_cot = later["head"], later["backbone"]
+    head_out = to_places((head * valid).astype(BF))
 
     root = math.sqrt(width)
     logits = mm(anchors[0], anchors[1], 1, 1) / root
@@ -675,9 +719,13 @@
     other = lax.dynamic_index_in_dim(anchors, 1 - side, 0, keepdims=False).astype(F32)
     dcls = jnp.dot(wanted, other, precision=HIGHEST) / root
 
+    def plain(name, value):
+        return value
+
     ffn1, attn1, ffn0, attn0 = (Reduction() for _ in range(4))
 
     dy, blocks, small1 = ffn_backward(head_cot.astype(F32) * valid, ffn_w1, vec1, kept1, plain)
+    dy, head_out = tie(dy, head_out)
     dy = ffn1.start(dy, blocks)
 
     def during_attn1(name, value):
@@ -690,7 +738,7 @@
     du = attn1.start(du, blocks)
     du = ffn1.summed(du)
     ffn_total1 = lax.psum(ffn1.total, "dp")
-    grad_skip = jnp.where(first_place, 0.0, du).astype(BF)
+    grad_skip = to_places(jnp.where(first_place, 0.0, du).astype(BF))
 
     seed = backbone_cot.astype(F32) * valid + jnp.where(first_place, du, 0.0)
     seed = seed + jnp.dot(picker.T, dcls, precision=HIGHEST)
@@ -701,6 +749,7 @@
         return attn1.crossed(value)
 
     dy, blocks, small0 = ffn_backward(seed, ffn_w0, vec0, kept0, during_ffn0)
+    dy, grad_skip = tie(dy, grad_skip)
     dy = ffn0.start(dy, blocks)
     dy = attn1.summed(dy)
 
@@ -749,11 +798,11 @@
     gh0, gp0 = attn_unpack(*finish_part(attn_total0, side))
 
     return (
-        to_places((backbone * valid).astype(BF))[None],
-        to_places((head * valid).astype(BF))[None],
+        later["backbone_out"][None],
+        head_out[None],
         span_loss,
         to_places(dx.astype(BF))[None],
-        to_places(grad_skip)[None],
+        grad_skip[None],
         jnp.stack([gh0, gh1]),
         jnp.stack(hb),
         jnp.stack([gp0, gp1]),

time: 732 us -> 691 us (0.944)
  waiting for transfers between devices: 128 us -> 108 us
  other arithmetic: 127 us -> 110 us
    ppermute x60, waiting for transfers between devices: 59.3 us -> 24.5 us  [send(): return lax.ppermute(values, PLANE, plane_pairs(kind))]
    unnamed x557 -> x497, local copies, waits for them, and re-layouts: 62.2 us -> 77.5 us
    psum x1, waiting for transfers between devices: 5.26 us -> 20.4 us  [shards(): attn_total1 = lax.psum(attn_total1, 'dp')]
    psum x1, waiting for transfers between devices: 9.2 us -> 21.4 us  [shards(): ffn_total0 = lax.psum(late, 'dp')]
    all_to_all x4, waiting for transfers between devices: 10.5 us -> 0.01 us  [to_places(): lax.all_to_all(blocks, 'tensor', split_axis=0, concat_axis=0, tiled=True)]
    pallas_call x8, Pallas kernels: 62.4 us -> 55 us  [attend_forward(): pl.pallas_call(body, name='attend_forward', out_shape=(narrow, narrow, na...]
  transfers between devices with their start and end apart: 72 -> 72, of which waited for: 13 -> 11; matrix products, arithmetic and copies ran while one was open for 24% -> 22% of each run, Pallas kernels for 28% -> 34%
where the time goes in v6:
time: 691 us; the launch traced here: 681 us
  Pallas kernels  229 us (33%)
  other arithmetic  110 us (16%)
  waiting for transfers between devices  108 us (16%)
  local copies, waits for them, and re-layouts  89.8 us (13%)
  starting transfers between devices  74.8 us (11%)
  matrix products  50.2 us (7%)
  between operations  19.8 us (3%)
    unnamed x497, local copies, waits for them, and re-layouts  77.5 us
    pallas_call x8, Pallas kernels, attend_backward(): pl.pallas_call(attend_backward_kernel, name='attend_backward', out_shape=...  71.7 us
    pallas_call x8, Pallas kernels, ffn_block_backward(): pl.pallas_call(ffn_backward_kernel, name='ffn_backward', out_shape=(jax.S...  62.3 us
    pallas_call x8, Pallas kernels, attend_forward(): pl.pallas_call(body, name='attend_forward', out_shape=(narrow, narrow, na...  55 us
    dot_general x18, matrix products, mm(): lax.dot_general(a, b, (((ca,), (cb,)), ((), ())), preferred_element_type=...  44.2 us
    psum x1, waiting for transfers between devices, shards(): attn_total0 = lax.psum(attn_total0, 'dp')  40.7 us
    ppermute x60, starting transfers between devices, send(): return lax.ppermute(values, PLANE, plane_pairs(kind))  40 us
    convert_element_type x24, other arithmetic, plus(): return total.astype(BF)  39.2 us
  transfers between devices with their start and end apart: 72, of which 11 were waited for; matrix products, arithmetic and copies ran while one was open for 22% of the time, Pallas kernels for 34%

profile of v6, /device:TPU:0, one launch (start us, length us, event | category | flops | bytes accessed | tf_op | source)
XLA Modules:
  0.0 681.4 jit_solution(9462125159809831067)
XLA Ops:
  7.2 5.2 all-to-all-start
  26.7 6.4 attend_forward.8
  40.3 6.4 attend_forward.9
  50.3 6.4 attend_forward.10
  59.3 6.6 attend_forward.11
  74.5 3.6 fusion.34
  80.5 3.4 fusion.29
  86.5 3.3 fusion.24
  94.9 4.2 all-to-all-start.1
  116.9 7.6 %attend_forward.12 = (bf16[512,192]{1,0:T(8,128)(2,1)S(1)}, bf16[512,192]{1,0:T(8,128)(2,1)S(1)}, bf16[512,192]{1,0:T(8,128)(2,1)S(1)}, bf16[512,192]{1,0:T(8,12...) custom-call(bf16[512,768]{1,0:T(8,128)(2,1)S(1)} %get-tuple-element.516.refs_0_.x_ref, ...), custom_call_target="tpu_custom_call" | custom-call | flops 1048576 | bytes 1024 | tf_op jit(solution)/shard_map/attend_forward/pallas_call | solution.py:276
  129.2 4.6 all-to-all-start.2
  135.2 7.6 %attend_forward.13 = (bf16[512,192]{1,0:T(8,128)(2,1)S(1)}, bf16[512,192]{1,0:T(8,128)(2,1)S(1)}, bf16[512,192]{1,0:T(8,128)(2,1)S(1)}, bf16[512,192]{1,0:T(8,12...) custom-call(bf16[512,768]{1,0:T(8,128)(2,1)S(1)} %get-tuple-element.516.refs_0_.x_ref, ...), custom_call_target="tpu_custom_call" | custom-call | flops 1048576 | bytes 1024 | tf_op jit(solution)/shard_map/attend_forward/pallas_call | solution.py:276
  146.4 7.6 %attend_forward.14 = (bf16[512,192]{1,0:T(8,128)(2,1)S(1)}, bf16[512,192]{1,0:T(8,128)(2,1)S(1)}, bf16[512,192]{1,0:T(8,128)(2,1)S(1)}, bf16[512,192]{1,0:T(8,12...) custom-call(bf16[512,768]{1,0:T(8,128)(2,1)S(1)} %get-tuple-element.516.refs_0_.x_ref, ...), custom_call_target="tpu_custom_call" | custom-call | flops 1048576 | bytes 1024 | tf_op jit(solution)/shard_map/attend_forward/pallas_call | solution.py:276
  160.5 6.4 attend_forward.15
  180.4 3.7 fusion.19
  186.5 3.4 fusion.14
  192.2 3.4 fusion.9
  195.6 3.5 add_add_fusion
  199.3 4.2 all-to-all-start.3
  206.6 17.6 %gather_anchors.1 = bf16[4,8,4,768]{3,2,1,0:T(4,128)(2,1)} custom-call(bf16[4,768]{1,0:T(4,128)(2,1)} %convolution_convert_fusion.refs_0_), custom_call_target="tpu_custom_call" | custom-call | tf_op jit(solution)/shard_map/gather_anchors/pallas_call | solution.py:362
  238.5 4.4 all-to-all-start.4
  246.7 8.2 %ffn_backward.8 = (bf16[768,768]{1,0:T(8,128)(2,1)S(1)}, bf16[768,768]{1,0:T(8,128)(2,1)S(1)}, f32[1,768]{1,0:T(1,128)S(1)}, f32[512,768]{1,0:T(8,128)S(1)}) custom-call(bf16[512,768]{1,0:T(8,128)(2,1)S(1)} %convert_element_type.534.dz_ref, bf16[512,768]{1,0:T(8,128)(2,1)S(1)} %copy-done.7, bf16[512,768]{1,0:T(8,128)(2,1)S(1)} %copy-done.84, ...), custom_call_target="tpu_custom_call" | custom-call | flops 1048576 | bytes 1024 | tf_op jit(solution)/shard_map/ffn_backward/pallas_call | solution.py:254
  257.0 8.2 %ffn_backward.9 = (bf16[768,768]{1,0:T(8,128)(2,1)S(1)}, bf16[768,768]{1,0:T(8,128)(2,1)S(1)}, f32[1,768]{1,0:T(1,128)S(1)}, f32[512,768]{1,0:T(8,128)S(1)}) custom-call(bf16[512,768]{1,0:T(8,128)(2,1)S(1)} %convert_element_type.534.dz_ref, bf16[512,768]{1,0:T(8,128)(2,1)S(1)} %copy-done.7, bf16[512,768]{1,0:T(8,128)(2,1)S(1)} %copy-done.81, ...), custom_call_target="tpu_custom_call" | custom-call | flops 1048576 | bytes 1024 | tf_op jit(solution)/shard_map/ffn_backward/pallas_call | solution.py:254
  267.3 8.2 %ffn_backward.10 = (bf16[768,768]{1,0:T(8,128)(2,1)S(1)}, bf16[768,768]{1,0:T(8,128)(2,1)S(1)}, f32[1,768]{1,0:T(1,128)S(1)}, f32[512,768]{1,0:T(8,128)S(1)}) custom-call(bf16[512,768]{1,0:T(8,128)(2,1)S(1)} %convert_element_type.534.dz_ref, bf16[512,768]{1,0:T(8,128)(2,1)S(1)} %copy-done.7, bf16[512,768]{1,0:T(8,128)(2,1)S(1)} %copy-done.42, ...), custom_call_target="tpu_custom_call" | custom-call | flops 1048576 | bytes 1024 | tf_op jit(solution)/shard_map/ffn_backward/pallas_call | solution.py:254
  277.6 6.5 ffn_backward.11
  304.4 9.5 %attend_backward.8 = (bf16[384,768]{1,0:T(8,128)(2,1)S(1)}, bf16[384,768]{1,0:T(8,128)(2,1)S(1)}, f32[1,384]{1,0:T(1,128)S(1)}, f32[512,768]{1,0:T(8,128)S(1)}) custom-call(bf16[512,768]{1,0:T(8,128)(2,1)S(1)} %convert_element_type.559.da_ref, bf16[512,768]{1,0:T(8,128)(2,1)S(1)} %get-tuple-element.516.refs_0_.x_ref, ...), custom_call_target="tpu_custom_call" | custom-call | flops 1048576 | bytes 1024 | tf_op jit(solution)/shard_map/attend_backward/pallas_call | solution.py:291
  314.8 9.9 %attend_backward.9 = (bf16[384,768]{1,0:T(8,128)(2,1)S(1)}, bf16[384,768]{1,0:T(8,128)(2,1)S(1)}, f32[1,384]{1,0:T(1,128)S(1)}, f32[512,768]{1,0:T(8,128)S(1)}) custom-call(bf16[512,768]{1,0:T(8,128)(2,1)S(1)} %convert_element_type.559.da_ref, bf16[512,768]{1,0:T(8,128)(2,1)S(1)} %get-tuple-element.516.refs_0_.x_ref, ...), custom_call_target="tpu_custom_call" | custom-call | flops 1048576 | bytes 1024 | tf_op jit(solution)/shard_map/attend_backward/pallas_call | solution.py:291
  326.9 10.3 %attend_backward.10 = (bf16[384,768]{1,0:T(8,128)(2,1)}, bf16[384,768]{1,0:T(8,128)(2,1)}, f32[1,384]{1,0:T(1,128)S(1)}, f32[512,768]{1,0:T(8,128)S(1)}) custom-call(bf16[512,768]{1,0:T(8,128)(2,1)S(1)} %convert_element_type.559.da_ref, bf16[512,768]{1,0:T(8,128)(2,1)S(1)} %get-tuple-element.516.refs_0_.x_ref, ...), custom_call_target="tpu_custom_call" | custom-call | flops 1048576 | bytes 1024 | tf_op jit(solution)/shard_map/attend_backward/pallas_call | solution.py:291
  339.2 8.1 %attend_backward.11 = (bf16[384,768]{1,0:T(8,128)(2,1)S(1)}, bf16[384,768]{1,0:T(8,128)(2,1)S(1)}, f32[1,384]{1,0:T(1,128)S(1)}, f32[512,768]{1,0:T(8,128)S(1)}) custom-call(bf16[512,768]{1,0:T(8,128)(2,1)S(1)} %convert_element_type.559.da_ref, bf16[512,768]{1,0:T(8,128)(2,1)S(1)} %get-tuple-element.516.refs_0_.x_ref, bf16[384,768]{1,0:T(8,128)(2,1)S(1)} %copy-done.30, ...), custom_call_target="tpu_custom_call" | custom-call | flops 1048576 | bytes 1024 | tf_op jit(solution)/shard_map/attend_backward/pallas_call | solution.py:291
  353.3 4.2 all-to-all-start.5
  365.1 6.7 collective-permute-done.29
  376.1 4.8 multiply_reduce_fusion.2
  388.0 4.2 all-to-all-start.6
  397.1 8.2 %ffn_backward.12 = (bf16[768,768]{1,0:T(8,128)(2,1)S(1)}, bf16[768,768]{1,0:T(8,128)(2,1)S(1)}, f32[1,768]{1,0:T(1,128)S(1)}, f32[512,768]{1,0:T(8,128)S(1)}) custom-call(bf16[512,768]{1,0:T(8,128)(2,1)S(1)} %copy-done.8, bf16[512,768]{1,0:T(8,128)(2,1)S(1)} %copy-done.4, bf16[512,768]{1,0:T(8,128)(2,1)S(1)} %copy-done.71, bf16[512,768]{1,0:T(8,128)(2,1)S(1)} %copy-done.69, ...), custom_call_target="tpu_custom_call" | custom-call | flops 1048576 | bytes 1024 | tf_op jit(solution)/shard_map/ffn_backward/pallas_call | solution.py:254
  407.5 8.2 %ffn_backward.13 = (bf16[768,768]{1,0:T(8,128)(2,1)S(1)}, bf16[768,768]{1,0:T(8,128)(2,1)S(1)}, f32[1,768]{1,0:T(1,128)S(1)}, f32[512,768]{1,0:T(8,128)S(1)}) custom-call(bf16[512,768]{1,0:T(8,128)(2,1)S(1)} %copy-done.8, bf16[512,768]{1,0:T(8,128)(2,1)S(1)} %copy-done.4, bf16[512,768]{1,0:T(8,128)(2,1)S(1)} %copy-done.40, bf16[512,768]{1,0:T(8,128)(2,1)S(1)} %copy-done.68, ...), custom_call_target="tpu_custom_call" | custom-call | flops 1048576 | bytes 1024 | tf_op jit(solution)/shard_map/ffn_backward/pallas_call | solution.py:254
  417.8 8.3 %ffn_backward.14 = (bf16[768,768]{1,0:T(8,128)(2,1)S(1)}, bf16[768,768]{1,0:T(8,128)(2,1)S(1)}, f32[1,768]{1,0:T(1,128)S(1)}, f32[512,768]{1,0:T(8,128)S(1)}) custom-call(bf16[512,768]{1,0:T(8,128)(2,1)S(1)} %copy-done.8, bf16[512,768]{1,0:T(8,128)(2,1)S(1)} %copy-done.4, bf16[512,768]{1,0:T(8,128)(2,1)S(1)} %copy-done.74, bf16[512,768]{1,0:T(8,128)(2,1)S(1)} %copy-done.72, ...), custom_call_target="tpu_custom_call" | custom-call | flops 1048576 | bytes 1024 | tf_op jit(solution)/shard_map/ffn_backward/pallas_call | solution.py:254
  431.6 6.5 ffn_backward.15
  460.6 8.3 %attend_backward.12 = (bf16[384,768]{1,0:T(8,128)(2,1)S(1)}, bf16[384,768]{1,0:T(8,128)(2,1)S(1)}, f32[1,384]{1,0:T(1,128)S(1)}, f32[512,768]{1,0:T(8,128)S(1)}) custom-call(bf16[512,768]{1,0:T(8,128)(2,1)S(1)} %convert_element_type.604.da_ref, bf16[512,768]{1,0:T(8,128)(2,1)S(1)} %bitcast.171, bf16[400,768]{1,0:T(8,128)(2,1)S(1)} %copy-done.18, ...), custom_call_target="tpu_custom_call" | custom-call | flops 1048576 | bytes 1024 | tf_op jit(solution)/shard_map/attend_backward/pallas_call | solution.py:291
  469.9 8.2 %attend_backward.13 = (bf16[384,768]{1,0:T(8,128)(2,1)S(1)}, bf16[384,768]{1,0:T(8,128)(2,1)S(1)}, f32[1,384]{1,0:T(1,128)S(1)}, f32[512,768]{1,0:T(8,128)S(1)}) custom-call(bf16[512,768]{1,0:T(8,128)(2,1)S(1)} %convert_element_type.604.da_ref, bf16[512,768]{1,0:T(8,128)(2,1)S(1)} %bitcast.172, bf16[400,768]{1,0:T(8,128)(2,1)S(1)} %copy-done.16, ...), custom_call_target="tpu_custom_call" | custom-call | flops 1048576 | bytes 1024 | tf_op jit(solution)/shard_map/attend_backward/pallas_call | solution.py:291
  480.3 9.0 %attend_backward.14 = (bf16[384,768]{1,0:T(8,128)(2,1)}, bf16[384,768]{1,0:T(8,128)(2,1)}, f32[1,384]{1,0:T(1,128)S(1)}, f32[512,768]{1,0:T(8,128)S(1)}) custom-call(bf16[512,768]{1,0:T(8,128)(2,1)S(1)} %convert_element_type.604.da_ref, bf16[512,768]{1,0:T(8,128)(2,1)S(1)} %bitcast.173, bf16[400,768]{1,0:T(8,128)(2,1)S(1)} %copy-done.44, ...), custom_call_target="tpu_custom_call" | custom-call | flops 1048576 | bytes 1024 | tf_op jit(solution)/shard_map/attend_backward/pallas_call | solution.py:291
  491.5 8.4 %attend_backward.15 = (bf16[384,768]{1,0:T(8,128)(2,1)S(1)}, bf16[384,768]{1,0:T(8,128)(2,1)S(1)}, f32[1,384]{1,0:T(1,128)S(1)}, f32[512,768]{1,0:T(8,128)S(1)}) custom-call(bf16[512,768]{1,0:T(8,128)(2,1)S(1)} %convert_element_type.604.da_ref, bf16[512,768]{1,0:T(8,128)(2,1)S(1)} %bitcast.174, bf16[400,768]{1,0:T(8,128)(2,1)S(1)} %copy-done.20, ...), custom_call_target="tpu_custom_call" | custom-call | flops 1048576 | bytes 1024 | tf_op jit(solution)/shard_map/attend_backward/pallas_call | solution.py:291
  512.5 6.7 collective-permute-done.45
  520.7 20.4 %all-reduce.9.cloned.1.call-done = bf16[384,768]{1,0:T(8,128)(2,1)} async-done(((bf16[384,768]{1,0:T(8,128)(2,1)}), bf16[384,768]{1,0:T(8,128)(2,1)}) %all-reduce.9.cloned.1.call-update) | async-done | bytes 589840 | tf_op jit(solution)/shard_map/psum | solution.py:762
  542.1 3.6 all-to-all-start.7
  555.2 22.5 %total_over_all.1 = f32[8,4,768]{2,1,0:T(4,128)} custom-call(f32[8,4,768]{2,1,0:T(4,128)} %select_add_fusion.rows_ref, f32[1,768]{1,0:T(1,128)} %copy-done.184, f32[1,768]{1,0:T(1,128)} %copy-done.185, f32[1,768]{1,0:T(1,128)} %copy-done.186, f32[1,768]{1,0:T(1,128)} %copy-done.187, f32[1,384]{1,0:T(1,128)} %copy-done.192, f32[1,384]{1,0:T(1,128)} %copy-done.193, ...), custom_call_target="tpu_custom_call" | custom-call | tf_op jit(solution)/shard_map/total_over_all/pallas_call | solution.py:469
  583.1 4.8 collective-permute-done.53
  589.2 21.4 %all-reduce.11.cloned.1.call-done = bf16[768,768]{1,0:T(8,128)(2,1)} async-done(((bf16[768,768]{1,0:T(8,128)(2,1)}), bf16[768,768]{1,0:T(8,128)(2,1)}) %all-reduce.11.cloned.1.call-update) | async-done | bytes 1179664 | tf_op jit(solution)/shard_map/psum | solution.py:769
  611.9 40.7 %all-reduce.13.cloned.1.call-done = bf16[384,768]{1,0:T(8,128)(2,1)} async-done(((bf16[384,768]{1,0:T(8,128)(2,1)}), bf16[384,768]{1,0:T(8,128)(2,1)}) %all-reduce.13.cloned.1.call-update) | async-done | bytes 589840 | tf_op jit(solution)/shard_map/psum | solution.py:783
  (807 shorter events, 268.3 us)
Async XLA Ops:
  7.2 19.4 %all-to-all-start = ((bf16[4,128,768]{2,1,0:T(8,128)(2,1)}), bf16[4,128,768]{2,1,0:T(8,128)(2,1)S(1)}, u32[]{:S(2)}, u32[]{:S(2)}) async-start(bf16[4,128,768]{2,1,0:T(8,128)(2,1)} %bitcast.182), calls=%async_computation | async-start | bytes 1572864 | tf_op jit(solution)/shard_map/all_to_all | solution.py:486
  16.0 18.6 %collective-permute-start = (bf16[400,768]{1,0:T(8,128)(2,1)S(1)}, bf16[400,768]{1,0:T(8,128)(2,1)S(1)}, u32[]{:S(2)}, u32[]{:S(2)}) collective-permute-start(bf16[400,768]{1,0:T(8,128)(2,1)S(1)} %pad_maximum_fusion.2.refs_1_.first_ref), channel_id=1, source_target_pairs={{0,1},{1,0},{2,3},{3,2},{4,6},{5,7},{6,4},{7,5},{8,9},{9,8},{10,11... | collective-permute-start | bytes 1843208 | tf_op jit(solution)/shard_map/ppermute | solution.py:62
  18.1 18.3 %collective-permute-start.1 = (bf16[400,768]{1,0:T(8,128)(2,1)S(1)}, bf16[400,768]{1,0:T(8,128)(2,1)S(1)}, u32[]{:S(2)}, u32[]{:S(2)}) collective-permute-start(bf16[400,768]{1,0:T(8,128)(2,1)S(1)} %fusion.54.refs_2_.second_ref), channel_id=1, source_target_pairs={{0,1},{1,0},{2,3},{3,2},{4,6},{5,7},{6,4},{7,5},{8,9},{9,8},{10,11... | collective-permute-start | bytes 1843208 | tf_op jit(solution)/shard_map/ppermute | solution.py:62
  20.4 45.6 %collective-permute-start.6 = (bf16[768,768]{1,0:T(8,128)(2,1)}, bf16[768,768]{1,0:T(8,128)(2,1)}, u32[]{:S(2)}, u32[]{:S(2)}) collective-permute-start(bf16[768,768]{1,0:T(8,128)(2,1)} %get-tuple-element.249.first_ref), channel_id=1, source_target_pairs={{0,1},{1,0},{2,3},{3,2},{4,6},{5,7},{6,4},{7,5},{8,9},{9,8},{10,11... | collective-permute-start | bytes 3538952 | tf_op jit(solution)/shard_map/ppermute | solution.py:62
  22.4 45.9 %collective-permute-start.7 = (bf16[768,768]{1,0:T(8,128)(2,1)}, bf16[768,768]{1,0:T(8,128)(2,1)}, u32[]{:S(2)}, u32[]{:S(2)}) collective-permute-start(bf16[768,768]{1,0:T(8,128)(2,1)} %get-tuple-element.250.second_ref), channel_id=1, source_target_pairs={{0,1},{1,0},{2,3},{3,2},{4,6},{5,7},{6,4},{7,5},{8,9},{9,8},{10,11... | collective-permute-start | bytes 3538952 | tf_op jit(solution)/shard_map/ppermute | solution.py:62
  36.4 13.8 %collective-permute-start.2 = (bf16[400,768]{1,0:T(8,128)(2,1)S(1)}, bf16[400,768]{1,0:T(8,128)(2,1)S(1)}, u32[]{:S(2)}, u32[]{:S(2)}) collective-permute-start(bf16[400,768]{1,0:T(8,128)(2,1)S(1)} %collective-permute-done.refs_1_.first_ref), channel_id=1, source_target_pairs={{0,4},{1,5},{2,6},{3,7},{4,0},{5,1},{6,2},{7,3},{8,12},{9,13},{10,... | collective-permute-start | bytes 1843208 | tf_op jit(solution)/shard_map/ppermute | solution.py:62
  36.5 13.8 %collective-permute-start.3 = (bf16[400,768]{1,0:T(8,128)(2,1)S(1)}, bf16[400,768]{1,0:T(8,128)(2,1)S(1)}, u32[]{:S(2)}, u32[]{:S(2)}) collective-permute-start(bf16[400,768]{1,0:T(8,128)(2,1)S(1)} %collective-permute-done.1.refs_2_.second_ref), channel_id=1, source_target_pairs={{0,4},{1,5},{2,6},{3,7},{4,0},{5,1},{6,2},{7,3},{8,12},{9,13},{10,... | collective-permute-start | bytes 1843208 | tf_op jit(solution)/shard_map/ppermute | solution.py:62
  37.0 19.8 %collective-permute-start.4 = (bf16[400,768]{1,0:T(8,128)(2,1)S(1)}, bf16[400,768]{1,0:T(8,128)(2,1)S(1)}, u32[]{:S(2)}, u32[]{:S(2)}) collective-permute-start(bf16[400,768]{1,0:T(8,128)(2,1)S(1)} %broadcast_select_fusion.8), channel_id=1, source_target_pairs={{0,2},{1,3},{2,0},{3,1},{4,5},{5,4},{6,7},{7,6},{8,10},{9,11},{10,... | collective-permute-start | bytes 1843208 | tf_op jit(solution)/shard_map/ppermute | solution.py:62
  57.0 29.2 %collective-permute-start.8 = (bf16[384,768]{1,0:T(8,128)(2,1)}, bf16[384,768]{1,0:T(8,128)(2,1)}, u32[]{:S(2)}, u32[]{:S(2)}) collective-permute-start(bf16[384,768]{1,0:T(8,128)(2,1)} %bitcast.16.refs_1_.first_ref), channel_id=1, source_target_pairs={{0,1},{1,0},{2,3},{3,2},{4,6},{5,7},{6,4},{7,5},{8,9},{9,8},{10,11... | collective-permute-start | bytes 1769480 | tf_op jit(solution)/shard_map/ppermute | solution.py:62
  57.7 28.8 %collective-permute-start.9 = (bf16[384,768]{1,0:T(8,128)(2,1)}, bf16[384,768]{1,0:T(8,128)(2,1)}, u32[]{:S(2)}, u32[]{:S(2)}) collective-permute-start(bf16[384,768]{1,0:T(8,128)(2,1)} %pad_maximum_fusion.3.refs_2_.second_ref), channel_id=1, source_target_pairs={{0,1},{1,0},{2,3},{3,2},{4,6},{5,7},{6,4},{7,5},{8,9},{9,8},{10,11... | collective-permute-start | bytes 1769480 | tf_op jit(solution)/shard_map/ppermute | solution.py:62
  68.4 18.1 %collective-permute-start.10 = (bf16[768,768]{1,0:T(8,128)(2,1)}, bf16[768,768]{1,0:T(8,128)(2,1)}, u32[]{:S(2)}, u32[]{:S(2)}) collective-permute-start(bf16[768,768]{1,0:T(8,128)(2,1)} %collective-permute-done.6.first_ref), channel_id=1, source_target_pairs={{0,4},{1,5},{2,6},{3,7},{4,0},{5,1},{6,2},{7,3},{8,12},{9,13},{10,... | collective-permute-start | bytes 3538952 | tf_op jit(solution)/shard_map/ppermute | solution.py:62
  68.4 21.4 %collective-permute-start.11 = (bf16[768,768]{1,0:T(8,128)(2,1)}, bf16[768,768]{1,0:T(8,128)(2,1)}, u32[]{:S(2)}, u32[]{:S(2)}) collective-permute-start(bf16[768,768]{1,0:T(8,128)(2,1)} %collective-permute-done.7.second_ref), channel_id=1, source_target_pairs={{0,4},{1,5},{2,6},{3,7},{4,0},{5,1},{6,2},{7,3},{8,12},{9,13},{10,... | collective-permute-start | bytes 3538952 | tf_op jit(solution)/shard_map/ppermute | solution.py:62
  72.7 21.4 %collective-permute-start.12 = (bf16[768,768]{1,0:T(8,128)(2,1)S(1)}, bf16[768,768]{1,0:T(8,128)(2,1)}, u32[]{:S(2)}, u32[]{:S(2)}) collective-permute-start(bf16[768,768]{1,0:T(8,128)(2,1)S(1)} %copy-done.225), channel_id=1, source_target_pairs={{0,2},{1,3},{2,0},{3,1},{4,5},{5,4},{6,7},{7,6},{8,10},{9,11},{10,... | collective-permute-start | bytes 3538952 | tf_op jit(solution)/shard_map/ppermute | solution.py:62
  94.9 18.9 %all-to-all-start.1 = ((bf16[4,128,768]{2,1,0:T(8,128)(2,1)}), bf16[4,128,768]{2,1,0:T(8,128)(2,1)}, u32[]{:S(2)}, u32[]{:S(2)}) async-start(bf16[4,128,768]{2,1,0:T(8,128)(2,1)} %bitcast.183), calls=%async_computation.1 | async-start | bytes 1572864 | tf_op jit(solution)/shard_map/all_to_all | solution.py:486
  99.1 47.3 %collective-permute-start.14 = (bf16[384,768]{1,0:T(8,128)(2,1)}, bf16[384,768]{1,0:T(8,128)(2,1)}, u32[]{:S(2)}, u32[]{:S(2)}) collective-permute-start(bf16[384,768]{1,0:T(8,128)(2,1)} %collective-permute-done.8.refs_1_.first_ref), channel_id=1, source_target_pairs={{0,4},{1,5},{2,6},{3,7},{4,0},{5,1},{6,2},{7,3},{8,12},{9,13},{10,... | collective-permute-start | bytes 1769480 | tf_op jit(solution)/shard_map/ppermute | solution.py:62
  99.6 46.8 %collective-permute-start.15 = (bf16[384,768]{1,0:T(8,128)(2,1)}, bf16[384,768]{1,0:T(8,128)(2,1)}, u32[]{:S(2)}, u32[]{:S(2)}) collective-permute-start(bf16[384,768]{1,0:T(8,128)(2,1)} %collective-permute-done.9.refs_2_.second_ref), channel_id=1, source_target_pairs={{0,4},{1,5},{2,6},{3,7},{4,0},{5,1},{6,2},{7,3},{8,12},{9,13},{10,... | collective-permute-start | bytes 1769480 | tf_op jit(solution)/shard_map/ppermute | solution.py:62
  101.7 44.7 %collective-permute-start.16 = (bf16[384,768]{1,0:T(8,128)(2,1)}, bf16[384,768]{1,0:T(8,128)(2,1)}, u32[]{:S(2)}, u32[]{:S(2)}) collective-permute-start(bf16[384,768]{1,0:T(8,128)(2,1)} %broadcast_select_fusion.11), channel_id=1, source_target_pairs={{0,2},{1,3},{2,0},{3,1},{4,5},{5,4},{6,7},{7,6},{8,10},{9,11},{10,... | collective-permute-start | bytes 1769480 | tf_op jit(solution)/shard_map/ppermute | solution.py:62
  103.5 68.0 %collective-permute-start.18 = (bf16[768,768]{1,0:T(8,128)(2,1)}, bf16[768,768]{1,0:T(8,128)(2,1)}, u32[]{:S(2)}, u32[]{:S(2)}) collective-permute-start(bf16[768,768]{1,0:T(8,128)(2,1)} %get-tuple-element.274.first_ref), channel_id=1, source_target_pairs={{0,1},{1,0},{2,3},{3,2},{4,6},{5,7},{6,4},{7,5},{8,9},{9,8},{10,11... | collective-permute-start | bytes 3538952 | tf_op jit(solution)/shard_map/ppermute | solution.py:62
  105.8 65.7 %collective-permute-start.19 = (bf16[768,768]{1,0:T(8,128)(2,1)}, bf16[768,768]{1,0:T(8,128)(2,1)}, u32[]{:S(2)}, u32[]{:S(2)}) collective-permute-start(bf16[768,768]{1,0:T(8,128)(2,1)} %get-tuple-element.275.second_ref), channel_id=1, source_target_pairs={{0,1},{1,0},{2,3},{3,2},{4,6},{5,7},{6,4},{7,5},{8,9},{9,8},{10,11... | collective-permute-start | bytes 3538952 | tf_op jit(solution)/shard_map/ppermute | solution.py:62
  129.2 29.5 %all-to-all-start.2 = ((bf16[4,128,768]{2,1,0:T(8,128)(2,1)}), bf16[4,128,768]{2,1,0:T(8,128)(2,1)}, u32[]{:S(2)}, u32[]{:S(2)}) async-start(bf16[4,128,768]{2,1,0:T(8,128)(2,1)} %bitcast.178), calls=%async_computation.2 | async-start | bytes 1572864 | tf_op jit(solution)/shard_map/all_to_all | solution.py:493
  171.5 20.6 %collective-permute-start.20 = (bf16[768,768]{1,0:T(8,128)(2,1)}, bf16[768,768]{1,0:T(8,128)(2,1)}, u32[]{:S(2)}, u32[]{:S(2)}) collective-permute-start(bf16[768,768]{1,0:T(8,128)(2,1)} %collective-permute-done.18.first_ref), channel_id=1, source_target_pairs={{0,4},{1,5},{2,6},{3,7},{4,0},{5,1},{6,2},{7,3},{8,12},{9,13},{10,... | collective-permute-start | bytes 3538952 | tf_op jit(solution)/shard_map/ppermute | solution.py:62
  172.0 23.5 %collective-permute-start.21 = (bf16[768,768]{1,0:T(8,128)(2,1)}, bf16[768,768]{1,0:T(8,128)(2,1)}, u32[]{:S(2)}, u32[]{:S(2)}) collective-permute-start(bf16[768,768]{1,0:T(8,128)(2,1)} %collective-permute-done.19.second_ref), channel_id=1, source_target_pairs={{0,4},{1,5},{2,6},{3,7},{4,0},{5,1},{6,2},{7,3},{8,12},{9,13},{10,... | collective-permute-start | bytes 3538952 | tf_op jit(solution)/shard_map/ppermute | solution.py:62
  178.0 21.1 %collective-permute-start.22 = (bf16[768,768]{1,0:T(8,128)(2,1)}, bf16[768,768]{1,0:T(8,128)(2,1)}, u32[]{:S(2)}, u32[]{:S(2)}) collective-permute-start(bf16[768,768]{1,0:T(8,128)(2,1)} %broadcast_select_fusion.2), channel_id=1, source_target_pairs={{0,2},{1,3},{2,0},{3,1},{4,5},{5,4},{6,7},{7,6},{8,10},{9,11},{10,... | collective-permute-start | bytes 3538952 | tf_op jit(solution)/shard_map/ppermute | solution.py:62
  199.1 30.0 %collective-permute-start.23 = (bf16[768,768]{1,0:T(8,128)(2,1)}, bf16[768,768]{1,0:T(8,128)(2,1)}, u32[]{:S(2)}, u32[]{:S(2)}) collective-permute-start(bf16[768,768]{1,0:T(8,128)(2,1)} %collective-permute-done.22), channel_id=1, source_target_pairs={{0,4},{1,5},{2,6},{3,7},{4,0},{5,1},{6,2},{7,3},{8,12},{9,13},{10,... | collective-permute-start | bytes 3538952 | tf_op jit(solution)/shard_map/ppermute | solution.py:62
  199.3 28.2 %all-to-all-start.3 = ((bf16[4,128,768]{2,1,0:T(8,128)(2,1)}), bf16[4,128,768]{2,1,0:T(8,128)(2,1)}, u32[]{:S(2)}, u32[]{:S(2)}) async-start(bf16[4,128,768]{2,1,0:T(8,128)(2,1)} %bitcast.184), calls=%async_computation.3 | async-start | bytes 1572864 | tf_op jit(solution)/shard_map/all_to_all | solution.py:486
  238.5 48.8 %all-to-all-start.4 = ((bf16[4,128,768]{2,1,0:T(8,128)(2,1)}), bf16[4,128,768]{2,1,0:T(8,128)(2,1)}, u32[]{:S(2)}, u32[]{:S(2)}) async-start(bf16[4,128,768]{2,1,0:T(8,128)(2,1)} %bitcast.177), calls=%async_computation.4 | async-start | bytes 1572864 | tf_op jit(solution)/shard_map/all_to_all | solution.py:493
  298.9 38.4 %collective-permute-start.28 = (bf16[768,768]{1,0:T(8,128)(2,1)S(1)}, bf16[768,768]{1,0:T(8,128)(2,1)S(1)}, u32[]{:S(2)}, u32[]{:S(2)}) collective-permute-start(bf16[768,768]{1,0:T(8,128)(2,1)S(1)} %add_convert_fusion.9), channel_id=1, source_target_pairs={{0,2},{1,3},{2,0},{3,1},{4,5},{5,4},{6,7},{7,6},{8,10},{9,11},{10,... | collective-permute-start | bytes 3538952 | tf_op jit(solution)/shard_map/ppermute | solution.py:62
  301.4 50.2 %collective-permute-start.30 = (bf16[768,768]{1,0:T(8,128)(2,1)}, bf16[768,768]{1,0:T(8,128)(2,1)}, u32[]{:S(2)}, u32[]{:S(2)}) collective-permute-start(bf16[768,768]{1,0:T(8,128)(2,1)} %add_convert_fusion.11), channel_id=1, source_target_pairs={{0,1},{1,0},{2,3},{3,2},{4,6},{5,7},{6,4},{7,5},{8,9},{9,8},{10,11... | collective-permute-start | bytes 3538952 | tf_op jit(solution)/shard_map/ppermute | solution.py:62
  351.0 20.8 %collective-permute-start.29 = (bf16[768,768]{1,0:T(8,128)(2,1)}, bf16[768,768]{1,0:T(8,128)(2,1)}, u32[]{:S(2)}, u32[]{:S(2)}) collective-permute-start(bf16[768,768]{1,0:T(8,128)(2,1)} %add_convert_fusion.7), channel_id=1, source_target_pairs={{0,1},{1,0},{2,3},{3,2},{4,6},{5,7},{6,4},{7,5},{8,9},{9,8},{10,11... | collective-permute-start | bytes 3538952 | tf_op jit(solution)/shard_map/ppermute | solution.py:62
  351.6 13.5 %collective-permute-start.31 = (bf16[768,768]{1,0:T(8,128)(2,1)}, bf16[768,768]{1,0:T(8,128)(2,1)}, u32[]{:S(2)}, u32[]{:S(2)}) collective-permute-start(bf16[768,768]{1,0:T(8,128)(2,1)} %collective-permute-done.30), channel_id=1, source_target_pairs={{0,4},{1,5},{2,6},{3,7},{4,0},{5,1},{6,2},{7,3},{8,12},{9,13},{10,... | collective-permute-start | bytes 3538952 | tf_op jit(solution)/shard_map/ppermute | solution.py:62
  353.3 22.7 %all-to-all-start.5 = ((bf16[4,128,768]{2,1,0:T(8,128)(2,1)}), bf16[4,128,768]{2,1,0:T(8,128)(2,1)}, u32[]{:S(2)}, u32[]{:S(2)}) async-start(bf16[4,128,768]{2,1,0:T(8,128)(2,1)} %bitcast.185), calls=%async_computation.5 | async-start | bytes 1572864 | tf_op jit(solution)/shard_map/all_to_all | solution.py:486
  357.5 87.2 %all-reduce.7.cloned.1.call-start = ((), (), s32[]{:S(2)}) async-start(), calls=%async_computation.8 | async-start | bytes 2359296 | tf_op jit(solution)/shard_map/psum | solution.py:740
  382.5 44.6 %collective-permute-start.36 = (bf16[384,768]{1,0:T(8,128)(2,1)}, bf16[384,768]{1,0:T(8,128)(2,1)}, u32[]{:S(2)}, u32[]{:S(2)}) collective-permute-start(bf16[384,768]{1,0:T(8,128)(2,1)} %add_convert_fusion.21), channel_id=1, source_target_pairs={{0,2},{1,3},{2,0},{3,1},{4,5},{5,4},{6,7},{7,6},{8,10},{9,11},{10,... | collective-permute-start | bytes 1769480 | tf_op jit(solution)/shard_map/ppermute | solution.py:62
  383.1 46.6 %collective-permute-start.38 = (bf16[384,768]{1,0:T(8,128)(2,1)}, bf16[384,768]{1,0:T(8,128)(2,1)}, u32[]{:S(2)}, u32[]{:S(2)}) collective-permute-start(bf16[384,768]{1,0:T(8,128)(2,1)} %add_convert_fusion.23), channel_id=1, source_target_pairs={{0,1},{1,0},{2,3},{3,2},{4,6},{5,7},{6,4},{7,5},{8,9},{9,8},{10,11... | collective-permute-start | bytes 1769480 | tf_op jit(solution)/shard_map/ppermute | solution.py:62
  388.0 53.2 %all-to-all-start.6 = ((bf16[4,128,768]{2,1,0:T(8,128)(2,1)}), bf16[4,128,768]{2,1,0:T(8,128)(2,1)}, u32[]{:S(2)}, u32[]{:S(2)}) async-start(bf16[4,128,768]{2,1,0:T(8,128)(2,1)} %bitcast.175), calls=%async_computation.6 | async-start | bytes 1572864 | tf_op jit(solution)/shard_map/all_to_all | solution.py:493
  392.2 148.9 %all-reduce.9.cloned.1.call-start = ((), (), s32[]{:S(2)}) async-start(), calls=%async_computation.9 | async-start | bytes 1179648 | tf_op jit(solution)/shard_map/psum | solution.py:762
  429.6 12.6 %collective-permute-start.37 = (bf16[384,768]{1,0:T(8,128)(2,1)}, bf16[384,768]{1,0:T(8,128)(2,1)}, u32[]{:S(2)}, u32[]{:S(2)}) collective-permute-start(bf16[384,768]{1,0:T(8,128)(2,1)} %add_convert_fusion.19), channel_id=1, source_target_pairs={{0,1},{1,0},{2,3},{3,2},{4,6},{5,7},{6,4},{7,5},{8,9},{9,8},{10,11... | collective-permute-start | bytes 1769480 | tf_op jit(solution)/shard_map/ppermute | solution.py:62
  442.0 12.5 %collective-permute-start.43 = (bf16[768,768]{1,0:T(8,128)(2,1)}, bf16[768,768]{1,0:T(8,128)(2,1)}, u32[]{:S(2)}, u32[]{:S(2)}) collective-permute-start(bf16[768,768]{1,0:T(8,128)(2,1)} %copy-done.196), channel_id=1, source_target_pairs={{0,4},{1,5},{2,6},{3,7},{4,0},{5,1},{6,2},{7,3},{8,12},{9,13},{10,... | collective-permute-start | bytes 3538952 | tf_op jit(solution)/shard_map/ppermute | solution.py:62
  457.1 32.3 %collective-permute-start.44 = (bf16[768,768]{1,0:T(8,128)(2,1)S(1)}, bf16[768,768]{1,0:T(8,128)(2,1)S(1)}, u32[]{:S(2)}, u32[]{:S(2)}) collective-permute-start(bf16[768,768]{1,0:T(8,128)(2,1)S(1)} %add_convert_fusion.3), channel_id=1, source_target_pairs={{0,2},{1,3},{2,0},{3,1},{4,5},{5,4},{6,7},{7,6},{8,10},{9,11},{10,... | collective-permute-start | bytes 3538952 | tf_op jit(solution)/shard_map/ppermute | solution.py:62
  458.7 45.6 %collective-permute-start.46 = (bf16[768,768]{1,0:T(8,128)(2,1)}, bf16[768,768]{1,0:T(8,128)(2,1)}, u32[]{:S(2)}, u32[]{:S(2)}) collective-permute-start(bf16[768,768]{1,0:T(8,128)(2,1)} %add_convert_fusion.5), channel_id=1, source_target_pairs={{0,1},{1,0},{2,3},{3,2},{4,6},{5,7},{6,4},{7,5},{8,9},{9,8},{10,11... | collective-permute-start | bytes 3538952 | tf_op jit(solution)/shard_map/ppermute | solution.py:62
  502.7 16.5 %collective-permute-start.45 = (bf16[768,768]{1,0:T(8,128)(2,1)}, bf16[768,768]{1,0:T(8,128)(2,1)S(1)}, u32[]{:S(2)}, u32[]{:S(2)}) collective-permute-start(bf16[768,768]{1,0:T(8,128)(2,1)} %add_convert_fusion.1), channel_id=1, source_target_pairs={{0,1},{1,0},{2,3},{3,2},{4,6},{5,7},{6,4},{7,5},{8,9},{9,8},{10,11... | collective-permute-start | bytes 3538952 | tf_op jit(solution)/shard_map/ppermute | solution.py:62
  508.0 43.9 %collective-permute-start.59 = (bf16[768,768]{1,0:T(8,128)(2,1)}, bf16[768,768]{1,0:T(8,128)(2,1)}, u32[]{:S(2)}, u32[]{:S(2)}) collective-permute-start(bf16[768,768]{1,0:T(8,128)(2,1)} %all-reduce.7.cloned.1.call-done), channel_id=1, source_target_pairs={{0,4},{1,5},{2,6},{3,7},{4,0},{5,1},{6,2},{7,3},{8,12},{9,13},{10,... | collective-permute-start | bytes 3538952 | tf_op jit(solution)/shard_map/ppermute | solution.py:62
  542.1 35.7 %all-to-all-start.7 = ((bf16[4,128,768]{2,1,0:T(8,128)(2,1)}), bf16[4,128,768]{2,1,0:T(8,128)(2,1)S(1)}, u32[]{:S(2)}, u32[]{:S(2)}) async-start(bf16[4,128,768]{2,1,0:T(8,128)(2,1)} %bitcast.41), calls=%async_computation.7 | async-start | bytes 1572864 | tf_op jit(solution)/shard_map/all_to_all | solution.py:493
  545.7 64.9 %all-reduce.11.cloned.1.call-start = ((), (), s32[]{:S(2)}) async-start(), calls=%async_computation.10 | async-start | bytes 2359296 | tf_op jit(solution)/shard_map/psum | solution.py:769
  545.7 32.1 %collective-permute-start.52 = (bf16[384,768]{1,0:T(8,128)(2,1)}, bf16[384,768]{1,0:T(8,128)(2,1)S(1)}, u32[]{:S(2)}, u32[]{:S(2)}) collective-permute-start(bf16[384,768]{1,0:T(8,128)(2,1)} %add_convert_fusion.15), channel_id=1, source_target_pairs={{0,2},{1,3},{2,0},{3,1},{4,5},{5,4},{6,7},{7,6},{8,10},{9,11},{10,... | collective-permute-start | bytes 1769480 | tf_op jit(solution)/shard_map/ppermute | solution.py:62
  550.3 29.1 %collective-permute-start.57 = (bf16[384,768]{1,0:T(8,128)(2,1)}, bf16[384,768]{1,0:T(8,128)(2,1)}, u32[]{:S(2)}, u32[]{:S(2)}) collective-permute-start(bf16[384,768]{1,0:T(8,128)(2,1)} %all-reduce.9.cloned.1.call-done), channel_id=1, source_target_pairs={{0,4},{1,5},{2,6},{3,7},{4,0},{5,1},{6,2},{7,3},{8,12},{9,13},{10,... | collective-permute-start | bytes 1769480 | tf_op jit(solution)/shard_map/ppermute | solution.py:62
  550.4 30.4 %collective-permute-start.54 = (bf16[384,768]{1,0:T(8,128)(2,1)S(1)}, bf16[384,768]{1,0:T(8,128)(2,1)}, u32[]{:S(2)}, u32[]{:S(2)}) collective-permute-start(bf16[384,768]{1,0:T(8,128)(2,1)S(1)} %copy-done.227), channel_id=1, source_target_pairs={{0,1},{1,0},{2,3},{3,2},{4,6},{5,7},{6,4},{7,5},{8,9},{9,8},{10,11... | collective-permute-start | bytes 1769480 | tf_op jit(solution)/shard_map/ppermute | solution.py:62
  555.2 97.4 %all-reduce.13.cloned.1.call-start = ((), (), s32[]{:S(2)}) async-start(), calls=%async_computation.11 | async-start | bytes 1179648 | tf_op jit(solution)/shard_map/psum | solution.py:783
  (269 other events, 1465.4 us)
Sparse Core Ops, SparseCore 0:
  384.6 54.5 all-reduce.6
  502.8 38.2 all-reduce.8
  555.3 55.2 all-reduce.10
  613.4 39.1 all-reduce.12

commit v7 on v6

--- a/solution.py
+++ b/solution.py
@@ -115,9 +115,8 @@
     return plus(main_own, send(across, DIAG))
 
 
-def finish_part(mine, side):
-    other = send(mine, SWAP)
-    return pick(side, mine, other).astype(F32), pick(side, other, mine).astype(F32)
+def in_order(side, own, other):
+    return pick(side, own, other).astype(F32), pick(side, other, own).astype(F32)
 
 
 Q_ROWS = 128
@@ -382,8 +381,20 @@
     return tensor, flip_one + swing, flip_two - swing, TENSORS - 1 - tensor
 
 
-def total_kernel(dps, planes, rows_ref, blocks, out_ref, x_ref, parts, sums, sems):
-    one_send, one_recv, two_send, two_recv, three_send, three_recv = sems
+def remote(src, dst, sems, i, device):
+    return pltpu.make_async_remote_copy(
+        src_ref=src, dst_ref=dst, send_sem=sems.at[0, i], recv_sem=sems.at[1, i],
+        device_id=device, device_id_type=MESH,
+    )
+
+
+def last_kernel(dps, planes, ffn_ref, own, rest, rows_ref, blocks, outs, scratch):
+    ffn_own, ffn_other, attn_own, attn_other, out_ref = outs
+    (
+        swapped, main_rest, main_own, across, mine, got_rest, got_own, got_across, got_peer, total_ref,
+        ffn_parts, attn_parts, x_ref, parts, sums,
+        swap_sems, plane_sems, ffn_one, ffn_two, attn_one, attn_two, one_sems, two_sems, three_sems,
+    ) = scratch
     dp = lax.axis_index("dp")
     side = lax.axis_index("span")
     tensor = lax.axis_index("tensor")
@@ -403,83 +414,148 @@
         peer = near_peer(k)
         return {"span": peer // TENSORS, "tensor": lax.rem(peer, TENSORS)}
 
+    def far_peer(k):
+        return lax.rem(dp + k, dps)
+
     def far(k):
-        return {"dp": lax.rem(dp + k, dps)}
+        return {"dp": far_peer(k)}
+
+    peer_core, main_peer, diag_peer = {"span": 1 - side}, {"tensor": order[1]}, {"tensor": order[2]}
+    nears, fars = range(1, planes), range(1, dps)
 
     barrier = pltpu.get_barrier_semaphore()
-    for k in range(1, planes):
+    for k in nears:
         pl.semaphore_signal(barrier, inc=1, device_id=near(k), device_id_type=MESH)
-    for k in range(1, dps):
+    for k in fars:
         pl.semaphore_signal(barrier, inc=1, device_id=far(k), device_id_type=MESH)
     pl.semaphore_wait(barrier, planes + dps - 2)
 
-    def one(k):
-        return pltpu.make_async_remote_copy(
-            src_ref=x_ref.at[near_peer(k)], dst_ref=parts.at[k], send_sem=one_send.at[k],
-            recv_sem=one_recv.at[k], device_id=near(k), device_id_type=MESH,
-        )
-
-    def two(k):
-        return pltpu.make_async_remote_copy(
-            src_ref=sums.at[dp], dst_ref=sums.at[dp], send_sem=two_send.at[k],
-            recv_sem=two_recv.at[k], device_id=far(k), device_id_type=MESH,
-        )
-
-    def three(k):
-        return pltpu.make_async_remote_copy(
-            src_ref=out_ref.at[me], dst_ref=out_ref.at[me], send_sem=three_send.at[k],
-            recv_sem=three_recv.at[k], device_id=near(k), device_id_type=MESH,
-        )
-
-    for k in range(1, planes):
-        one(k).start()
-    for k in range(1, planes):
-        one(k).wait()
+    swaps = [
+        remote(src, swapped.at[i], swap_sems, i, peer_core)
+        for i, src in enumerate((own[2], rest[2], rest[3], rest[0]))
+    ]
+    for copy in swaps:
+        copy.start()
+    ones = [remote(x_ref.at[near_peer(k)], parts.at[k], one_sems, k, near(k)) for k in nears]
+    for copy in ones:
+        copy.start()
+    ffn_ones = [remote(ffn_ref.at[far_peer(k)], ffn_parts.at[k], ffn_one, k, far(k)) for k in fars]
+    for copy in ffn_ones:
+        copy.start()
+
+    for copy in swaps:
+        copy.wait()
+    across[...] = plus(own[3][...], swapped[2])
+    main_rest[...] = plus(rest[1][...], swapped[0])
+    send_across = remote(across, got_across, plane_sems, 0, diag_peer)
+    send_across.start()
+    send_rest = remote(main_rest, got_rest, plane_sems, 1, main_peer)
+    send_rest.start()
+    mine[...] = plus(own[0][...], swapped[3])
+    for copy in ones:
+        copy.wait()
     total = x_ref[me]
-    for k in range(1, planes):
+    for k in nears:
         total = total + parts[k]
     sums[dp] = total
-    for k in range(1, dps):
-        two(k).start()
-    for k in range(1, dps):
-        two(k).wait()
+    twos = [remote(sums.at[dp], sums.at[dp], two_sems, k, far(k)) for k in fars]
+    for copy in twos:
+        copy.start()
+
+    send_across.wait()
+    main_own[...] = plus(own[1][...], swapped[1], got_across[...])
+    send_own = remote(main_own, got_own, plane_sems, 2, main_peer)
+    send_own.start()
+    send_rest.wait()
+    send_peer = remote(got_rest, got_peer, swap_sems, 4, peer_core)
+    send_peer.start()
+    send_peer.wait()
+    send_own.wait()
+    total_ref[...] = plus(mine[...], got_own[...], got_peer[...])
+    attn_ones = [remote(total_ref.at[far_peer(k)], attn_parts.at[k], attn_one, k, far(k)) for k in fars]
+    for copy in attn_ones:
+        copy.start()
+
+    for copy in ffn_ones:
+        copy.wait()
+    ffn_own[dp] = plus(ffn_ref[dp], *[ffn_parts[k] for k in fars])
+    ffn_twos = [remote(ffn_own.at[dp], ffn_own.at[dp], ffn_two, k, far(k)) for k in fars]
+    for copy in ffn_twos:
+        copy.start()
+
+    for copy in twos:
+        copy.wait()
     total = sums[0]
-    for k in range(1, dps):
+    for k in fars:
         total = total + sums[k]
     out_ref[me] = total
-    for k in range(1, planes):
-        three(k).start()
-    for k in range(1, planes):
-        three(k).wait()
-
-
-def total_over_all(rows, blocks):
+    threes = [remote(out_ref.at[me], out_ref.at[me], three_sems, k, near(k)) for k in nears]
+    for copy in threes:
+        copy.start()
+
+    for copy in attn_ones:
+        copy.wait()
+    attn_own[dp] = plus(total_ref[dp], *[attn_parts[k] for k in fars])
+    attn_twos = [remote(attn_own.at[dp], attn_own.at[dp], attn_two, k, far(k)) for k in fars]
+    for copy in attn_twos:
+        copy.start()
+
+    for copy in ffn_twos:
+        copy.wait()
+    swap_ffn = remote(ffn_own, ffn_other, swap_sems, 5, peer_core)
+    swap_ffn.start()
+    for copy in attn_twos:
+        copy.wait()
+    swap_attn = remote(attn_own, attn_other, swap_sems, 6, peer_core)
+    swap_attn.start()
+    for copy in threes:
+        copy.wait()
+    swap_ffn.wait()
+    swap_attn.wait()
+
+
+def last_sums(ffn_total, attn_blocks, rows, blocks):
     dps = lax.axis_size("dp")
     planes = lax.axis_size("span") * lax.axis_size("tensor")
     flat, tree = jax.tree.flatten(blocks)
-    shape = rows.shape
+
+    def by_dp(values):
+        return values.reshape(dps, values.shape[0] // dps, values.shape[1])
+
+    ffn_total = by_dp(ffn_total)
+    own = [by_dp(o) for o, r in attn_blocks]
+    rest = [by_dp(r) for o, r in attn_blocks]
     dma = pltpu.SemaphoreType.DMA
     vmem = pl.BlockSpec(memory_space=pltpu.VMEM)
-
-    def body(rows_ref, *refs):
+    attn, ffn = own[0].shape, ffn_total.shape
+
+    def body(ffn_ref, *refs):
+        own_refs, rest_refs, rows_ref = refs[:TENSORS], refs[TENSORS : 2 * TENSORS], refs[2 * TENSORS]
+        refs = refs[2 * TENSORS + 1 :]
         inputs = jax.tree.unflatten(tree, refs[: len(flat)])
-        out_ref, x_ref, parts, sums = refs[len(flat) : len(flat) + 4]
-        total_kernel(dps, planes, rows_ref, inputs, out_ref, x_ref, parts, sums, refs[len(flat) + 4 :])
-
-    return pl.pallas_call(
+        outs, scratch = refs[len(flat) : len(flat) + 5], refs[len(flat) + 5 :]
+        last_kernel(dps, planes, ffn_ref, own_refs, rest_refs, rows_ref, inputs, outs, scratch)
+
+    outs = pl.pallas_call(
         body,
-        name="total_over_all",
-        out_shape=jax.ShapeDtypeStruct(shape, F32),
-        in_specs=[vmem] * (1 + len(flat)),
-        out_specs=vmem,
-        scratch_shapes=[
-            pltpu.VMEM(shape, F32),
-            pltpu.VMEM(shape, F32),
-            pltpu.VMEM((dps,) + shape[1:], F32),
-            dma((planes,)), dma((planes,)), dma((dps,)), dma((dps,)), dma((planes,)), dma((planes,)),
-        ],
-        compiler_params=pltpu.CompilerParams(collective_id=1, has_side_effects=True),
-    )(rows, *flat)
+        name="last_sums",
+        out_shape=tuple(jax.ShapeDtypeStruct(shape, BF) for shape in (ffn, ffn, attn, attn))
+        + (jax.ShapeDtypeStruct(rows.shape, F32),),
+        in_specs=[vmem] * (2 + 2 * TENSORS + len(flat)),
+        out_specs=(vmem,) * 5,
+        scratch_shapes=[pltpu.VMEM((TENSORS,) + attn, BF)]
+        + [pltpu.VMEM(attn, BF)] * 9
+        + [pltpu.VMEM(ffn, BF), pltpu.VMEM(attn, BF)]
+        + [pltpu.VMEM(rows.shape, F32), pltpu.VMEM(rows.shape, F32), pltpu.VMEM((dps,) + rows.shape[1:], F32)]
+        + [dma((2, 7)), dma((2, 3))]
+        + [dma((2, dps))] * 4
+        + [dma((2, planes)), dma((2, dps)), dma((2, planes))],
+        compiler_params=pltpu.CompilerParams(
+            collective_id=1, has_side_effects=True, vmem_limit_bytes=36 << 20
+        ),
+    )(ffn_total, *own, *rest, rows, *flat)
+    whole = [o.reshape(-1, o.shape[-1]) for o in outs[:4]]
+    return (*whole, outs[4])
 
 
 def to_rows(values):
@@ -722,7 +798,7 @@
     def plain(name, value):
         return value
 
-    ffn1, attn1, ffn0, attn0 = (Reduction() for _ in range(4))
+    ffn1, attn1, ffn0 = (Reduction() for _ in range(3))
 
     dy, blocks, small1 = ffn_backward(head_cot.astype(F32) * valid, ffn_w1, vec1, kept1, plain)
     dy, head_out = tie(dy, head_out)
@@ -753,20 +829,21 @@
     dy = ffn0.start(dy, blocks)
     dy = attn1.summed(dy)
 
+    dy, ffn_total1, late = tie(dy, ffn_total1, attn1.total)
+    attn_total1 = lax.psum(late, "dp")
+    finished = {}
+
     def during_attn0(name, value):
         if name == "normed":
             return ffn0.swapped(value)
-        return ffn0.crossed(value)
-
-    dy, ffn_total1, attn_total1 = tie(dy, ffn_total1, attn1.total)
-    attn_total1 = lax.psum(attn_total1, "dp")
-
-    dx, blocks, more = attn_backward(dy, seg, attn_w0, vec0, kept0, during_attn0)
+        value = ffn0.crossed(value)
+        value, finished["attn"] = tie(value, attn_total1)
+        return value
+
+    dx, attn_blocks, more = attn_backward(dy, seg, attn_w0, vec0, kept0, during_attn0)
     small0.update(more)
-    dx = attn0.start(dx, blocks)
-    dx = ffn0.summed(dx)
-    dx, late, attn_total1 = tie(dx, ffn0.total, attn_total1)
-    ffn_total0 = lax.psum(late, "dp")
+    attn_total1 = finished["attn"]
+    grad_input = to_places(dx.astype(BF))
 
     place = lax.broadcasted_iota(jnp.int32, (2 * CHUNKS_PER_LAYER * ROWS_PER_CHUNK, 1), 0)
     rows = jnp.zeros((place.shape[0], width), F32)
@@ -774,13 +851,13 @@
         base = l * CHUNKS_PER_LAYER * ROWS_PER_CHUNK
         for i, k in enumerate(VECTORS):
             rows = rows + jnp.where(place == base + 2 * ROWS_PER_CHUNK + i, small[k][None], 0.0)
-    rows, mark = tie(rows.reshape(2 * CHUNKS_PER_LAYER, ROWS_PER_CHUNK, width), late)
-    rows = attn0.swapped(rows)
-    total = total_over_all(rows, [(small["eb"], small["heads"]) for small in (small0, small1)])
-    total = attn0.crossed(total)
-    total = attn0.summed(total)
-    attn_total0, ffn_total0 = tie(attn0.total, ffn_total0)
-    attn_total0 = lax.psum(attn_total0, "dp")
+    rows = ffn0.summed(rows.reshape(2 * CHUNKS_PER_LAYER, ROWS_PER_CHUNK, width))
+    ffn_total1, attn_total1 = tie(ffn_total1, attn_total1)
+    other_ffn1, other_attn1 = send(ffn_total1, SWAP), send(attn_total1, SWAP)
+    rows, other_ffn1, other_attn1 = tie(rows, other_ffn1, other_attn1)
+    ffn_own, ffn_other, attn_own, attn_other, total = last_sums(
+        ffn0.total, attn_blocks, rows, [(small["eb"], small["heads"]) for small in (small0, small1)]
+    )
 
     hb, eb, vector_sums = [], [], []
     for l in range(2):
@@ -792,16 +869,16 @@
         vector_sums.append({k: rows[i] for i, k in enumerate(VECTORS)})
     sums = vector_sums
 
-    ge1, gs1 = finish_part(ffn_total1, side)
-    gh1, gp1 = attn_unpack(*finish_part(attn_total1, side))
-    ge0, gs0 = finish_part(ffn_total0, side)
-    gh0, gp0 = attn_unpack(*finish_part(attn_total0, side))
+    ge1, gs1 = in_order(side, ffn_total1, other_ffn1)
+    gh1, gp1 = attn_unpack(*in_order(side, attn_total1, other_attn1))
+    ge0, gs0 = in_order(side, ffn_own, ffn_other)
+    gh0, gp0 = attn_unpack(*in_order(side, attn_own, attn_other))
 
     return (
         later["backbone_out"][None],
         head_out[None],
         span_loss,
-        to_places(dx.astype(BF))[None],
+        grad_input[None],
         grad_skip[None],
         jnp.stack([gh0, gh1]),
         jnp.stack(hb),

time: 691 us -> 674 us (0.975)
  waiting for transfers between devices: 108 us -> 18.4 us
  Pallas kernels: 229 us -> 287 us
  local copies, waits for them, and re-layouts: 89.8 us -> 108 us
    psum x3 -> x1, waiting for transfers between devices: 82.5 us -> 0.01 us  [shards(): attn_total1 = lax.psum(late, 'dp')]
    pallas_call x1, Pallas kernels: 22.5 us -> 82.7 us  [last_sums(): pl.pallas_call(body, name='last_sums', out_shape=tuple((jax.ShapeDtypeStr...]
    ppermute x60 -> x50, waiting for transfers between devices: 24.5 us -> 9.78 us  [send(): return lax.ppermute(values, PLANE, plane_pairs(kind))]
    unnamed x497 -> x555, local copies, waits for them, and re-layouts: 77.5 us -> 86.1 us
    all_to_all x4, waiting for transfers between devices: 0.01 us -> 7.48 us  [to_places(): lax.all_to_all(blocks, 'tensor', split_axis=0, concat_axis=0, tiled=True)]
    ppermute x60 -> x50, starting transfers between devices: 40 us -> 33.4 us  [send(): return lax.ppermute(values, PLANE, plane_pairs(kind))]
    convert_element_type x24 -> x18, other arithmetic: 39.2 us -> 37.2 us  [plus(): return total.astype(BF)]
  transfers between devices with their start and end apart: 72 -> 60, of which waited for: 11 -> 6; matrix products, arithmetic and copies ran while one was open for 22% -> 21% of each run, Pallas kernels for 34% -> 31%
where the time goes in v7:
time: 674 us; the launch traced here: 664 us
  Pallas kernels  287 us (43%)
  other arithmetic  110 us (16%)
  local copies, waits for them, and re-layouts  108 us (16%)
  starting transfers between devices  68.3 us (10%)
  matrix products  50.4 us (7%)
  between operations  20.3 us (3%)
  waiting for transfers between devices  18.4 us (3%)
    unnamed x555, local copies, waits for them, and re-layouts  86.1 us
    pallas_call x1, Pallas kernels, last_sums(): pl.pallas_call(body, name='last_sums', out_shape=tuple((jax.ShapeDtypeStr...  82.7 us
    pallas_call x8, Pallas kernels, attend_backward(): pl.pallas_call(attend_backward_kernel, name='attend_backward', out_shape=...  70.6 us
    pallas_call x8, Pallas kernels, ffn_block_backward(): pl.pallas_call(ffn_backward_kernel, name='ffn_backward', out_shape=(jax.S...  62.3 us
    pallas_call x8, Pallas kernels, attend_forward(): pl.pallas_call(body, name='attend_forward', out_shape=(narrow, narrow, na...  55 us
    dot_general x18, matrix products, mm(): lax.dot_general(a, b, (((ca,), (cb,)), ((), ())), preferred_element_type=...  44.2 us
    convert_element_type x18, other arithmetic, plus(): return total.astype(BF)  37.2 us
    ppermute x50, starting transfers between devices, send(): return lax.ppermute(values, PLANE, plane_pairs(kind))  33.4 us
  transfers between devices with their start and end apart: 60, of which 6 were waited for; matrix products, arithmetic and copies ran while one was open for 21% of the time, Pallas kernels for 31%

profile of v7, /device:TPU:0, one launch (start us, length us, event | category | flops | bytes accessed | tf_op | source)
XLA Modules:
  0.0 663.6 jit_solution(14866757947114307299)
XLA Ops:
  7.2 5.2 all-to-all-start
  27.9 6.4 attend_forward.8
  40.3 6.4 attend_forward.9
  50.3 6.4 attend_forward.10
  59.3 6.6 attend_forward.11
  74.5 3.6 fusion.34
  80.6 3.4 fusion.29
  86.5 3.4 fusion.24
  95.5 4.2 all-to-all-start.1
  117.5 7.6 %attend_forward.12 = (bf16[512,192]{1,0:T(8,128)(2,1)S(1)}, bf16[512,192]{1,0:T(8,128)(2,1)S(1)}, bf16[512,192]{1,0:T(8,128)(2,1)S(1)}, bf16[512,192]{1,0:T(8,12...) custom-call(bf16[512,768]{1,0:T(8,128)(2,1)S(1)} %get-tuple-element.502.refs_0_.x_ref, ...), custom_call_target="tpu_custom_call" | custom-call | flops 1048576 | bytes 1024 | tf_op jit(solution)/shard_map/attend_forward/pallas_call | solution.py:275
  129.8 4.6 all-to-all-start.2
  135.8 7.6 %attend_forward.13 = (bf16[512,192]{1,0:T(8,128)(2,1)S(1)}, bf16[512,192]{1,0:T(8,128)(2,1)S(1)}, bf16[512,192]{1,0:T(8,128)(2,1)S(1)}, bf16[512,192]{1,0:T(8,12...) custom-call(bf16[512,768]{1,0:T(8,128)(2,1)S(1)} %get-tuple-element.502.refs_0_.x_ref, ...), custom_call_target="tpu_custom_call" | custom-call | flops 1048576 | bytes 1024 | tf_op jit(solution)/shard_map/attend_forward/pallas_call | solution.py:275
  146.9 7.6 %attend_forward.14 = (bf16[512,192]{1,0:T(8,128)(2,1)S(1)}, bf16[512,192]{1,0:T(8,128)(2,1)S(1)}, bf16[512,192]{1,0:T(8,128)(2,1)S(1)}, bf16[512,192]{1,0:T(8,12...) custom-call(bf16[512,768]{1,0:T(8,128)(2,1)S(1)} %get-tuple-element.502.refs_0_.x_ref, ...), custom_call_target="tpu_custom_call" | custom-call | flops 1048576 | bytes 1024 | tf_op jit(solution)/shard_map/attend_forward/pallas_call | solution.py:275
  161.0 6.4 attend_forward.15
  180.9 3.6 fusion.19
  186.9 3.4 fusion.14
  192.7 3.3 fusion.9
  196.0 3.5 add_add_fusion
  199.8 4.2 all-to-all-start.3
  207.7 16.9 %gather_anchors.1 = bf16[4,8,4,768]{3,2,1,0:T(4,128)(2,1)} custom-call(bf16[4,768]{1,0:T(4,128)(2,1)} %convolution_convert_fusion.refs_0_), custom_call_target="tpu_custom_call" | custom-call | tf_op jit(solution)/shard_map/gather_anchors/pallas_call | solution.py:361
  236.3 3.7 multiply_reduce_fusion
  240.0 4.4 all-to-all-start.4
  248.8 8.2 %ffn_backward.8 = (bf16[768,768]{1,0:T(8,128)(2,1)S(1)}, bf16[768,768]{1,0:T(8,128)(2,1)S(1)}, f32[1,768]{1,0:T(1,128)S(1)}, f32[512,768]{1,0:T(8,128)S(1)}) custom-call(bf16[512,768]{1,0:T(8,128)(2,1)S(1)} %convert_element_type.499.dz_ref, bf16[512,768]{1,0:T(8,128)(2,1)S(1)} %copy-done.7, bf16[512,768]{1,0:T(8,128)(2,1)S(1)} %copy-done.87, ...), custom_call_target="tpu_custom_call" | custom-call | flops 1048576 | bytes 1024 | tf_op jit(solution)/shard_map/ffn_backward/pallas_call | solution.py:253
  259.1 8.2 %ffn_backward.9 = (bf16[768,768]{1,0:T(8,128)(2,1)S(1)}, bf16[768,768]{1,0:T(8,128)(2,1)S(1)}, f32[1,768]{1,0:T(1,128)S(1)}, f32[512,768]{1,0:T(8,128)S(1)}) custom-call(bf16[512,768]{1,0:T(8,128)(2,1)S(1)} %convert_element_type.499.dz_ref, bf16[512,768]{1,0:T(8,128)(2,1)S(1)} %copy-done.7, bf16[512,768]{1,0:T(8,128)(2,1)S(1)} %copy-done.84, ...), custom_call_target="tpu_custom_call" | custom-call | flops 1048576 | bytes 1024 | tf_op jit(solution)/shard_map/ffn_backward/pallas_call | solution.py:253
  269.5 8.2 %ffn_backward.10 = (bf16[768,768]{1,0:T(8,128)(2,1)S(1)}, bf16[768,768]{1,0:T(8,128)(2,1)S(1)}, f32[1,768]{1,0:T(1,128)S(1)}, f32[512,768]{1,0:T(8,128)S(1)}) custom-call(bf16[512,768]{1,0:T(8,128)(2,1)S(1)} %convert_element_type.499.dz_ref, bf16[512,768]{1,0:T(8,128)(2,1)S(1)} %copy-done.7, bf16[512,768]{1,0:T(8,128)(2,1)S(1)} %copy-done.43, ...), custom_call_target="tpu_custom_call" | custom-call | flops 1048576 | bytes 1024 | tf_op jit(solution)/shard_map/ffn_backward/pallas_call | solution.py:253
  279.7 6.5 ffn_backward.11
  291.0 3.5 multiply_reduce_fusion.1
  307.1 9.5 %attend_backward.8 = (bf16[384,768]{1,0:T(8,128)(2,1)S(1)}, bf16[384,768]{1,0:T(8,128)(2,1)S(1)}, f32[1,384]{1,0:T(1,128)S(1)}, f32[512,768]{1,0:T(8,128)S(1)}) custom-call(bf16[512,768]{1,0:T(8,128)(2,1)S(1)} %convert_element_type.524.da_ref, bf16[512,768]{1,0:T(8,128)(2,1)S(1)} %get-tuple-element.502.refs_0_.x_ref, ...), custom_call_target="tpu_custom_call" | custom-call | flops 1048576 | bytes 1024 | tf_op jit(solution)/shard_map/attend_backward/pallas_call | solution.py:290
  317.6 9.9 %attend_backward.9 = (bf16[384,768]{1,0:T(8,128)(2,1)S(1)}, bf16[384,768]{1,0:T(8,128)(2,1)S(1)}, f32[1,384]{1,0:T(1,128)S(1)}, f32[512,768]{1,0:T(8,128)S(1)}) custom-call(bf16[512,768]{1,0:T(8,128)(2,1)S(1)} %convert_element_type.524.da_ref, bf16[512,768]{1,0:T(8,128)(2,1)S(1)} %get-tuple-element.502.refs_0_.x_ref, ...), custom_call_target="tpu_custom_call" | custom-call | flops 1048576 | bytes 1024 | tf_op jit(solution)/shard_map/attend_backward/pallas_call | solution.py:290
  329.7 10.2 %attend_backward.10 = (bf16[384,768]{1,0:T(8,128)(2,1)}, bf16[384,768]{1,0:T(8,128)(2,1)}, f32[1,384]{1,0:T(1,128)S(1)}, f32[512,768]{1,0:T(8,128)S(1)}) custom-call(bf16[512,768]{1,0:T(8,128)(2,1)S(1)} %convert_element_type.524.da_ref, bf16[512,768]{1,0:T(8,128)(2,1)S(1)} %get-tuple-element.502.refs_0_.x_ref, ...), custom_call_target="tpu_custom_call" | custom-call | flops 1048576 | bytes 1024 | tf_op jit(solution)/shard_map/attend_backward/pallas_call | solution.py:290
  342.0 8.1 %attend_backward.11 = (bf16[384,768]{1,0:T(8,128)(2,1)S(1)}, bf16[384,768]{1,0:T(8,128)(2,1)S(1)}, f32[1,384]{1,0:T(1,128)S(1)}, f32[512,768]{1,0:T(8,128)S(1)}) custom-call(bf16[512,768]{1,0:T(8,128)(2,1)S(1)} %convert_element_type.524.da_ref, bf16[512,768]{1,0:T(8,128)(2,1)S(1)} %get-tuple-element.502.refs_0_.x_ref, bf16[384,768]{1,0:T(8,128)(2,1)S(1)} %copy-done.31, ...), custom_call_target="tpu_custom_call" | custom-call | flops 1048576 | bytes 1024 | tf_op jit(solution)/shard_map/attend_backward/pallas_call | solution.py:290
  356.1 4.2 all-to-all-start.5
  368.0 6.5 collective-permute-done.29
  374.6 3.1 add_convert_fusion.6
  378.8 5.0 multiply_reduce_fusion.2
  391.0 4.2 all-to-all-start.6
  400.1 8.2 %ffn_backward.12 = (bf16[768,768]{1,0:T(8,128)(2,1)S(1)}, bf16[768,768]{1,0:T(8,128)(2,1)S(1)}, f32[1,768]{1,0:T(1,128)S(1)}, f32[512,768]{1,0:T(8,128)S(1)}) custom-call(bf16[512,768]{1,0:T(8,128)(2,1)S(1)} %copy-done.8, bf16[512,768]{1,0:T(8,128)(2,1)S(1)} %copy-done.4, bf16[512,768]{1,0:T(8,128)(2,1)S(1)} %copy-done.74, bf16[512,768]{1,0:T(8,128)(2,1)S(1)} %copy-done.72, ...), custom_call_target="tpu_custom_call" | custom-call | flops 1048576 | bytes 1024 | tf_op jit(solution)/shard_map/ffn_backward/pallas_call | solution.py:253
  410.4 8.2 %ffn_backward.13 = (bf16[768,768]{1,0:T(8,128)(2,1)S(1)}, bf16[768,768]{1,0:T(8,128)(2,1)S(1)}, f32[1,768]{1,0:T(1,128)S(1)}, f32[512,768]{1,0:T(8,128)S(1)}) custom-call(bf16[512,768]{1,0:T(8,128)(2,1)S(1)} %copy-done.8, bf16[512,768]{1,0:T(8,128)(2,1)S(1)} %copy-done.4, bf16[512,768]{1,0:T(8,128)(2,1)S(1)} %copy-done.41, bf16[512,768]{1,0:T(8,128)(2,1)S(1)} %copy-done.71, ...), custom_call_target="tpu_custom_call" | custom-call | flops 1048576 | bytes 1024 | tf_op jit(solution)/shard_map/ffn_backward/pallas_call | solution.py:253
  420.8 8.3 %ffn_backward.14 = (bf16[768,768]{1,0:T(8,128)(2,1)S(1)}, bf16[768,768]{1,0:T(8,128)(2,1)S(1)}, f32[1,768]{1,0:T(1,128)S(1)}, f32[512,768]{1,0:T(8,128)S(1)}) custom-call(bf16[512,768]{1,0:T(8,128)(2,1)S(1)} %copy-done.8, bf16[512,768]{1,0:T(8,128)(2,1)S(1)} %copy-done.4, bf16[512,768]{1,0:T(8,128)(2,1)S(1)} %copy-done.77, bf16[512,768]{1,0:T(8,128)(2,1)S(1)} %copy-done.75, ...), custom_call_target="tpu_custom_call" | custom-call | flops 1048576 | bytes 1024 | tf_op jit(solution)/shard_map/ffn_backward/pallas_call | solution.py:253
  434.6 6.5 ffn_backward.15
  471.7 8.3 %attend_backward.12 = (bf16[384,768]{1,0:T(8,128)(2,1)S(1)}, bf16[384,768]{1,0:T(8,128)(2,1)S(1)}, f32[1,384]{1,0:T(1,128)S(1)}, f32[512,768]{1,0:T(8,128)S(1)}) custom-call(bf16[512,768]{1,0:T(8,128)(2,1)S(1)} %convert_element_type.569.da_ref, bf16[512,768]{1,0:T(8,128)(2,1)S(1)} %bitcast.174, bf16[400,768]{1,0:T(8,128)(2,1)S(1)} %copy-done.19, ...), custom_call_target="tpu_custom_call" | custom-call | flops 1048576 | bytes 1024 | tf_op jit(solution)/shard_map/attend_backward/pallas_call | solution.py:290
  480.2 8.2 %attend_backward.13 = (bf16[384,768]{1,0:T(8,128)(2,1)S(1)}, bf16[384,768]{1,0:T(8,128)(2,1)S(1)}, f32[1,384]{1,0:T(1,128)S(1)}, f32[512,768]{1,0:T(8,128)S(1)}) custom-call(bf16[512,768]{1,0:T(8,128)(2,1)S(1)} %convert_element_type.569.da_ref, bf16[512,768]{1,0:T(8,128)(2,1)S(1)} %bitcast.175, bf16[400,768]{1,0:T(8,128)(2,1)S(1)} %copy-done.17, ...), custom_call_target="tpu_custom_call" | custom-call | flops 1048576 | bytes 1024 | tf_op jit(solution)/shard_map/attend_backward/pallas_call | solution.py:290
  490.2 8.2 %attend_backward.14 = (bf16[384,768]{1,0:T(8,128)(2,1)S(1)}, bf16[384,768]{1,0:T(8,128)(2,1)S(1)}, f32[1,384]{1,0:T(1,128)S(1)}, f32[512,768]{1,0:T(8,128)S(1)}) custom-call(bf16[512,768]{1,0:T(8,128)(2,1)S(1)} %convert_element_type.569.da_ref, bf16[512,768]{1,0:T(8,128)(2,1)S(1)} %bitcast.176, bf16[400,768]{1,0:T(8,128)(2,1)S(1)} %copy-done.45, ...), custom_call_target="tpu_custom_call" | custom-call | flops 1048576 | bytes 1024 | tf_op jit(solution)/shard_map/attend_backward/pallas_call | solution.py:290
  498.4 3.6 add_convert_fusion.1
  509.0 8.1 %attend_backward.15 = (bf16[384,768]{1,0:T(8,128)(2,1)S(1)}, bf16[384,768]{1,0:T(8,128)(2,1)S(1)}, f32[1,384]{1,0:T(1,128)S(1)}, f32[512,768]{1,0:T(8,128)S(1)}) custom-call(bf16[512,768]{1,0:T(8,128)(2,1)S(1)} %convert_element_type.569.da_ref, bf16[512,768]{1,0:T(8,128)(2,1)S(1)} %bitcast.177, bf16[400,768]{1,0:T(8,128)(2,1)S(1)} %copy-done.21, ...), custom_call_target="tpu_custom_call" | custom-call | flops 1048576 | bytes 1024 | tf_op jit(solution)/shard_map/attend_backward/pallas_call | solution.py:290
  518.4 3.8 all-to-all-start.7
  526.5 7.5 %all-to-all-done.7 = bf16[4,128,768]{2,1,0:T(8,128)(2,1)S(1)} async-done(((bf16[4,128,768]{2,1,0:T(8,128)(2,1)}), bf16[4,128,768]{2,1,0:T(8,128)(2,1)S(1)}, u32[]{:S(2)}, u32[]{:S(2)}) %all-to-all-start.7) | async-done | bytes 786464 | tf_op jit(solution)/shard_map/all_to_all | solution.py:569
  538.6 82.7 %last_sums.1 = (bf16[4,192,768]{2,1,0:T(8,128)(2,1)S(1)}, bf16[4,192,768]{2,1,0:T(8,128)(2,1)S(1)}, bf16[4,96,768]{2,1,0:T(8,128)(2,1)S(1)}, bf16[4,96,768]{2,1,0:T(8,128)(2,1)S(1)}, f32[8,4,768]{2,1,0:T(4,128)S(1)}) custom-call(bf16[4,192,768]{2,1,0:T(8,128)(2,1)S(1)} %bitcast.178, bf16[4,96,768]{2,1,0:T(8,128)(2,1)S(1)} %bitcast.179, ...), custom_call_target="tpu_custom_call" | custom-call | tf_op jit(solution)/shard_map/last_sums/pallas_call | solution.py:539
  (833 shorter events, 263.8 us)
Async XLA Ops:
  7.2 20.5 %all-to-all-start = ((bf16[4,128,768]{2,1,0:T(8,128)(2,1)}), bf16[4,128,768]{2,1,0:T(8,128)(2,1)S(1)}, u32[]{:S(2)}, u32[]{:S(2)}) async-start(bf16[4,128,768]{2,1,0:T(8,128)(2,1)} %bitcast.200), calls=%async_computation | async-start | bytes 1572864 | tf_op jit(solution)/shard_map/all_to_all | solution.py:562
  16.0 19.7 %collective-permute-start = (bf16[400,768]{1,0:T(8,128)(2,1)S(1)}, bf16[400,768]{1,0:T(8,128)(2,1)S(1)}, u32[]{:S(2)}, u32[]{:S(2)}) collective-permute-start(bf16[400,768]{1,0:T(8,128)(2,1)S(1)} %pad_maximum_fusion.2.refs_1_.first_ref), channel_id=1, source_target_pairs={{0,1},{1,0},{2,3},{3,2},{4,6},{5,7},{6,4},{7,5},{8,9},{9,8},{10,11... | collective-permute-start | bytes 1843208 | tf_op jit(solution)/shard_map/ppermute | solution.py:62
  18.1 18.3 %collective-permute-start.1 = (bf16[400,768]{1,0:T(8,128)(2,1)S(1)}, bf16[400,768]{1,0:T(8,128)(2,1)S(1)}, u32[]{:S(2)}, u32[]{:S(2)}) collective-permute-start(bf16[400,768]{1,0:T(8,128)(2,1)S(1)} %fusion.54.refs_2_.second_ref), channel_id=1, source_target_pairs={{0,1},{1,0},{2,3},{3,2},{4,6},{5,7},{6,4},{7,5},{8,9},{9,8},{10,11... | collective-permute-start | bytes 1843208 | tf_op jit(solution)/shard_map/ppermute | solution.py:62
  20.5 45.5 %collective-permute-start.6 = (bf16[768,768]{1,0:T(8,128)(2,1)}, bf16[768,768]{1,0:T(8,128)(2,1)}, u32[]{:S(2)}, u32[]{:S(2)}) collective-permute-start(bf16[768,768]{1,0:T(8,128)(2,1)} %get-tuple-element.242.first_ref), channel_id=1, source_target_pairs={{0,1},{1,0},{2,3},{3,2},{4,6},{5,7},{6,4},{7,5},{8,9},{9,8},{10,11... | collective-permute-start | bytes 3538952 | tf_op jit(solution)/shard_map/ppermute | solution.py:62
  22.5 45.9 %collective-permute-start.7 = (bf16[768,768]{1,0:T(8,128)(2,1)}, bf16[768,768]{1,0:T(8,128)(2,1)}, u32[]{:S(2)}, u32[]{:S(2)}) collective-permute-start(bf16[768,768]{1,0:T(8,128)(2,1)} %get-tuple-element.243.second_ref), channel_id=1, source_target_pairs={{0,1},{1,0},{2,3},{3,2},{4,6},{5,7},{6,4},{7,5},{8,9},{9,8},{10,11... | collective-permute-start | bytes 3538952 | tf_op jit(solution)/shard_map/ppermute | solution.py:62
  36.4 13.9 %collective-permute-start.2 = (bf16[400,768]{1,0:T(8,128)(2,1)S(1)}, bf16[400,768]{1,0:T(8,128)(2,1)S(1)}, u32[]{:S(2)}, u32[]{:S(2)}) collective-permute-start(bf16[400,768]{1,0:T(8,128)(2,1)S(1)} %collective-permute-done.refs_1_.first_ref), channel_id=1, source_target_pairs={{0,4},{1,5},{2,6},{3,7},{4,0},{5,1},{6,2},{7,3},{8,12},{9,13},{10,... | collective-permute-start | bytes 1843208 | tf_op jit(solution)/shard_map/ppermute | solution.py:62
  36.5 13.8 %collective-permute-start.3 = (bf16[400,768]{1,0:T(8,128)(2,1)S(1)}, bf16[400,768]{1,0:T(8,128)(2,1)S(1)}, u32[]{:S(2)}, u32[]{:S(2)}) collective-permute-start(bf16[400,768]{1,0:T(8,128)(2,1)S(1)} %collective-permute-done.1.refs_2_.second_ref), channel_id=1, source_target_pairs={{0,4},{1,5},{2,6},{3,7},{4,0},{5,1},{6,2},{7,3},{8,12},{9,13},{10,... | collective-permute-start | bytes 1843208 | tf_op jit(solution)/shard_map/ppermute | solution.py:62
  37.0 19.8 %collective-permute-start.4 = (bf16[400,768]{1,0:T(8,128)(2,1)S(1)}, bf16[400,768]{1,0:T(8,128)(2,1)S(1)}, u32[]{:S(2)}, u32[]{:S(2)}) collective-permute-start(bf16[400,768]{1,0:T(8,128)(2,1)S(1)} %broadcast_select_fusion.10), channel_id=1, source_target_pairs={{0,2},{1,3},{2,0},{3,1},{4,5},{5,4},{6,7},{7,6},{8,10},{9,11},{10,... | collective-permute-start | bytes 1843208 | tf_op jit(solution)/shard_map/ppermute | solution.py:62
  57.0 29.2 %collective-permute-start.8 = (bf16[384,768]{1,0:T(8,128)(2,1)}, bf16[384,768]{1,0:T(8,128)(2,1)}, u32[]{:S(2)}, u32[]{:S(2)}) collective-permute-start(bf16[384,768]{1,0:T(8,128)(2,1)} %bitcast.16.refs_1_.first_ref), channel_id=1, source_target_pairs={{0,1},{1,0},{2,3},{3,2},{4,6},{5,7},{6,4},{7,5},{8,9},{9,8},{10,11... | collective-permute-start | bytes 1769480 | tf_op jit(solution)/shard_map/ppermute | solution.py:62
  58.5 27.9 %collective-permute-start.9 = (bf16[384,768]{1,0:T(8,128)(2,1)}, bf16[384,768]{1,0:T(8,128)(2,1)}, u32[]{:S(2)}, u32[]{:S(2)}) collective-permute-start(bf16[384,768]{1,0:T(8,128)(2,1)} %pad_maximum_fusion.3.refs_2_.second_ref), channel_id=1, source_target_pairs={{0,1},{1,0},{2,3},{3,2},{4,6},{5,7},{6,4},{7,5},{8,9},{9,8},{10,11... | collective-permute-start | bytes 1769480 | tf_op jit(solution)/shard_map/ppermute | solution.py:62
  68.4 18.1 %collective-permute-start.10 = (bf16[768,768]{1,0:T(8,128)(2,1)}, bf16[768,768]{1,0:T(8,128)(2,1)}, u32[]{:S(2)}, u32[]{:S(2)}) collective-permute-start(bf16[768,768]{1,0:T(8,128)(2,1)} %collective-permute-done.6.first_ref), channel_id=1, source_target_pairs={{0,4},{1,5},{2,6},{3,7},{4,0},{5,1},{6,2},{7,3},{8,12},{9,13},{10,... | collective-permute-start | bytes 3538952 | tf_op jit(solution)/shard_map/ppermute | solution.py:62
  68.4 21.4 %collective-permute-start.11 = (bf16[768,768]{1,0:T(8,128)(2,1)}, bf16[768,768]{1,0:T(8,128)(2,1)}, u32[]{:S(2)}, u32[]{:S(2)}) collective-permute-start(bf16[768,768]{1,0:T(8,128)(2,1)} %collective-permute-done.7.second_ref), channel_id=1, source_target_pairs={{0,4},{1,5},{2,6},{3,7},{4,0},{5,1},{6,2},{7,3},{8,12},{9,13},{10,... | collective-permute-start | bytes 3538952 | tf_op jit(solution)/shard_map/ppermute | solution.py:62
  72.7 21.4 %collective-permute-start.12 = (bf16[768,768]{1,0:T(8,128)(2,1)S(1)}, bf16[768,768]{1,0:T(8,128)(2,1)}, u32[]{:S(2)}, u32[]{:S(2)}) collective-permute-start(bf16[768,768]{1,0:T(8,128)(2,1)S(1)} %copy-done.245), channel_id=1, source_target_pairs={{0,2},{1,3},{2,0},{3,1},{4,5},{5,4},{6,7},{7,6},{8,10},{9,11},{10,... | collective-permute-start | bytes 3538952 | tf_op jit(solution)/shard_map/ppermute | solution.py:62
  95.5 18.9 %all-to-all-start.1 = ((bf16[4,128,768]{2,1,0:T(8,128)(2,1)}), bf16[4,128,768]{2,1,0:T(8,128)(2,1)}, u32[]{:S(2)}, u32[]{:S(2)}) async-start(bf16[4,128,768]{2,1,0:T(8,128)(2,1)} %bitcast.201), calls=%async_computation.1 | async-start | bytes 1572864 | tf_op jit(solution)/shard_map/all_to_all | solution.py:562
  99.7 47.2 %collective-permute-start.14 = (bf16[384,768]{1,0:T(8,128)(2,1)}, bf16[384,768]{1,0:T(8,128)(2,1)}, u32[]{:S(2)}, u32[]{:S(2)}) collective-permute-start(bf16[384,768]{1,0:T(8,128)(2,1)} %collective-permute-done.8.refs_1_.first_ref), channel_id=1, source_target_pairs={{0,4},{1,5},{2,6},{3,7},{4,0},{5,1},{6,2},{7,3},{8,12},{9,13},{10,... | collective-permute-start | bytes 1769480 | tf_op jit(solution)/shard_map/ppermute | solution.py:62
  100.3 46.7 %collective-permute-start.15 = (bf16[384,768]{1,0:T(8,128)(2,1)}, bf16[384,768]{1,0:T(8,128)(2,1)}, u32[]{:S(2)}, u32[]{:S(2)}) collective-permute-start(bf16[384,768]{1,0:T(8,128)(2,1)} %collective-permute-done.9.refs_2_.second_ref), channel_id=1, source_target_pairs={{0,4},{1,5},{2,6},{3,7},{4,0},{5,1},{6,2},{7,3},{8,12},{9,13},{10,... | collective-permute-start | bytes 1769480 | tf_op jit(solution)/shard_map/ppermute | solution.py:62
  102.3 44.6 %collective-permute-start.16 = (bf16[384,768]{1,0:T(8,128)(2,1)}, bf16[384,768]{1,0:T(8,128)(2,1)}, u32[]{:S(2)}, u32[]{:S(2)}) collective-permute-start(bf16[384,768]{1,0:T(8,128)(2,1)} %broadcast_select_fusion.13), channel_id=1, source_target_pairs={{0,2},{1,3},{2,0},{3,1},{4,5},{5,4},{6,7},{7,6},{8,10},{9,11},{10,... | collective-permute-start | bytes 1769480 | tf_op jit(solution)/shard_map/ppermute | solution.py:62
  104.2 67.9 %collective-permute-start.18 = (bf16[768,768]{1,0:T(8,128)(2,1)}, bf16[768,768]{1,0:T(8,128)(2,1)}, u32[]{:S(2)}, u32[]{:S(2)}) collective-permute-start(bf16[768,768]{1,0:T(8,128)(2,1)} %get-tuple-element.267.first_ref), channel_id=1, source_target_pairs={{0,1},{1,0},{2,3},{3,2},{4,6},{5,7},{6,4},{7,5},{8,9},{9,8},{10,11... | collective-permute-start | bytes 3538952 | tf_op jit(solution)/shard_map/ppermute | solution.py:62
  106.4 65.6 %collective-permute-start.19 = (bf16[768,768]{1,0:T(8,128)(2,1)}, bf16[768,768]{1,0:T(8,128)(2,1)}, u32[]{:S(2)}, u32[]{:S(2)}) collective-permute-start(bf16[768,768]{1,0:T(8,128)(2,1)} %get-tuple-element.268.second_ref), channel_id=1, source_target_pairs={{0,1},{1,0},{2,3},{3,2},{4,6},{5,7},{6,4},{7,5},{8,9},{9,8},{10,11... | collective-permute-start | bytes 3538952 | tf_op jit(solution)/shard_map/ppermute | solution.py:62
  129.8 29.5 %all-to-all-start.2 = ((bf16[4,128,768]{2,1,0:T(8,128)(2,1)}), bf16[4,128,768]{2,1,0:T(8,128)(2,1)}, u32[]{:S(2)}, u32[]{:S(2)}) async-start(bf16[4,128,768]{2,1,0:T(8,128)(2,1)} %bitcast.192), calls=%async_computation.2 | async-start | bytes 1572864 | tf_op jit(solution)/shard_map/all_to_all | solution.py:569
  146.9 12.3 %collective-permute-start.17 = (bf16[384,768]{1,0:T(8,128)(2,1)}, bf16[384,768]{1,0:T(8,128)(2,1)}, u32[]{:S(2)}, u32[]{:S(2)}) collective-permute-start(bf16[384,768]{1,0:T(8,128)(2,1)} %collective-permute-done.16), channel_id=1, source_target_pairs={{0,4},{1,5},{2,6},{3,7},{4,0},{5,1},{6,2},{7,3},{8,12},{9,13},{10,... | collective-permute-start | bytes 1769480 | tf_op jit(solution)/shard_map/ppermute | solution.py:62
  172.1 20.6 %collective-permute-start.20 = (bf16[768,768]{1,0:T(8,128)(2,1)}, bf16[768,768]{1,0:T(8,128)(2,1)}, u32[]{:S(2)}, u32[]{:S(2)}) collective-permute-start(bf16[768,768]{1,0:T(8,128)(2,1)} %collective-permute-done.18.first_ref), channel_id=1, source_target_pairs={{0,4},{1,5},{2,6},{3,7},{4,0},{5,1},{6,2},{7,3},{8,12},{9,13},{10,... | collective-permute-start | bytes 3538952 | tf_op jit(solution)/shard_map/ppermute | solution.py:62
  172.6 23.5 %collective-permute-start.21 = (bf16[768,768]{1,0:T(8,128)(2,1)}, bf16[768,768]{1,0:T(8,128)(2,1)}, u32[]{:S(2)}, u32[]{:S(2)}) collective-permute-start(bf16[768,768]{1,0:T(8,128)(2,1)} %collective-permute-done.19.second_ref), channel_id=1, source_target_pairs={{0,4},{1,5},{2,6},{3,7},{4,0},{5,1},{6,2},{7,3},{8,12},{9,13},{10,... | collective-permute-start | bytes 3538952 | tf_op jit(solution)/shard_map/ppermute | solution.py:62
  178.5 21.1 %collective-permute-start.22 = (bf16[768,768]{1,0:T(8,128)(2,1)}, bf16[768,768]{1,0:T(8,128)(2,1)}, u32[]{:S(2)}, u32[]{:S(2)}) collective-permute-start(bf16[768,768]{1,0:T(8,128)(2,1)} %broadcast_select_fusion.4), channel_id=1, source_target_pairs={{0,2},{1,3},{2,0},{3,1},{4,5},{5,4},{6,7},{7,6},{8,10},{9,11},{10,... | collective-permute-start | bytes 3538952 | tf_op jit(solution)/shard_map/ppermute | solution.py:62
  199.5 30.5 %collective-permute-start.23 = (bf16[768,768]{1,0:T(8,128)(2,1)}, bf16[768,768]{1,0:T(8,128)(2,1)}, u32[]{:S(2)}, u32[]{:S(2)}) collective-permute-start(bf16[768,768]{1,0:T(8,128)(2,1)} %collective-permute-done.22), channel_id=1, source_target_pairs={{0,4},{1,5},{2,6},{3,7},{4,0},{5,1},{6,2},{7,3},{8,12},{9,13},{10,... | collective-permute-start | bytes 3538952 | tf_op jit(solution)/shard_map/ppermute | solution.py:62
  199.8 28.1 %all-to-all-start.3 = ((bf16[4,128,768]{2,1,0:T(8,128)(2,1)}), bf16[4,128,768]{2,1,0:T(8,128)(2,1)}, u32[]{:S(2)}, u32[]{:S(2)}) async-start(bf16[4,128,768]{2,1,0:T(8,128)(2,1)} %bitcast.202), calls=%async_computation.3 | async-start | bytes 1572864 | tf_op jit(solution)/shard_map/all_to_all | solution.py:562
  240.0 49.5 %all-to-all-start.4 = ((bf16[4,128,768]{2,1,0:T(8,128)(2,1)}), bf16[4,128,768]{2,1,0:T(8,128)(2,1)}, u32[]{:S(2)}, u32[]{:S(2)}) async-start(bf16[4,128,768]{2,1,0:T(8,128)(2,1)} %bitcast.191), calls=%async_computation.4 | async-start | bytes 1572864 | tf_op jit(solution)/shard_map/all_to_all | solution.py:569
  301.6 38.4 %collective-permute-start.28 = (bf16[768,768]{1,0:T(8,128)(2,1)S(1)}, bf16[768,768]{1,0:T(8,128)(2,1)S(1)}, u32[]{:S(2)}, u32[]{:S(2)}) collective-permute-start(bf16[768,768]{1,0:T(8,128)(2,1)S(1)} %add_convert_fusion.9), channel_id=1, source_target_pairs={{0,2},{1,3},{2,0},{3,1},{4,5},{5,4},{6,7},{7,6},{8,10},{9,11},{10,... | collective-permute-start | bytes 3538952 | tf_op jit(solution)/shard_map/ppermute | solution.py:62
  304.1 50.2 %collective-permute-start.30 = (bf16[768,768]{1,0:T(8,128)(2,1)}, bf16[768,768]{1,0:T(8,128)(2,1)}, u32[]{:S(2)}, u32[]{:S(2)}) collective-permute-start(bf16[768,768]{1,0:T(8,128)(2,1)} %add_convert_fusion.11), channel_id=1, source_target_pairs={{0,1},{1,0},{2,3},{3,2},{4,6},{5,7},{6,4},{7,5},{8,9},{9,8},{10,11... | collective-permute-start | bytes 3538952 | tf_op jit(solution)/shard_map/ppermute | solution.py:62
  353.8 20.8 %collective-permute-start.29 = (bf16[768,768]{1,0:T(8,128)(2,1)}, bf16[768,768]{1,0:T(8,128)(2,1)}, u32[]{:S(2)}, u32[]{:S(2)}) collective-permute-start(bf16[768,768]{1,0:T(8,128)(2,1)} %add_convert_fusion.7), channel_id=1, source_target_pairs={{0,1},{1,0},{2,3},{3,2},{4,6},{5,7},{6,4},{7,5},{8,9},{9,8},{10,11... | collective-permute-start | bytes 3538952 | tf_op jit(solution)/shard_map/ppermute | solution.py:62
  354.4 13.6 %collective-permute-start.31 = (bf16[768,768]{1,0:T(8,128)(2,1)}, bf16[768,768]{1,0:T(8,128)(2,1)}, u32[]{:S(2)}, u32[]{:S(2)}) collective-permute-start(bf16[768,768]{1,0:T(8,128)(2,1)} %collective-permute-done.30), channel_id=1, source_target_pairs={{0,4},{1,5},{2,6},{3,7},{4,0},{5,1},{6,2},{7,3},{8,12},{9,13},{10,... | collective-permute-start | bytes 3538952 | tf_op jit(solution)/shard_map/ppermute | solution.py:62
  356.1 22.7 %all-to-all-start.5 = ((bf16[4,128,768]{2,1,0:T(8,128)(2,1)}), bf16[4,128,768]{2,1,0:T(8,128)(2,1)}, u32[]{:S(2)}, u32[]{:S(2)}) async-start(bf16[4,128,768]{2,1,0:T(8,128)(2,1)} %bitcast.203), calls=%async_computation.5 | async-start | bytes 1572864 | tf_op jit(solution)/shard_map/all_to_all | solution.py:562
  360.3 87.4 %all-reduce.5.cloned.1.call-start = ((), (), s32[]{:S(2)}) async-start(), calls=%async_computation.8 | async-start | bytes 2359296 | tf_op jit(solution)/shard_map/psum | solution.py:816
  385.5 44.6 %collective-permute-start.36 = (bf16[384,768]{1,0:T(8,128)(2,1)}, bf16[384,768]{1,0:T(8,128)(2,1)}, u32[]{:S(2)}, u32[]{:S(2)}) collective-permute-start(bf16[384,768]{1,0:T(8,128)(2,1)} %add_convert_fusion.15), channel_id=1, source_target_pairs={{0,2},{1,3},{2,0},{3,1},{4,5},{5,4},{6,7},{7,6},{8,10},{9,11},{10,... | collective-permute-start | bytes 1769480 | tf_op jit(solution)/shard_map/ppermute | solution.py:62
  386.0 46.6 %collective-permute-start.38 = (bf16[384,768]{1,0:T(8,128)(2,1)}, bf16[384,768]{1,0:T(8,128)(2,1)}, u32[]{:S(2)}, u32[]{:S(2)}) collective-permute-start(bf16[384,768]{1,0:T(8,128)(2,1)} %add_convert_fusion.17), channel_id=1, source_target_pairs={{0,1},{1,0},{2,3},{3,2},{4,6},{5,7},{6,4},{7,5},{8,9},{9,8},{10,11... | collective-permute-start | bytes 1769480 | tf_op jit(solution)/shard_map/ppermute | solution.py:62
  391.0 53.2 %all-to-all-start.6 = ((bf16[4,128,768]{2,1,0:T(8,128)(2,1)}), bf16[4,128,768]{2,1,0:T(8,128)(2,1)}, u32[]{:S(2)}, u32[]{:S(2)}) async-start(bf16[4,128,768]{2,1,0:T(8,128)(2,1)} %bitcast.189), calls=%async_computation.6 | async-start | bytes 1572864 | tf_op jit(solution)/shard_map/all_to_all | solution.py:569
  395.2 108.5 %all-reduce.7.cloned.1.call-start = ((), (), s32[]{:S(2)}) async-start(), calls=%async_computation.9 | async-start | bytes 1179648 | tf_op jit(solution)/shard_map/psum | solution.py:833
  432.6 12.4 %collective-permute-start.39 = (bf16[384,768]{1,0:T(8,128)(2,1)}, bf16[384,768]{1,0:T(8,128)(2,1)}, u32[]{:S(2)}, u32[]{:S(2)}) collective-permute-start(bf16[384,768]{1,0:T(8,128)(2,1)} %collective-permute-done.38), channel_id=1, source_target_pairs={{0,4},{1,5},{2,6},{3,7},{4,0},{5,1},{6,2},{7,3},{8,12},{9,13},{10,... | collective-permute-start | bytes 1769480 | tf_op jit(solution)/shard_map/ppermute | solution.py:62
  432.6 12.7 %collective-permute-start.37 = (bf16[384,768]{1,0:T(8,128)(2,1)}, bf16[384,768]{1,0:T(8,128)(2,1)}, u32[]{:S(2)}, u32[]{:S(2)}) collective-permute-start(bf16[384,768]{1,0:T(8,128)(2,1)} %add_convert_fusion.13), channel_id=1, source_target_pairs={{0,1},{1,0},{2,3},{3,2},{4,6},{5,7},{6,4},{7,5},{8,9},{9,8},{10,11... | collective-permute-start | bytes 1769480 | tf_op jit(solution)/shard_map/ppermute | solution.py:62
  444.8 12.4 %collective-permute-start.42 = (bf16[768,768]{1,0:T(8,128)(2,1)}, bf16[768,768]{1,0:T(8,128)(2,1)}, u32[]{:S(2)}, u32[]{:S(2)}) collective-permute-start(bf16[768,768]{1,0:T(8,128)(2,1)} %copy-done.223), channel_id=1, source_target_pairs={{0,4},{1,5},{2,6},{3,7},{4,0},{5,1},{6,2},{7,3},{8,12},{9,13},{10,... | collective-permute-start | bytes 3538952 | tf_op jit(solution)/shard_map/ppermute | solution.py:62
  445.0 14.9 %collective-permute-start.43 = (bf16[768,768]{1,0:T(8,128)(2,1)}, bf16[768,768]{1,0:T(8,128)(2,1)}, u32[]{:S(2)}, u32[]{:S(2)}) collective-permute-start(bf16[768,768]{1,0:T(8,128)(2,1)} %copy-done.219), channel_id=1, source_target_pairs={{0,4},{1,5},{2,6},{3,7},{4,0},{5,1},{6,2},{7,3},{8,12},{9,13},{10,... | collective-permute-start | bytes 3538952 | tf_op jit(solution)/shard_map/ppermute | solution.py:62
  462.6 35.8 %collective-permute-start.44 = (bf16[768,768]{1,0:T(8,128)(2,1)}, bf16[768,768]{1,0:T(8,128)(2,1)}, u32[]{:S(2)}, u32[]{:S(2)}) collective-permute-start(bf16[768,768]{1,0:T(8,128)(2,1)} %add_convert_fusion.3), channel_id=1, source_target_pairs={{0,2},{1,3},{2,0},{3,1},{4,5},{5,4},{6,7},{7,6},{8,10},{9,11},{10,... | collective-permute-start | bytes 3538952 | tf_op jit(solution)/shard_map/ppermute | solution.py:62
  464.0 38.0 %collective-permute-start.46 = (bf16[768,768]{1,0:T(8,128)(2,1)}, bf16[768,768]{1,0:T(8,128)(2,1)}, u32[]{:S(2)}, u32[]{:S(2)}) collective-permute-start(bf16[768,768]{1,0:T(8,128)(2,1)} %add_convert_fusion.5), channel_id=1, source_target_pairs={{0,1},{1,0},{2,3},{3,2},{4,6},{5,7},{6,4},{7,5},{8,9},{9,8},{10,11... | collective-permute-start | bytes 3538952 | tf_op jit(solution)/shard_map/ppermute | solution.py:62
  502.1 32.1 %collective-permute-start.47 = (bf16[768,768]{1,0:T(8,128)(2,1)}, bf16[768,768]{1,0:T(8,128)(2,1)}, u32[]{:S(2)}, u32[]{:S(2)}) collective-permute-start(bf16[768,768]{1,0:T(8,128)(2,1)} %collective-permute-done.46), channel_id=1, source_target_pairs={{0,4},{1,5},{2,6},{3,7},{4,0},{5,1},{6,2},{7,3},{8,12},{9,13},{10,... | collective-permute-start | bytes 3538952 | tf_op jit(solution)/shard_map/ppermute | solution.py:62
  502.2 32.0 %collective-permute-start.45 = (bf16[768,768]{1,0:T(8,128)(2,1)}, bf16[768,768]{1,0:T(8,128)(2,1)}, u32[]{:S(2)}, u32[]{:S(2)}) collective-permute-start(bf16[768,768]{1,0:T(8,128)(2,1)} %add_convert_fusion.1), channel_id=1, source_target_pairs={{0,1},{1,0},{2,3},{3,2},{4,6},{5,7},{6,4},{7,5},{8,9},{9,8},{10,11... | collective-permute-start | bytes 3538952 | tf_op jit(solution)/shard_map/ppermute | solution.py:62
  503.7 33.0 %collective-permute-start.48 = (bf16[768,768]{1,0:T(8,128)(2,1)}, bf16[768,768]{1,0:T(8,128)(2,1)}, u32[]{:S(2)}, u32[]{:S(2)}) collective-permute-start(bf16[768,768]{1,0:T(8,128)(2,1)} %all-reduce.5.cloned.1.call-done), channel_id=1, source_target_pairs={{0,4},{1,5},{2,6},{3,7},{4,0},{5,1},{6,2},{7,3},{8,12},{9,13},{10,... | collective-permute-start | bytes 3538952 | tf_op jit(solution)/shard_map/ppermute | solution.py:62
  518.4 15.6 %all-to-all-start.7 = ((bf16[4,128,768]{2,1,0:T(8,128)(2,1)}), bf16[4,128,768]{2,1,0:T(8,128)(2,1)S(1)}, u32[]{:S(2)}, u32[]{:S(2)}) async-start(bf16[4,128,768]{2,1,0:T(8,128)(2,1)} %bitcast.41), calls=%async_computation.7 | async-start | bytes 1572864 | tf_op jit(solution)/shard_map/all_to_all | solution.py:569
  522.4 14.3 %collective-permute-start.49 = (bf16[384,768]{1,0:T(8,128)(2,1)S(1)}, bf16[384,768]{1,0:T(8,128)(2,1)S(1)}, u32[]{:S(2)}, u32[]{:S(2)}) collective-permute-start(bf16[384,768]{1,0:T(8,128)(2,1)S(1)} %copy-done.247), channel_id=1, source_target_pairs={{0,4},{1,5},{2,6},{3,7},{4,0},{5,1},{6,2},{7,3},{8,12},{9,13},{10,... | collective-permute-start | bytes 1769480 | tf_op jit(solution)/shard_map/ppermute | solution.py:62
  (286 other events, 1507.2 us)
Sparse Core Ops, SparseCore 0:
  387.6 54.5 all-reduce.4
  464.8 38.0 all-reduce.6

commit v8 on v7

--- a/solution.py
+++ b/solution.py
@@ -388,12 +388,48 @@
     )
 
 
+class Halving:
+    def __init__(self, dps, dp, src, result, scratch, sums, sems):
+        self.src, self.result, self.scratch, self.sums, self.sems = src, result, scratch, sums, sems
+        self.steps = []
+        base, size, bit = 0, dps, 1
+        while bit < dps:
+            size = size // 2
+            up = lax.rem(dp // bit, 2)
+            self.steps.append((base + (1 - up) * size, base + up * size, size, {"dp": dp + bit * (1 - 2 * up)}))
+            base = base + up * size
+            bit *= 2
+
+    def current(self, s):
+        return self.src if s == 0 else self.sums
+
+    def down(self, s):
+        away, kept, size, partner = self.steps[s]
+        room = self.scratch.at[pl.ds(self.steps_room(s), size)]
+        return remote(self.current(s).at[pl.ds(away, size)], room, self.sems, s, partner)
+
+    def steps_room(self, s):
+        return sum(step[2] for step in self.steps[:s])
+
+    def add(self, s):
+        self.down(s).wait()
+        away, kept, size, partner = self.steps[s]
+        came = self.scratch[pl.ds(self.steps_room(s), size)]
+        into = self.result if s == len(self.steps) - 1 else self.sums
+        into[pl.ds(kept, size)] = plus(self.current(s)[pl.ds(kept, size)], came)
+
+    def up(self, s):
+        away, kept, size, partner = self.steps[s]
+        part = self.result.at[pl.ds(kept, size)]
+        return remote(part, part, self.sems, len(self.steps) + s, partner)
+
+
 def last_kernel(dps, planes, ffn_ref, own, rest, rows_ref, blocks, outs, scratch):
     ffn_own, ffn_other, attn_own, attn_other, out_ref = outs
     (
         swapped, main_rest, main_own, across, mine, got_rest, got_own, got_across, got_peer, total_ref,
-        ffn_parts, attn_parts, x_ref, parts, sums,
-        swap_sems, plane_sems, ffn_one, ffn_two, attn_one, attn_two, one_sems, two_sems, three_sems,
+        ffn_room, attn_room, ffn_sums, attn_sums, x_ref, parts, sums,
+        swap_sems, plane_sems, ffn_sems, attn_sems, one_sems, two_sems, three_sems,
     ) = scratch
     dp = lax.axis_index("dp")
     side = lax.axis_index("span")
@@ -439,9 +475,33 @@
     ones = [remote(x_ref.at[near_peer(k)], parts.at[k], one_sems, k, near(k)) for k in nears]
     for copy in ones:
         copy.start()
-    ffn_ones = [remote(ffn_ref.at[far_peer(k)], ffn_parts.at[k], ffn_one, k, far(k)) for k in fars]
-    for copy in ffn_ones:
-        copy.start()
+    ffn_chunks = [
+        Halving(dps, dp, ffn_ref.at[c], ffn_own.at[c], ffn_room.at[c], ffn_sums.at[c], ffn_sems.at[c])
+        for c in range(ffn_ref.shape[0])
+    ]
+    attn_chunks = [
+        Halving(dps, dp, total_ref.at[c], attn_own.at[c], attn_room.at[c], attn_sums.at[c], attn_sems.at[c])
+        for c in range(total_ref.shape[0])
+    ]
+    stages = range(len(ffn_chunks[0].steps))
+    last = len(stages) - 1
+
+    def down_from(chunks, s):
+        for chunk in chunks:
+            chunk.down(s).start()
+
+    def down_to_end(chunks, s):
+        for chunk in chunks:
+            chunk.add(s)
+            (chunk.down(s + 1) if s < last else chunk.up(last)).start()
+
+    def up_next(chunks, s):
+        for chunk in chunks:
+            chunk.up(s).wait()
+            if s > 0:
+                chunk.up(s - 1).start()
+
+    down_from(ffn_chunks, 0)
 
     for copy in swaps:
         copy.wait()
@@ -462,26 +522,20 @@
     for copy in twos:
         copy.start()
 
+    down_to_end(ffn_chunks, 0)
     send_across.wait()
     main_own[...] = plus(own[1][...], swapped[1], got_across[...])
     send_own = remote(main_own, got_own, plane_sems, 2, main_peer)
     send_own.start()
+    for s in stages[1:]:
+        down_to_end(ffn_chunks, s)
     send_rest.wait()
     send_peer = remote(got_rest, got_peer, swap_sems, 4, peer_core)
     send_peer.start()
     send_peer.wait()
     send_own.wait()
     total_ref[...] = plus(mine[...], got_own[...], got_peer[...])
-    attn_ones = [remote(total_ref.at[far_peer(k)], attn_parts.at[k], attn_one, k, far(k)) for k in fars]
-    for copy in attn_ones:
-        copy.start()
-
-    for copy in ffn_ones:
-        copy.wait()
-    ffn_own[dp] = plus(ffn_ref[dp], *[ffn_parts[k] for k in fars])
-    ffn_twos = [remote(ffn_own.at[dp], ffn_own.at[dp], ffn_two, k, far(k)) for k in fars]
-    for copy in ffn_twos:
-        copy.start()
+    down_from(attn_chunks, 0)
 
     for copy in twos:
         copy.wait()
@@ -493,19 +547,15 @@
     for copy in threes:
         copy.start()
 
-    for copy in attn_ones:
-        copy.wait()
-    attn_own[dp] = plus(total_ref[dp], *[attn_parts[k] for k in fars])
-    attn_twos = [remote(attn_own.at[dp], attn_own.at[dp], attn_two, k, far(k)) for k in fars]
-    for copy in attn_twos:
-        copy.start()
-
-    for copy in ffn_twos:
-        copy.wait()
+    for s in reversed(stages[1:]):
+        up_next(ffn_chunks, s)
+    for s in stages:
+        down_to_end(attn_chunks, s)
+    up_next(ffn_chunks, 0)
     swap_ffn = remote(ffn_own, ffn_other, swap_sems, 5, peer_core)
     swap_ffn.start()
-    for copy in attn_twos:
-        copy.wait()
+    for s in reversed(stages):
+        up_next(attn_chunks, s)
     swap_attn = remote(attn_own, attn_other, swap_sems, 6, peer_core)
     swap_attn.start()
     for copy in threes:
@@ -520,7 +570,9 @@
     flat, tree = jax.tree.flatten(blocks)
 
     def by_dp(values):
-        return values.reshape(dps, values.shape[0] // dps, values.shape[1])
+        rows = values.shape[0]
+        chunks = 2 if rows % (32 * dps) == 0 else 1
+        return values.reshape(chunks, dps, rows // (chunks * dps), values.shape[1])
 
     ffn_total = by_dp(ffn_total)
     own = [by_dp(o) for o, r in attn_blocks]
@@ -545,10 +597,10 @@
         out_specs=(vmem,) * 5,
         scratch_shapes=[pltpu.VMEM((TENSORS,) + attn, BF)]
         + [pltpu.VMEM(attn, BF)] * 9
-        + [pltpu.VMEM(ffn, BF), pltpu.VMEM(attn, BF)]
+        + [pltpu.VMEM(ffn, BF), pltpu.VMEM(attn, BF)] * 2
         + [pltpu.VMEM(rows.shape, F32), pltpu.VMEM(rows.shape, F32), pltpu.VMEM((dps,) + rows.shape[1:], F32)]
         + [dma((2, 7)), dma((2, 3))]
-        + [dma((2, dps))] * 4
+        + [dma((ffn[0], 2, dps)), dma((attn[0], 2, dps))]
         + [dma((2, planes)), dma((2, dps)), dma((2, planes))],
         compiler_params=pltpu.CompilerParams(
             collective_id=1, has_side_effects=True, vmem_limit_bytes=36 << 20
@@ -721,7 +773,7 @@
             if j == 1:
                 value = gather_attn1.crossed(value)
             if j == 2:
-                value, later["backbone_out"] = tie(value, later["backbone_out"])
+                value, mark = tie(value, later["backbone_out"])
             if j == 3:
                 value = gather_ffn1.arrived(value)
         else:
@@ -801,7 +853,7 @@
     ffn1, attn1, ffn0 = (Reduction() for _ in range(3))
 
     dy, blocks, small1 = ffn_backward(head_cot.astype(F32) * valid, ffn_w1, vec1, kept1, plain)
-    dy, head_out = tie(dy, head_out)
+    dy, mark = tie(dy, head_out)
     dy = ffn1.start(dy, blocks)
 
     def during_attn1(name, value):
@@ -825,7 +877,7 @@
         return attn1.crossed(value)
 
     dy, blocks, small0 = ffn_backward(seed, ffn_w0, vec0, kept0, during_ffn0)
-    dy, grad_skip = tie(dy, grad_skip)
+    dy, mark = tie(dy, grad_skip)
     dy = ffn0.start(dy, blocks)
     dy = attn1.summed(dy)
 

time: 674 us -> 679 us (level)
  waiting for transfers between devices: 18.4 us -> 31.6 us
  Pallas kernels: 287 us -> 277 us
    all_to_all x4, waiting for transfers between devices: 1.13 us -> 17.3 us  [to_rows(): lax.all_to_all(values, 'tensor', split_axis=0, concat_axis=0, tiled=True)]
    pallas_call x1, Pallas kernels: 82.7 us -> 73.8 us  [last_sums(): pl.pallas_call(body, name='last_sums', out_shape=tuple((jax.ShapeDtypeStr...]
    unnamed x555 -> x605, local copies, waits for them, and re-layouts: 86.1 us -> 89 us
  transfers between devices with their start and end apart: 60 -> 60, of which waited for: 6 -> 6; matrix products, arithmetic and copies ran while one was open for 21% -> 20% of each run, Pallas kernels for 31% -> 30%
where the time goes in v8:
time: 679 us; the launch traced here: 669 us
  Pallas kernels  277 us (41%)
  local copies, waits for them, and re-layouts  113 us (17%)
  other arithmetic  112 us (16%)
  starting transfers between devices  67.5 us (10%)
  matrix products  47.1 us (7%)
  waiting for transfers between devices  31.6 us (5%)
  between operations  20.3 us (3%)
    unnamed x605, local copies, waits for them, and re-layouts  89 us
    pallas_call x1, Pallas kernels, last_sums(): pl.pallas_call(body, name='last_sums', out_shape=tuple((jax.ShapeDtypeStr...  73.8 us
    pallas_call x8, Pallas kernels, attend_backward(): pl.pallas_call(attend_backward_kernel, name='attend_backward', out_shape=...  70.9 us
    pallas_call x8, Pallas kernels, ffn_block_backward(): pl.pallas_call(ffn_backward_kernel, name='ffn_backward', out_shape=(jax.S...  60.6 us
    pallas_call x8, Pallas kernels, attend_forward(): pl.pallas_call(body, name='attend_forward', out_shape=(narrow, narrow, na...  55 us
    dot_general x18, matrix products, mm(): lax.dot_general(a, b, (((ca,), (cb,)), ((), ())), preferred_element_type=...  41.2 us
    convert_element_type x18, other arithmetic, plus(): return total.astype(BF)  37 us
    ppermute x50, starting transfers between devices, send(): return lax.ppermute(values, PLANE, plane_pairs(kind))  32.4 us
  transfers between devices with their start and end apart: 60, of which 6 were waited for; matrix products, arithmetic and copies ran while one was open for 20% of the time, Pallas kernels for 30%

profile of v8, /device:TPU:0, one launch (start us, length us, event | category | flops | bytes accessed | tf_op | source)
XLA Modules:
  0.0 668.6 jit_solution(13031525236649353763)
XLA Ops:
  7.2 5.2 all-to-all-start
  18.2 3.9 slice_bitcast_fusion
  29.5 6.4 attend_forward.8
  40.5 6.4 attend_forward.9
  49.2 6.4 attend_forward.10
  62.0 6.6 attend_forward.11
  74.6 3.6 fusion.34
  80.7 3.4 fusion.29
  86.5 3.3 fusion.24
  98.9 4.2 all-to-all-start.2
  113.3 5.0 all-to-all-done.2
  121.4 7.6 %attend_forward.12 = (bf16[512,192]{1,0:T(8,128)(2,1)S(1)}, bf16[512,192]{1,0:T(8,128)(2,1)S(1)}, bf16[512,192]{1,0:T(8,128)(2,1)S(1)}, bf16[512,192]{1,0:T(8,12...) custom-call(bf16[512,768]{1,0:T(8,128)(2,1)S(1)} %get-tuple-element.496.refs_0_.x_ref, ...), custom_call_target="tpu_custom_call" | custom-call | flops 1048576 | bytes 1024 | tf_op jit(solution)/shard_map/attend_forward/pallas_call | solution.py:275
  133.7 4.6 all-to-all-start.1
  139.7 7.6 %attend_forward.13 = (bf16[512,192]{1,0:T(8,128)(2,1)S(1)}, bf16[512,192]{1,0:T(8,128)(2,1)S(1)}, bf16[512,192]{1,0:T(8,128)(2,1)S(1)}, bf16[512,192]{1,0:T(8,12...) custom-call(bf16[512,768]{1,0:T(8,128)(2,1)S(1)} %get-tuple-element.496.refs_0_.x_ref, ...), custom_call_target="tpu_custom_call" | custom-call | flops 1048576 | bytes 1024 | tf_op jit(solution)/shard_map/attend_forward/pallas_call | solution.py:275
  150.9 7.6 %attend_forward.14 = (bf16[512,192]{1,0:T(8,128)(2,1)S(1)}, bf16[512,192]{1,0:T(8,128)(2,1)S(1)}, bf16[512,192]{1,0:T(8,128)(2,1)S(1)}, bf16[512,192]{1,0:T(8,12...) custom-call(bf16[512,768]{1,0:T(8,128)(2,1)S(1)} %get-tuple-element.496.refs_0_.x_ref, ...), custom_call_target="tpu_custom_call" | custom-call | flops 1048576 | bytes 1024 | tf_op jit(solution)/shard_map/attend_forward/pallas_call | solution.py:275
  164.9 6.4 attend_forward.15
  185.2 3.4 fusion.14
  190.9 3.4 fusion.9
  194.3 3.5 add_add_fusion
  197.8 4.2 all-to-all-start.5
  202.7 11.2 %all-to-all-done.5 = bf16[4,128,768]{2,1,0:T(8,128)(2,1)} async-done(((bf16[4,128,768]{2,1,0:T(8,128)(2,1)}), bf16[4,128,768]{2,1,0:T(8,128)(2,1)}, u32[]{:S(2)}, u32[]{:S(2)}) %all-to-all-start.5) | async-done | bytes 786464 | tf_op jit(solution)/shard_map/all_to_all | solution.py:614
  224.8 3.9 fusion.105
  228.7 4.5 all-to-all-start.3
  236.2 16.9 %gather_anchors.1 = bf16[4,8,4,768]{3,2,1,0:T(4,128)(2,1)} custom-call(bf16[4,768]{1,0:T(4,128)(2,1)} %convolution_convert_fusion.refs_0_), custom_call_target="tpu_custom_call" | custom-call | tf_op jit(solution)/shard_map/gather_anchors/pallas_call | solution.py:361
  262.8 6.5 ffn_backward.8
  271.4 8.2 %ffn_backward.9 = (bf16[768,768]{1,0:T(8,128)(2,1)S(1)}, bf16[768,768]{1,0:T(8,128)(2,1)S(1)}, f32[1,768]{1,0:T(1,128)S(1)}, f32[512,768]{1,0:T(8,128)S(1)}) custom-call(bf16[512,768]{1,0:T(8,128)(2,1)S(1)} %convert_element_type.507.dz_ref, bf16[512,768]{1,0:T(8,128)(2,1)S(1)} %copy-done.7, bf16[512,768]{1,0:T(8,128)(2,1)S(1)} %copy-done.89, ...), custom_call_target="tpu_custom_call" | custom-call | flops 1048576 | bytes 1024 | tf_op jit(solution)/shard_map/ffn_backward/pallas_call | solution.py:253
  281.8 8.2 %ffn_backward.10 = (bf16[768,768]{1,0:T(8,128)(2,1)S(1)}, bf16[768,768]{1,0:T(8,128)(2,1)S(1)}, f32[1,768]{1,0:T(1,128)S(1)}, f32[512,768]{1,0:T(8,128)S(1)}) custom-call(bf16[512,768]{1,0:T(8,128)(2,1)S(1)} %convert_element_type.507.dz_ref, bf16[512,768]{1,0:T(8,128)(2,1)S(1)} %copy-done.7, bf16[512,768]{1,0:T(8,128)(2,1)S(1)} %copy-done.48, ...), custom_call_target="tpu_custom_call" | custom-call | flops 1048576 | bytes 1024 | tf_op jit(solution)/shard_map/ffn_backward/pallas_call | solution.py:253
  292.1 6.5 ffn_backward.11
  317.1 10.1 %attend_backward.8 = (bf16[384,768]{1,0:T(8,128)(2,1)S(1)}, bf16[384,768]{1,0:T(8,128)(2,1)}, f32[1,384]{1,0:T(1,128)S(1)}, f32[512,768]{1,0:T(8,128)S(1)}) custom-call(bf16[512,768]{1,0:T(8,128)(2,1)S(1)} %convert_element_type.524.da_ref, bf16[512,768]{1,0:T(8,128)(2,1)S(1)} %get-tuple-element.496.refs_0_.x_ref, ...), custom_call_target="tpu_custom_call" | custom-call | flops 1048576 | bytes 1024 | tf_op jit(solution)/shard_map/attend_backward/pallas_call | solution.py:290
  328.1 9.7 %attend_backward.9 = (bf16[384,768]{1,0:T(8,128)(2,1)S(1)}, bf16[384,768]{1,0:T(8,128)(2,1)S(1)}, f32[1,384]{1,0:T(1,128)S(1)}, f32[512,768]{1,0:T(8,128)S(1)}) custom-call(bf16[512,768]{1,0:T(8,128)(2,1)S(1)} %convert_element_type.524.da_ref, bf16[512,768]{1,0:T(8,128)(2,1)S(1)} %get-tuple-element.496.refs_0_.x_ref, ...), custom_call_target="tpu_custom_call" | custom-call | flops 1048576 | bytes 1024 | tf_op jit(solution)/shard_map/attend_backward/pallas_call | solution.py:290
  340.1 9.4 %attend_backward.10 = (bf16[384,768]{1,0:T(8,128)(2,1)S(1)}, bf16[384,768]{1,0:T(8,128)(2,1)S(1)}, f32[1,384]{1,0:T(1,128)S(1)}, f32[512,768]{1,0:T(8,128)S(1)}) custom-call(bf16[512,768]{1,0:T(8,128)(2,1)S(1)} %convert_element_type.524.da_ref, bf16[512,768]{1,0:T(8,128)(2,1)S(1)} %get-tuple-element.496.refs_0_.x_ref, ...), custom_call_target="tpu_custom_call" | custom-call | flops 1048576 | bytes 1024 | tf_op jit(solution)/shard_map/attend_backward/pallas_call | solution.py:290
  352.0 8.8 %attend_backward.11 = (bf16[384,768]{1,0:T(8,128)(2,1)S(1)}, bf16[384,768]{1,0:T(8,128)(2,1)}, f32[1,384]{1,0:T(1,128)S(1)}, f32[512,768]{1,0:T(8,128)S(1)}) custom-call(bf16[512,768]{1,0:T(8,128)(2,1)S(1)} %convert_element_type.524.da_ref, bf16[512,768]{1,0:T(8,128)(2,1)S(1)} %get-tuple-element.496.refs_0_.x_ref, bf16[384,768]{1,0:T(8,128)(2,1)S(1)} %copy-done.32, ...), custom_call_target="tpu_custom_call" | custom-call | flops 1048576 | bytes 1024 | tf_op jit(solution)/shard_map/attend_backward/pallas_call | solution.py:290
  367.2 4.2 all-to-all-start.4
  379.0 6.1 collective-permute-done.29
  389.4 4.8 multiply_reduce_fusion.2
  402.1 4.2 all-to-all-start.6
  411.1 8.2 %ffn_backward.12 = (bf16[768,768]{1,0:T(8,128)(2,1)S(1)}, bf16[768,768]{1,0:T(8,128)(2,1)S(1)}, f32[1,768]{1,0:T(1,128)S(1)}, f32[512,768]{1,0:T(8,128)S(1)}) custom-call(bf16[512,768]{1,0:T(8,128)(2,1)S(1)} %copy-done.8, bf16[512,768]{1,0:T(8,128)(2,1)S(1)} %copy-done.4, bf16[512,768]{1,0:T(8,128)(2,1)S(1)} %copy-done.79, bf16[512,768]{1,0:T(8,128)(2,1)S(1)} %copy-done.77, ...), custom_call_target="tpu_custom_call" | custom-call | flops 1048576 | bytes 1024 | tf_op jit(solution)/shard_map/ffn_backward/pallas_call | solution.py:253
  422.0 8.2 %ffn_backward.13 = (bf16[768,768]{1,0:T(8,128)(2,1)S(1)}, bf16[768,768]{1,0:T(8,128)(2,1)S(1)}, f32[1,768]{1,0:T(1,128)S(1)}, f32[512,768]{1,0:T(8,128)S(1)}) custom-call(bf16[512,768]{1,0:T(8,128)(2,1)S(1)} %copy-done.8, bf16[512,768]{1,0:T(8,128)(2,1)S(1)} %copy-done.4, bf16[512,768]{1,0:T(8,128)(2,1)S(1)} %copy-done.46, bf16[512,768]{1,0:T(8,128)(2,1)S(1)} %copy-done.76, ...), custom_call_target="tpu_custom_call" | custom-call | flops 1048576 | bytes 1024 | tf_op jit(solution)/shard_map/ffn_backward/pallas_call | solution.py:253
  432.9 8.2 %ffn_backward.14 = (bf16[768,768]{1,0:T(8,128)(2,1)S(1)}, bf16[768,768]{1,0:T(8,128)(2,1)S(1)}, f32[1,768]{1,0:T(1,128)S(1)}, f32[512,768]{1,0:T(8,128)S(1)}) custom-call(bf16[512,768]{1,0:T(8,128)(2,1)S(1)} %copy-done.8, bf16[512,768]{1,0:T(8,128)(2,1)S(1)} %copy-done.4, bf16[512,768]{1,0:T(8,128)(2,1)S(1)} %copy-done.82, bf16[512,768]{1,0:T(8,128)(2,1)S(1)} %copy-done.80, ...), custom_call_target="tpu_custom_call" | custom-call | flops 1048576 | bytes 1024 | tf_op jit(solution)/shard_map/ffn_backward/pallas_call | solution.py:253
  446.7 6.5 ffn_backward.15
  483.9 8.3 %attend_backward.12 = (bf16[384,768]{1,0:T(8,128)(2,1)S(1)}, bf16[384,768]{1,0:T(8,128)(2,1)S(1)}, f32[1,384]{1,0:T(1,128)S(1)}, f32[512,768]{1,0:T(8,128)S(1)}) custom-call(bf16[512,768]{1,0:T(8,128)(2,1)S(1)} %convert_element_type.569.da_ref, bf16[512,768]{1,0:T(8,128)(2,1)S(1)} %bitcast.174, bf16[400,768]{1,0:T(8,128)(2,1)S(1)} %copy-done.20, ...), custom_call_target="tpu_custom_call" | custom-call | flops 1048576 | bytes 1024 | tf_op jit(solution)/shard_map/attend_backward/pallas_call | solution.py:290
  494.0 8.2 %attend_backward.13 = (bf16[384,768]{1,0:T(8,128)(2,1)S(1)}, bf16[384,768]{1,0:T(8,128)(2,1)S(1)}, f32[1,384]{1,0:T(1,128)S(1)}, f32[512,768]{1,0:T(8,128)S(1)}) custom-call(bf16[512,768]{1,0:T(8,128)(2,1)S(1)} %convert_element_type.569.da_ref, bf16[512,768]{1,0:T(8,128)(2,1)S(1)} %bitcast.175, bf16[400,768]{1,0:T(8,128)(2,1)S(1)} %copy-done.18, ...), custom_call_target="tpu_custom_call" | custom-call | flops 1048576 | bytes 1024 | tf_op jit(solution)/shard_map/attend_backward/pallas_call | solution.py:290
  504.5 8.2 %attend_backward.14 = (bf16[384,768]{1,0:T(8,128)(2,1)S(1)}, bf16[384,768]{1,0:T(8,128)(2,1)S(1)}, f32[1,384]{1,0:T(1,128)S(1)}, f32[512,768]{1,0:T(8,128)S(1)}) custom-call(bf16[512,768]{1,0:T(8,128)(2,1)S(1)} %convert_element_type.569.da_ref, bf16[512,768]{1,0:T(8,128)(2,1)S(1)} %bitcast.176, bf16[400,768]{1,0:T(8,128)(2,1)S(1)} %copy-done.50, ...), custom_call_target="tpu_custom_call" | custom-call | flops 1048576 | bytes 1024 | tf_op jit(solution)/shard_map/attend_backward/pallas_call | solution.py:290
  512.7 3.6 add_convert_fusion.1
  523.7 8.2 %attend_backward.15 = (bf16[384,768]{1,0:T(8,128)(2,1)S(1)}, bf16[384,768]{1,0:T(8,128)(2,1)S(1)}, f32[1,384]{1,0:T(1,128)S(1)}, f32[512,768]{1,0:T(8,128)S(1)}) custom-call(bf16[512,768]{1,0:T(8,128)(2,1)S(1)} %convert_element_type.569.da_ref, bf16[512,768]{1,0:T(8,128)(2,1)S(1)} %bitcast.177, bf16[400,768]{1,0:T(8,128)(2,1)S(1)} %copy-done.22, ...), custom_call_target="tpu_custom_call" | custom-call | flops 1048576 | bytes 1024 | tf_op jit(solution)/shard_map/attend_backward/pallas_call | solution.py:290
  533.1 3.8 all-to-all-start.7
  540.6 7.6 %all-to-all-done.7 = bf16[4,128,768]{2,1,0:T(8,128)(2,1)S(1)} async-done(((bf16[4,128,768]{2,1,0:T(8,128)(2,1)}), bf16[4,128,768]{2,1,0:T(8,128)(2,1)S(1)}, u32[]{:S(2)}, u32[]{:S(2)}) %all-to-all-start.7) | async-done | bytes 786464 | tf_op jit(solution)/shard_map/all_to_all | solution.py:621
  552.8 73.8 %last_sums.1 = (bf16[2,4,96,768]{3,2,1,0:T(8,128)(2,1)S(1)}, bf16[2,4,96,768]{3,2,1,0:T(8,128)(2,1)S(1)}, bf16[2,4,48,768]{3,2,1,0:T(8,128)(2,1)S(1)}, bf16[2,4,...) custom-call(bf16[2,4,96,768]{3,2,1,0:T(8,128)(2,1)S(1)} %bitcast.178, bf16[2,4,48,768]{3,2,1,0:T(8,128)(2,1)S(1)} %bitcast.179, ...), custom_call_target="tpu_custom_call" | custom-call | tf_op jit(solution)/shard_map/last_sums/pallas_call | solution.py:591
  (883 shorter events, 269.6 us)
Async XLA Ops:
  7.2 22.1 %all-to-all-start = ((bf16[4,128,768]{2,1,0:T(8,128)(2,1)}), bf16[4,128,768]{2,1,0:T(8,128)(2,1)S(1)}, u32[]{:S(2)}, u32[]{:S(2)}) async-start(bf16[4,128,768]{2,1,0:T(8,128)(2,1)} %bitcast.200), calls=%async_computation | async-start | bytes 1572864 | tf_op jit(solution)/shard_map/all_to_all | solution.py:614
  16.0 19.9 %collective-permute-start = (bf16[400,768]{1,0:T(8,128)(2,1)S(1)}, bf16[400,768]{1,0:T(8,128)(2,1)S(1)}, u32[]{:S(2)}, u32[]{:S(2)}) collective-permute-start(bf16[400,768]{1,0:T(8,128)(2,1)S(1)} %pad_maximum_fusion.2.refs_1_.first_ref), channel_id=1, source_target_pairs={{0,1},{1,0},{2,3},{3,2},{4,6},{5,7},{6,4},{7,5},{8,9},{9,8},{10,11... | collective-permute-start | bytes 1843208 | tf_op jit(solution)/shard_map/ppermute | solution.py:62
  18.1 18.3 %collective-permute-start.1 = (bf16[400,768]{1,0:T(8,128)(2,1)S(1)}, bf16[400,768]{1,0:T(8,128)(2,1)S(1)}, u32[]{:S(2)}, u32[]{:S(2)}) collective-permute-start(bf16[400,768]{1,0:T(8,128)(2,1)S(1)} %fusion.54.refs_2_.second_ref), channel_id=1, source_target_pairs={{0,1},{1,0},{2,3},{3,2},{4,6},{5,7},{6,4},{7,5},{8,9},{9,8},{10,11... | collective-permute-start | bytes 1843208 | tf_op jit(solution)/shard_map/ppermute | solution.py:62
  22.1 46.6 %collective-permute-start.6 = (bf16[768,768]{1,0:T(8,128)(2,1)}, bf16[768,768]{1,0:T(8,128)(2,1)}, u32[]{:S(2)}, u32[]{:S(2)}) collective-permute-start(bf16[768,768]{1,0:T(8,128)(2,1)} %get-tuple-element.239.first_ref), channel_id=1, source_target_pairs={{0,1},{1,0},{2,3},{3,2},{4,6},{5,7},{6,4},{7,5},{8,9},{9,8},{10,11... | collective-permute-start | bytes 3538952 | tf_op jit(solution)/shard_map/ppermute | solution.py:62
  24.0 44.6 %collective-permute-start.7 = (bf16[768,768]{1,0:T(8,128)(2,1)}, bf16[768,768]{1,0:T(8,128)(2,1)}, u32[]{:S(2)}, u32[]{:S(2)}) collective-permute-start(bf16[768,768]{1,0:T(8,128)(2,1)} %get-tuple-element.240.second_ref), channel_id=1, source_target_pairs={{0,1},{1,0},{2,3},{3,2},{4,6},{5,7},{6,4},{7,5},{8,9},{9,8},{10,11... | collective-permute-start | bytes 3538952 | tf_op jit(solution)/shard_map/ppermute | solution.py:62
  36.4 12.7 %collective-permute-start.2 = (bf16[400,768]{1,0:T(8,128)(2,1)S(1)}, bf16[400,768]{1,0:T(8,128)(2,1)S(1)}, u32[]{:S(2)}, u32[]{:S(2)}) collective-permute-start(bf16[400,768]{1,0:T(8,128)(2,1)S(1)} %collective-permute-done.refs_1_.first_ref), channel_id=1, source_target_pairs={{0,4},{1,5},{2,6},{3,7},{4,0},{5,1},{6,2},{7,3},{8,12},{9,13},{10,... | collective-permute-start | bytes 1843208 | tf_op jit(solution)/shard_map/ppermute | solution.py:62
  36.5 12.7 %collective-permute-start.3 = (bf16[400,768]{1,0:T(8,128)(2,1)S(1)}, bf16[400,768]{1,0:T(8,128)(2,1)S(1)}, u32[]{:S(2)}, u32[]{:S(2)}) collective-permute-start(bf16[400,768]{1,0:T(8,128)(2,1)S(1)} %collective-permute-done.1.refs_2_.second_ref), channel_id=1, source_target_pairs={{0,4},{1,5},{2,6},{3,7},{4,0},{5,1},{6,2},{7,3},{8,12},{9,13},{10,... | collective-permute-start | bytes 1843208 | tf_op jit(solution)/shard_map/ppermute | solution.py:62
  37.0 20.0 %collective-permute-start.4 = (bf16[400,768]{1,0:T(8,128)(2,1)S(1)}, bf16[400,768]{1,0:T(8,128)(2,1)S(1)}, u32[]{:S(2)}, u32[]{:S(2)}) collective-permute-start(bf16[400,768]{1,0:T(8,128)(2,1)S(1)} %broadcast_select_fusion.10), channel_id=1, source_target_pairs={{0,2},{1,3},{2,0},{3,1},{4,5},{5,4},{6,7},{7,6},{8,10},{9,11},{10,... | collective-permute-start | bytes 1843208 | tf_op jit(solution)/shard_map/ppermute | solution.py:62
  58.5 27.9 %collective-permute-start.8 = (bf16[384,768]{1,0:T(8,128)(2,1)}, bf16[384,768]{1,0:T(8,128)(2,1)}, u32[]{:S(2)}, u32[]{:S(2)}) collective-permute-start(bf16[384,768]{1,0:T(8,128)(2,1)} %bitcast.16.refs_1_.first_ref), channel_id=1, source_target_pairs={{0,1},{1,0},{2,3},{3,2},{4,6},{5,7},{6,4},{7,5},{8,9},{9,8},{10,11... | collective-permute-start | bytes 1769480 | tf_op jit(solution)/shard_map/ppermute | solution.py:62
  60.0 26.4 %collective-permute-start.9 = (bf16[384,768]{1,0:T(8,128)(2,1)}, bf16[384,768]{1,0:T(8,128)(2,1)}, u32[]{:S(2)}, u32[]{:S(2)}) collective-permute-start(bf16[384,768]{1,0:T(8,128)(2,1)} %pad_maximum_fusion.3.refs_2_.second_ref), channel_id=1, source_target_pairs={{0,1},{1,0},{2,3},{3,2},{4,6},{5,7},{6,4},{7,5},{8,9},{9,8},{10,11... | collective-permute-start | bytes 1769480 | tf_op jit(solution)/shard_map/ppermute | solution.py:62
  68.7 17.8 %collective-permute-start.10 = (bf16[768,768]{1,0:T(8,128)(2,1)}, bf16[768,768]{1,0:T(8,128)(2,1)}, u32[]{:S(2)}, u32[]{:S(2)}) collective-permute-start(bf16[768,768]{1,0:T(8,128)(2,1)} %collective-permute-done.6.first_ref), channel_id=1, source_target_pairs={{0,4},{1,5},{2,6},{3,7},{4,0},{5,1},{6,2},{7,3},{8,12},{9,13},{10,... | collective-permute-start | bytes 3538952 | tf_op jit(solution)/shard_map/ppermute | solution.py:62
  71.5 18.3 %collective-permute-start.11 = (bf16[768,768]{1,0:T(8,128)(2,1)}, bf16[768,768]{1,0:T(8,128)(2,1)}, u32[]{:S(2)}, u32[]{:S(2)}) collective-permute-start(bf16[768,768]{1,0:T(8,128)(2,1)} %collective-permute-done.7.second_ref), channel_id=1, source_target_pairs={{0,4},{1,5},{2,6},{3,7},{4,0},{5,1},{6,2},{7,3},{8,12},{9,13},{10,... | collective-permute-start | bytes 3538952 | tf_op jit(solution)/shard_map/ppermute | solution.py:62
  73.2 20.9 %collective-permute-start.12 = (bf16[768,768]{1,0:T(8,128)(2,1)S(1)}, bf16[768,768]{1,0:T(8,128)(2,1)}, u32[]{:S(2)}, u32[]{:S(2)}) collective-permute-start(bf16[768,768]{1,0:T(8,128)(2,1)S(1)} %copy-done.248), channel_id=1, source_target_pairs={{0,2},{1,3},{2,0},{3,1},{4,5},{5,4},{6,7},{7,6},{8,10},{9,11},{10,... | collective-permute-start | bytes 3538952 | tf_op jit(solution)/shard_map/ppermute | solution.py:62
  94.1 11.8 %collective-permute-start.13 = (bf16[768,768]{1,0:T(8,128)(2,1)}, bf16[768,768]{1,0:T(8,128)(2,1)}, u32[]{:S(2)}, u32[]{:S(2)}) collective-permute-start(bf16[768,768]{1,0:T(8,128)(2,1)} %collective-permute-done.12), channel_id=1, source_target_pairs={{0,4},{1,5},{2,6},{3,7},{4,0},{5,1},{6,2},{7,3},{8,12},{9,13},{10,... | collective-permute-start | bytes 3538952 | tf_op jit(solution)/shard_map/ppermute | solution.py:62
  95.3 55.6 %collective-permute-start.16 = (bf16[384,768]{1,0:T(8,128)(2,1)}, bf16[384,768]{1,0:T(8,128)(2,1)}, u32[]{:S(2)}, u32[]{:S(2)}) collective-permute-start(bf16[384,768]{1,0:T(8,128)(2,1)} %collective-permute-done.8.refs_1_.first_ref), channel_id=1, source_target_pairs={{0,4},{1,5},{2,6},{3,7},{4,0},{5,1},{6,2},{7,3},{8,12},{9,13},{10,... | collective-permute-start | bytes 1769480 | tf_op jit(solution)/shard_map/ppermute | solution.py:62
  95.4 55.4 %collective-permute-start.17 = (bf16[384,768]{1,0:T(8,128)(2,1)}, bf16[384,768]{1,0:T(8,128)(2,1)}, u32[]{:S(2)}, u32[]{:S(2)}) collective-permute-start(bf16[384,768]{1,0:T(8,128)(2,1)} %collective-permute-done.9.refs_2_.second_ref), channel_id=1, source_target_pairs={{0,4},{1,5},{2,6},{3,7},{4,0},{5,1},{6,2},{7,3},{8,12},{9,13},{10,... | collective-permute-start | bytes 1769480 | tf_op jit(solution)/shard_map/ppermute | solution.py:62
  97.8 53.1 %collective-permute-start.14 = (bf16[384,768]{1,0:T(8,128)(2,1)}, bf16[384,768]{1,0:T(8,128)(2,1)}, u32[]{:S(2)}, u32[]{:S(2)}) collective-permute-start(bf16[384,768]{1,0:T(8,128)(2,1)} %broadcast_select_fusion.13), channel_id=1, source_target_pairs={{0,2},{1,3},{2,0},{3,1},{4,5},{5,4},{6,7},{7,6},{8,10},{9,11},{10,... | collective-permute-start | bytes 1769480 | tf_op jit(solution)/shard_map/ppermute | solution.py:62
  98.9 19.5 %all-to-all-start.2 = ((bf16[4,128,768]{2,1,0:T(8,128)(2,1)}), bf16[4,128,768]{2,1,0:T(8,128)(2,1)}, u32[]{:S(2)}, u32[]{:S(2)}) async-start(bf16[4,128,768]{2,1,0:T(8,128)(2,1)} %bitcast.201), calls=%async_computation.2 | async-start | bytes 1572864 | tf_op jit(solution)/shard_map/all_to_all | solution.py:614
  103.1 68.3 %collective-permute-start.18 = (bf16[768,768]{1,0:T(8,128)(2,1)}, bf16[768,768]{1,0:T(8,128)(2,1)}, u32[]{:S(2)}, u32[]{:S(2)}) collective-permute-start(bf16[768,768]{1,0:T(8,128)(2,1)} %get-tuple-element.262.first_ref), channel_id=1, source_target_pairs={{0,1},{1,0},{2,3},{3,2},{4,6},{5,7},{6,4},{7,5},{8,9},{9,8},{10,11... | collective-permute-start | bytes 3538952 | tf_op jit(solution)/shard_map/ppermute | solution.py:62
  105.9 65.5 %collective-permute-start.19 = (bf16[768,768]{1,0:T(8,128)(2,1)}, bf16[768,768]{1,0:T(8,128)(2,1)}, u32[]{:S(2)}, u32[]{:S(2)}) collective-permute-start(bf16[768,768]{1,0:T(8,128)(2,1)} %get-tuple-element.263.second_ref), channel_id=1, source_target_pairs={{0,1},{1,0},{2,3},{3,2},{4,6},{5,7},{6,4},{7,5},{8,9},{9,8},{10,11... | collective-permute-start | bytes 3538952 | tf_op jit(solution)/shard_map/ppermute | solution.py:62
  133.7 29.5 %all-to-all-start.1 = ((bf16[4,128,768]{2,1,0:T(8,128)(2,1)}), bf16[4,128,768]{2,1,0:T(8,128)(2,1)}, u32[]{:S(2)}, u32[]{:S(2)}) async-start(bf16[4,128,768]{2,1,0:T(8,128)(2,1)} %bitcast.192), calls=%async_computation.1 | async-start | bytes 1572864 | tf_op jit(solution)/shard_map/all_to_all | solution.py:621
  150.9 12.3 %collective-permute-start.15 = (bf16[384,768]{1,0:T(8,128)(2,1)}, bf16[384,768]{1,0:T(8,128)(2,1)}, u32[]{:S(2)}, u32[]{:S(2)}) collective-permute-start(bf16[384,768]{1,0:T(8,128)(2,1)} %collective-permute-done.14), channel_id=1, source_target_pairs={{0,4},{1,5},{2,6},{3,7},{4,0},{5,1},{6,2},{7,3},{8,12},{9,13},{10,... | collective-permute-start | bytes 1769480 | tf_op jit(solution)/shard_map/ppermute | solution.py:62
  171.4 19.5 %collective-permute-start.20 = (bf16[768,768]{1,0:T(8,128)(2,1)}, bf16[768,768]{1,0:T(8,128)(2,1)}, u32[]{:S(2)}, u32[]{:S(2)}) collective-permute-start(bf16[768,768]{1,0:T(8,128)(2,1)} %collective-permute-done.18.first_ref), channel_id=1, source_target_pairs={{0,4},{1,5},{2,6},{3,7},{4,0},{5,1},{6,2},{7,3},{8,12},{9,13},{10,... | collective-permute-start | bytes 3538952 | tf_op jit(solution)/shard_map/ppermute | solution.py:62
  174.8 19.5 %collective-permute-start.21 = (bf16[768,768]{1,0:T(8,128)(2,1)}, bf16[768,768]{1,0:T(8,128)(2,1)}, u32[]{:S(2)}, u32[]{:S(2)}) collective-permute-start(bf16[768,768]{1,0:T(8,128)(2,1)} %collective-permute-done.19.second_ref), channel_id=1, source_target_pairs={{0,4},{1,5},{2,6},{3,7},{4,0},{5,1},{6,2},{7,3},{8,12},{9,13},{10,... | collective-permute-start | bytes 3538952 | tf_op jit(solution)/shard_map/ppermute | solution.py:62
  175.4 22.4 %collective-permute-start.22 = (bf16[768,768]{1,0:T(8,128)(2,1)}, bf16[768,768]{1,0:T(8,128)(2,1)}, u32[]{:S(2)}, u32[]{:S(2)}) collective-permute-start(bf16[768,768]{1,0:T(8,128)(2,1)} %broadcast_select_fusion.4), channel_id=1, source_target_pairs={{0,2},{1,3},{2,0},{3,1},{4,5},{5,4},{6,7},{7,6},{8,10},{9,11},{10,... | collective-permute-start | bytes 3538952 | tf_op jit(solution)/shard_map/ppermute | solution.py:62
  197.8 18.2 %collective-permute-start.23 = (bf16[768,768]{1,0:T(8,128)(2,1)}, bf16[768,768]{1,0:T(8,128)(2,1)}, u32[]{:S(2)}, u32[]{:S(2)}) collective-permute-start(bf16[768,768]{1,0:T(8,128)(2,1)} %collective-permute-done.22), channel_id=1, source_target_pairs={{0,4},{1,5},{2,6},{3,7},{4,0},{5,1},{6,2},{7,3},{8,12},{9,13},{10,... | collective-permute-start | bytes 3538952 | tf_op jit(solution)/shard_map/ppermute | solution.py:62
  197.8 16.0 %all-to-all-start.5 = ((bf16[4,128,768]{2,1,0:T(8,128)(2,1)}), bf16[4,128,768]{2,1,0:T(8,128)(2,1)}, u32[]{:S(2)}, u32[]{:S(2)}) async-start(bf16[4,128,768]{2,1,0:T(8,128)(2,1)} %bitcast.202), calls=%async_computation.5 | async-start | bytes 1572864 | tf_op jit(solution)/shard_map/all_to_all | solution.py:614
  228.7 73.1 %all-to-all-start.3 = ((bf16[4,128,768]{2,1,0:T(8,128)(2,1)}), bf16[4,128,768]{2,1,0:T(8,128)(2,1)}, u32[]{:S(2)}, u32[]{:S(2)}) async-start(bf16[4,128,768]{2,1,0:T(8,128)(2,1)} %bitcast.189), calls=%async_computation.3 | async-start | bytes 1572864 | tf_op jit(solution)/shard_map/all_to_all | solution.py:621
  313.6 36.0 %collective-permute-start.28 = (bf16[768,768]{1,0:T(8,128)(2,1)S(1)}, bf16[768,768]{1,0:T(8,128)(2,1)S(1)}, u32[]{:S(2)}, u32[]{:S(2)}) collective-permute-start(bf16[768,768]{1,0:T(8,128)(2,1)S(1)} %add_convert_fusion.9), channel_id=1, source_target_pairs={{0,2},{1,3},{2,0},{3,1},{4,5},{5,4},{6,7},{7,6},{8,10},{9,11},{10,... | collective-permute-start | bytes 3538952 | tf_op jit(solution)/shard_map/ppermute | solution.py:62
  314.8 50.8 %collective-permute-start.30 = (bf16[768,768]{1,0:T(8,128)(2,1)}, bf16[768,768]{1,0:T(8,128)(2,1)}, u32[]{:S(2)}, u32[]{:S(2)}) collective-permute-start(bf16[768,768]{1,0:T(8,128)(2,1)} %add_convert_fusion.11), channel_id=1, source_target_pairs={{0,1},{1,0},{2,3},{3,2},{4,6},{5,7},{6,4},{7,5},{8,9},{9,8},{10,11... | collective-permute-start | bytes 3538952 | tf_op jit(solution)/shard_map/ppermute | solution.py:62
  364.3 20.8 %collective-permute-start.29 = (bf16[768,768]{1,0:T(8,128)(2,1)}, bf16[768,768]{1,0:T(8,128)(2,1)}, u32[]{:S(2)}, u32[]{:S(2)}) collective-permute-start(bf16[768,768]{1,0:T(8,128)(2,1)} %add_convert_fusion.7), channel_id=1, source_target_pairs={{0,1},{1,0},{2,3},{3,2},{4,6},{5,7},{6,4},{7,5},{8,9},{9,8},{10,11... | collective-permute-start | bytes 3538952 | tf_op jit(solution)/shard_map/ppermute | solution.py:62
  365.6 19.5 %collective-permute-start.31 = (bf16[768,768]{1,0:T(8,128)(2,1)}, bf16[768,768]{1,0:T(8,128)(2,1)}, u32[]{:S(2)}, u32[]{:S(2)}) collective-permute-start(bf16[768,768]{1,0:T(8,128)(2,1)} %collective-permute-done.30), channel_id=1, source_target_pairs={{0,4},{1,5},{2,6},{3,7},{4,0},{5,1},{6,2},{7,3},{8,12},{9,13},{10,... | collective-permute-start | bytes 3538952 | tf_op jit(solution)/shard_map/ppermute | solution.py:62
  367.2 22.2 %all-to-all-start.4 = ((bf16[4,128,768]{2,1,0:T(8,128)(2,1)}), bf16[4,128,768]{2,1,0:T(8,128)(2,1)}, u32[]{:S(2)}, u32[]{:S(2)}) async-start(bf16[4,128,768]{2,1,0:T(8,128)(2,1)} %bitcast.203), calls=%async_computation.4 | async-start | bytes 1572864 | tf_op jit(solution)/shard_map/all_to_all | solution.py:614
  371.4 88.6 %all-reduce.5.cloned.1.call-start = ((), (), s32[]{:S(2)}) async-start(), calls=%async_computation.8 | async-start | bytes 2359296 | tf_op jit(solution)/shard_map/psum | solution.py:868
  395.8 46.4 %collective-permute-start.36 = (bf16[384,768]{1,0:T(8,128)(2,1)}, bf16[384,768]{1,0:T(8,128)(2,1)}, u32[]{:S(2)}, u32[]{:S(2)}) collective-permute-start(bf16[384,768]{1,0:T(8,128)(2,1)} %add_convert_fusion.15), channel_id=1, source_target_pairs={{0,2},{1,3},{2,0},{3,1},{4,5},{5,4},{6,7},{7,6},{8,10},{9,11},{10,... | collective-permute-start | bytes 1769480 | tf_op jit(solution)/shard_map/ppermute | solution.py:62
  397.3 49.3 %collective-permute-start.38 = (bf16[384,768]{1,0:T(8,128)(2,1)}, bf16[384,768]{1,0:T(8,128)(2,1)}, u32[]{:S(2)}, u32[]{:S(2)}) collective-permute-start(bf16[384,768]{1,0:T(8,128)(2,1)} %add_convert_fusion.17), channel_id=1, source_target_pairs={{0,1},{1,0},{2,3},{3,2},{4,6},{5,7},{6,4},{7,5},{8,9},{9,8},{10,11... | collective-permute-start | bytes 1769480 | tf_op jit(solution)/shard_map/ppermute | solution.py:62
  402.1 54.3 %all-to-all-start.6 = ((bf16[4,128,768]{2,1,0:T(8,128)(2,1)}), bf16[4,128,768]{2,1,0:T(8,128)(2,1)}, u32[]{:S(2)}, u32[]{:S(2)}) async-start(bf16[4,128,768]{2,1,0:T(8,128)(2,1)} %bitcast.190), calls=%async_computation.6 | async-start | bytes 1572864 | tf_op jit(solution)/shard_map/all_to_all | solution.py:621
  406.2 111.7 %all-reduce.7.cloned.1.call-start = ((), (), s32[]{:S(2)}) async-start(), calls=%async_computation.9 | async-start | bytes 1179648 | tf_op jit(solution)/shard_map/psum | solution.py:885
  444.7 12.7 %collective-permute-start.37 = (bf16[384,768]{1,0:T(8,128)(2,1)}, bf16[384,768]{1,0:T(8,128)(2,1)}, u32[]{:S(2)}, u32[]{:S(2)}) collective-permute-start(bf16[384,768]{1,0:T(8,128)(2,1)} %add_convert_fusion.13), channel_id=1, source_target_pairs={{0,1},{1,0},{2,3},{3,2},{4,6},{5,7},{6,4},{7,5},{8,9},{9,8},{10,11... | collective-permute-start | bytes 1769480 | tf_op jit(solution)/shard_map/ppermute | solution.py:62
  457.0 12.4 %collective-permute-start.41 = (bf16[768,768]{1,0:T(8,128)(2,1)}, bf16[768,768]{1,0:T(8,128)(2,1)}, u32[]{:S(2)}, u32[]{:S(2)}) collective-permute-start(bf16[768,768]{1,0:T(8,128)(2,1)} %copy-done.227), channel_id=1, source_target_pairs={{0,4},{1,5},{2,6},{3,7},{4,0},{5,1},{6,2},{7,3},{8,12},{9,13},{10,... | collective-permute-start | bytes 3538952 | tf_op jit(solution)/shard_map/ppermute | solution.py:62
  457.4 14.7 %collective-permute-start.40 = (bf16[768,768]{1,0:T(8,128)(2,1)}, bf16[768,768]{1,0:T(8,128)(2,1)}, u32[]{:S(2)}, u32[]{:S(2)}) collective-permute-start(bf16[768,768]{1,0:T(8,128)(2,1)} %copy-done.226), channel_id=1, source_target_pairs={{0,4},{1,5},{2,6},{3,7},{4,0},{5,1},{6,2},{7,3},{8,12},{9,13},{10,... | collective-permute-start | bytes 3538952 | tf_op jit(solution)/shard_map/ppermute | solution.py:62
  474.8 37.9 %collective-permute-start.44 = (bf16[768,768]{1,0:T(8,128)(2,1)}, bf16[768,768]{1,0:T(8,128)(2,1)}, u32[]{:S(2)}, u32[]{:S(2)}) collective-permute-start(bf16[768,768]{1,0:T(8,128)(2,1)} %add_convert_fusion.3), channel_id=1, source_target_pairs={{0,2},{1,3},{2,0},{3,1},{4,5},{5,4},{6,7},{7,6},{8,10},{9,11},{10,... | collective-permute-start | bytes 3538952 | tf_op jit(solution)/shard_map/ppermute | solution.py:62
  476.3 41.6 %collective-permute-start.46 = (bf16[768,768]{1,0:T(8,128)(2,1)}, bf16[768,768]{1,0:T(8,128)(2,1)}, u32[]{:S(2)}, u32[]{:S(2)}) collective-permute-start(bf16[768,768]{1,0:T(8,128)(2,1)} %add_convert_fusion.5), channel_id=1, source_target_pairs={{0,1},{1,0},{2,3},{3,2},{4,6},{5,7},{6,4},{7,5},{8,9},{9,8},{10,11... | collective-permute-start | bytes 3538952 | tf_op jit(solution)/shard_map/ppermute | solution.py:62
  516.4 32.1 %collective-permute-start.45 = (bf16[768,768]{1,0:T(8,128)(2,1)}, bf16[768,768]{1,0:T(8,128)(2,1)}, u32[]{:S(2)}, u32[]{:S(2)}) collective-permute-start(bf16[768,768]{1,0:T(8,128)(2,1)} %add_convert_fusion.1), channel_id=1, source_target_pairs={{0,1},{1,0},{2,3},{3,2},{4,6},{5,7},{6,4},{7,5},{8,9},{9,8},{10,11... | collective-permute-start | bytes 3538952 | tf_op jit(solution)/shard_map/ppermute | solution.py:62
  517.9 30.6 %collective-permute-start.47 = (bf16[768,768]{1,0:T(8,128)(2,1)}, bf16[768,768]{1,0:T(8,128)(2,1)}, u32[]{:S(2)}, u32[]{:S(2)}) collective-permute-start(bf16[768,768]{1,0:T(8,128)(2,1)} %collective-permute-done.46), channel_id=1, source_target_pairs={{0,4},{1,5},{2,6},{3,7},{4,0},{5,1},{6,2},{7,3},{8,12},{9,13},{10,... | collective-permute-start | bytes 3538952 | tf_op jit(solution)/shard_map/ppermute | solution.py:62
  517.9 33.0 %collective-permute-start.48 = (bf16[768,768]{1,0:T(8,128)(2,1)}, bf16[768,768]{1,0:T(8,128)(2,1)}, u32[]{:S(2)}, u32[]{:S(2)}) collective-permute-start(bf16[768,768]{1,0:T(8,128)(2,1)} %all-reduce.5.cloned.1.call-done), channel_id=1, source_target_pairs={{0,4},{1,5},{2,6},{3,7},{4,0},{5,1},{6,2},{7,3},{8,12},{9,13},{10,... | collective-permute-start | bytes 3538952 | tf_op jit(solution)/shard_map/ppermute | solution.py:62
  533.1 15.1 %all-to-all-start.7 = ((bf16[4,128,768]{2,1,0:T(8,128)(2,1)}), bf16[4,128,768]{2,1,0:T(8,128)(2,1)S(1)}, u32[]{:S(2)}, u32[]{:S(2)}) async-start(bf16[4,128,768]{2,1,0:T(8,128)(2,1)} %bitcast.41), calls=%async_computation.7 | async-start | bytes 1572864 | tf_op jit(solution)/shard_map/all_to_all | solution.py:621
  537.1 13.8 %collective-permute-start.49 = (bf16[384,768]{1,0:T(8,128)(2,1)S(1)}, bf16[384,768]{1,0:T(8,128)(2,1)S(1)}, u32[]{:S(2)}, u32[]{:S(2)}) collective-permute-start(bf16[384,768]{1,0:T(8,128)(2,1)S(1)} %copy-done.250), channel_id=1, source_target_pairs={{0,4},{1,5},{2,6},{3,7},{4,0},{5,1},{6,2},{7,3},{8,12},{9,13},{10,... | collective-permute-start | bytes 1769480 | tf_op jit(solution)/shard_map/ppermute | solution.py:62
  (311 other events, 1860.3 us)
Sparse Core Ops, SparseCore 0:
  398.6 54.3 all-reduce.4
  477.0 38.4 all-reduce.6

commit v9 on v8

--- a/solution.py
+++ b/solution.py
@@ -249,20 +249,100 @@
     lax.fori_loop(0, model // Q_ROWS, weights, 0)
 
 
-def ffn_block_backward(dzb, yb, act, slope, first, second, dy):
-    return pl.pallas_call(
-        ffn_backward_kernel,
-        name="ffn_backward",
-        out_shape=(
-            jax.ShapeDtypeStruct(first.shape, BF),
-            jax.ShapeDtypeStruct(first.shape, BF),
-            jax.ShapeDtypeStruct((1, act.shape[1]), F32),
-            jax.ShapeDtypeStruct(dy.shape, F32),
-        ),
-        scratch_shapes=[pltpu.VMEM(act.shape, BF)],
-        compiler_params=kernel_params(),
+def streamed_blocks(name, body, shared, total, blocks, big, small, scratch):
+    count, takes, gives = len(blocks), len(blocks[0]), len(big)
+    vmem, anywhere = pl.BlockSpec(memory_space=pltpu.VMEM), pl.BlockSpec(memory_space=pl.ANY)
+    dma = pltpu.SemaphoreType.DMA
+
+    def kernel(*refs):
+        refs = list(refs)
+
+        def take(n):
+            taken = refs[:n]
+            del refs[:n]
+            return taken
+
+        shared_refs, (total_ref,), ins = take(len(shared)), take(1), take(count * takes)
+        (out_ref,), smalls, outs = take(1), take(count), take(count * gives)
+        in_bufs, out_bufs, (in_sems, out_sems), extra = take(takes), take(gives), take(2), take(len(scratch))
+
+        def fetch(j):
+            return [
+                pltpu.make_async_copy(ins[j * takes + i], in_bufs[i].at[j % 2], in_sems.at[j % 2, i])
+                for i in range(takes)
+            ]
+
+        def put(j):
+            return [
+                pltpu.make_async_copy(out_bufs[i].at[j % 2], outs[j * gives + i], out_sems.at[j % 2, i])
+                for i in range(gives)
+            ]
+
+        for copy in fetch(0):
+            copy.start()
+        for j in range(count):
+            if j + 1 < count:
+                for copy in fetch(j + 1):
+                    copy.start()
+            for copy in fetch(j):
+                copy.wait()
+            if j >= 2:
+                for copy in put(j - 2):
+                    copy.wait()
+            body(
+                shared_refs, total_ref if j == 0 else out_ref, [r.at[j % 2] for r in in_bufs],
+                [r.at[j % 2] for r in out_bufs], smalls[j], out_ref, extra,
+            )
+            for copy in put(j):
+                copy.start()
+        for j in range(max(0, count - 2), count):
+            for copy in put(j):
+                copy.wait()
+
+    out = pl.pallas_call(
+        kernel,
+        name=name,
+        out_shape=(jax.ShapeDtypeStruct(total.shape, F32),)
+        + (jax.ShapeDtypeStruct(small, F32),) * count
+        + tuple(jax.ShapeDtypeStruct(shape, BF) for shape in big) * count,
+        in_specs=[vmem] * (len(shared) + 1) + [anywhere] * (count * takes),
+        out_specs=(vmem,) * (1 + count) + (anywhere,) * (count * gives),
+        scratch_shapes=[pltpu.VMEM((2,) + x.shape, x.dtype) for x in blocks[0]]
+        + [pltpu.VMEM((2,) + shape, BF) for shape in big]
+        + [dma((2, takes)), dma((2, gives))]
+        + list(scratch),
+        compiler_params=pltpu.CompilerParams(vmem_limit_bytes=28 << 20),
         cost_estimate=small_cost(),
-    )(dzb, yb, act, slope, first, second, dy)
+    )(*shared, total, *[x for block in blocks for x in block])
+    smalls, bigs = out[1 : 1 + count], out[1 + count :]
+    return out[0], smalls, [tuple(bigs[j * gives : (j + 1) * gives]) for j in range(count)]
+
+
+def ffn_blocks_backward(dzb, yb, dy, blocks):
+    def body(shared, total, ins, outs, small, out, extra):
+        ffn_backward_kernel(*shared, *ins, total, *outs, small, out, *extra)
+
+    first = blocks[0][2].shape
+    act = blocks[0][0].shape
+    return streamed_blocks(
+        "ffn_backward", body, (dzb, yb), dy, blocks, (first, first), (1, act[1]), [pltpu.VMEM(act, BF)]
+    )
+
+
+def attend_blocks_backward(cols, da, x, dx, blocks, seg):
+    tokens, model = x.shape
+
+    def body(shared, total, ins, outs, small, out, extra):
+        da_ref, x_ref, down_ref, across_ref = shared
+        attend_backward_kernel(
+            da_ref, x_ref, *ins, total, down_ref, across_ref, *outs, small, out, *extra
+        )
+
+    grad = (2 * cols, model)
+    scratch = [pltpu.VMEM((tokens, cols), kind) for kind in (BF, BF, F32, F32)]
+    return streamed_blocks(
+        "attend_backward", body, (da, x, *seg), dx, blocks, (grad, grad), (1, 2 * cols), scratch
+    )
 
 
 def attend_forward(layer, cols, x, first, second, bias, z, seg):
@@ -283,26 +363,6 @@
         compiler_params=kernel_params(),
         cost_estimate=small_cost(),
     )(x, first, second, bias, z, *seg)
-
-
-def attend_backward(cols, da, x, first, second, kept, dx, seg):
-    tokens, model = x.shape
-    return pl.pallas_call(
-        attend_backward_kernel,
-        name="attend_backward",
-        out_shape=(
-            jax.ShapeDtypeStruct((2 * cols, model), BF),
-            jax.ShapeDtypeStruct((2 * cols, model), BF),
-            jax.ShapeDtypeStruct((1, 2 * cols), F32),
-            jax.ShapeDtypeStruct(dx.shape, F32),
-        ),
-        scratch_shapes=[
-            pltpu.VMEM((tokens, cols), BF), pltpu.VMEM((tokens, cols), BF),
-            pltpu.VMEM((tokens, cols), F32), pltpu.VMEM((tokens, cols), F32),
-        ],
-        compiler_params=kernel_params(),
-        cost_estimate=small_cost(),
-    )(da, x, first, second, *kept, dx, *seg)
 
 
 def anchors_kernel(dps, planes, x_ref, out_ref, near_send, near_recv, far_send, far_recv, own_sem):
@@ -651,7 +711,7 @@
     return jnp.sum(values, axis=0)
 
 
-def ffn_backward(dout, ffn_w, vec, kept, hook):
+def ffn_backward(dout, ffn_w, vec, kept, hook, cut):
     xb, saved, n1, r1, yb, act, slope, n2, r2 = kept
     dz2 = normal_back(dout, n2, r2, vec["g1"])
     small = {"g1": total_rows(dout * n2), "s1": total_rows(dout), "sb": total_rows(dz2), "eb": []}
@@ -659,11 +719,14 @@
     dzb = dz2.astype(BF)
     dy = dz2
     blocks = []
-    for j, (first, second) in enumerate(ffn_w):
-        own, rest, sums, dy = ffn_block_backward(dzb, yb, act[j], slope[j], first, second, dy)
-        small["eb"].append(sums)
-        blocks.append((own, rest))
-        if j == 2:
+    for lo, hi in ((0, cut), (cut, TENSORS)):
+        if lo == hi:
+            continue
+        parts = [(act[j], slope[j], *ffn_w[j]) for j in range(lo, hi)]
+        dy, sums, grads = ffn_blocks_backward(dzb, yb, dy, parts)
+        small["eb"] += sums
+        blocks += grads
+        if hi < TENSORS:
             dzb, dy = hook("three", (dzb, dy))
     return dy, blocks, small
 
@@ -676,11 +739,12 @@
     da = dz1.astype(BF)
     dx = dz1
     blocks = []
-    for j, (first, second) in enumerate(attn_w):
-        dfirst, dsecond, sums, dx = attend_backward(vec["cols"], da, xb, first, second, saved[j], dx, seg)
-        small["heads"].append(sums)
-        blocks.append((dfirst, dsecond))
-        if j == 2:
+    for lo, hi in ((0, TENSORS - 1), (TENSORS - 1, TENSORS)):
+        parts = [(*attn_w[j], *saved[j]) for j in range(lo, hi)]
+        dx, sums, grads = attend_blocks_backward(vec["cols"], da, xb, dx, parts, seg)
+        small["heads"] += sums
+        blocks += grads
+        if lo == 0:
             da, dx = hook("three", (da, dx))
     return dx, blocks, small
 
@@ -852,7 +916,7 @@
 
     ffn1, attn1, ffn0 = (Reduction() for _ in range(3))
 
-    dy, blocks, small1 = ffn_backward(head_cot.astype(F32) * valid, ffn_w1, vec1, kept1, plain)
+    dy, blocks, small1 = ffn_backward(head_cot.astype(F32) * valid, ffn_w1, vec1, kept1, plain, 0)
     dy, mark = tie(dy, head_out)
     dy = ffn1.start(dy, blocks)
 
@@ -876,7 +940,7 @@
             return attn1.swapped(value)
         return attn1.crossed(value)
 
-    dy, blocks, small0 = ffn_backward(seed, ffn_w0, vec0, kept0, during_ffn0)
+    dy, blocks, small0 = ffn_backward(seed, ffn_w0, vec0, kept0, during_ffn0, 2)
     dy, mark = tie(dy, grad_skip)
     dy = ffn0.start(dy, blocks)
     dy = attn1.summed(dy)

time: 679 us -> 705 us (1.038)
  local copies, waits for them, and re-layouts: 113 us -> 129 us
    unnamed x605 -> x561, local copies, waits for them, and re-layouts: 89 us -> 105 us
    pallas_call x16 -> x7, Pallas kernels: 131 us -> 138 us  [streamed_blocks(): pl.pallas_call(kernel, name=name, out_shape=(jax.ShapeDtypeStruct(total.s...]
  transfers between devices with their start and end apart: 60 -> 60, of which waited for: 6 -> 8; matrix products, arithmetic and copies ran while one was open for 20% -> 19% of each run, Pallas kernels for 30% -> 30%
where the time goes in v9:
time: 705 us; the launch traced here: 694 us
  Pallas kernels  283 us (40%)
  local copies, waits for them, and re-layouts  129 us (18%)
  other arithmetic  110 us (16%)
  starting transfers between devices  69.5 us (10%)
  matrix products  47 us (7%)
  waiting for transfers between devices  34.7 us (5%)
  between operations  20.5 us (3%)
    pallas_call x7, Pallas kernels, streamed_blocks(): pl.pallas_call(kernel, name=name, out_shape=(jax.ShapeDtypeStruct(total.s...  138 us
    unnamed x561, local copies, waits for them, and re-layouts  105 us
    pallas_call x1, Pallas kernels, last_sums(): pl.pallas_call(body, name='last_sums', out_shape=tuple((jax.ShapeDtypeStr...  73.7 us
    pallas_call x8, Pallas kernels, attend_forward(): pl.pallas_call(body, name='attend_forward', out_shape=(narrow, narrow, na...  55 us
    dot_general x18, matrix products, mm(): lax.dot_general(a, b, (((ca,), (cb,)), ((), ())), preferred_element_type=...  41.1 us
    convert_element_type x18, other arithmetic, plus(): return total.astype(BF)  37.1 us
    ppermute x50, starting transfers between devices, send(): return lax.ppermute(values, PLANE, plane_pairs(kind))  34.1 us
    reduce_sum x8, other arithmetic, total_rows(): return jnp.sum(values, axis=0)  18.3 us
  transfers between devices with their start and end apart: 60, of which 8 were waited for; matrix products, arithmetic and copies ran while one was open for 19% of the time, Pallas kernels for 30%

profile of v9, /device:TPU:0, one launch (start us, length us, event | category | flops | bytes accessed | tf_op | source)
XLA Modules:
  0.0 694.1 jit_solution(10646915317390028980)
XLA Ops:
  7.2 5.2 all-to-all-start
  18.2 3.9 slice_bitcast_fusion
  29.6 6.4 attend_forward.8
  40.6 6.4 attend_forward.9
  49.2 6.4 attend_forward.10
  58.2 6.6 attend_forward.11
  65.0 3.4 collective-permute-done.7.refs_10_
  74.6 3.6 fusion.24
  80.6 3.3 fusion.29
  86.4 3.4 fusion.34
  99.6 4.2 all-to-all-start.2
  114.0 4.9 all-to-all-done.2
  118.9 3.1 fusion.49
  122.0 7.6 %attend_forward.12 = (bf16[512,192]{1,0:T(8,128)(2,1)S(1)}, bf16[512,192]{1,0:T(8,128)(2,1)S(1)}, bf16[512,192]{1,0:T(8,128)(2,1)S(1)}, bf16[512,192]{1,0:T(8,12...) custom-call(bf16[512,768]{1,0:T(8,128)(2,1)S(1)} %get-tuple-element.478.refs_0_.refs_1_, ...), custom_call_target="tpu_custom_call" | custom-call | flops 1048576 | bytes 1024 | tf_op jit(solution)/shard_map/attend_forward/pallas_call | solution.py:355
  134.3 4.7 all-to-all-start.1
  140.4 7.6 %attend_forward.13 = (bf16[512,192]{1,0:T(8,128)(2,1)S(1)}, bf16[512,192]{1,0:T(8,128)(2,1)S(1)}, bf16[512,192]{1,0:T(8,128)(2,1)S(1)}, bf16[512,192]{1,0:T(8,12...) custom-call(bf16[512,768]{1,0:T(8,128)(2,1)S(1)} %get-tuple-element.478.refs_0_.refs_1_, ...), custom_call_target="tpu_custom_call" | custom-call | flops 1048576 | bytes 1024 | tf_op jit(solution)/shard_map/attend_forward/pallas_call | solution.py:355
  151.5 7.6 %attend_forward.14 = (bf16[512,192]{1,0:T(8,128)(2,1)S(1)}, bf16[512,192]{1,0:T(8,128)(2,1)S(1)}, bf16[512,192]{1,0:T(8,128)(2,1)S(1)}, bf16[512,192]{1,0:T(8,12...) custom-call(bf16[512,768]{1,0:T(8,128)(2,1)S(1)} %get-tuple-element.478.refs_0_.refs_1_, ...), custom_call_target="tpu_custom_call" | custom-call | flops 1048576 | bytes 1024 | tf_op jit(solution)/shard_map/attend_forward/pallas_call | solution.py:355
  165.6 6.4 attend_forward.15
  172.6 2.8 broadcast_select_fusion.4
  186.2 3.4 fusion.9
  192.0 3.4 fusion.14
  195.3 3.5 add_add_fusion
  198.9 4.2 all-to-all-start.5
  203.7 11.2 %all-to-all-done.5 = bf16[4,128,768]{2,1,0:T(8,128)(2,1)} async-done(((bf16[4,128,768]{2,1,0:T(8,128)(2,1)}), bf16[4,128,768]{2,1,0:T(8,128)(2,1)}, u32[]{:S(2)}, u32[]{:S(2)}) %all-to-all-start.5) | async-done | bytes 786464 | tf_op jit(solution)/shard_map/all_to_all | solution.py:674
  225.8 3.9 fusion.105
  229.7 4.5 all-to-all-start.3
  237.3 16.5 %gather_anchors.1 = bf16[4,8,4,768]{3,2,1,0:T(4,128)(2,1)} custom-call(bf16[4,768]{1,0:T(4,128)(2,1)} %convolution_convert_fusion.refs_0_), custom_call_target="tpu_custom_call" | custom-call | tf_op jit(solution)/shard_map/gather_anchors/pallas_call | solution.py:421
  271.4 31.9 %ffn_backward.3 = (f32[512,768]{1,0:T(8,128)}, f32[1,768]{1,0:T(1,128)S(1)}, f32[1,768]{1,0:T(1,128)S(1)}, f32[1,768]{1,0:T(1,128)S(1)}, f32[1,768]{1,0:T(1,128)...) custom-call(bf16[512,768]{1,0:T(8,128)(2,1)S(1)} %convert_element_ty, ...), custom_call_target="tpu_custom_call" | custom-call | flops 1048576 | bytes 1024 | tf_op jit(solution)/shard_map/ffn_backward/pallas_call | solution.py:302
  313.7 3.2 multiply_reduce_fusion.1
  327.5 27.9 %attend_backward.4 = (f32[512,768]{1,0:T(8,128)S(1)}, f32[1,384]{1,0:T(1,128)S(1)}, f32[1,384]{1,0:T(1,128)S(1)}, f32[1,384]{1,0:T(1,128)S(1)}, bf16[384,768]{1,...) custom-call(bf16[512,768]{1,0:T(8,128)(2,1)S(1)} %convert_element_ty, ...), custom_call_target="tpu_custom_call" | custom-call | flops 1048576 | bytes 1024 | tf_op jit(solution)/shard_map/attend_backward/pallas_call | solution.py:302
  359.2 9.6 %attend_backward.5 = (f32[512,768]{1,0:T(8,128)S(1)}, f32[1,384]{1,0:T(1,128)S(1)}, bf16[384,768]{1,0:T(8,128)(2,1)S(1)}, bf16[384,768]{1,0:T(8,128)(2,1)}) custom-call(bf16[512,768]{1,0:T(8,128)(2,1)S(1)} %convert_element_type.524.refs_0_, bf16[512,768]{1,0:T(8,128)(2,1)S(1)} %get-tuple-element.478.refs_0_.refs_1_, s32[512,1]{1,0:T(8,128)S(1)} %fusion.55.refs_5_.refs_2_, ...), custom_call_target="tpu_custom_call" | custom-call | flops 1048576 | bytes 1024 | tf_op jit(solution)/shard_map/attend_backward/pallas_call | solution.py:302
  374.3 4.2 all-to-all-start.4
  386.3 6.1 collective-permute-done.29
  392.4 3.1 add_convert_fusion.6
  396.7 4.7 multiply_reduce_fusion.2
  409.2 4.2 all-to-all-start.6
  420.8 15.9 %ffn_backward.4 = (f32[512,768]{1,0:T(8,128)S(1)}, f32[1,768]{1,0:T(1,128)S(1)}, f32[1,768]{1,0:T(1,128)S(1)}, bf16[768,768]{1,0:T(8,128)(2,1)S(1)}, bf16[768,76...) custom-call(bf16[512,768]{1,0:T(8,128)(2,1)S(1)} %copy-done.8, ...), custom_call_target="tpu_custom_call" | custom-call | flops 1048576 | bytes 1024 | tf_op jit(solution)/shard_map/ffn_backward/pallas_call | solution.py:302
  444.3 15.8 %ffn_backward.5 = (f32[512,768]{1,0:T(8,128)S(1)}, f32[1,768]{1,0:T(1,128)S(1)}, f32[1,768]{1,0:T(1,128)S(1)}, bf16[768,768]{1,0:T(8,128)(2,1)S(1)}, bf16[768,76...) custom-call(bf16[512,768]{1,0:T(8,128)(2,1)S(1)} %copy-done.8, ...), custom_call_target="tpu_custom_call" | custom-call | flops 1048576 | bytes 1024 | tf_op jit(solution)/shard_map/ffn_backward/pallas_call | solution.py:302
  472.9 2.7 add_convert_fusion.2
  475.6 2.7 add_convert_fusion.3
  478.3 2.7 add_convert_fusion.4
  481.1 2.7 add_convert_fusion.5
  506.7 27.7 %attend_backward.6 = (f32[512,768]{1,0:T(8,128)S(1)}, f32[1,384]{1,0:T(1,128)S(1)}, f32[1,384]{1,0:T(1,128)S(1)}, f32[1,384]{1,0:T(1,128)S(1)}, bf16[384,768]{1,...) custom-call(bf16[512,768]{1,0:T(8,128)(2,1)S(1)} %convert_element_ty, ...), custom_call_target="tpu_custom_call" | custom-call | flops 1048576 | bytes 1024 | tf_op jit(solution)/shard_map/attend_backward/pallas_call | solution.py:302
  537.1 3.7 add_convert_fusion.1
  548.2 8.9 %attend_backward.7 = (f32[512,768]{1,0:T(8,128)S(1)}, f32[1,384]{1,0:T(1,128)S(1)}, bf16[384,768]{1,0:T(8,128)(2,1)S(1)}, bf16[384,768]{1,0:T(8,128)(2,1)S(1)}) custom-call(bf16[512,768]{1,0:T(8,128)(2,1)S(1)} %convert_element_type.569.refs_0_, bf16[512,768]{1,0:T(8,128)(2,1)S(1)} %bitcast.175, s32[512,1]{1,0:T(8,128)S(1)} %fusion.55.refs_5_.refs_2_, ...), custom_call_target="tpu_custom_call" | custom-call | flops 1048576 | bytes 1024 | tf_op jit(solution)/shard_map/attend_backward/pallas_call | solution.py:302
  558.4 3.9 all-to-all-start.7
  566.0 7.5 %all-to-all-done.7 = bf16[4,128,768]{2,1,0:T(8,128)(2,1)S(1)} async-done(((bf16[4,128,768]{2,1,0:T(8,128)(2,1)}), bf16[4,128,768]{2,1,0:T(8,128)(2,1)S(1)}, u32[]{:S(2)}, u32[]{:S(2)}) %all-to-all-start.7) | async-done | bytes 786464 | tf_op jit(solution)/shard_map/all_to_all | solution.py:681
  578.1 73.7 %last_sums.1 = (bf16[2,4,96,768]{3,2,1,0:T(8,128)(2,1)S(1)}, bf16[2,4,96,768]{3,2,1,0:T(8,128)(2,1)S(1)}, bf16[2,4,48,768]{3,2,1,0:T(8,128)(2,1)S(1)}, bf16[2,4,...) custom-call(bf16[2,4,96,768]{3,2,1,0:T(8,128)(2,1)S(1)} %bitcast.176, bf16[2,4,48,768]{3,2,1,0:T(8,128)(2,1)S(1)} %bitcast.177, ...), custom_call_target="tpu_custom_call" | custom-call | tf_op jit(solution)/shard_map/last_sums/pallas_call | solution.py:651
  (830 shorter events, 262.7 us)
Async XLA Ops:
  7.2 22.2 %all-to-all-start = ((bf16[4,128,768]{2,1,0:T(8,128)(2,1)}), bf16[4,128,768]{2,1,0:T(8,128)(2,1)S(1)}, u32[]{:S(2)}, u32[]{:S(2)}) async-start(bf16[4,128,768]{2,1,0:T(8,128)(2,1)} %bitcast.198), calls=%async_computation | async-start | bytes 1572864 | tf_op jit(solution)/shard_map/all_to_all | solution.py:674
  16.0 20.0 %collective-permute-start = (bf16[400,768]{1,0:T(8,128)(2,1)S(1)}, bf16[400,768]{1,0:T(8,128)(2,1)S(1)}, u32[]{:S(2)}, u32[]{:S(2)}) collective-permute-start(bf16[400,768]{1,0:T(8,128)(2,1)S(1)} %pad_maximum_fusion.2.refs_1_.refs_5_), channel_id=1, source_target_pairs={{0,1},{1,0},{2,3},{3,2},{4,6},{5,7},{6,4},{7,5},{8,9},{9,8},{10,11... | collective-permute-start | bytes 1843208 | tf_op jit(solution)/shard_map/ppermute | solution.py:62
  18.1 18.2 %collective-permute-start.1 = (bf16[400,768]{1,0:T(8,128)(2,1)S(1)}, bf16[400,768]{1,0:T(8,128)(2,1)S(1)}, u32[]{:S(2)}, u32[]{:S(2)}) collective-permute-start(bf16[400,768]{1,0:T(8,128)(2,1)S(1)} %fusion.54.refs_2_.refs_6_), channel_id=1, source_target_pairs={{0,1},{1,0},{2,3},{3,2},{4,6},{5,7},{6,4},{7,5},{8,9},{9,8},{10,11... | collective-permute-start | bytes 1843208 | tf_op jit(solution)/shard_map/ppermute | solution.py:62
  22.1 42.8 %collective-permute-start.6 = (bf16[768,768]{1,0:T(8,128)(2,1)}, bf16[768,768]{1,0:T(8,128)(2,1)}, u32[]{:S(2)}, u32[]{:S(2)}) collective-permute-start(bf16[768,768]{1,0:T(8,128)(2,1)} %get-tuple-element.230.refs_5_), channel_id=1, source_target_pairs={{0,1},{1,0},{2,3},{3,2},{4,6},{5,7},{6,4},{7,5},{8,9},{9,8},{10,11... | collective-permute-start | bytes 3538952 | tf_op jit(solution)/shard_map/ppermute | solution.py:62
  24.1 44.3 %collective-permute-start.7 = (bf16[768,768]{1,0:T(8,128)(2,1)}, bf16[768,768]{1,0:T(8,128)(2,1)}, u32[]{:S(2)}, u32[]{:S(2)}) collective-permute-start(bf16[768,768]{1,0:T(8,128)(2,1)} %get-tuple-element.231.refs_6_), channel_id=1, source_target_pairs={{0,1},{1,0},{2,3},{3,2},{4,6},{5,7},{6,4},{7,5},{8,9},{9,8},{10,11... | collective-permute-start | bytes 3538952 | tf_op jit(solution)/shard_map/ppermute | solution.py:62
  36.4 12.7 %collective-permute-start.2 = (bf16[400,768]{1,0:T(8,128)(2,1)S(1)}, bf16[400,768]{1,0:T(8,128)(2,1)S(1)}, u32[]{:S(2)}, u32[]{:S(2)}) collective-permute-start(bf16[400,768]{1,0:T(8,128)(2,1)S(1)} %collective-permute-done.refs_1_.refs_12_), channel_id=1, source_target_pairs={{0,4},{1,5},{2,6},{3,7},{4,0},{5,1},{6,2},{7,3},{8,12},{9,13},{10,... | collective-permute-start | bytes 1843208 | tf_op jit(solution)/shard_map/ppermute | solution.py:62
  36.5 12.7 %collective-permute-start.3 = (bf16[400,768]{1,0:T(8,128)(2,1)S(1)}, bf16[400,768]{1,0:T(8,128)(2,1)S(1)}, u32[]{:S(2)}, u32[]{:S(2)}) collective-permute-start(bf16[400,768]{1,0:T(8,128)(2,1)S(1)} %collective-permute-done.1.refs_2_.refs_13_), channel_id=1, source_target_pairs={{0,4},{1,5},{2,6},{3,7},{4,0},{5,1},{6,2},{7,3},{8,12},{9,13},{10,... | collective-permute-start | bytes 1843208 | tf_op jit(solution)/shard_map/ppermute | solution.py:62
  37.0 18.7 %collective-permute-start.4 = (bf16[400,768]{1,0:T(8,128)(2,1)S(1)}, bf16[400,768]{1,0:T(8,128)(2,1)S(1)}, u32[]{:S(2)}, u32[]{:S(2)}) collective-permute-start(bf16[400,768]{1,0:T(8,128)(2,1)S(1)} %broadcast_select_fusion.10), channel_id=1, source_target_pairs={{0,2},{1,3},{2,0},{3,1},{4,5},{5,4},{6,7},{7,6},{8,10},{9,11},{10,... | collective-permute-start | bytes 1843208 | tf_op jit(solution)/shard_map/ppermute | solution.py:62
  55.9 30.4 %collective-permute-start.8 = (bf16[384,768]{1,0:T(8,128)(2,1)}, bf16[384,768]{1,0:T(8,128)(2,1)}, u32[]{:S(2)}, u32[]{:S(2)}) collective-permute-start(bf16[384,768]{1,0:T(8,128)(2,1)} %bitcast.16.refs_1_.refs_5_), channel_id=1, source_target_pairs={{0,1},{1,0},{2,3},{3,2},{4,6},{5,7},{6,4},{7,5},{8,9},{9,8},{10,11... | collective-permute-start | bytes 1769480 | tf_op jit(solution)/shard_map/ppermute | solution.py:62
  57.5 28.9 %collective-permute-start.9 = (bf16[384,768]{1,0:T(8,128)(2,1)}, bf16[384,768]{1,0:T(8,128)(2,1)}, u32[]{:S(2)}, u32[]{:S(2)}) collective-permute-start(bf16[384,768]{1,0:T(8,128)(2,1)} %pad_maximum_fusion.3.refs_2_.refs_6_), channel_id=1, source_target_pairs={{0,1},{1,0},{2,3},{3,2},{4,6},{5,7},{6,4},{7,5},{8,9},{9,8},{10,11... | collective-permute-start | bytes 1769480 | tf_op jit(solution)/shard_map/ppermute | solution.py:62
  68.3 18.1 %collective-permute-start.10 = (bf16[768,768]{1,0:T(8,128)(2,1)}, bf16[768,768]{1,0:T(8,128)(2,1)}, u32[]{:S(2)}, u32[]{:S(2)}) collective-permute-start(bf16[768,768]{1,0:T(8,128)(2,1)} %collective-permute-done.6.refs_9_), channel_id=1, source_target_pairs={{0,4},{1,5},{2,6},{3,7},{4,0},{5,1},{6,2},{7,3},{8,12},{9,13},{10,... | collective-permute-start | bytes 3538952 | tf_op jit(solution)/shard_map/ppermute | solution.py:62
  70.9 18.9 %collective-permute-start.11 = (bf16[768,768]{1,0:T(8,128)(2,1)}, bf16[768,768]{1,0:T(8,128)(2,1)}, u32[]{:S(2)}, u32[]{:S(2)}) collective-permute-start(bf16[768,768]{1,0:T(8,128)(2,1)} %collective-permute-done.7.refs_10_), channel_id=1, source_target_pairs={{0,4},{1,5},{2,6},{3,7},{4,0},{5,1},{6,2},{7,3},{8,12},{9,13},{10,... | collective-permute-start | bytes 3538952 | tf_op jit(solution)/shard_map/ppermute | solution.py:62
  72.8 21.3 %collective-permute-start.12 = (bf16[768,768]{1,0:T(8,128)(2,1)S(1)}, bf16[768,768]{1,0:T(8,128)(2,1)}, u32[]{:S(2)}, u32[]{:S(2)}) collective-permute-start(bf16[768,768]{1,0:T(8,128)(2,1)S(1)} %copy-done.246), channel_id=1, source_target_pairs={{0,2},{1,3},{2,0},{3,1},{4,5},{5,4},{6,7},{7,6},{8,10},{9,11},{10,... | collective-permute-start | bytes 3538952 | tf_op jit(solution)/shard_map/ppermute | solution.py:62
  94.1 12.5 %collective-permute-start.13 = (bf16[768,768]{1,0:T(8,128)(2,1)}, bf16[768,768]{1,0:T(8,128)(2,1)}, u32[]{:S(2)}, u32[]{:S(2)}) collective-permute-start(bf16[768,768]{1,0:T(8,128)(2,1)} %collective-permute-done.12), channel_id=1, source_target_pairs={{0,4},{1,5},{2,6},{3,7},{4,0},{5,1},{6,2},{7,3},{8,12},{9,13},{10,... | collective-permute-start | bytes 3538952 | tf_op jit(solution)/shard_map/ppermute | solution.py:62
  95.4 56.1 %collective-permute-start.16 = (bf16[384,768]{1,0:T(8,128)(2,1)}, bf16[384,768]{1,0:T(8,128)(2,1)}, u32[]{:S(2)}, u32[]{:S(2)}) collective-permute-start(bf16[384,768]{1,0:T(8,128)(2,1)} %collective-permute-done.8.refs_1_.refs_12_), channel_id=1, source_target_pairs={{0,4},{1,5},{2,6},{3,7},{4,0},{5,1},{6,2},{7,3},{8,12},{9,13},{10,... | collective-permute-start | bytes 1769480 | tf_op jit(solution)/shard_map/ppermute | solution.py:62
  96.0 55.5 %collective-permute-start.17 = (bf16[384,768]{1,0:T(8,128)(2,1)}, bf16[384,768]{1,0:T(8,128)(2,1)}, u32[]{:S(2)}, u32[]{:S(2)}) collective-permute-start(bf16[384,768]{1,0:T(8,128)(2,1)} %collective-permute-done.9.refs_2_.refs_13_), channel_id=1, source_target_pairs={{0,4},{1,5},{2,6},{3,7},{4,0},{5,1},{6,2},{7,3},{8,12},{9,13},{10,... | collective-permute-start | bytes 1769480 | tf_op jit(solution)/shard_map/ppermute | solution.py:62
  98.0 53.5 %collective-permute-start.14 = (bf16[384,768]{1,0:T(8,128)(2,1)}, bf16[384,768]{1,0:T(8,128)(2,1)}, u32[]{:S(2)}, u32[]{:S(2)}) collective-permute-start(bf16[384,768]{1,0:T(8,128)(2,1)} %broadcast_select_fusion.13), channel_id=1, source_target_pairs={{0,2},{1,3},{2,0},{3,1},{4,5},{5,4},{6,7},{7,6},{8,10},{9,11},{10,... | collective-permute-start | bytes 1769480 | tf_op jit(solution)/shard_map/ppermute | solution.py:62
  99.6 19.3 %all-to-all-start.2 = ((bf16[4,128,768]{2,1,0:T(8,128)(2,1)}), bf16[4,128,768]{2,1,0:T(8,128)(2,1)}, u32[]{:S(2)}, u32[]{:S(2)}) async-start(bf16[4,128,768]{2,1,0:T(8,128)(2,1)} %bitcast.199), calls=%async_computation.2 | async-start | bytes 1572864 | tf_op jit(solution)/shard_map/all_to_all | solution.py:674
  103.8 68.3 %collective-permute-start.18 = (bf16[768,768]{1,0:T(8,128)(2,1)}, bf16[768,768]{1,0:T(8,128)(2,1)}, u32[]{:S(2)}, u32[]{:S(2)}) collective-permute-start(bf16[768,768]{1,0:T(8,128)(2,1)} %get-tuple-element.253.refs_5_), channel_id=1, source_target_pairs={{0,1},{1,0},{2,3},{3,2},{4,6},{5,7},{6,4},{7,5},{8,9},{9,8},{10,11... | collective-permute-start | bytes 3538952 | tf_op jit(solution)/shard_map/ppermute | solution.py:62
  106.6 65.5 %collective-permute-start.19 = (bf16[768,768]{1,0:T(8,128)(2,1)}, bf16[768,768]{1,0:T(8,128)(2,1)}, u32[]{:S(2)}, u32[]{:S(2)}) collective-permute-start(bf16[768,768]{1,0:T(8,128)(2,1)} %get-tuple-element.254.refs_6_), channel_id=1, source_target_pairs={{0,1},{1,0},{2,3},{3,2},{4,6},{5,7},{6,4},{7,5},{8,9},{9,8},{10,11... | collective-permute-start | bytes 3538952 | tf_op jit(solution)/shard_map/ppermute | solution.py:62
  134.3 29.5 %all-to-all-start.1 = ((bf16[4,128,768]{2,1,0:T(8,128)(2,1)}), bf16[4,128,768]{2,1,0:T(8,128)(2,1)}, u32[]{:S(2)}, u32[]{:S(2)}) async-start(bf16[4,128,768]{2,1,0:T(8,128)(2,1)} %bitcast.190), calls=%async_computation.1 | async-start | bytes 1572864 | tf_op jit(solution)/shard_map/all_to_all | solution.py:681
  172.1 19.9 %collective-permute-start.20 = (bf16[768,768]{1,0:T(8,128)(2,1)}, bf16[768,768]{1,0:T(8,128)(2,1)}, u32[]{:S(2)}, u32[]{:S(2)}) collective-permute-start(bf16[768,768]{1,0:T(8,128)(2,1)} %collective-permute-done.18.refs_9_), channel_id=1, source_target_pairs={{0,4},{1,5},{2,6},{3,7},{4,0},{5,1},{6,2},{7,3},{8,12},{9,13},{10,... | collective-permute-start | bytes 3538952 | tf_op jit(solution)/shard_map/ppermute | solution.py:62
  175.4 19.9 %collective-permute-start.21 = (bf16[768,768]{1,0:T(8,128)(2,1)}, bf16[768,768]{1,0:T(8,128)(2,1)}, u32[]{:S(2)}, u32[]{:S(2)}) collective-permute-start(bf16[768,768]{1,0:T(8,128)(2,1)} %collective-permute-done.19.refs_10_), channel_id=1, source_target_pairs={{0,4},{1,5},{2,6},{3,7},{4,0},{5,1},{6,2},{7,3},{8,12},{9,13},{10,... | collective-permute-start | bytes 3538952 | tf_op jit(solution)/shard_map/ppermute | solution.py:62
  176.0 22.8 %collective-permute-start.22 = (bf16[768,768]{1,0:T(8,128)(2,1)}, bf16[768,768]{1,0:T(8,128)(2,1)}, u32[]{:S(2)}, u32[]{:S(2)}) collective-permute-start(bf16[768,768]{1,0:T(8,128)(2,1)} %broadcast_select_fusion.4), channel_id=1, source_target_pairs={{0,2},{1,3},{2,0},{3,1},{4,5},{5,4},{6,7},{7,6},{8,10},{9,11},{10,... | collective-permute-start | bytes 3538952 | tf_op jit(solution)/shard_map/ppermute | solution.py:62
  198.8 18.2 %collective-permute-start.23 = (bf16[768,768]{1,0:T(8,128)(2,1)}, bf16[768,768]{1,0:T(8,128)(2,1)}, u32[]{:S(2)}, u32[]{:S(2)}) collective-permute-start(bf16[768,768]{1,0:T(8,128)(2,1)} %collective-permute-done.22), channel_id=1, source_target_pairs={{0,4},{1,5},{2,6},{3,7},{4,0},{5,1},{6,2},{7,3},{8,12},{9,13},{10,... | collective-permute-start | bytes 3538952 | tf_op jit(solution)/shard_map/ppermute | solution.py:62
  198.9 16.1 %all-to-all-start.5 = ((bf16[4,128,768]{2,1,0:T(8,128)(2,1)}), bf16[4,128,768]{2,1,0:T(8,128)(2,1)}, u32[]{:S(2)}, u32[]{:S(2)}) async-start(bf16[4,128,768]{2,1,0:T(8,128)(2,1)} %bitcast.200), calls=%async_computation.5 | async-start | bytes 1572864 | tf_op jit(solution)/shard_map/all_to_all | solution.py:674
  229.7 81.9 %all-to-all-start.3 = ((bf16[4,128,768]{2,1,0:T(8,128)(2,1)}), bf16[4,128,768]{2,1,0:T(8,128)(2,1)}, u32[]{:S(2)}, u32[]{:S(2)}) async-start(bf16[4,128,768]{2,1,0:T(8,128)(2,1)} %bitcast.187), calls=%async_computation.3 | async-start | bytes 1572864 | tf_op jit(solution)/shard_map/all_to_all | solution.py:681
  323.5 32.9 %collective-permute-start.28 = (bf16[768,768]{1,0:T(8,128)(2,1)S(1)}, bf16[768,768]{1,0:T(8,128)(2,1)S(1)}, u32[]{:S(2)}, u32[]{:S(2)}) collective-permute-start(bf16[768,768]{1,0:T(8,128)(2,1)S(1)} %add_convert_fusion.9), channel_id=1, source_target_pairs={{0,2},{1,3},{2,0},{3,1},{4,5},{5,4},{6,7},{7,6},{8,10},{9,11},{10,... | collective-permute-start | bytes 3538952 | tf_op jit(solution)/shard_map/ppermute | solution.py:62
  325.2 47.8 %collective-permute-start.30 = (bf16[768,768]{1,0:T(8,128)(2,1)}, bf16[768,768]{1,0:T(8,128)(2,1)}, u32[]{:S(2)}, u32[]{:S(2)}) collective-permute-start(bf16[768,768]{1,0:T(8,128)(2,1)} %add_convert_fusion.11), channel_id=1, source_target_pairs={{0,1},{1,0},{2,3},{3,2},{4,6},{5,7},{6,4},{7,5},{8,9},{9,8},{10,11... | collective-permute-start | bytes 3538952 | tf_op jit(solution)/shard_map/ppermute | solution.py:62
  371.6 20.8 %collective-permute-start.29 = (bf16[768,768]{1,0:T(8,128)(2,1)}, bf16[768,768]{1,0:T(8,128)(2,1)}, u32[]{:S(2)}, u32[]{:S(2)}) collective-permute-start(bf16[768,768]{1,0:T(8,128)(2,1)} %add_convert_fusion.7), channel_id=1, source_target_pairs={{0,1},{1,0},{2,3},{3,2},{4,6},{5,7},{6,4},{7,5},{8,9},{9,8},{10,11... | collective-permute-start | bytes 3538952 | tf_op jit(solution)/shard_map/ppermute | solution.py:62
  372.9 19.5 %collective-permute-start.31 = (bf16[768,768]{1,0:T(8,128)(2,1)}, bf16[768,768]{1,0:T(8,128)(2,1)}, u32[]{:S(2)}, u32[]{:S(2)}) collective-permute-start(bf16[768,768]{1,0:T(8,128)(2,1)} %collective-permute-done.30), channel_id=1, source_target_pairs={{0,4},{1,5},{2,6},{3,7},{4,0},{5,1},{6,2},{7,3},{8,12},{9,13},{10,... | collective-permute-start | bytes 3538952 | tf_op jit(solution)/shard_map/ppermute | solution.py:62
  374.3 22.4 %all-to-all-start.4 = ((bf16[4,128,768]{2,1,0:T(8,128)(2,1)}), bf16[4,128,768]{2,1,0:T(8,128)(2,1)}, u32[]{:S(2)}, u32[]{:S(2)}) async-start(bf16[4,128,768]{2,1,0:T(8,128)(2,1)} %bitcast.201), calls=%async_computation.4 | async-start | bytes 1572864 | tf_op jit(solution)/shard_map/all_to_all | solution.py:674
  378.5 90.4 %all-reduce.5.cloned.1.call-start = ((), (), s32[]{:S(2)}) async-start(), calls=%async_computation.8 | async-start | bytes 2359296 | tf_op jit(solution)/shard_map/psum | solution.py:932
  403.0 36.8 %collective-permute-start.36 = (bf16[384,768]{1,0:T(8,128)(2,1)}, bf16[384,768]{1,0:T(8,128)(2,1)}, u32[]{:S(2)}, u32[]{:S(2)}) collective-permute-start(bf16[384,768]{1,0:T(8,128)(2,1)} %add_convert_fusion.15), channel_id=1, source_target_pairs={{0,2},{1,3},{2,0},{3,1},{4,5},{5,4},{6,7},{7,6},{8,10},{9,11},{10,... | collective-permute-start | bytes 1769480 | tf_op jit(solution)/shard_map/ppermute | solution.py:62
  404.3 40.0 %collective-permute-start.38 = (bf16[384,768]{1,0:T(8,128)(2,1)}, bf16[384,768]{1,0:T(8,128)(2,1)}, u32[]{:S(2)}, u32[]{:S(2)}) collective-permute-start(bf16[384,768]{1,0:T(8,128)(2,1)} %add_convert_fusion.17), channel_id=1, source_target_pairs={{0,1},{1,0},{2,3},{3,2},{4,6},{5,7},{6,4},{7,5},{8,9},{9,8},{10,11... | collective-permute-start | bytes 1769480 | tf_op jit(solution)/shard_map/ppermute | solution.py:62
  409.2 56.1 %all-to-all-start.6 = ((bf16[4,128,768]{2,1,0:T(8,128)(2,1)}), bf16[4,128,768]{2,1,0:T(8,128)(2,1)}, u32[]{:S(2)}, u32[]{:S(2)}) async-start(bf16[4,128,768]{2,1,0:T(8,128)(2,1)} %bitcast.188), calls=%async_computation.6 | async-start | bytes 1572864 | tf_op jit(solution)/shard_map/all_to_all | solution.py:681
  413.5 128.9 %all-reduce.7.cloned.1.call-start = ((), (), s32[]{:S(2)}) async-start(), calls=%async_computation.9 | async-start | bytes 1179648 | tf_op jit(solution)/shard_map/psum | solution.py:949
  442.3 24.1 %collective-permute-start.37 = (bf16[384,768]{1,0:T(8,128)(2,1)}, bf16[384,768]{1,0:T(8,128)(2,1)}, u32[]{:S(2)}, u32[]{:S(2)}) collective-permute-start(bf16[384,768]{1,0:T(8,128)(2,1)} %add_convert_fusion.13), channel_id=1, source_target_pairs={{0,1},{1,0},{2,3},{3,2},{4,6},{5,7},{6,4},{7,5},{8,9},{9,8},{10,11... | collective-permute-start | bytes 1769480 | tf_op jit(solution)/shard_map/ppermute | solution.py:62
  444.2 22.2 %collective-permute-start.39 = (bf16[384,768]{1,0:T(8,128)(2,1)}, bf16[384,768]{1,0:T(8,128)(2,1)}, u32[]{:S(2)}, u32[]{:S(2)}) collective-permute-start(bf16[384,768]{1,0:T(8,128)(2,1)} %collective-permute-done.38), channel_id=1, source_target_pairs={{0,4},{1,5},{2,6},{3,7},{4,0},{5,1},{6,2},{7,3},{8,12},{9,13},{10,... | collective-permute-start | bytes 1769480 | tf_op jit(solution)/shard_map/ppermute | solution.py:62
  466.0 12.4 %collective-permute-start.41 = (bf16[768,768]{1,0:T(8,128)(2,1)}, bf16[768,768]{1,0:T(8,128)(2,1)}, u32[]{:S(2)}, u32[]{:S(2)}) collective-permute-start(bf16[768,768]{1,0:T(8,128)(2,1)} %copy-done.225), channel_id=1, source_target_pairs={{0,4},{1,5},{2,6},{3,7},{4,0},{5,1},{6,2},{7,3},{8,12},{9,13},{10,... | collective-permute-start | bytes 3538952 | tf_op jit(solution)/shard_map/ppermute | solution.py:62
  466.4 14.7 %collective-permute-start.40 = (bf16[768,768]{1,0:T(8,128)(2,1)}, bf16[768,768]{1,0:T(8,128)(2,1)}, u32[]{:S(2)}, u32[]{:S(2)}) collective-permute-start(bf16[768,768]{1,0:T(8,128)(2,1)} %copy-done.223), channel_id=1, source_target_pairs={{0,4},{1,5},{2,6},{3,7},{4,0},{5,1},{6,2},{7,3},{8,12},{9,13},{10,... | collective-permute-start | bytes 3538952 | tf_op jit(solution)/shard_map/ppermute | solution.py:62
  483.8 53.2 %collective-permute-start.44 = (bf16[768,768]{1,0:T(8,128)(2,1)}, bf16[768,768]{1,0:T(8,128)(2,1)}, u32[]{:S(2)}, u32[]{:S(2)}) collective-permute-start(bf16[768,768]{1,0:T(8,128)(2,1)} %add_convert_fusion.3), channel_id=1, source_target_pairs={{0,2},{1,3},{2,0},{3,1},{4,5},{5,4},{6,7},{7,6},{8,10},{9,11},{10,... | collective-permute-start | bytes 3538952 | tf_op jit(solution)/shard_map/ppermute | solution.py:62
  485.3 57.1 %collective-permute-start.46 = (bf16[768,768]{1,0:T(8,128)(2,1)}, bf16[768,768]{1,0:T(8,128)(2,1)}, u32[]{:S(2)}, u32[]{:S(2)}) collective-permute-start(bf16[768,768]{1,0:T(8,128)(2,1)} %add_convert_fusion.5), channel_id=1, source_target_pairs={{0,1},{1,0},{2,3},{3,2},{4,6},{5,7},{6,4},{7,5},{8,9},{9,8},{10,11... | collective-permute-start | bytes 3538952 | tf_op jit(solution)/shard_map/ppermute | solution.py:62
  540.8 32.9 %collective-permute-start.45 = (bf16[768,768]{1,0:T(8,128)(2,1)}, bf16[768,768]{1,0:T(8,128)(2,1)}, u32[]{:S(2)}, u32[]{:S(2)}) collective-permute-start(bf16[768,768]{1,0:T(8,128)(2,1)} %add_convert_fusion.1), channel_id=1, source_target_pairs={{0,1},{1,0},{2,3},{3,2},{4,6},{5,7},{6,4},{7,5},{8,9},{9,8},{10,11... | collective-permute-start | bytes 3538952 | tf_op jit(solution)/shard_map/ppermute | solution.py:62
  542.4 31.4 %collective-permute-start.47 = (bf16[768,768]{1,0:T(8,128)(2,1)}, bf16[768,768]{1,0:T(8,128)(2,1)}, u32[]{:S(2)}, u32[]{:S(2)}) collective-permute-start(bf16[768,768]{1,0:T(8,128)(2,1)} %collective-permute-done.46), channel_id=1, source_target_pairs={{0,4},{1,5},{2,6},{3,7},{4,0},{5,1},{6,2},{7,3},{8,12},{9,13},{10,... | collective-permute-start | bytes 3538952 | tf_op jit(solution)/shard_map/ppermute | solution.py:62
  542.4 33.8 %collective-permute-start.48 = (bf16[768,768]{1,0:T(8,128)(2,1)}, bf16[768,768]{1,0:T(8,128)(2,1)}, u32[]{:S(2)}, u32[]{:S(2)}) collective-permute-start(bf16[768,768]{1,0:T(8,128)(2,1)} %all-reduce.5.cloned.1.call-done), channel_id=1, source_target_pairs={{0,4},{1,5},{2,6},{3,7},{4,0},{5,1},{6,2},{7,3},{8,12},{9,13},{10,... | collective-permute-start | bytes 3538952 | tf_op jit(solution)/shard_map/ppermute | solution.py:62
  558.4 15.1 %all-to-all-start.7 = ((bf16[4,128,768]{2,1,0:T(8,128)(2,1)}), bf16[4,128,768]{2,1,0:T(8,128)(2,1)S(1)}, u32[]{:S(2)}, u32[]{:S(2)}) async-start(bf16[4,128,768]{2,1,0:T(8,128)(2,1)} %bitcast.41), calls=%async_computation.7 | async-start | bytes 1572864 | tf_op jit(solution)/shard_map/all_to_all | solution.py:681
  562.4 13.8 %collective-permute-start.49 = (bf16[384,768]{1,0:T(8,128)(2,1)S(1)}, bf16[384,768]{1,0:T(8,128)(2,1)S(1)}, u32[]{:S(2)}, u32[]{:S(2)}) collective-permute-start(bf16[384,768]{1,0:T(8,128)(2,1)S(1)} %copy-done.248), channel_id=1, source_target_pairs={{0,4},{1,5},{2,6},{3,7},{4,0},{5,1},{6,2},{7,3},{8,12},{9,13},{10,... | collective-permute-start | bytes 1769480 | tf_op jit(solution)/shard_map/ppermute | solution.py:62
  (289 other events, 1331.2 us)
Sparse Core Ops, SparseCore 0:
  405.8 54.3 all-reduce.4
  486.0 38.4 all-reduce.6

commit v10 on v9

--- a/solution.py
+++ b/solution.py
@@ -311,7 +311,7 @@
         + [pltpu.VMEM((2,) + shape, BF) for shape in big]
         + [dma((2, takes)), dma((2, gives))]
         + list(scratch),
-        compiler_params=pltpu.CompilerParams(vmem_limit_bytes=28 << 20),
+        compiler_params=pltpu.CompilerParams(vmem_limit_bytes=63 << 20),
         cost_estimate=small_cost(),
     )(*shared, total, *[x for block in blocks for x in block])
     smalls, bigs = out[1 : 1 + count], out[1 + count :]

time: 705 us -> 647 us (0.918)
  local copies, waits for them, and re-layouts: 129 us -> 54 us
  Pallas kernels: 283 us -> 308 us
    unnamed x561 -> x357, local copies, waits for them, and re-layouts: 105 us -> 33.2 us
    pallas_call x7, Pallas kernels: 138 us -> 162 us  [streamed_blocks(): pl.pallas_call(kernel, name=name, out_shape=(jax.ShapeDtypeStruct(total.s...]
    reduce_sum x8, other arithmetic: 18.3 us -> 10.4 us  [total_rows(): return jnp.sum(values, axis=0)]
  transfers between devices with their start and end apart: 60 -> 60, of which waited for: 8 -> 8; matrix products, arithmetic and copies ran while one was open for 19% -> 20% of each run, Pallas kernels for 30% -> 37%
where the time goes in v10:
time: 647 us; the launch traced here: 637 us
  Pallas kernels  308 us (48%)
  other arithmetic  103 us (16%)
  starting transfers between devices  67.1 us (10%)
  local copies, waits for them, and re-layouts  54 us (8%)
  matrix products  46.4 us (7%)
  waiting for transfers between devices  39.5 us (6%)
  between operations  19.9 us (3%)
    pallas_call x7, Pallas kernels, streamed_blocks(): pl.pallas_call(kernel, name=name, out_shape=(jax.ShapeDtypeStruct(total.s...  162 us
    pallas_call x1, Pallas kernels, last_sums(): pl.pallas_call(body, name='last_sums', out_shape=tuple((jax.ShapeDtypeStr...  73.6 us
    pallas_call x8, Pallas kernels, attend_forward(): pl.pallas_call(body, name='attend_forward', out_shape=(narrow, narrow, na...  54.1 us
    dot_general x18, matrix products, mm(): lax.dot_general(a, b, (((ca,), (cb,)), ((), ())), preferred_element_type=...  42.3 us
    convert_element_type x18, other arithmetic, plus(): return total.astype(BF)  37.2 us
    ppermute x50, starting transfers between devices, send(): return lax.ppermute(values, PLANE, plane_pairs(kind))  33.7 us
    unnamed x357, local copies, waits for them, and re-layouts  33.2 us
    pallas_call x1, Pallas kernels, gather_anchors(): pl.pallas_call(body, name='gather_anchors', out_shape=jax.ShapeDtypeStruc...  17.8 us
  transfers between devices with their start and end apart: 60, of which 8 were waited for; matrix products, arithmetic and copies ran while one was open for 20% of the time, Pallas kernels for 37%

profile of v10, /device:TPU:0, one launch (start us, length us, event | category | flops | bytes accessed | tf_op | source)
XLA Modules:
  0.0 637.2 jit_solution(16474895474180464169)
XLA Ops:
  7.2 5.2 all-to-all-start
  18.2 3.9 slice_bitcast_fusion
  29.6 6.4 %attend_forward.8 = (bf16[512,192]{1,0:T(8,128)(2,1)S(1)}, bf16[512,192]{1,0:T(8,128)(2,1)S(1)}, bf16[512,192]{1,0:T(8,128)(2,1)S(1)}, bf16[512,192]{1,0:T(8,128...) custom-call(bf16[512,768]{1,0:T(8,128)(2,1)S(1)} %bitcast.170, ...), custom_call_target="tpu_custom_call" | custom-call | flops 1048576 | bytes 1024 | tf_op jit(solution)/shard_map/attend_forward/pallas_call | solution.py:355
  40.6 6.4 %attend_forward.9 = (bf16[512,192]{1,0:T(8,128)(2,1)S(1)}, bf16[512,192]{1,0:T(8,128)(2,1)S(1)}, bf16[512,192]{1,0:T(8,128)(2,1)S(1)}, bf16[512,192]{1,0:T(8,128...) custom-call(bf16[512,768]{1,0:T(8,128)(2,1)S(1)} %bitcast.171, ...), custom_call_target="tpu_custom_call" | custom-call | flops 1048576 | bytes 1024 | tf_op jit(solution)/shard_map/attend_forward/pallas_call | solution.py:355
  49.2 6.4 %attend_forward.10 = (bf16[512,192]{1,0:T(8,128)(2,1)S(1)}, bf16[512,192]{1,0:T(8,128)(2,1)S(1)}, bf16[512,192]{1,0:T(8,128)(2,1)S(1)}, bf16[512,192]{1,0:T(8,12...) custom-call(bf16[512,768]{1,0:T(8,128)(2,1)S(1)} %bitcast.172, ...), custom_call_target="tpu_custom_call" | custom-call | flops 1048576 | bytes 1024 | tf_op jit(solution)/shard_map/attend_forward/pallas_call | solution.py:355
  58.9 6.6 %attend_forward.11 = (bf16[512,192]{1,0:T(8,128)(2,1)S(1)}, bf16[512,192]{1,0:T(8,128)(2,1)S(1)}, bf16[512,192]{1,0:T(8,128)(2,1)S(1)}, bf16[512,192]{1,0:T(8,12...) custom-call(bf16[512,768]{1,0:T(8,128)(2,1)S(1)} %bitcast.173, ...), custom_call_target="tpu_custom_call" | custom-call | flops 1048576 | bytes 1024 | tf_op jit(solution)/shard_map/attend_forward/pallas_call | solution.py:355
  65.6 2.8 collective-permute-done.7.refs_10_
  74.6 3.6 fusion.24
  80.6 3.4 fusion.29
  86.4 3.4 fusion.34
  99.6 3.5 all-to-all-start.2
  113.8 5.9 all-to-all-done.2
  119.7 2.9 fusion.49
  122.6 7.9 %attend_forward.12 = (bf16[512,192]{1,0:T(8,128)(2,1)S(1)}, bf16[512,192]{1,0:T(8,128)(2,1)S(1)}, bf16[512,192]{1,0:T(8,128)(2,1)S(1)}, bf16[512,192]{1,0:T(8,12...) custom-call(bf16[512,768]{1,0:T(8,128)(2,1)S(1)} %get-tuple-element.478.refs_0_.refs_1_, ...), custom_call_target="tpu_custom_call" | custom-call | flops 1048576 | bytes 1024 | tf_op jit(solution)/shard_map/attend_forward/pallas_call | solution.py:355
  135.2 4.0 all-to-all-start.1
  140.7 7.6 %attend_forward.13 = (bf16[512,192]{1,0:T(8,128)(2,1)S(1)}, bf16[512,192]{1,0:T(8,128)(2,1)S(1)}, bf16[512,192]{1,0:T(8,128)(2,1)S(1)}, bf16[512,192]{1,0:T(8,12...) custom-call(bf16[512,768]{1,0:T(8,128)(2,1)S(1)} %get-tuple-element.478.refs_0_.refs_1_, ...), custom_call_target="tpu_custom_call" | custom-call | flops 1048576 | bytes 1024 | tf_op jit(solution)/shard_map/attend_forward/pallas_call | solution.py:355
  151.9 6.4 %attend_forward.14 = (bf16[512,192]{1,0:T(8,128)(2,1)S(1)}, bf16[512,192]{1,0:T(8,128)(2,1)S(1)}, bf16[512,192]{1,0:T(8,128)(2,1)S(1)}, bf16[512,192]{1,0:T(8,12...) custom-call(bf16[512,768]{1,0:T(8,128)(2,1)S(1)} %get-tuple-element.478.refs_0_.refs_1_, ...), custom_call_target="tpu_custom_call" | custom-call | flops 1048576 | bytes 1024 | tf_op jit(solution)/shard_map/attend_forward/pallas_call | solution.py:355
  164.5 6.4 %attend_forward.15 = (bf16[512,192]{1,0:T(8,128)(2,1)S(1)}, bf16[512,192]{1,0:T(8,128)(2,1)S(1)}, bf16[512,192]{1,0:T(8,128)(2,1)S(1)}, bf16[512,192]{1,0:T(8,12...) custom-call(bf16[512,768]{1,0:T(8,128)(2,1)S(1)} %get-tuple-element.478.refs_0_.refs_1_, ...), custom_call_target="tpu_custom_call" | custom-call | flops 1048576 | bytes 1024 | tf_op jit(solution)/shard_map/attend_forward/pallas_call | solution.py:355
  171.5 2.8 broadcast_select_fusion.4
  178.0 3.7 fusion.4
  184.1 3.4 fusion.9
  189.8 3.4 fusion.14
  195.7 3.5 all-to-all-start.5
  200.4 10.5 %all-to-all-done.5 = bf16[4,128,768]{2,1,0:T(8,128)(2,1)S(1)} async-done(((bf16[4,128,768]{2,1,0:T(8,128)(2,1)}), bf16[4,128,768]{2,1,0:T(8,128)(2,1)S(1)}, u32[]{:S(2)}, u32[]{:S(2)}) %all-to-all-start.5) | async-done | bytes 786464 | tf_op jit(solution)/shard_map/all_to_all | solution.py:674
  221.4 4.6 all-to-all-start.3
  227.8 17.8 %gather_anchors.1 = bf16[4,8,4,768]{3,2,1,0:T(4,128)(2,1)} custom-call(bf16[4,768]{1,0:T(4,128)(2,1)} %convolution_convert_fusion.refs_0_), custom_call_target="tpu_custom_call" | custom-call | tf_op jit(solution)/shard_map/gather_anchors/pallas_call | solution.py:421
  247.6 32.6 %ffn_backward.3 = (f32[512,768]{1,0:T(8,128)}, f32[1,768]{1,0:T(1,128)}, f32[1,768]{1,0:T(1,128)}, f32[1,768]{1,0:T(1,128)}, f32[1,768]{1,0:T(1,128)}, /*index=5...) custom-call(bf16[512,768]{1,0:T(8,128)(2,1)} %convert_element_type.5, ...), custom_call_target="tpu_custom_call" | custom-call | flops 1048576 | bytes 1024 | tf_op jit(solution)/shard_map/ffn_backward/pallas_call | solution.py:302
  281.3 2.6 multiply_reduce_fusion.1
  295.3 31.2 %attend_backward.4 = (f32[512,768]{1,0:T(8,128)}, f32[1,384]{1,0:T(1,128)}, f32[1,384]{1,0:T(1,128)}, f32[1,384]{1,0:T(1,128)}, bf16[384,768]{1,0:T(8,128)(2,1)}...) custom-call(bf16[512,768]{1,0:T(8,128)(2,1)} %convert_element_type.5, ...), custom_call_target="tpu_custom_call" | custom-call | flops 1048576 | bytes 1024 | tf_op jit(solution)/shard_map/attend_backward/pallas_call | solution.py:302
  326.6 2.9 add_convert_fusion.7
  329.5 13.9 %attend_backward.5 = (f32[512,768]{1,0:T(8,128)}, f32[1,384]{1,0:T(1,128)}, bf16[384,768]{1,0:T(8,128)(2,1)}, bf16[384,768]{1,0:T(8,128)(2,1)}) custom-call(bf16[512,768]{1,0:T(8,128)(2,1)} %convert_element_type.524.refs_0_, bf16[512,768]{1,0:T(8,128)(2,1)} %copy-done.6, s32[512,1]{1,0:T(8,128)} %copy-done.1, s32[1,512]{1,0:T(1,128)} %copy-done.32, ...), custom_call_target="tpu_custom_call" | custom-call | flops 1048576 | bytes 1024 | tf_op jit(solution)/shard_map/attend_backward/pallas_call | solution.py:302
  346.1 4.3 all-to-all-start.4
  356.0 9.1 %collective-permute-done.29 = bf16[768,768]{1,0:T(8,128)(2,1)} collective-permute-done((bf16[768,768]{1,0:T(8,128)(2,1)}, bf16[768,768]{1,0:T(8,128)(2,1)}, u32[]{:S(2)}, u32[]{:S(2)}) %collective-permute-start.29) | collective-permute-done | bytes 1179680 | tf_op jit(solution)/shard_map/ppermute | solution.py:62
  365.1 3.1 add_convert_fusion.6
  369.4 3.7 multiply_reduce_fusion.2
  379.9 4.2 all-to-all-start.6
  384.1 19.6 %ffn_backward.4 = (f32[512,768]{1,0:T(8,128)}, f32[1,768]{1,0:T(1,128)}, f32[1,768]{1,0:T(1,128)}, bf16[768,768]{1,0:T(8,128)(2,1)}, bf16[768,768]{1,0:T(8,128)(...) custom-call(bf16[512,768]{1,0:T(8,128)(2,1)} %convert_element_type.544.refs_0_, bf16[512,768]{1,0:T(8,128)(2,1)} %copy-done.96, ...), custom_call_target="tpu_custom_call" | custom-call | flops 1048576 | bytes 1024 | tf_op jit(solution)/shard_map/ffn_backward/pallas_call | solution.py:302
  407.8 19.8 %ffn_backward.5 = (f32[512,768]{1,0:T(8,128)}, f32[1,768]{1,0:T(1,128)}, f32[1,768]{1,0:T(1,128)}, bf16[768,768]{1,0:T(8,128)(2,1)}, bf16[768,768]{1,0:T(8,128)(...) custom-call(bf16[512,768]{1,0:T(8,128)(2,1)} %convert_element_type.544.refs_0_, bf16[512,768]{1,0:T(8,128)(2,1)} %copy-done.96, ...), custom_call_target="tpu_custom_call" | custom-call | flops 1048576 | bytes 1024 | tf_op jit(solution)/shard_map/ffn_backward/pallas_call | solution.py:302
  434.8 2.7 add_convert_fusion.2
  437.5 2.7 add_convert_fusion.3
  440.2 2.7 add_convert_fusion.4
  443.0 2.6 add_convert_fusion.5
  449.3 31.3 %attend_backward.6 = (f32[512,768]{1,0:T(8,128)}, f32[1,384]{1,0:T(1,128)}, f32[1,384]{1,0:T(1,128)}, f32[1,384]{1,0:T(1,128)}, bf16[384,768]{1,0:T(8,128)(2,1)}...) custom-call(bf16[512,768]{1,0:T(8,128)(2,1)} %convert_element_type.5, ...), custom_call_target="tpu_custom_call" | custom-call | flops 1048576 | bytes 1024 | tf_op jit(solution)/shard_map/attend_backward/pallas_call | solution.py:302
  480.6 2.9 add_convert_fusion.1
  486.3 13.9 %attend_backward.7 = (f32[512,768]{1,0:T(8,128)}, f32[1,384]{1,0:T(1,128)}, bf16[384,768]{1,0:T(8,128)(2,1)}, bf16[384,768]{1,0:T(8,128)(2,1)}) custom-call(bf16[512,768]{1,0:T(8,128)(2,1)} %convert_element_type.569.refs_0_, bf16[512,768]{1,0:T(8,128)(2,1)} %bitcast.175, s32[512,1]{1,0:T(8,128)} %copy-done.1, s32[1,512]{1,0:T(1,128)} %copy-done.32, ...), custom_call_target="tpu_custom_call" | custom-call | flops 1048576 | bytes 1024 | tf_op jit(solution)/shard_map/attend_backward/pallas_call | solution.py:302
  502.7 3.8 all-to-all-start.7
  510.5 7.7 %all-to-all-done.7 = bf16[4,128,768]{2,1,0:T(8,128)(2,1)S(1)} async-done(((bf16[4,128,768]{2,1,0:T(8,128)(2,1)}), bf16[4,128,768]{2,1,0:T(8,128)(2,1)S(1)}, u32[]{:S(2)}, u32[]{:S(2)}) %all-to-all-start.7) | async-done | bytes 786464 | tf_op jit(solution)/shard_map/all_to_all | solution.py:681
  522.8 73.6 %last_sums.1 = (bf16[2,4,96,768]{3,2,1,0:T(8,128)(2,1)S(1)}, bf16[2,4,96,768]{3,2,1,0:T(8,128)(2,1)S(1)}, bf16[2,4,48,768]{3,2,1,0:T(8,128)(2,1)S(1)}, bf16[2,4,...) custom-call(bf16[2,4,96,768]{3,2,1,0:T(8,128)(2,1)S(1)} %bitcast.176, bf16[2,4,48,768]{3,2,1,0:T(8,128)(2,1)S(1)} %bitcast.177, ...), custom_call_target="tpu_custom_call" | custom-call | tf_op jit(solution)/shard_map/last_sums/pallas_call | solution.py:651
  (626 shorter events, 184.0 us)
Async XLA Ops:
  7.2 22.2 %all-to-all-start = ((bf16[4,128,768]{2,1,0:T(8,128)(2,1)}), bf16[4,128,768]{2,1,0:T(8,128)(2,1)S(1)}, u32[]{:S(2)}, u32[]{:S(2)}) async-start(bf16[4,128,768]{2,1,0:T(8,128)(2,1)} %bitcast.198), calls=%async_computation | async-start | bytes 1572864 | tf_op jit(solution)/shard_map/all_to_all | solution.py:674
  16.0 20.1 %collective-permute-start = (bf16[400,768]{1,0:T(8,128)(2,1)S(1)}, bf16[400,768]{1,0:T(8,128)(2,1)S(1)}, u32[]{:S(2)}, u32[]{:S(2)}) collective-permute-start(bf16[400,768]{1,0:T(8,128)(2,1)S(1)} %pad_maximum_fusion.2.refs_1_.refs_5_), channel_id=1, source_target_pairs={{0,1},{1,0},{2,3},{3,2},{4,6},{5,7},{6,4},{7,5},{8,9},{9,8},{10,11... | collective-permute-start | bytes 1843208 | tf_op jit(solution)/shard_map/ppermute | solution.py:62
  18.1 18.3 %collective-permute-start.1 = (bf16[400,768]{1,0:T(8,128)(2,1)S(1)}, bf16[400,768]{1,0:T(8,128)(2,1)S(1)}, u32[]{:S(2)}, u32[]{:S(2)}) collective-permute-start(bf16[400,768]{1,0:T(8,128)(2,1)S(1)} %fusion.54.refs_2_.refs_6_), channel_id=1, source_target_pairs={{0,1},{1,0},{2,3},{3,2},{4,6},{5,7},{6,4},{7,5},{8,9},{9,8},{10,11... | collective-permute-start | bytes 1843208 | tf_op jit(solution)/shard_map/ppermute | solution.py:62
  22.1 43.5 %collective-permute-start.6 = (bf16[768,768]{1,0:T(8,128)(2,1)}, bf16[768,768]{1,0:T(8,128)(2,1)}, u32[]{:S(2)}, u32[]{:S(2)}) collective-permute-start(bf16[768,768]{1,0:T(8,128)(2,1)} %get-tuple-element.230.refs_5_), channel_id=1, source_target_pairs={{0,1},{1,0},{2,3},{3,2},{4,6},{5,7},{6,4},{7,5},{8,9},{9,8},{10,11... | collective-permute-start | bytes 3538952 | tf_op jit(solution)/shard_map/ppermute | solution.py:62
  24.0 44.3 %collective-permute-start.7 = (bf16[768,768]{1,0:T(8,128)(2,1)}, bf16[768,768]{1,0:T(8,128)(2,1)}, u32[]{:S(2)}, u32[]{:S(2)}) collective-permute-start(bf16[768,768]{1,0:T(8,128)(2,1)} %get-tuple-element.231.refs_6_), channel_id=1, source_target_pairs={{0,1},{1,0},{2,3},{3,2},{4,6},{5,7},{6,4},{7,5},{8,9},{9,8},{10,11... | collective-permute-start | bytes 3538952 | tf_op jit(solution)/shard_map/ppermute | solution.py:62
  36.4 12.7 %collective-permute-start.2 = (bf16[400,768]{1,0:T(8,128)(2,1)S(1)}, bf16[400,768]{1,0:T(8,128)(2,1)S(1)}, u32[]{:S(2)}, u32[]{:S(2)}) collective-permute-start(bf16[400,768]{1,0:T(8,128)(2,1)S(1)} %collective-permute-done.refs_1_.refs_12_), channel_id=1, source_target_pairs={{0,4},{1,5},{2,6},{3,7},{4,0},{5,1},{6,2},{7,3},{8,12},{9,13},{10,... | collective-permute-start | bytes 1843208 | tf_op jit(solution)/shard_map/ppermute | solution.py:62
  36.5 12.7 %collective-permute-start.3 = (bf16[400,768]{1,0:T(8,128)(2,1)S(1)}, bf16[400,768]{1,0:T(8,128)(2,1)S(1)}, u32[]{:S(2)}, u32[]{:S(2)}) collective-permute-start(bf16[400,768]{1,0:T(8,128)(2,1)S(1)} %collective-permute-done.1.refs_2_.refs_13_), channel_id=1, source_target_pairs={{0,4},{1,5},{2,6},{3,7},{4,0},{5,1},{6,2},{7,3},{8,12},{9,13},{10,... | collective-permute-start | bytes 1843208 | tf_op jit(solution)/shard_map/ppermute | solution.py:62
  37.0 18.7 %collective-permute-start.4 = (bf16[400,768]{1,0:T(8,128)(2,1)S(1)}, bf16[400,768]{1,0:T(8,128)(2,1)S(1)}, u32[]{:S(2)}, u32[]{:S(2)}) collective-permute-start(bf16[400,768]{1,0:T(8,128)(2,1)S(1)} %broadcast_select_fusion.10), channel_id=1, source_target_pairs={{0,2},{1,3},{2,0},{3,1},{4,5},{5,4},{6,7},{7,6},{8,10},{9,11},{10,... | collective-permute-start | bytes 1843208 | tf_op jit(solution)/shard_map/ppermute | solution.py:62
  56.6 29.7 %collective-permute-start.8 = (bf16[384,768]{1,0:T(8,128)(2,1)}, bf16[384,768]{1,0:T(8,128)(2,1)}, u32[]{:S(2)}, u32[]{:S(2)}) collective-permute-start(bf16[384,768]{1,0:T(8,128)(2,1)} %bitcast.16.refs_1_.refs_5_), channel_id=1, source_target_pairs={{0,1},{1,0},{2,3},{3,2},{4,6},{5,7},{6,4},{7,5},{8,9},{9,8},{10,11... | collective-permute-start | bytes 1769480 | tf_op jit(solution)/shard_map/ppermute | solution.py:62
  58.1 28.3 %collective-permute-start.9 = (bf16[384,768]{1,0:T(8,128)(2,1)}, bf16[384,768]{1,0:T(8,128)(2,1)}, u32[]{:S(2)}, u32[]{:S(2)}) collective-permute-start(bf16[384,768]{1,0:T(8,128)(2,1)} %pad_maximum_fusion.3.refs_2_.refs_6_), channel_id=1, source_target_pairs={{0,1},{1,0},{2,3},{3,2},{4,6},{5,7},{6,4},{7,5},{8,9},{9,8},{10,11... | collective-permute-start | bytes 1769480 | tf_op jit(solution)/shard_map/ppermute | solution.py:62
  68.3 18.1 %collective-permute-start.10 = (bf16[768,768]{1,0:T(8,128)(2,1)}, bf16[768,768]{1,0:T(8,128)(2,1)}, u32[]{:S(2)}, u32[]{:S(2)}) collective-permute-start(bf16[768,768]{1,0:T(8,128)(2,1)} %collective-permute-done.6.refs_9_), channel_id=1, source_target_pairs={{0,4},{1,5},{2,6},{3,7},{4,0},{5,1},{6,2},{7,3},{8,12},{9,13},{10,... | collective-permute-start | bytes 3538952 | tf_op jit(solution)/shard_map/ppermute | solution.py:62
  70.9 18.9 %collective-permute-start.11 = (bf16[768,768]{1,0:T(8,128)(2,1)}, bf16[768,768]{1,0:T(8,128)(2,1)}, u32[]{:S(2)}, u32[]{:S(2)}) collective-permute-start(bf16[768,768]{1,0:T(8,128)(2,1)} %collective-permute-done.7.refs_10_), channel_id=1, source_target_pairs={{0,4},{1,5},{2,6},{3,7},{4,0},{5,1},{6,2},{7,3},{8,12},{9,13},{10,... | collective-permute-start | bytes 3538952 | tf_op jit(solution)/shard_map/ppermute | solution.py:62
  72.8 21.3 %collective-permute-start.12 = (bf16[768,768]{1,0:T(8,128)(2,1)S(1)}, bf16[768,768]{1,0:T(8,128)(2,1)}, u32[]{:S(2)}, u32[]{:S(2)}) collective-permute-start(bf16[768,768]{1,0:T(8,128)(2,1)S(1)} %copy-done.128), channel_id=1, source_target_pairs={{0,2},{1,3},{2,0},{3,1},{4,5},{5,4},{6,7},{7,6},{8,10},{9,11},{10,... | collective-permute-start | bytes 3538952 | tf_op jit(solution)/shard_map/ppermute | solution.py:62
  94.1 11.7 %collective-permute-start.13 = (bf16[768,768]{1,0:T(8,128)(2,1)}, bf16[768,768]{1,0:T(8,128)(2,1)}, u32[]{:S(2)}, u32[]{:S(2)}) collective-permute-start(bf16[768,768]{1,0:T(8,128)(2,1)} %collective-permute-done.12), channel_id=1, source_target_pairs={{0,4},{1,5},{2,6},{3,7},{4,0},{5,1},{6,2},{7,3},{8,12},{9,13},{10,... | collective-permute-start | bytes 3538952 | tf_op jit(solution)/shard_map/ppermute | solution.py:62
  95.5 56.4 %collective-permute-start.16 = (bf16[384,768]{1,0:T(8,128)(2,1)}, bf16[384,768]{1,0:T(8,128)(2,1)S(1)}, u32[]{:S(2)}, u32[]{:S(2)}) collective-permute-start(bf16[384,768]{1,0:T(8,128)(2,1)} %collective-permute-done.8.refs_1_.refs_12_), channel_id=1, source_target_pairs={{0,4},{1,5},{2,6},{3,7},{4,0},{5,1},{6,2},{7,3},{8,12},{9,13},{10,... | collective-permute-start | bytes 1769480 | tf_op jit(solution)/shard_map/ppermute | solution.py:62
  96.1 55.9 %collective-permute-start.17 = (bf16[384,768]{1,0:T(8,128)(2,1)}, bf16[384,768]{1,0:T(8,128)(2,1)S(1)}, u32[]{:S(2)}, u32[]{:S(2)}) collective-permute-start(bf16[384,768]{1,0:T(8,128)(2,1)} %collective-permute-done.9.refs_2_.refs_13_), channel_id=1, source_target_pairs={{0,4},{1,5},{2,6},{3,7},{4,0},{5,1},{6,2},{7,3},{8,12},{9,13},{10,... | collective-permute-start | bytes 1769480 | tf_op jit(solution)/shard_map/ppermute | solution.py:62
  98.1 53.8 %collective-permute-start.14 = (bf16[384,768]{1,0:T(8,128)(2,1)}, bf16[384,768]{1,0:T(8,128)(2,1)}, u32[]{:S(2)}, u32[]{:S(2)}) collective-permute-start(bf16[384,768]{1,0:T(8,128)(2,1)} %broadcast_select_fusion.13), channel_id=1, source_target_pairs={{0,2},{1,3},{2,0},{3,1},{4,5},{5,4},{6,7},{7,6},{8,10},{9,11},{10,... | collective-permute-start | bytes 1769480 | tf_op jit(solution)/shard_map/ppermute | solution.py:62
  99.6 20.1 %all-to-all-start.2 = ((bf16[4,128,768]{2,1,0:T(8,128)(2,1)}), bf16[4,128,768]{2,1,0:T(8,128)(2,1)S(1)}, u32[]{:S(2)}, u32[]{:S(2)}) async-start(bf16[4,128,768]{2,1,0:T(8,128)(2,1)} %bitcast.199), calls=%async_computation.2 | async-start | bytes 1572864 | tf_op jit(solution)/shard_map/all_to_all | solution.py:674
  103.1 67.8 %collective-permute-start.18 = (bf16[768,768]{1,0:T(8,128)(2,1)}, bf16[768,768]{1,0:T(8,128)(2,1)}, u32[]{:S(2)}, u32[]{:S(2)}) collective-permute-start(bf16[768,768]{1,0:T(8,128)(2,1)} %get-tuple-element.253.refs_5_), channel_id=1, source_target_pairs={{0,1},{1,0},{2,3},{3,2},{4,6},{5,7},{6,4},{7,5},{8,9},{9,8},{10,11... | collective-permute-start | bytes 3538952 | tf_op jit(solution)/shard_map/ppermute | solution.py:62
  105.7 65.2 %collective-permute-start.19 = (bf16[768,768]{1,0:T(8,128)(2,1)}, bf16[768,768]{1,0:T(8,128)(2,1)}, u32[]{:S(2)}, u32[]{:S(2)}) collective-permute-start(bf16[768,768]{1,0:T(8,128)(2,1)} %get-tuple-element.254.refs_6_), channel_id=1, source_target_pairs={{0,1},{1,0},{2,3},{3,2},{4,6},{5,7},{6,4},{7,5},{8,9},{9,8},{10,11... | collective-permute-start | bytes 3538952 | tf_op jit(solution)/shard_map/ppermute | solution.py:62
  135.2 27.2 %all-to-all-start.1 = ((bf16[4,128,768]{2,1,0:T(8,128)(2,1)}), bf16[4,128,768]{2,1,0:T(8,128)(2,1)S(1)}, u32[]{:S(2)}, u32[]{:S(2)}) async-start(bf16[4,128,768]{2,1,0:T(8,128)(2,1)} %bitcast.190), calls=%async_computation.1 | async-start | bytes 1572864 | tf_op jit(solution)/shard_map/all_to_all | solution.py:681
  171.0 18.8 %collective-permute-start.20 = (bf16[768,768]{1,0:T(8,128)(2,1)}, bf16[768,768]{1,0:T(8,128)(2,1)}, u32[]{:S(2)}, u32[]{:S(2)}) collective-permute-start(bf16[768,768]{1,0:T(8,128)(2,1)} %collective-permute-done.18.refs_9_), channel_id=1, source_target_pairs={{0,4},{1,5},{2,6},{3,7},{4,0},{5,1},{6,2},{7,3},{8,12},{9,13},{10,... | collective-permute-start | bytes 3538952 | tf_op jit(solution)/shard_map/ppermute | solution.py:62
  174.3 18.9 %collective-permute-start.21 = (bf16[768,768]{1,0:T(8,128)(2,1)}, bf16[768,768]{1,0:T(8,128)(2,1)}, u32[]{:S(2)}, u32[]{:S(2)}) collective-permute-start(bf16[768,768]{1,0:T(8,128)(2,1)} %collective-permute-done.19.refs_10_), channel_id=1, source_target_pairs={{0,4},{1,5},{2,6},{3,7},{4,0},{5,1},{6,2},{7,3},{8,12},{9,13},{10,... | collective-permute-start | bytes 3538952 | tf_op jit(solution)/shard_map/ppermute | solution.py:62
  174.9 20.6 %collective-permute-start.22 = (bf16[768,768]{1,0:T(8,128)(2,1)}, bf16[768,768]{1,0:T(8,128)(2,1)}, u32[]{:S(2)}, u32[]{:S(2)}) collective-permute-start(bf16[768,768]{1,0:T(8,128)(2,1)} %broadcast_select_fusion.4), channel_id=1, source_target_pairs={{0,2},{1,3},{2,0},{3,1},{4,5},{5,4},{6,7},{7,6},{8,10},{9,11},{10,... | collective-permute-start | bytes 3538952 | tf_op jit(solution)/shard_map/ppermute | solution.py:62
  195.6 17.0 %collective-permute-start.23 = (bf16[768,768]{1,0:T(8,128)(2,1)}, bf16[768,768]{1,0:T(8,128)(2,1)S(1)}, u32[]{:S(2)}, u32[]{:S(2)}) collective-permute-start(bf16[768,768]{1,0:T(8,128)(2,1)} %collective-permute-done.22), channel_id=1, source_target_pairs={{0,4},{1,5},{2,6},{3,7},{4,0},{5,1},{6,2},{7,3},{8,12},{9,13},{10,... | collective-permute-start | bytes 3538952 | tf_op jit(solution)/shard_map/ppermute | solution.py:62
  195.7 15.2 %all-to-all-start.5 = ((bf16[4,128,768]{2,1,0:T(8,128)(2,1)}), bf16[4,128,768]{2,1,0:T(8,128)(2,1)S(1)}, u32[]{:S(2)}, u32[]{:S(2)}) async-start(bf16[4,128,768]{2,1,0:T(8,128)(2,1)} %bitcast.200), calls=%async_computation.5 | async-start | bytes 1572864 | tf_op jit(solution)/shard_map/all_to_all | solution.py:674
  221.4 58.8 %all-to-all-start.3 = ((bf16[4,128,768]{2,1,0:T(8,128)(2,1)}), bf16[4,128,768]{2,1,0:T(8,128)(2,1)}, u32[]{:S(2)}, u32[]{:S(2)}) async-start(bf16[4,128,768]{2,1,0:T(8,128)(2,1)} %bitcast.187), calls=%async_computation.3 | async-start | bytes 1572864 | tf_op jit(solution)/shard_map/all_to_all | solution.py:681
  290.7 35.9 %collective-permute-start.28 = (bf16[768,768]{1,0:T(8,128)(2,1)}, bf16[768,768]{1,0:T(8,128)(2,1)}, u32[]{:S(2)}, u32[]{:S(2)}) collective-permute-start(bf16[768,768]{1,0:T(8,128)(2,1)} %add_convert_fusion.9), channel_id=1, source_target_pairs={{0,2},{1,3},{2,0},{3,1},{4,5},{5,4},{6,7},{7,6},{8,10},{9,11},{10,... | collective-permute-start | bytes 3538952 | tf_op jit(solution)/shard_map/ppermute | solution.py:62
  292.3 53.4 %collective-permute-start.30 = (bf16[768,768]{1,0:T(8,128)(2,1)}, bf16[768,768]{1,0:T(8,128)(2,1)}, u32[]{:S(2)}, u32[]{:S(2)}) collective-permute-start(bf16[768,768]{1,0:T(8,128)(2,1)} %add_convert_fusion.11), channel_id=1, source_target_pairs={{0,1},{1,0},{2,3},{3,2},{4,6},{5,7},{6,4},{7,5},{8,9},{9,8},{10,11... | collective-permute-start | bytes 3538952 | tf_op jit(solution)/shard_map/ppermute | solution.py:62
  344.3 20.8 %collective-permute-start.29 = (bf16[768,768]{1,0:T(8,128)(2,1)}, bf16[768,768]{1,0:T(8,128)(2,1)}, u32[]{:S(2)}, u32[]{:S(2)}) collective-permute-start(bf16[768,768]{1,0:T(8,128)(2,1)} %add_convert_fusion.7), channel_id=1, source_target_pairs={{0,1},{1,0},{2,3},{3,2},{4,6},{5,7},{6,4},{7,5},{8,9},{9,8},{10,11... | collective-permute-start | bytes 3538952 | tf_op jit(solution)/shard_map/ppermute | solution.py:62
  345.6 19.5 %collective-permute-start.31 = (bf16[768,768]{1,0:T(8,128)(2,1)}, bf16[768,768]{1,0:T(8,128)(2,1)}, u32[]{:S(2)}, u32[]{:S(2)}) collective-permute-start(bf16[768,768]{1,0:T(8,128)(2,1)} %collective-permute-done.30), channel_id=1, source_target_pairs={{0,4},{1,5},{2,6},{3,7},{4,0},{5,1},{6,2},{7,3},{8,12},{9,13},{10,... | collective-permute-start | bytes 3538952 | tf_op jit(solution)/shard_map/ppermute | solution.py:62
  346.1 23.3 %all-to-all-start.4 = ((bf16[4,128,768]{2,1,0:T(8,128)(2,1)}), bf16[4,128,768]{2,1,0:T(8,128)(2,1)}, u32[]{:S(2)}, u32[]{:S(2)}) async-start(bf16[4,128,768]{2,1,0:T(8,128)(2,1)} %bitcast.201), calls=%async_computation.4 | async-start | bytes 1572864 | tf_op jit(solution)/shard_map/all_to_all | solution.py:674
  350.5 80.7 %all-reduce.5.cloned.1.call-start = ((), (), s32[]{:S(2)}) async-start(), calls=%async_computation.8 | async-start | bytes 2359296 | tf_op jit(solution)/shard_map/psum | solution.py:932
  373.7 30.1 %collective-permute-start.36 = (bf16[384,768]{1,0:T(8,128)(2,1)}, bf16[384,768]{1,0:T(8,128)(2,1)}, u32[]{:S(2)}, u32[]{:S(2)}) collective-permute-start(bf16[384,768]{1,0:T(8,128)(2,1)} %add_convert_fusion.15), channel_id=1, source_target_pairs={{0,2},{1,3},{2,0},{3,1},{4,5},{5,4},{6,7},{7,6},{8,10},{9,11},{10,... | collective-permute-start | bytes 1769480 | tf_op jit(solution)/shard_map/ppermute | solution.py:62
  375.0 32.7 %collective-permute-start.38 = (bf16[384,768]{1,0:T(8,128)(2,1)}, bf16[384,768]{1,0:T(8,128)(2,1)}, u32[]{:S(2)}, u32[]{:S(2)}) collective-permute-start(bf16[384,768]{1,0:T(8,128)(2,1)} %add_convert_fusion.17), channel_id=1, source_target_pairs={{0,1},{1,0},{2,3},{3,2},{4,6},{5,7},{6,4},{7,5},{8,9},{9,8},{10,11... | collective-permute-start | bytes 1769480 | tf_op jit(solution)/shard_map/ppermute | solution.py:62
  379.9 47.7 %all-to-all-start.6 = ((bf16[4,128,768]{2,1,0:T(8,128)(2,1)}), bf16[4,128,768]{2,1,0:T(8,128)(2,1)}, u32[]{:S(2)}, u32[]{:S(2)}) async-start(bf16[4,128,768]{2,1,0:T(8,128)(2,1)} %bitcast.40), calls=%async_computation.6 | async-start | bytes 1572864 | tf_op jit(solution)/shard_map/all_to_all | solution.py:681
  384.1 102.2 %all-reduce.7.cloned.1.call-start = ((), (), s32[]{:S(2)}) async-start(), calls=%async_computation.9 | async-start | bytes 1179648 | tf_op jit(solution)/shard_map/psum | solution.py:949
  405.8 22.8 %collective-permute-start.37 = (bf16[384,768]{1,0:T(8,128)(2,1)}, bf16[384,768]{1,0:T(8,128)(2,1)}, u32[]{:S(2)}, u32[]{:S(2)}) collective-permute-start(bf16[384,768]{1,0:T(8,128)(2,1)} %add_convert_fusion.13), channel_id=1, source_target_pairs={{0,1},{1,0},{2,3},{3,2},{4,6},{5,7},{6,4},{7,5},{8,9},{9,8},{10,11... | collective-permute-start | bytes 1769480 | tf_op jit(solution)/shard_map/ppermute | solution.py:62
  407.8 21.0 %collective-permute-start.39 = (bf16[384,768]{1,0:T(8,128)(2,1)}, bf16[384,768]{1,0:T(8,128)(2,1)}, u32[]{:S(2)}, u32[]{:S(2)}) collective-permute-start(bf16[384,768]{1,0:T(8,128)(2,1)} %collective-permute-done.38), channel_id=1, source_target_pairs={{0,4},{1,5},{2,6},{3,7},{4,0},{5,1},{6,2},{7,3},{8,12},{9,13},{10,... | collective-permute-start | bytes 1769480 | tf_op jit(solution)/shard_map/ppermute | solution.py:62
  428.2 12.0 %collective-permute-start.41 = (bf16[768,768]{1,0:T(8,128)(2,1)}, bf16[768,768]{1,0:T(8,128)(2,1)}, u32[]{:S(2)}, u32[]{:S(2)}) collective-permute-start(bf16[768,768]{1,0:T(8,128)(2,1)} %get-tuple-element.345), channel_id=1, source_target_pairs={{0,4},{1,5},{2,6},{3,7},{4,0},{5,1},{6,2},{7,3},{8,12},{9,13},{10,... | collective-permute-start | bytes 3538952 | tf_op jit(solution)/shard_map/ppermute | solution.py:62
  428.7 14.3 %collective-permute-start.40 = (bf16[768,768]{1,0:T(8,128)(2,1)}, bf16[768,768]{1,0:T(8,128)(2,1)}, u32[]{:S(2)}, u32[]{:S(2)}) collective-permute-start(bf16[768,768]{1,0:T(8,128)(2,1)} %get-tuple-element.343), channel_id=1, source_target_pairs={{0,4},{1,5},{2,6},{3,7},{4,0},{5,1},{6,2},{7,3},{8,12},{9,13},{10,... | collective-permute-start | bytes 3538952 | tf_op jit(solution)/shard_map/ppermute | solution.py:62
  445.6 35.0 %collective-permute-start.44 = (bf16[768,768]{1,0:T(8,128)(2,1)}, bf16[768,768]{1,0:T(8,128)(2,1)}, u32[]{:S(2)}, u32[]{:S(2)}) collective-permute-start(bf16[768,768]{1,0:T(8,128)(2,1)} %add_convert_fusion.3), channel_id=1, source_target_pairs={{0,2},{1,3},{2,0},{3,1},{4,5},{5,4},{6,7},{7,6},{8,10},{9,11},{10,... | collective-permute-start | bytes 3538952 | tf_op jit(solution)/shard_map/ppermute | solution.py:62
  447.0 37.2 %collective-permute-start.46 = (bf16[768,768]{1,0:T(8,128)(2,1)}, bf16[768,768]{1,0:T(8,128)(2,1)}, u32[]{:S(2)}, u32[]{:S(2)}) collective-permute-start(bf16[768,768]{1,0:T(8,128)(2,1)} %add_convert_fusion.5), channel_id=1, source_target_pairs={{0,1},{1,0},{2,3},{3,2},{4,6},{5,7},{6,4},{7,5},{8,9},{9,8},{10,11... | collective-permute-start | bytes 3538952 | tf_op jit(solution)/shard_map/ppermute | solution.py:62
  483.5 34.9 %collective-permute-start.45 = (bf16[768,768]{1,0:T(8,128)(2,1)}, bf16[768,768]{1,0:T(8,128)(2,1)}, u32[]{:S(2)}, u32[]{:S(2)}) collective-permute-start(bf16[768,768]{1,0:T(8,128)(2,1)} %add_convert_fusion.1), channel_id=1, source_target_pairs={{0,1},{1,0},{2,3},{3,2},{4,6},{5,7},{6,4},{7,5},{8,9},{9,8},{10,11... | collective-permute-start | bytes 3538952 | tf_op jit(solution)/shard_map/ppermute | solution.py:62
  484.3 34.1 %collective-permute-start.47 = (bf16[768,768]{1,0:T(8,128)(2,1)}, bf16[768,768]{1,0:T(8,128)(2,1)}, u32[]{:S(2)}, u32[]{:S(2)}) collective-permute-start(bf16[768,768]{1,0:T(8,128)(2,1)} %collective-permute-done.46), channel_id=1, source_target_pairs={{0,4},{1,5},{2,6},{3,7},{4,0},{5,1},{6,2},{7,3},{8,12},{9,13},{10,... | collective-permute-start | bytes 3538952 | tf_op jit(solution)/shard_map/ppermute | solution.py:62
  486.2 34.7 %collective-permute-start.48 = (bf16[768,768]{1,0:T(8,128)(2,1)}, bf16[768,768]{1,0:T(8,128)(2,1)}, u32[]{:S(2)}, u32[]{:S(2)}) collective-permute-start(bf16[768,768]{1,0:T(8,128)(2,1)} %all-reduce.5.cloned.1.call-done), channel_id=1, source_target_pairs={{0,4},{1,5},{2,6},{3,7},{4,0},{5,1},{6,2},{7,3},{8,12},{9,13},{10,... | collective-permute-start | bytes 3538952 | tf_op jit(solution)/shard_map/ppermute | solution.py:62
  502.7 15.4 %all-to-all-start.7 = ((bf16[4,128,768]{2,1,0:T(8,128)(2,1)}), bf16[4,128,768]{2,1,0:T(8,128)(2,1)S(1)}, u32[]{:S(2)}, u32[]{:S(2)}) async-start(bf16[4,128,768]{2,1,0:T(8,128)(2,1)} %bitcast.41), calls=%async_computation.7 | async-start | bytes 1572864 | tf_op jit(solution)/shard_map/all_to_all | solution.py:681
  506.7 14.2 %collective-permute-start.49 = (bf16[384,768]{1,0:T(8,128)(2,1)S(1)}, bf16[384,768]{1,0:T(8,128)(2,1)S(1)}, u32[]{:S(2)}, u32[]{:S(2)}) collective-permute-start(bf16[384,768]{1,0:T(8,128)(2,1)S(1)} %copy-done.140), channel_id=1, source_target_pairs={{0,4},{1,5},{2,6},{3,7},{4,0},{5,1},{6,2},{7,3},{8,12},{9,13},{10,... | collective-permute-start | bytes 1769480 | tf_op jit(solution)/shard_map/ppermute | solution.py:62
  (187 other events, 1440.1 us)
Sparse Core Ops, SparseCore 0:
  376.6 54.3 all-reduce.4
  448.4 37.7 all-reduce.6

commit v11 on v10

--- a/solution.py
+++ b/solution.py
@@ -120,6 +120,8 @@
 
 
 Q_ROWS = 128
+DATA_ROWS = 512
+GRAD_ROWS = 768
 
 
 def attend_forward_kernel(
@@ -230,7 +232,7 @@
     sums_ref[...] = jnp.zeros_like(sums_ref)
 
     def data(i, carry):
-        rows = pl.ds(pl.multiple_of(i * Q_ROWS, Q_ROWS), Q_ROWS)
+        rows = pl.ds(pl.multiple_of(i * DATA_ROWS, DATA_ROWS), DATA_ROWS)
         dhid = mm(dz_ref[rows, :], second_ref[...], 1, 1) * slope_ref[rows, :].astype(F32)
         sums_ref[...] += jnp.sum(dhid, axis=0, keepdims=True)
         dhb = dhid.astype(BF)
@@ -239,14 +241,14 @@
         return carry
 
     def weights(i, carry):
-        rows = pl.ds(pl.multiple_of(i * Q_ROWS, Q_ROWS), Q_ROWS)
+        rows = pl.ds(pl.multiple_of(i * GRAD_ROWS, GRAD_ROWS), GRAD_ROWS)
         first = mm(y_ref[:, rows], dh_ref[...], 0, 0).astype(BF)
         second = mm(act_ref[:, rows], dz_ref[...], 0, 0).astype(BF)
         store_both(side, own_ref, rest_ref, rows, first, second)
         return carry
 
-    lax.fori_loop(0, tokens // Q_ROWS, data, 0)
-    lax.fori_loop(0, model // Q_ROWS, weights, 0)
+    lax.fori_loop(0, tokens // DATA_ROWS, data, 0)
+    lax.fori_loop(0, model // GRAD_ROWS, weights, 0)
 
 
 def streamed_blocks(name, body, shared, total, blocks, big, small, scratch):

time: 647 us -> 632 us (0.977)
  Pallas kernels: 308 us -> 280 us
  waiting for transfers between devices: 39.5 us -> 52.2 us
    pallas_call x7, Pallas kernels: 162 us -> 135 us  [streamed_blocks(): pl.pallas_call(kernel, name=name, out_shape=(jax.ShapeDtypeStruct(total.s...]
    psum x1, waiting for transfers between devices: 0.01 us -> 13.5 us  [shards(): ffn_total1 = lax.psum(ffn1.total, 'dp')]
  transfers between devices with their start and end apart: 60 -> 60, of which waited for: 8 -> 9; matrix products, arithmetic and copies ran while one was open for 20% -> 21% of each run, Pallas kernels for 37% -> 33%
where the time goes in v11:
time: 632 us; the launch traced here: 623 us
  Pallas kernels  280 us (44%)
  other arithmetic  103 us (16%)
  starting transfers between devices  67.7 us (11%)
  local copies, waits for them, and re-layouts  54 us (9%)
  waiting for transfers between devices  52.2 us (8%)
  matrix products  46 us (7%)
  between operations  19.9 us (3%)
    pallas_call x7, Pallas kernels, streamed_blocks(): pl.pallas_call(kernel, name=name, out_shape=(jax.ShapeDtypeStruct(total.s...  135 us
    pallas_call x1, Pallas kernels, last_sums(): pl.pallas_call(body, name='last_sums', out_shape=tuple((jax.ShapeDtypeStr...  73.7 us
    pallas_call x8, Pallas kernels, attend_forward(): pl.pallas_call(body, name='attend_forward', out_shape=(narrow, narrow, na...  54.1 us
    dot_general x18, matrix products, mm(): lax.dot_general(a, b, (((ca,), (cb,)), ((), ())), preferred_element_type=...  42.3 us
    convert_element_type x18, other arithmetic, plus(): return total.astype(BF)  37.2 us
    ppermute x50, starting transfers between devices, send(): return lax.ppermute(values, PLANE, plane_pairs(kind))  33.8 us
    unnamed x357, local copies, waits for them, and re-layouts  33.2 us
    pallas_call x1, Pallas kernels, gather_anchors(): pl.pallas_call(body, name='gather_anchors', out_shape=jax.ShapeDtypeStruc...  17.8 us
  transfers between devices with their start and end apart: 60, of which 9 were waited for; matrix products, arithmetic and copies ran while one was open for 21% of the time, Pallas kernels for 33%

profile of v11, /device:TPU:0, one launch (start us, length us, event | category | flops | bytes accessed | tf_op | source)
XLA Modules:
  0.0 622.8 jit_solution(4917938222951004003)
XLA Ops:
  7.2 5.2 all-to-all-start
  18.2 3.9 slice_bitcast_fusion
  29.6 6.4 %attend_forward.8 = (bf16[512,192]{1,0:T(8,128)(2,1)S(1)}, bf16[512,192]{1,0:T(8,128)(2,1)S(1)}, bf16[512,192]{1,0:T(8,128)(2,1)S(1)}, bf16[512,192]{1,0:T(8,128...) custom-call(bf16[512,768]{1,0:T(8,128)(2,1)S(1)} %bitcast.170, ...), custom_call_target="tpu_custom_call" | custom-call | flops 1048576 | bytes 1024 | tf_op jit(solution)/shard_map/attend_forward/pallas_call | solution.py:357
  40.6 6.4 %attend_forward.9 = (bf16[512,192]{1,0:T(8,128)(2,1)S(1)}, bf16[512,192]{1,0:T(8,128)(2,1)S(1)}, bf16[512,192]{1,0:T(8,128)(2,1)S(1)}, bf16[512,192]{1,0:T(8,128...) custom-call(bf16[512,768]{1,0:T(8,128)(2,1)S(1)} %bitcast.171, ...), custom_call_target="tpu_custom_call" | custom-call | flops 1048576 | bytes 1024 | tf_op jit(solution)/shard_map/attend_forward/pallas_call | solution.py:357
  49.2 6.4 %attend_forward.10 = (bf16[512,192]{1,0:T(8,128)(2,1)S(1)}, bf16[512,192]{1,0:T(8,128)(2,1)S(1)}, bf16[512,192]{1,0:T(8,128)(2,1)S(1)}, bf16[512,192]{1,0:T(8,12...) custom-call(bf16[512,768]{1,0:T(8,128)(2,1)S(1)} %bitcast.172, ...), custom_call_target="tpu_custom_call" | custom-call | flops 1048576 | bytes 1024 | tf_op jit(solution)/shard_map/attend_forward/pallas_call | solution.py:357
  58.9 6.6 %attend_forward.11 = (bf16[512,192]{1,0:T(8,128)(2,1)S(1)}, bf16[512,192]{1,0:T(8,128)(2,1)S(1)}, bf16[512,192]{1,0:T(8,128)(2,1)S(1)}, bf16[512,192]{1,0:T(8,12...) custom-call(bf16[512,768]{1,0:T(8,128)(2,1)S(1)} %bitcast.173, ...), custom_call_target="tpu_custom_call" | custom-call | flops 1048576 | bytes 1024 | tf_op jit(solution)/shard_map/attend_forward/pallas_call | solution.py:357
  65.6 2.8 collective-permute-done.7.refs_10_
  74.6 3.6 fusion.24
  80.6 3.4 fusion.29
  86.4 3.4 fusion.34
  99.6 3.5 all-to-all-start.2
  113.8 5.9 all-to-all-done.2
  119.7 2.9 fusion.49
  122.6 7.9 %attend_forward.12 = (bf16[512,192]{1,0:T(8,128)(2,1)S(1)}, bf16[512,192]{1,0:T(8,128)(2,1)S(1)}, bf16[512,192]{1,0:T(8,128)(2,1)S(1)}, bf16[512,192]{1,0:T(8,12...) custom-call(bf16[512,768]{1,0:T(8,128)(2,1)S(1)} %get-tuple-element.478.refs_0_.refs_1_, ...), custom_call_target="tpu_custom_call" | custom-call | flops 1048576 | bytes 1024 | tf_op jit(solution)/shard_map/attend_forward/pallas_call | solution.py:357
  135.2 3.9 all-to-all-start.1
  140.5 7.6 %attend_forward.13 = (bf16[512,192]{1,0:T(8,128)(2,1)S(1)}, bf16[512,192]{1,0:T(8,128)(2,1)S(1)}, bf16[512,192]{1,0:T(8,128)(2,1)S(1)}, bf16[512,192]{1,0:T(8,12...) custom-call(bf16[512,768]{1,0:T(8,128)(2,1)S(1)} %get-tuple-element.478.refs_0_.refs_1_, ...), custom_call_target="tpu_custom_call" | custom-call | flops 1048576 | bytes 1024 | tf_op jit(solution)/shard_map/attend_forward/pallas_call | solution.py:357
  151.7 6.4 %attend_forward.14 = (bf16[512,192]{1,0:T(8,128)(2,1)S(1)}, bf16[512,192]{1,0:T(8,128)(2,1)S(1)}, bf16[512,192]{1,0:T(8,128)(2,1)S(1)}, bf16[512,192]{1,0:T(8,12...) custom-call(bf16[512,768]{1,0:T(8,128)(2,1)S(1)} %get-tuple-element.478.refs_0_.refs_1_, ...), custom_call_target="tpu_custom_call" | custom-call | flops 1048576 | bytes 1024 | tf_op jit(solution)/shard_map/attend_forward/pallas_call | solution.py:357
  164.3 6.4 %attend_forward.15 = (bf16[512,192]{1,0:T(8,128)(2,1)S(1)}, bf16[512,192]{1,0:T(8,128)(2,1)S(1)}, bf16[512,192]{1,0:T(8,128)(2,1)S(1)}, bf16[512,192]{1,0:T(8,12...) custom-call(bf16[512,768]{1,0:T(8,128)(2,1)S(1)} %get-tuple-element.478.refs_0_.refs_1_, ...), custom_call_target="tpu_custom_call" | custom-call | flops 1048576 | bytes 1024 | tf_op jit(solution)/shard_map/attend_forward/pallas_call | solution.py:357
  171.3 2.8 broadcast_select_fusion.4
  177.8 3.7 fusion.4
  183.9 3.4 fusion.9
  189.6 3.4 fusion.14
  195.5 3.9 all-to-all-start.5
  200.6 10.5 %all-to-all-done.5 = bf16[4,128,768]{2,1,0:T(8,128)(2,1)S(1)} async-done(((bf16[4,128,768]{2,1,0:T(8,128)(2,1)}), bf16[4,128,768]{2,1,0:T(8,128)(2,1)S(1)}, u32[]{:S(2)}, u32[]{:S(2)}) %all-to-all-start.5) | async-done | bytes 786464 | tf_op jit(solution)/shard_map/all_to_all | solution.py:676
  221.6 4.5 all-to-all-start.3
  227.8 17.8 %gather_anchors.1 = bf16[4,8,4,768]{3,2,1,0:T(4,128)(2,1)} custom-call(bf16[4,768]{1,0:T(4,128)(2,1)} %convolution_convert_fusion.refs_0_), custom_call_target="tpu_custom_call" | custom-call | tf_op jit(solution)/shard_map/gather_anchors/pallas_call | solution.py:423
  247.6 18.9 %ffn_backward.3 = (f32[512,768]{1,0:T(8,128)}, f32[1,768]{1,0:T(1,128)}, f32[1,768]{1,0:T(1,128)}, f32[1,768]{1,0:T(1,128)}, f32[1,768]{1,0:T(1,128)}, /*index=5...) custom-call(bf16[512,768]{1,0:T(8,128)(2,1)} %convert_element_type.5, ...), custom_call_target="tpu_custom_call" | custom-call | flops 1048576 | bytes 1024 | tf_op jit(solution)/shard_map/ffn_backward/pallas_call | solution.py:304
  281.7 31.3 %attend_backward.4 = (f32[512,768]{1,0:T(8,128)}, f32[1,384]{1,0:T(1,128)}, f32[1,384]{1,0:T(1,128)}, f32[1,384]{1,0:T(1,128)}, bf16[384,768]{1,0:T(8,128)(2,1)}...) custom-call(bf16[512,768]{1,0:T(8,128)(2,1)} %convert_element_type.5, ...), custom_call_target="tpu_custom_call" | custom-call | flops 1048576 | bytes 1024 | tf_op jit(solution)/shard_map/attend_backward/pallas_call | solution.py:304
  312.9 2.9 add_convert_fusion.7
  315.9 13.9 %attend_backward.5 = (f32[512,768]{1,0:T(8,128)}, f32[1,384]{1,0:T(1,128)}, bf16[384,768]{1,0:T(8,128)(2,1)}, bf16[384,768]{1,0:T(8,128)(2,1)}) custom-call(bf16[512,768]{1,0:T(8,128)(2,1)} %convert_element_type.524.refs_0_, bf16[512,768]{1,0:T(8,128)(2,1)} %copy-done.6, s32[512,1]{1,0:T(8,128)} %copy-done.1, s32[1,512]{1,0:T(1,128)} %copy-done.32, ...), custom_call_target="tpu_custom_call" | custom-call | flops 1048576 | bytes 1024 | tf_op jit(solution)/shard_map/attend_backward/pallas_call | solution.py:304
  332.5 4.3 all-to-all-start.4
  342.8 8.7 %collective-permute-done.29 = bf16[768,768]{1,0:T(8,128)(2,1)} collective-permute-done((bf16[768,768]{1,0:T(8,128)(2,1)}, bf16[768,768]{1,0:T(8,128)(2,1)}, u32[]{:S(2)}, u32[]{:S(2)}) %collective-permute-start.29) | collective-permute-done | bytes 1179680 | tf_op jit(solution)/shard_map/ppermute | solution.py:62
  351.5 3.1 add_convert_fusion.6
  355.8 3.3 multiply_reduce_fusion.2
  365.9 4.2 all-to-all-start.6
  370.1 12.8 %ffn_backward.4 = (f32[512,768]{1,0:T(8,128)}, f32[1,768]{1,0:T(1,128)}, f32[1,768]{1,0:T(1,128)}, bf16[768,768]{1,0:T(8,128)(2,1)}, bf16[768,768]{1,0:T(8,128)(...) custom-call(bf16[512,768]{1,0:T(8,128)(2,1)} %convert_element_type.544.refs_0_, bf16[512,768]{1,0:T(8,128)(2,1)} %copy-done.96, ...), custom_call_target="tpu_custom_call" | custom-call | flops 1048576 | bytes 1024 | tf_op jit(solution)/shard_map/ffn_backward/pallas_call | solution.py:304
  386.9 13.0 %ffn_backward.5 = (f32[512,768]{1,0:T(8,128)}, f32[1,768]{1,0:T(1,128)}, f32[1,768]{1,0:T(1,128)}, bf16[768,768]{1,0:T(8,128)(2,1)}, bf16[768,768]{1,0:T(8,128)(...) custom-call(bf16[512,768]{1,0:T(8,128)(2,1)} %convert_element_type.544.refs_0_, bf16[512,768]{1,0:T(8,128)(2,1)} %copy-done.96, ...), custom_call_target="tpu_custom_call" | custom-call | flops 1048576 | bytes 1024 | tf_op jit(solution)/shard_map/ffn_backward/pallas_call | solution.py:304
  403.5 13.5 %all-reduce.5.cloned.1.call-done = bf16[768,768]{1,0:T(8,128)(2,1)} async-done(((bf16[768,768]{1,0:T(8,128)(2,1)}), bf16[768,768]{1,0:T(8,128)(2,1)}) %all-reduce.5.cloned.1.call-update) | async-done | bytes 1179664 | tf_op jit(solution)/shard_map/psum | solution.py:934
  420.5 2.7 add_convert_fusion.2
  423.3 2.7 add_convert_fusion.3
  426.0 2.7 add_convert_fusion.4
  428.7 2.6 add_convert_fusion.5
  435.3 31.3 %attend_backward.6 = (f32[512,768]{1,0:T(8,128)}, f32[1,384]{1,0:T(1,128)}, f32[1,384]{1,0:T(1,128)}, f32[1,384]{1,0:T(1,128)}, bf16[384,768]{1,0:T(8,128)(2,1)}...) custom-call(bf16[512,768]{1,0:T(8,128)(2,1)} %convert_element_type.5, ...), custom_call_target="tpu_custom_call" | custom-call | flops 1048576 | bytes 1024 | tf_op jit(solution)/shard_map/attend_backward/pallas_call | solution.py:304
  466.6 2.9 add_convert_fusion.1
  471.8 13.9 %attend_backward.7 = (f32[512,768]{1,0:T(8,128)}, f32[1,384]{1,0:T(1,128)}, bf16[384,768]{1,0:T(8,128)(2,1)}, bf16[384,768]{1,0:T(8,128)(2,1)}) custom-call(bf16[512,768]{1,0:T(8,128)(2,1)} %convert_element_type.569.refs_0_, bf16[512,768]{1,0:T(8,128)(2,1)} %bitcast.175, s32[512,1]{1,0:T(8,128)} %copy-done.1, s32[1,512]{1,0:T(1,128)} %copy-done.32, ...), custom_call_target="tpu_custom_call" | custom-call | flops 1048576 | bytes 1024 | tf_op jit(solution)/shard_map/attend_backward/pallas_call | solution.py:304
  488.2 3.9 all-to-all-start.7
  496.0 7.7 %all-to-all-done.7 = bf16[4,128,768]{2,1,0:T(8,128)(2,1)S(1)} async-done(((bf16[4,128,768]{2,1,0:T(8,128)(2,1)}), bf16[4,128,768]{2,1,0:T(8,128)(2,1)S(1)}, u32[]{:S(2)}, u32[]{:S(2)}) %all-to-all-start.7) | async-done | bytes 786464 | tf_op jit(solution)/shard_map/all_to_all | solution.py:683
  508.4 73.7 %last_sums.1 = (bf16[2,4,96,768]{3,2,1,0:T(8,128)(2,1)S(1)}, bf16[2,4,96,768]{3,2,1,0:T(8,128)(2,1)S(1)}, bf16[2,4,48,768]{3,2,1,0:T(8,128)(2,1)S(1)}, bf16[2,4,...) custom-call(bf16[2,4,96,768]{3,2,1,0:T(8,128)(2,1)S(1)} %bitcast.176, bf16[2,4,48,768]{3,2,1,0:T(8,128)(2,1)S(1)} %bitcast.177, ...), custom_call_target="tpu_custom_call" | custom-call | tf_op jit(solution)/shard_map/last_sums/pallas_call | solution.py:653
  (626 shorter events, 186.7 us)
Async XLA Ops:
  7.2 22.2 %all-to-all-start = ((bf16[4,128,768]{2,1,0:T(8,128)(2,1)}), bf16[4,128,768]{2,1,0:T(8,128)(2,1)S(1)}, u32[]{:S(2)}, u32[]{:S(2)}) async-start(bf16[4,128,768]{2,1,0:T(8,128)(2,1)} %bitcast.198), calls=%async_computation | async-start | bytes 1572864 | tf_op jit(solution)/shard_map/all_to_all | solution.py:676
  16.0 20.1 %collective-permute-start = (bf16[400,768]{1,0:T(8,128)(2,1)S(1)}, bf16[400,768]{1,0:T(8,128)(2,1)S(1)}, u32[]{:S(2)}, u32[]{:S(2)}) collective-permute-start(bf16[400,768]{1,0:T(8,128)(2,1)S(1)} %pad_maximum_fusion.2.refs_1_.refs_5_), channel_id=1, source_target_pairs={{0,1},{1,0},{2,3},{3,2},{4,6},{5,7},{6,4},{7,5},{8,9},{9,8},{10,11... | collective-permute-start | bytes 1843208 | tf_op jit(solution)/shard_map/ppermute | solution.py:62
  18.1 18.3 %collective-permute-start.1 = (bf16[400,768]{1,0:T(8,128)(2,1)S(1)}, bf16[400,768]{1,0:T(8,128)(2,1)S(1)}, u32[]{:S(2)}, u32[]{:S(2)}) collective-permute-start(bf16[400,768]{1,0:T(8,128)(2,1)S(1)} %fusion.54.refs_2_.refs_6_), channel_id=1, source_target_pairs={{0,1},{1,0},{2,3},{3,2},{4,6},{5,7},{6,4},{7,5},{8,9},{9,8},{10,11... | collective-permute-start | bytes 1843208 | tf_op jit(solution)/shard_map/ppermute | solution.py:62
  22.1 43.5 %collective-permute-start.6 = (bf16[768,768]{1,0:T(8,128)(2,1)}, bf16[768,768]{1,0:T(8,128)(2,1)}, u32[]{:S(2)}, u32[]{:S(2)}) collective-permute-start(bf16[768,768]{1,0:T(8,128)(2,1)} %get-tuple-element.230.refs_5_), channel_id=1, source_target_pairs={{0,1},{1,0},{2,3},{3,2},{4,6},{5,7},{6,4},{7,5},{8,9},{9,8},{10,11... | collective-permute-start | bytes 3538952 | tf_op jit(solution)/shard_map/ppermute | solution.py:62
  24.0 44.3 %collective-permute-start.7 = (bf16[768,768]{1,0:T(8,128)(2,1)}, bf16[768,768]{1,0:T(8,128)(2,1)}, u32[]{:S(2)}, u32[]{:S(2)}) collective-permute-start(bf16[768,768]{1,0:T(8,128)(2,1)} %get-tuple-element.231.refs_6_), channel_id=1, source_target_pairs={{0,1},{1,0},{2,3},{3,2},{4,6},{5,7},{6,4},{7,5},{8,9},{9,8},{10,11... | collective-permute-start | bytes 3538952 | tf_op jit(solution)/shard_map/ppermute | solution.py:62
  36.4 12.7 %collective-permute-start.2 = (bf16[400,768]{1,0:T(8,128)(2,1)S(1)}, bf16[400,768]{1,0:T(8,128)(2,1)S(1)}, u32[]{:S(2)}, u32[]{:S(2)}) collective-permute-start(bf16[400,768]{1,0:T(8,128)(2,1)S(1)} %collective-permute-done.refs_1_.refs_12_), channel_id=1, source_target_pairs={{0,4},{1,5},{2,6},{3,7},{4,0},{5,1},{6,2},{7,3},{8,12},{9,13},{10,... | collective-permute-start | bytes 1843208 | tf_op jit(solution)/shard_map/ppermute | solution.py:62
  37.0 18.7 %collective-permute-start.4 = (bf16[400,768]{1,0:T(8,128)(2,1)S(1)}, bf16[400,768]{1,0:T(8,128)(2,1)S(1)}, u32[]{:S(2)}, u32[]{:S(2)}) collective-permute-start(bf16[400,768]{1,0:T(8,128)(2,1)S(1)} %broadcast_select_fusion.10), channel_id=1, source_target_pairs={{0,2},{1,3},{2,0},{3,1},{4,5},{5,4},{6,7},{7,6},{8,10},{9,11},{10,... | collective-permute-start | bytes 1843208 | tf_op jit(solution)/shard_map/ppermute | solution.py:62
  56.6 29.7 %collective-permute-start.8 = (bf16[384,768]{1,0:T(8,128)(2,1)}, bf16[384,768]{1,0:T(8,128)(2,1)}, u32[]{:S(2)}, u32[]{:S(2)}) collective-permute-start(bf16[384,768]{1,0:T(8,128)(2,1)} %bitcast.16.refs_1_.refs_5_), channel_id=1, source_target_pairs={{0,1},{1,0},{2,3},{3,2},{4,6},{5,7},{6,4},{7,5},{8,9},{9,8},{10,11... | collective-permute-start | bytes 1769480 | tf_op jit(solution)/shard_map/ppermute | solution.py:62
  58.1 28.3 %collective-permute-start.9 = (bf16[384,768]{1,0:T(8,128)(2,1)}, bf16[384,768]{1,0:T(8,128)(2,1)}, u32[]{:S(2)}, u32[]{:S(2)}) collective-permute-start(bf16[384,768]{1,0:T(8,128)(2,1)} %pad_maximum_fusion.3.refs_2_.refs_6_), channel_id=1, source_target_pairs={{0,1},{1,0},{2,3},{3,2},{4,6},{5,7},{6,4},{7,5},{8,9},{9,8},{10,11... | collective-permute-start | bytes 1769480 | tf_op jit(solution)/shard_map/ppermute | solution.py:62
  68.3 18.1 %collective-permute-start.10 = (bf16[768,768]{1,0:T(8,128)(2,1)}, bf16[768,768]{1,0:T(8,128)(2,1)}, u32[]{:S(2)}, u32[]{:S(2)}) collective-permute-start(bf16[768,768]{1,0:T(8,128)(2,1)} %collective-permute-done.6.refs_9_), channel_id=1, source_target_pairs={{0,4},{1,5},{2,6},{3,7},{4,0},{5,1},{6,2},{7,3},{8,12},{9,13},{10,... | collective-permute-start | bytes 3538952 | tf_op jit(solution)/shard_map/ppermute | solution.py:62
  70.9 18.9 %collective-permute-start.11 = (bf16[768,768]{1,0:T(8,128)(2,1)}, bf16[768,768]{1,0:T(8,128)(2,1)}, u32[]{:S(2)}, u32[]{:S(2)}) collective-permute-start(bf16[768,768]{1,0:T(8,128)(2,1)} %collective-permute-done.7.refs_10_), channel_id=1, source_target_pairs={{0,4},{1,5},{2,6},{3,7},{4,0},{5,1},{6,2},{7,3},{8,12},{9,13},{10,... | collective-permute-start | bytes 3538952 | tf_op jit(solution)/shard_map/ppermute | solution.py:62
  72.8 21.3 %collective-permute-start.12 = (bf16[768,768]{1,0:T(8,128)(2,1)S(1)}, bf16[768,768]{1,0:T(8,128)(2,1)}, u32[]{:S(2)}, u32[]{:S(2)}) collective-permute-start(bf16[768,768]{1,0:T(8,128)(2,1)S(1)} %copy-done.128), channel_id=1, source_target_pairs={{0,2},{1,3},{2,0},{3,1},{4,5},{5,4},{6,7},{7,6},{8,10},{9,11},{10,... | collective-permute-start | bytes 3538952 | tf_op jit(solution)/shard_map/ppermute | solution.py:62
  95.5 56.2 %collective-permute-start.16 = (bf16[384,768]{1,0:T(8,128)(2,1)}, bf16[384,768]{1,0:T(8,128)(2,1)S(1)}, u32[]{:S(2)}, u32[]{:S(2)}) collective-permute-start(bf16[384,768]{1,0:T(8,128)(2,1)} %collective-permute-done.8.refs_1_.refs_12_), channel_id=1, source_target_pairs={{0,4},{1,5},{2,6},{3,7},{4,0},{5,1},{6,2},{7,3},{8,12},{9,13},{10,... | collective-permute-start | bytes 1769480 | tf_op jit(solution)/shard_map/ppermute | solution.py:62
  96.1 55.7 %collective-permute-start.17 = (bf16[384,768]{1,0:T(8,128)(2,1)}, bf16[384,768]{1,0:T(8,128)(2,1)S(1)}, u32[]{:S(2)}, u32[]{:S(2)}) collective-permute-start(bf16[384,768]{1,0:T(8,128)(2,1)} %collective-permute-done.9.refs_2_.refs_13_), channel_id=1, source_target_pairs={{0,4},{1,5},{2,6},{3,7},{4,0},{5,1},{6,2},{7,3},{8,12},{9,13},{10,... | collective-permute-start | bytes 1769480 | tf_op jit(solution)/shard_map/ppermute | solution.py:62
  98.1 53.6 %collective-permute-start.14 = (bf16[384,768]{1,0:T(8,128)(2,1)}, bf16[384,768]{1,0:T(8,128)(2,1)}, u32[]{:S(2)}, u32[]{:S(2)}) collective-permute-start(bf16[384,768]{1,0:T(8,128)(2,1)} %broadcast_select_fusion.13), channel_id=1, source_target_pairs={{0,2},{1,3},{2,0},{3,1},{4,5},{5,4},{6,7},{7,6},{8,10},{9,11},{10,... | collective-permute-start | bytes 1769480 | tf_op jit(solution)/shard_map/ppermute | solution.py:62
  99.6 20.1 %all-to-all-start.2 = ((bf16[4,128,768]{2,1,0:T(8,128)(2,1)}), bf16[4,128,768]{2,1,0:T(8,128)(2,1)S(1)}, u32[]{:S(2)}, u32[]{:S(2)}) async-start(bf16[4,128,768]{2,1,0:T(8,128)(2,1)} %bitcast.199), calls=%async_computation.2 | async-start | bytes 1572864 | tf_op jit(solution)/shard_map/all_to_all | solution.py:676
  103.1 67.6 %collective-permute-start.18 = (bf16[768,768]{1,0:T(8,128)(2,1)}, bf16[768,768]{1,0:T(8,128)(2,1)}, u32[]{:S(2)}, u32[]{:S(2)}) collective-permute-start(bf16[768,768]{1,0:T(8,128)(2,1)} %get-tuple-element.253.refs_5_), channel_id=1, source_target_pairs={{0,1},{1,0},{2,3},{3,2},{4,6},{5,7},{6,4},{7,5},{8,9},{9,8},{10,11... | collective-permute-start | bytes 3538952 | tf_op jit(solution)/shard_map/ppermute | solution.py:62
  105.7 65.0 %collective-permute-start.19 = (bf16[768,768]{1,0:T(8,128)(2,1)}, bf16[768,768]{1,0:T(8,128)(2,1)}, u32[]{:S(2)}, u32[]{:S(2)}) collective-permute-start(bf16[768,768]{1,0:T(8,128)(2,1)} %get-tuple-element.254.refs_6_), channel_id=1, source_target_pairs={{0,1},{1,0},{2,3},{3,2},{4,6},{5,7},{6,4},{7,5},{8,9},{9,8},{10,11... | collective-permute-start | bytes 3538952 | tf_op jit(solution)/shard_map/ppermute | solution.py:62
  135.2 27.0 %all-to-all-start.1 = ((bf16[4,128,768]{2,1,0:T(8,128)(2,1)}), bf16[4,128,768]{2,1,0:T(8,128)(2,1)S(1)}, u32[]{:S(2)}, u32[]{:S(2)}) async-start(bf16[4,128,768]{2,1,0:T(8,128)(2,1)} %bitcast.190), calls=%async_computation.1 | async-start | bytes 1572864 | tf_op jit(solution)/shard_map/all_to_all | solution.py:683
  170.8 18.8 %collective-permute-start.20 = (bf16[768,768]{1,0:T(8,128)(2,1)}, bf16[768,768]{1,0:T(8,128)(2,1)}, u32[]{:S(2)}, u32[]{:S(2)}) collective-permute-start(bf16[768,768]{1,0:T(8,128)(2,1)} %collective-permute-done.18.refs_9_), channel_id=1, source_target_pairs={{0,4},{1,5},{2,6},{3,7},{4,0},{5,1},{6,2},{7,3},{8,12},{9,13},{10,... | collective-permute-start | bytes 3538952 | tf_op jit(solution)/shard_map/ppermute | solution.py:62
  174.1 18.9 %collective-permute-start.21 = (bf16[768,768]{1,0:T(8,128)(2,1)}, bf16[768,768]{1,0:T(8,128)(2,1)}, u32[]{:S(2)}, u32[]{:S(2)}) collective-permute-start(bf16[768,768]{1,0:T(8,128)(2,1)} %collective-permute-done.19.refs_10_), channel_id=1, source_target_pairs={{0,4},{1,5},{2,6},{3,7},{4,0},{5,1},{6,2},{7,3},{8,12},{9,13},{10,... | collective-permute-start | bytes 3538952 | tf_op jit(solution)/shard_map/ppermute | solution.py:62
  174.7 20.6 %collective-permute-start.22 = (bf16[768,768]{1,0:T(8,128)(2,1)}, bf16[768,768]{1,0:T(8,128)(2,1)}, u32[]{:S(2)}, u32[]{:S(2)}) collective-permute-start(bf16[768,768]{1,0:T(8,128)(2,1)} %broadcast_select_fusion.4), channel_id=1, source_target_pairs={{0,2},{1,3},{2,0},{3,1},{4,5},{5,4},{6,7},{7,6},{8,10},{9,11},{10,... | collective-permute-start | bytes 3538952 | tf_op jit(solution)/shard_map/ppermute | solution.py:62
  195.4 17.4 %collective-permute-start.23 = (bf16[768,768]{1,0:T(8,128)(2,1)}, bf16[768,768]{1,0:T(8,128)(2,1)S(1)}, u32[]{:S(2)}, u32[]{:S(2)}) collective-permute-start(bf16[768,768]{1,0:T(8,128)(2,1)} %collective-permute-done.22), channel_id=1, source_target_pairs={{0,4},{1,5},{2,6},{3,7},{4,0},{5,1},{6,2},{7,3},{8,12},{9,13},{10,... | collective-permute-start | bytes 3538952 | tf_op jit(solution)/shard_map/ppermute | solution.py:62
  195.5 15.6 %all-to-all-start.5 = ((bf16[4,128,768]{2,1,0:T(8,128)(2,1)}), bf16[4,128,768]{2,1,0:T(8,128)(2,1)S(1)}, u32[]{:S(2)}, u32[]{:S(2)}) async-start(bf16[4,128,768]{2,1,0:T(8,128)(2,1)} %bitcast.200), calls=%async_computation.5 | async-start | bytes 1572864 | tf_op jit(solution)/shard_map/all_to_all | solution.py:676
  221.6 45.0 %all-to-all-start.3 = ((bf16[4,128,768]{2,1,0:T(8,128)(2,1)}), bf16[4,128,768]{2,1,0:T(8,128)(2,1)}, u32[]{:S(2)}, u32[]{:S(2)}) async-start(bf16[4,128,768]{2,1,0:T(8,128)(2,1)} %bitcast.187), calls=%async_computation.3 | async-start | bytes 1572864 | tf_op jit(solution)/shard_map/all_to_all | solution.py:683
  277.1 35.9 %collective-permute-start.28 = (bf16[768,768]{1,0:T(8,128)(2,1)}, bf16[768,768]{1,0:T(8,128)(2,1)}, u32[]{:S(2)}, u32[]{:S(2)}) collective-permute-start(bf16[768,768]{1,0:T(8,128)(2,1)} %add_convert_fusion.9), channel_id=1, source_target_pairs={{0,2},{1,3},{2,0},{3,1},{4,5},{5,4},{6,7},{7,6},{8,10},{9,11},{10,... | collective-permute-start | bytes 3538952 | tf_op jit(solution)/shard_map/ppermute | solution.py:62
  278.7 53.4 %collective-permute-start.30 = (bf16[768,768]{1,0:T(8,128)(2,1)}, bf16[768,768]{1,0:T(8,128)(2,1)}, u32[]{:S(2)}, u32[]{:S(2)}) collective-permute-start(bf16[768,768]{1,0:T(8,128)(2,1)} %add_convert_fusion.11), channel_id=1, source_target_pairs={{0,1},{1,0},{2,3},{3,2},{4,6},{5,7},{6,4},{7,5},{8,9},{9,8},{10,11... | collective-permute-start | bytes 3538952 | tf_op jit(solution)/shard_map/ppermute | solution.py:62
  330.7 20.8 %collective-permute-start.29 = (bf16[768,768]{1,0:T(8,128)(2,1)}, bf16[768,768]{1,0:T(8,128)(2,1)}, u32[]{:S(2)}, u32[]{:S(2)}) collective-permute-start(bf16[768,768]{1,0:T(8,128)(2,1)} %add_convert_fusion.7), channel_id=1, source_target_pairs={{0,1},{1,0},{2,3},{3,2},{4,6},{5,7},{6,4},{7,5},{8,9},{9,8},{10,11... | collective-permute-start | bytes 3538952 | tf_op jit(solution)/shard_map/ppermute | solution.py:62
  332.0 19.5 %collective-permute-start.31 = (bf16[768,768]{1,0:T(8,128)(2,1)}, bf16[768,768]{1,0:T(8,128)(2,1)}, u32[]{:S(2)}, u32[]{:S(2)}) collective-permute-start(bf16[768,768]{1,0:T(8,128)(2,1)} %collective-permute-done.30), channel_id=1, source_target_pairs={{0,4},{1,5},{2,6},{3,7},{4,0},{5,1},{6,2},{7,3},{8,12},{9,13},{10,... | collective-permute-start | bytes 3538952 | tf_op jit(solution)/shard_map/ppermute | solution.py:62
  332.5 23.3 %all-to-all-start.4 = ((bf16[4,128,768]{2,1,0:T(8,128)(2,1)}), bf16[4,128,768]{2,1,0:T(8,128)(2,1)}, u32[]{:S(2)}, u32[]{:S(2)}) async-start(bf16[4,128,768]{2,1,0:T(8,128)(2,1)} %bitcast.201), calls=%async_computation.4 | async-start | bytes 1572864 | tf_op jit(solution)/shard_map/all_to_all | solution.py:676
  336.9 80.1 %all-reduce.5.cloned.1.call-start = ((), (), s32[]{:S(2)}) async-start(), calls=%async_computation.8 | async-start | bytes 2359296 | tf_op jit(solution)/shard_map/psum | solution.py:934
  359.7 23.2 %collective-permute-start.36 = (bf16[384,768]{1,0:T(8,128)(2,1)}, bf16[384,768]{1,0:T(8,128)(2,1)}, u32[]{:S(2)}, u32[]{:S(2)}) collective-permute-start(bf16[384,768]{1,0:T(8,128)(2,1)} %add_convert_fusion.15), channel_id=1, source_target_pairs={{0,2},{1,3},{2,0},{3,1},{4,5},{5,4},{6,7},{7,6},{8,10},{9,11},{10,... | collective-permute-start | bytes 1769480 | tf_op jit(solution)/shard_map/ppermute | solution.py:62
  361.0 25.8 %collective-permute-start.38 = (bf16[384,768]{1,0:T(8,128)(2,1)}, bf16[384,768]{1,0:T(8,128)(2,1)}, u32[]{:S(2)}, u32[]{:S(2)}) collective-permute-start(bf16[384,768]{1,0:T(8,128)(2,1)} %add_convert_fusion.17), channel_id=1, source_target_pairs={{0,1},{1,0},{2,3},{3,2},{4,6},{5,7},{6,4},{7,5},{8,9},{9,8},{10,11... | collective-permute-start | bytes 1769480 | tf_op jit(solution)/shard_map/ppermute | solution.py:62
  365.9 34.0 %all-to-all-start.6 = ((bf16[4,128,768]{2,1,0:T(8,128)(2,1)}), bf16[4,128,768]{2,1,0:T(8,128)(2,1)}, u32[]{:S(2)}, u32[]{:S(2)}) async-start(bf16[4,128,768]{2,1,0:T(8,128)(2,1)} %bitcast.40), calls=%async_computation.6 | async-start | bytes 1572864 | tf_op jit(solution)/shard_map/all_to_all | solution.py:683
  370.1 101.7 %all-reduce.7.cloned.1.call-start = ((), (), s32[]{:S(2)}) async-start(), calls=%async_computation.9 | async-start | bytes 1179648 | tf_op jit(solution)/shard_map/psum | solution.py:951
  384.9 16.0 %collective-permute-start.37 = (bf16[384,768]{1,0:T(8,128)(2,1)}, bf16[384,768]{1,0:T(8,128)(2,1)}, u32[]{:S(2)}, u32[]{:S(2)}) collective-permute-start(bf16[384,768]{1,0:T(8,128)(2,1)} %add_convert_fusion.13), channel_id=1, source_target_pairs={{0,1},{1,0},{2,3},{3,2},{4,6},{5,7},{6,4},{7,5},{8,9},{9,8},{10,11... | collective-permute-start | bytes 1769480 | tf_op jit(solution)/shard_map/ppermute | solution.py:62
  386.9 14.2 %collective-permute-start.39 = (bf16[384,768]{1,0:T(8,128)(2,1)}, bf16[384,768]{1,0:T(8,128)(2,1)}, u32[]{:S(2)}, u32[]{:S(2)}) collective-permute-start(bf16[384,768]{1,0:T(8,128)(2,1)} %collective-permute-done.38), channel_id=1, source_target_pairs={{0,4},{1,5},{2,6},{3,7},{4,0},{5,1},{6,2},{7,3},{8,12},{9,13},{10,... | collective-permute-start | bytes 1769480 | tf_op jit(solution)/shard_map/ppermute | solution.py:62
  399.9 20.0 %collective-permute-start.43 = (bf16[768,768]{1,0:T(8,128)(2,1)}, bf16[768,768]{1,0:T(8,128)(2,1)}, u32[]{:S(2)}, u32[]{:S(2)}) collective-permute-start(bf16[768,768]{1,0:T(8,128)(2,1)} %get-tuple-element.349), channel_id=1, source_target_pairs={{0,4},{1,5},{2,6},{3,7},{4,0},{5,1},{6,2},{7,3},{8,12},{9,13},{10,... | collective-permute-start | bytes 3538952 | tf_op jit(solution)/shard_map/ppermute | solution.py:62
  400.4 22.8 %collective-permute-start.42 = (bf16[768,768]{1,0:T(8,128)(2,1)}, bf16[768,768]{1,0:T(8,128)(2,1)}, u32[]{:S(2)}, u32[]{:S(2)}) collective-permute-start(bf16[768,768]{1,0:T(8,128)(2,1)} %get-tuple-element.347), channel_id=1, source_target_pairs={{0,4},{1,5},{2,6},{3,7},{4,0},{5,1},{6,2},{7,3},{8,12},{9,13},{10,... | collective-permute-start | bytes 3538952 | tf_op jit(solution)/shard_map/ppermute | solution.py:62
  400.5 25.5 %collective-permute-start.41 = (bf16[768,768]{1,0:T(8,128)(2,1)}, bf16[768,768]{1,0:T(8,128)(2,1)}, u32[]{:S(2)}, u32[]{:S(2)}) collective-permute-start(bf16[768,768]{1,0:T(8,128)(2,1)} %get-tuple-element.345), channel_id=1, source_target_pairs={{0,4},{1,5},{2,6},{3,7},{4,0},{5,1},{6,2},{7,3},{8,12},{9,13},{10,... | collective-permute-start | bytes 3538952 | tf_op jit(solution)/shard_map/ppermute | solution.py:62
  400.9 27.8 %collective-permute-start.40 = (bf16[768,768]{1,0:T(8,128)(2,1)}, bf16[768,768]{1,0:T(8,128)(2,1)}, u32[]{:S(2)}, u32[]{:S(2)}) collective-permute-start(bf16[768,768]{1,0:T(8,128)(2,1)} %get-tuple-element.343), channel_id=1, source_target_pairs={{0,4},{1,5},{2,6},{3,7},{4,0},{5,1},{6,2},{7,3},{8,12},{9,13},{10,... | collective-permute-start | bytes 3538952 | tf_op jit(solution)/shard_map/ppermute | solution.py:62
  431.4 35.2 %collective-permute-start.44 = (bf16[768,768]{1,0:T(8,128)(2,1)}, bf16[768,768]{1,0:T(8,128)(2,1)}, u32[]{:S(2)}, u32[]{:S(2)}) collective-permute-start(bf16[768,768]{1,0:T(8,128)(2,1)} %add_convert_fusion.3), channel_id=1, source_target_pairs={{0,2},{1,3},{2,0},{3,1},{4,5},{5,4},{6,7},{7,6},{8,10},{9,11},{10,... | collective-permute-start | bytes 3538952 | tf_op jit(solution)/shard_map/ppermute | solution.py:62
  432.8 37.3 %collective-permute-start.46 = (bf16[768,768]{1,0:T(8,128)(2,1)}, bf16[768,768]{1,0:T(8,128)(2,1)}, u32[]{:S(2)}, u32[]{:S(2)}) collective-permute-start(bf16[768,768]{1,0:T(8,128)(2,1)} %add_convert_fusion.5), channel_id=1, source_target_pairs={{0,1},{1,0},{2,3},{3,2},{4,6},{5,7},{6,4},{7,5},{8,9},{9,8},{10,11... | collective-permute-start | bytes 3538952 | tf_op jit(solution)/shard_map/ppermute | solution.py:62
  469.5 34.4 %collective-permute-start.45 = (bf16[768,768]{1,0:T(8,128)(2,1)}, bf16[768,768]{1,0:T(8,128)(2,1)}, u32[]{:S(2)}, u32[]{:S(2)}) collective-permute-start(bf16[768,768]{1,0:T(8,128)(2,1)} %add_convert_fusion.1), channel_id=1, source_target_pairs={{0,1},{1,0},{2,3},{3,2},{4,6},{5,7},{6,4},{7,5},{8,9},{9,8},{10,11... | collective-permute-start | bytes 3538952 | tf_op jit(solution)/shard_map/ppermute | solution.py:62
  470.1 33.8 %collective-permute-start.47 = (bf16[768,768]{1,0:T(8,128)(2,1)}, bf16[768,768]{1,0:T(8,128)(2,1)}, u32[]{:S(2)}, u32[]{:S(2)}) collective-permute-start(bf16[768,768]{1,0:T(8,128)(2,1)} %collective-permute-done.46), channel_id=1, source_target_pairs={{0,4},{1,5},{2,6},{3,7},{4,0},{5,1},{6,2},{7,3},{8,12},{9,13},{10,... | collective-permute-start | bytes 3538952 | tf_op jit(solution)/shard_map/ppermute | solution.py:62
  471.8 34.7 %collective-permute-start.48 = (bf16[768,768]{1,0:T(8,128)(2,1)}, bf16[768,768]{1,0:T(8,128)(2,1)}, u32[]{:S(2)}, u32[]{:S(2)}) collective-permute-start(bf16[768,768]{1,0:T(8,128)(2,1)} %all-reduce.5.cloned.1.call-done), channel_id=1, source_target_pairs={{0,4},{1,5},{2,6},{3,7},{4,0},{5,1},{6,2},{7,3},{8,12},{9,13},{10,... | collective-permute-start | bytes 3538952 | tf_op jit(solution)/shard_map/ppermute | solution.py:62
  488.2 15.5 %all-to-all-start.7 = ((bf16[4,128,768]{2,1,0:T(8,128)(2,1)}), bf16[4,128,768]{2,1,0:T(8,128)(2,1)S(1)}, u32[]{:S(2)}, u32[]{:S(2)}) async-start(bf16[4,128,768]{2,1,0:T(8,128)(2,1)} %bitcast.41), calls=%async_computation.7 | async-start | bytes 1572864 | tf_op jit(solution)/shard_map/all_to_all | solution.py:683
  492.3 14.2 %collective-permute-start.49 = (bf16[384,768]{1,0:T(8,128)(2,1)S(1)}, bf16[384,768]{1,0:T(8,128)(2,1)S(1)}, u32[]{:S(2)}, u32[]{:S(2)}) collective-permute-start(bf16[384,768]{1,0:T(8,128)(2,1)S(1)} %copy-done.140), channel_id=1, source_target_pairs={{0,4},{1,5},{2,6},{3,7},{4,0},{5,1},{6,2},{7,3},{8,12},{9,13},{10,... | collective-permute-start | bytes 1769480 | tf_op jit(solution)/shard_map/ppermute | solution.py:62
  (187 other events, 1454.2 us)
Sparse Core Ops, SparseCore 0:
  362.6 54.3 all-reduce.4
  434.4 37.2 all-reduce.6

commit v12 on v11

--- a/solution.py
+++ b/solution.py
@@ -733,7 +733,7 @@
     return dy, blocks, small
 
 
-def attn_backward(dy, seg, attn_w, vec, kept, hook):
+def attn_backward(dy, seg, attn_w, vec, kept, hook, cut):
     xb, saved, n1, r1, yb, act, slope, n2, r2 = kept
     dz1 = normal_back(dy, n1, r1, vec["g0"])
     small = {"g0": total_rows(dy * n1), "s0": total_rows(dy), "pb": total_rows(dz1), "heads": []}
@@ -741,12 +741,14 @@
     da = dz1.astype(BF)
     dx = dz1
     blocks = []
-    for lo, hi in ((0, TENSORS - 1), (TENSORS - 1, TENSORS)):
+    for lo, hi in ((0, cut), (cut, TENSORS)):
+        if lo == hi:
+            continue
         parts = [(*attn_w[j], *saved[j]) for j in range(lo, hi)]
         dx, sums, grads = attend_blocks_backward(vec["cols"], da, xb, dx, parts, seg)
         small["heads"] += sums
         blocks += grads
-        if lo == 0:
+        if hi < TENSORS:
             da, dx = hook("three", (da, dx))
     return dx, blocks, small
 
@@ -927,19 +929,23 @@
             return ffn1.swapped(value)
         return ffn1.crossed(value)
 
-    du, blocks, more = attn_backward(dy, seg, attn_w1, vec1, kept1, during_attn1)
+    du, blocks, more = attn_backward(dy, seg, attn_w1, vec1, kept1, during_attn1, TENSORS)
     small1.update(more)
+    du = ffn1.crossed(du)
     du = attn1.start(du, blocks)
-    du = ffn1.summed(du)
-    ffn_total1 = lax.psum(ffn1.total, "dp")
     grad_skip = to_places(jnp.where(first_place, 0.0, du).astype(BF))
 
     seed = backbone_cot.astype(F32) * valid + jnp.where(first_place, du, 0.0)
     seed = seed + jnp.dot(picker.T, dcls, precision=HIGHEST)
 
+    finished = {}
+
     def during_ffn0(name, value):
         if name == "seeded":
-            return attn1.swapped(value)
+            value = attn1.swapped(value)
+            value = ffn1.summed(value)
+            finished["ffn"] = lax.psum(ffn1.total, "dp")
+            return value
         return attn1.crossed(value)
 
     dy, blocks, small0 = ffn_backward(seed, ffn_w0, vec0, kept0, during_ffn0, 2)
@@ -947,9 +953,8 @@
     dy = ffn0.start(dy, blocks)
     dy = attn1.summed(dy)
 
-    dy, ffn_total1, late = tie(dy, ffn_total1, attn1.total)
+    dy, ffn_total1, late = tie(dy, finished["ffn"], attn1.total)
     attn_total1 = lax.psum(late, "dp")
-    finished = {}
 
     def during_attn0(name, value):
         if name == "normed":
@@ -958,7 +963,7 @@
         value, finished["attn"] = tie(value, attn_total1)
         return value
 
-    dx, attn_blocks, more = attn_backward(dy, seg, attn_w0, vec0, kept0, during_attn0)
+    dx, attn_blocks, more = attn_backward(dy, seg, attn_w0, vec0, kept0, during_attn0, TENSORS - 1)
     small0.update(more)
     attn_total1 = finished["attn"]
     grad_input = to_places(dx.astype(BF))

time: 632 us -> 619 us (0.979)
  waiting for transfers between devices: 52.2 us -> 35.5 us
  other arithmetic: 103 us -> 112 us
    all_to_all x4, waiting for transfers between devices: 17.5 us -> 2.53 us  [to_rows(): lax.all_to_all(values, 'tensor', split_axis=0, concat_axis=0, tiled=True)]
    pallas_call x7 -> x6, Pallas kernels: 135 us -> 130 us  [streamed_blocks(): pl.pallas_call(kernel, name=name, out_shape=(jax.ShapeDtypeStruct(total.s...]
    unnamed x357 -> x389, local copies, waits for them, and re-layouts: 33.2 us -> 33 us
  transfers between devices with their start and end apart: 60 -> 60, of which waited for: 9 -> 7; matrix products, arithmetic and copies ran while one was open for 21% -> 23% of each run, Pallas kernels for 33% -> 33%
where the time goes in v12:
time: 619 us; the launch traced here: 610 us
  Pallas kernels  276 us (45%)
  other arithmetic  112 us (18%)
  starting transfers between devices  67.9 us (11%)
  local copies, waits for them, and re-layouts  53 us (9%)
  matrix products  45.3 us (7%)
  waiting for transfers between devices  35.5 us (6%)
  between operations  20.4 us (3%)
    pallas_call x6, Pallas kernels, streamed_blocks(): pl.pallas_call(kernel, name=name, out_shape=(jax.ShapeDtypeStruct(total.s...  130 us
    pallas_call x1, Pallas kernels, last_sums(): pl.pallas_call(body, name='last_sums', out_shape=tuple((jax.ShapeDtypeStr...  73.7 us
    pallas_call x8, Pallas kernels, attend_forward(): pl.pallas_call(body, name='attend_forward', out_shape=(narrow, narrow, na...  55.1 us
    dot_general x18, matrix products, mm(): lax.dot_general(a, b, (((ca,), (cb,)), ((), ())), preferred_element_type=...  41.3 us
    convert_element_type x18, other arithmetic, plus(): return total.astype(BF)  38.7 us
    ppermute x50, starting transfers between devices, send(): return lax.ppermute(values, PLANE, plane_pairs(kind))  35.1 us
    unnamed x389, local copies, waits for them, and re-layouts  33 us
    all_to_all x4, starting transfers between devices, to_rows(): lax.all_to_all(values, 'tensor', split_axis=0, concat_axis=0, tiled=True)  17.5 us
  transfers between devices with their start and end apart: 60, of which 7 were waited for; matrix products, arithmetic and copies ran while one was open for 23% of the time, Pallas kernels for 33%

profile of v12, /device:TPU:0, one launch (start us, length us, event | category | flops | bytes accessed | tf_op | source)
XLA Modules:
  0.0 610.0 jit_solution(8022102278769548545)
XLA Ops:
  7.2 5.2 all-to-all-start
  12.4 2.5 slice_bitcast_fusion.4
  18.2 3.9 slice_bitcast_fusion
  28.0 6.4 %attend_forward.8 = (bf16[512,192]{1,0:T(8,128)(2,1)S(1)}, bf16[512,192]{1,0:T(8,128)(2,1)S(1)}, bf16[512,192]{1,0:T(8,128)(2,1)S(1)}, bf16[512,192]{1,0:T(8,128...) custom-call(bf16[512,768]{1,0:T(8,128)(2,1)S(1)} %bitcast.170, ...), custom_call_target="tpu_custom_call" | custom-call | flops 1048576 | bytes 1024 | tf_op jit(solution)/shard_map/attend_forward/pallas_call | solution.py:357
  40.4 7.5 %attend_forward.9 = (bf16[512,192]{1,0:T(8,128)(2,1)S(1)}, bf16[512,192]{1,0:T(8,128)(2,1)S(1)}, bf16[512,192]{1,0:T(8,128)(2,1)S(1)}, bf16[512,192]{1,0:T(8,128...) custom-call(bf16[512,768]{1,0:T(8,128)(2,1)S(1)} %bitcast.171, ...), custom_call_target="tpu_custom_call" | custom-call | flops 1048576 | bytes 1024 | tf_op jit(solution)/shard_map/attend_forward/pallas_call | solution.py:357
  50.7 6.4 %attend_forward.10 = (bf16[512,192]{1,0:T(8,128)(2,1)S(1)}, bf16[512,192]{1,0:T(8,128)(2,1)S(1)}, bf16[512,192]{1,0:T(8,128)(2,1)S(1)}, bf16[512,192]{1,0:T(8,12...) custom-call(bf16[512,768]{1,0:T(8,128)(2,1)S(1)} %bitcast.172, ...), custom_call_target="tpu_custom_call" | custom-call | flops 1048576 | bytes 1024 | tf_op jit(solution)/shard_map/attend_forward/pallas_call | solution.py:357
  61.1 6.6 %attend_forward.11 = (bf16[512,192]{1,0:T(8,128)(2,1)S(1)}, bf16[512,192]{1,0:T(8,128)(2,1)S(1)}, bf16[512,192]{1,0:T(8,128)(2,1)S(1)}, bf16[512,192]{1,0:T(8,12...) custom-call(bf16[512,768]{1,0:T(8,128)(2,1)S(1)} %bitcast.173, ...), custom_call_target="tpu_custom_call" | custom-call | flops 1048576 | bytes 1024 | tf_op jit(solution)/shard_map/attend_forward/pallas_call | solution.py:357
  68.4 2.7 broadcast_select_fusion.7
  74.6 3.6 fusion.24
  80.6 3.4 fusion.29
  86.4 3.4 fusion.34
  99.5 4.2 all-to-all-start.2
  116.3 2.5 all-to-all-done.2
  118.9 3.1 fusion.49
  122.0 7.9 %attend_forward.12 = (bf16[512,192]{1,0:T(8,128)(2,1)S(1)}, bf16[512,192]{1,0:T(8,128)(2,1)S(1)}, bf16[512,192]{1,0:T(8,128)(2,1)S(1)}, bf16[512,192]{1,0:T(8,12...) custom-call(bf16[512,768]{1,0:T(8,128)(2,1)S(1)} %get-tuple-element.474.refs_0_.refs_1_, ...), custom_call_target="tpu_custom_call" | custom-call | flops 1048576 | bytes 1024 | tf_op jit(solution)/shard_map/attend_forward/pallas_call | solution.py:357
  132.4 4.4 all-to-all-start.1
  138.3 7.6 %attend_forward.13 = (bf16[512,192]{1,0:T(8,128)(2,1)S(1)}, bf16[512,192]{1,0:T(8,128)(2,1)S(1)}, bf16[512,192]{1,0:T(8,128)(2,1)S(1)}, bf16[512,192]{1,0:T(8,12...) custom-call(bf16[512,768]{1,0:T(8,128)(2,1)S(1)} %get-tuple-element.474.refs_0_.refs_1_, ...), custom_call_target="tpu_custom_call" | custom-call | flops 1048576 | bytes 1024 | tf_op jit(solution)/shard_map/attend_forward/pallas_call | solution.py:357
  152.3 6.4 %attend_forward.14 = (bf16[512,192]{1,0:T(8,128)(2,1)S(1)}, bf16[512,192]{1,0:T(8,128)(2,1)S(1)}, bf16[512,192]{1,0:T(8,128)(2,1)S(1)}, bf16[512,192]{1,0:T(8,12...) custom-call(bf16[512,768]{1,0:T(8,128)(2,1)S(1)} %get-tuple-element.474.refs_0_.refs_1_, ...), custom_call_target="tpu_custom_call" | custom-call | flops 1048576 | bytes 1024 | tf_op jit(solution)/shard_map/attend_forward/pallas_call | solution.py:357
  164.5 6.4 %attend_forward.15 = (bf16[512,192]{1,0:T(8,128)(2,1)S(1)}, bf16[512,192]{1,0:T(8,128)(2,1)S(1)}, bf16[512,192]{1,0:T(8,128)(2,1)S(1)}, bf16[512,192]{1,0:T(8,12...) custom-call(bf16[512,768]{1,0:T(8,128)(2,1)S(1)} %get-tuple-element.474.refs_0_.refs_1_, ...), custom_call_target="tpu_custom_call" | custom-call | flops 1048576 | bytes 1024 | tf_op jit(solution)/shard_map/attend_forward/pallas_call | solution.py:357
  171.6 2.8 broadcast_select_fusion.4
  179.0 3.6 fusion.4
  184.2 3.4 fusion.9
  190.0 3.4 fusion.14
  195.3 3.9 all-to-all-start.5
  202.4 17.3 %gather_anchors.1 = bf16[4,8,4,768]{3,2,1,0:T(4,128)(2,1)} custom-call(bf16[4,768]{1,0:T(4,128)(2,1)} %convolution_convert_fusion.refs_0_), custom_call_target="tpu_custom_call" | custom-call | tf_op jit(solution)/shard_map/gather_anchors/pallas_call | solution.py:423
  231.8 3.5 all-to-all-start.3
  238.3 18.9 %ffn_backward.3 = (f32[512,768]{1,0:T(8,128)}, f32[1,768]{1,0:T(1,128)}, f32[1,768]{1,0:T(1,128)}, f32[1,768]{1,0:T(1,128)}, f32[1,768]{1,0:T(1,128)}, /*index=5...) custom-call(bf16[512,768]{1,0:T(8,128)(2,1)} %convert_element_type.5, ...), custom_call_target="tpu_custom_call" | custom-call | flops 1048576 | bytes 1024 | tf_op jit(solution)/shard_map/ffn_backward/pallas_call | solution.py:304
  259.4 3.2 multiply_reduce_fusion.1
  274.3 4.2 all-to-all-start.4
  281.9 40.3 %attend_backward.3 = (f32[512,768]{1,0:T(8,128)}, f32[1,384]{1,0:T(1,128)}, f32[1,384]{1,0:T(1,128)}, f32[1,384]{1,0:T(1,128)}, f32[1,384]{1,0:T(1,128)}, /*inde...) custom-call(bf16[512,768]{1,0:T(8,128)(2,1)} %convert_element_type.5, ...), custom_call_target="tpu_custom_call" | custom-call | flops 1048576 | bytes 1024 | tf_op jit(solution)/shard_map/attend_backward/pallas_call | solution.py:304
  322.2 3.0 add_convert_fusion.7
  325.8 3.7 multiply_reduce_fusion.2
  333.4 2.7 add_convert_fusion.14
  343.1 4.6 collective-permute-done.33
  350.3 3.5 all-to-all-start.6
  354.9 12.9 %ffn_backward.4 = (f32[512,768]{1,0:T(8,128)}, f32[1,768]{1,0:T(1,128)}, f32[1,768]{1,0:T(1,128)}, bf16[768,768]{1,0:T(8,128)(2,1)}, bf16[768,768]{1,0:T(8,128)(...) custom-call(bf16[512,768]{1,0:T(8,128)(2,1)} %convert_element_type.544.refs_0_, bf16[512,768]{1,0:T(8,128)(2,1)} %copy-done.94, ...), custom_call_target="tpu_custom_call" | custom-call | flops 1048576 | bytes 1024 | tf_op jit(solution)/shard_map/ffn_backward/pallas_call | solution.py:304
  371.9 12.8 %ffn_backward.5 = (f32[512,768]{1,0:T(8,128)}, f32[1,768]{1,0:T(1,128)}, f32[1,768]{1,0:T(1,128)}, bf16[768,768]{1,0:T(8,128)(2,1)}, bf16[768,768]{1,0:T(8,128)(...) custom-call(bf16[512,768]{1,0:T(8,128)(2,1)} %convert_element_type.544.refs_0_, bf16[512,768]{1,0:T(8,128)(2,1)} %copy-done.94, ...), custom_call_target="tpu_custom_call" | custom-call | flops 1048576 | bytes 1024 | tf_op jit(solution)/shard_map/ffn_backward/pallas_call | solution.py:304
  388.4 16.7 %all-reduce.5.cloned.1.call-done = bf16[768,768]{1,0:T(8,128)(2,1)} async-done(((bf16[768,768]{1,0:T(8,128)(2,1)}), bf16[768,768]{1,0:T(8,128)(2,1)}) %all-reduce.5.cloned.1.call-update) | async-done | bytes 1179664 | tf_op jit(solution)/shard_map/psum | solution.py:947
  408.6 2.7 add_convert_fusion.2
  411.4 2.7 add_convert_fusion.3
  414.1 2.7 add_convert_fusion.4
  416.8 2.6 add_convert_fusion.5
  423.4 31.3 %attend_backward.4 = (f32[512,768]{1,0:T(8,128)}, f32[1,384]{1,0:T(1,128)}, f32[1,384]{1,0:T(1,128)}, f32[1,384]{1,0:T(1,128)}, bf16[384,768]{1,0:T(8,128)(2,1)}...) custom-call(bf16[512,768]{1,0:T(8,128)(2,1)} %convert_element_type.5, ...), custom_call_target="tpu_custom_call" | custom-call | flops 1048576 | bytes 1024 | tf_op jit(solution)/shard_map/attend_backward/pallas_call | solution.py:304
  454.7 2.9 add_convert_fusion.1
  459.8 13.9 %attend_backward.5 = (f32[512,768]{1,0:T(8,128)}, f32[1,384]{1,0:T(1,128)}, bf16[384,768]{1,0:T(8,128)(2,1)}, bf16[384,768]{1,0:T(8,128)(2,1)}) custom-call(bf16[512,768]{1,0:T(8,128)(2,1)} %convert_element_type.569.refs_0_, bf16[512,768]{1,0:T(8,128)(2,1)} %bitcast.175, s32[512,1]{1,0:T(8,128)} %copy-done.5, s32[1,512]{1,0:T(1,128)} %copy-done.33, ...), custom_call_target="tpu_custom_call" | custom-call | flops 1048576 | bytes 1024 | tf_op jit(solution)/shard_map/attend_backward/pallas_call | solution.py:304
  476.2 3.9 all-to-all-start.7
  484.3 7.5 %all-to-all-done.7 = bf16[4,128,768]{2,1,0:T(8,128)(2,1)S(1)} async-done(((bf16[4,128,768]{2,1,0:T(8,128)(2,1)}), bf16[4,128,768]{2,1,0:T(8,128)(2,1)S(1)}, u32[]{:S(2)}, u32[]{:S(2)}) %all-to-all-start.7) | async-done | bytes 786464 | tf_op jit(solution)/shard_map/all_to_all | solution.py:683
  496.4 73.7 %last_sums.1 = (bf16[2,4,96,768]{3,2,1,0:T(8,128)(2,1)S(1)}, bf16[2,4,96,768]{3,2,1,0:T(8,128)(2,1)S(1)}, bf16[2,4,48,768]{3,2,1,0:T(8,128)(2,1)S(1)}, bf16[2,4,...) custom-call(bf16[2,4,96,768]{3,2,1,0:T(8,128)(2,1)S(1)} %bitcast.176, bf16[2,4,48,768]{3,2,1,0:T(8,128)(2,1)S(1)} %bitcast.177, ...), custom_call_target="tpu_custom_call" | custom-call | tf_op jit(solution)/shard_map/last_sums/pallas_call | solution.py:653
  (657 shorter events, 187.5 us)
Async XLA Ops:
  7.2 20.6 %all-to-all-start = ((bf16[4,128,768]{2,1,0:T(8,128)(2,1)}), bf16[4,128,768]{2,1,0:T(8,128)(2,1)S(1)}, u32[]{:S(2)}, u32[]{:S(2)}) async-start(bf16[4,128,768]{2,1,0:T(8,128)(2,1)} %bitcast.198), calls=%async_computation | async-start | bytes 1572864 | tf_op jit(solution)/shard_map/all_to_all | solution.py:676
  16.0 18.4 %collective-permute-start = (bf16[400,768]{1,0:T(8,128)(2,1)S(1)}, bf16[400,768]{1,0:T(8,128)(2,1)S(1)}, u32[]{:S(2)}, u32[]{:S(2)}) collective-permute-start(bf16[400,768]{1,0:T(8,128)(2,1)S(1)} %pad_maximum_fusion.2.refs_1_.refs_5_), channel_id=1, source_target_pairs={{0,1},{1,0},{2,3},{3,2},{4,6},{5,7},{6,4},{7,5},{8,9},{9,8},{10,11... | collective-permute-start | bytes 1843208 | tf_op jit(solution)/shard_map/ppermute | solution.py:62
  18.1 18.4 %collective-permute-start.1 = (bf16[400,768]{1,0:T(8,128)(2,1)S(1)}, bf16[400,768]{1,0:T(8,128)(2,1)}, u32[]{:S(2)}, u32[]{:S(2)}) collective-permute-start(bf16[400,768]{1,0:T(8,128)(2,1)S(1)} %fusion.54.refs_2_.refs_6_), channel_id=1, source_target_pairs={{0,1},{1,0},{2,3},{3,2},{4,6},{5,7},{6,4},{7,5},{8,9},{9,8},{10,11... | collective-permute-start | bytes 1843208 | tf_op jit(solution)/shard_map/ppermute | solution.py:62
  22.1 45.7 %collective-permute-start.6 = (bf16[768,768]{1,0:T(8,128)(2,1)}, bf16[768,768]{1,0:T(8,128)(2,1)}, u32[]{:S(2)}, u32[]{:S(2)}) collective-permute-start(bf16[768,768]{1,0:T(8,128)(2,1)} %get-tuple-element.228.refs_5_), channel_id=1, source_target_pairs={{0,1},{1,0},{2,3},{3,2},{4,6},{5,7},{6,4},{7,5},{8,9},{9,8},{10,11... | collective-permute-start | bytes 3538952 | tf_op jit(solution)/shard_map/ppermute | solution.py:62
  24.1 44.3 %collective-permute-start.7 = (bf16[768,768]{1,0:T(8,128)(2,1)}, bf16[768,768]{1,0:T(8,128)(2,1)}, u32[]{:S(2)}, u32[]{:S(2)}) collective-permute-start(bf16[768,768]{1,0:T(8,128)(2,1)} %get-tuple-element.229.refs_6_), channel_id=1, source_target_pairs={{0,1},{1,0},{2,3},{3,2},{4,6},{5,7},{6,4},{7,5},{8,9},{9,8},{10,11... | collective-permute-start | bytes 3538952 | tf_op jit(solution)/shard_map/ppermute | solution.py:62
  36.5 14.2 %collective-permute-start.2 = (bf16[400,768]{1,0:T(8,128)(2,1)S(1)}, bf16[400,768]{1,0:T(8,128)(2,1)S(1)}, u32[]{:S(2)}, u32[]{:S(2)}) collective-permute-start(bf16[400,768]{1,0:T(8,128)(2,1)S(1)} %collective-permute-done.refs_1_.refs_12_), channel_id=1, source_target_pairs={{0,4},{1,5},{2,6},{3,7},{4,0},{5,1},{6,2},{7,3},{8,12},{9,13},{10,... | collective-permute-start | bytes 1843208 | tf_op jit(solution)/shard_map/ppermute | solution.py:62
  36.6 14.1 %collective-permute-start.3 = (bf16[400,768]{1,0:T(8,128)(2,1)}, bf16[400,768]{1,0:T(8,128)(2,1)S(1)}, u32[]{:S(2)}, u32[]{:S(2)}) collective-permute-start(bf16[400,768]{1,0:T(8,128)(2,1)} %collective-permute-done.1.refs_2_.refs_13_), channel_id=1, source_target_pairs={{0,4},{1,5},{2,6},{3,7},{4,0},{5,1},{6,2},{7,3},{8,12},{9,13},{10,... | collective-permute-start | bytes 1843208 | tf_op jit(solution)/shard_map/ppermute | solution.py:62
  37.1 20.1 %collective-permute-start.4 = (bf16[400,768]{1,0:T(8,128)(2,1)S(1)}, bf16[400,768]{1,0:T(8,128)(2,1)S(1)}, u32[]{:S(2)}, u32[]{:S(2)}) collective-permute-start(bf16[400,768]{1,0:T(8,128)(2,1)S(1)} %broadcast_select_fusion.10), channel_id=1, source_target_pairs={{0,2},{1,3},{2,0},{3,1},{4,5},{5,4},{6,7},{7,6},{8,10},{9,11},{10,... | collective-permute-start | bytes 1843208 | tf_op jit(solution)/shard_map/ppermute | solution.py:62
  58.9 27.5 %collective-permute-start.8 = (bf16[384,768]{1,0:T(8,128)(2,1)}, bf16[384,768]{1,0:T(8,128)(2,1)}, u32[]{:S(2)}, u32[]{:S(2)}) collective-permute-start(bf16[384,768]{1,0:T(8,128)(2,1)} %bitcast.16.refs_1_.refs_5_), channel_id=1, source_target_pairs={{0,1},{1,0},{2,3},{3,2},{4,6},{5,7},{6,4},{7,5},{8,9},{9,8},{10,11... | collective-permute-start | bytes 1769480 | tf_op jit(solution)/shard_map/ppermute | solution.py:62
  59.4 26.9 %collective-permute-start.9 = (bf16[384,768]{1,0:T(8,128)(2,1)}, bf16[384,768]{1,0:T(8,128)(2,1)}, u32[]{:S(2)}, u32[]{:S(2)}) collective-permute-start(bf16[384,768]{1,0:T(8,128)(2,1)} %pad_maximum_fusion.3.refs_2_.refs_6_), channel_id=1, source_target_pairs={{0,1},{1,0},{2,3},{3,2},{4,6},{5,7},{6,4},{7,5},{8,9},{9,8},{10,11... | collective-permute-start | bytes 1769480 | tf_op jit(solution)/shard_map/ppermute | solution.py:62
  68.3 18.0 %collective-permute-start.10 = (bf16[768,768]{1,0:T(8,128)(2,1)}, bf16[768,768]{1,0:T(8,128)(2,1)}, u32[]{:S(2)}, u32[]{:S(2)}) collective-permute-start(bf16[768,768]{1,0:T(8,128)(2,1)} %collective-permute-done.6.refs_9_), channel_id=1, source_target_pairs={{0,4},{1,5},{2,6},{3,7},{4,0},{5,1},{6,2},{7,3},{8,12},{9,13},{10,... | collective-permute-start | bytes 3538952 | tf_op jit(solution)/shard_map/ppermute | solution.py:62
  71.2 18.6 %collective-permute-start.11 = (bf16[768,768]{1,0:T(8,128)(2,1)}, bf16[768,768]{1,0:T(8,128)(2,1)}, u32[]{:S(2)}, u32[]{:S(2)}) collective-permute-start(bf16[768,768]{1,0:T(8,128)(2,1)} %collective-permute-done.7.refs_10_), channel_id=1, source_target_pairs={{0,4},{1,5},{2,6},{3,7},{4,0},{5,1},{6,2},{7,3},{8,12},{9,13},{10,... | collective-permute-start | bytes 3538952 | tf_op jit(solution)/shard_map/ppermute | solution.py:62
  72.8 21.2 %collective-permute-start.12 = (bf16[768,768]{1,0:T(8,128)(2,1)S(1)}, bf16[768,768]{1,0:T(8,128)(2,1)}, u32[]{:S(2)}, u32[]{:S(2)}) collective-permute-start(bf16[768,768]{1,0:T(8,128)(2,1)S(1)} %copy-done.129), channel_id=1, source_target_pairs={{0,2},{1,3},{2,0},{3,1},{4,5},{5,4},{6,7},{7,6},{8,10},{9,11},{10,... | collective-permute-start | bytes 3538952 | tf_op jit(solution)/shard_map/ppermute | solution.py:62
  95.4 55.2 %collective-permute-start.16 = (bf16[384,768]{1,0:T(8,128)(2,1)}, bf16[384,768]{1,0:T(8,128)(2,1)S(1)}, u32[]{:S(2)}, u32[]{:S(2)}) collective-permute-start(bf16[384,768]{1,0:T(8,128)(2,1)} %collective-permute-done.8.refs_1_.refs_12_), channel_id=1, source_target_pairs={{0,4},{1,5},{2,6},{3,7},{4,0},{5,1},{6,2},{7,3},{8,12},{9,13},{10,... | collective-permute-start | bytes 1769480 | tf_op jit(solution)/shard_map/ppermute | solution.py:62
  96.0 54.6 %collective-permute-start.17 = (bf16[384,768]{1,0:T(8,128)(2,1)}, bf16[384,768]{1,0:T(8,128)(2,1)S(1)}, u32[]{:S(2)}, u32[]{:S(2)}) collective-permute-start(bf16[384,768]{1,0:T(8,128)(2,1)} %collective-permute-done.9.refs_2_.refs_13_), channel_id=1, source_target_pairs={{0,4},{1,5},{2,6},{3,7},{4,0},{5,1},{6,2},{7,3},{8,12},{9,13},{10,... | collective-permute-start | bytes 1769480 | tf_op jit(solution)/shard_map/ppermute | solution.py:62
  98.0 52.6 %collective-permute-start.14 = (bf16[384,768]{1,0:T(8,128)(2,1)}, bf16[384,768]{1,0:T(8,128)(2,1)}, u32[]{:S(2)}, u32[]{:S(2)}) collective-permute-start(bf16[384,768]{1,0:T(8,128)(2,1)} %broadcast_select_fusion.13), channel_id=1, source_target_pairs={{0,2},{1,3},{2,0},{3,1},{4,5},{5,4},{6,7},{7,6},{8,10},{9,11},{10,... | collective-permute-start | bytes 1769480 | tf_op jit(solution)/shard_map/ppermute | solution.py:62
  99.5 19.3 %all-to-all-start.2 = ((bf16[4,128,768]{2,1,0:T(8,128)(2,1)}), bf16[4,128,768]{2,1,0:T(8,128)(2,1)}, u32[]{:S(2)}, u32[]{:S(2)}) async-start(bf16[4,128,768]{2,1,0:T(8,128)(2,1)} %bitcast), calls=%async_computation.2 | async-start | bytes 1572864 | tf_op jit(solution)/shard_map/all_to_all | solution.py:676
  103.7 67.3 %collective-permute-start.18 = (bf16[768,768]{1,0:T(8,128)(2,1)}, bf16[768,768]{1,0:T(8,128)(2,1)}, u32[]{:S(2)}, u32[]{:S(2)}) collective-permute-start(bf16[768,768]{1,0:T(8,128)(2,1)} %get-tuple-element.251.refs_5_), channel_id=1, source_target_pairs={{0,1},{1,0},{2,3},{3,2},{4,6},{5,7},{6,4},{7,5},{8,9},{9,8},{10,11... | collective-permute-start | bytes 3538952 | tf_op jit(solution)/shard_map/ppermute | solution.py:62
  106.3 64.7 %collective-permute-start.19 = (bf16[768,768]{1,0:T(8,128)(2,1)}, bf16[768,768]{1,0:T(8,128)(2,1)}, u32[]{:S(2)}, u32[]{:S(2)}) collective-permute-start(bf16[768,768]{1,0:T(8,128)(2,1)} %get-tuple-element.252.refs_6_), channel_id=1, source_target_pairs={{0,1},{1,0},{2,3},{3,2},{4,6},{5,7},{6,4},{7,5},{8,9},{9,8},{10,11... | collective-permute-start | bytes 3538952 | tf_op jit(solution)/shard_map/ppermute | solution.py:62
  132.4 30.2 %all-to-all-start.1 = ((bf16[4,128,768]{2,1,0:T(8,128)(2,1)}), bf16[4,128,768]{2,1,0:T(8,128)(2,1)}, u32[]{:S(2)}, u32[]{:S(2)}) async-start(bf16[4,128,768]{2,1,0:T(8,128)(2,1)} %bitcast.190), calls=%async_computation.1 | async-start | bytes 1572864 | tf_op jit(solution)/shard_map/all_to_all | solution.py:683
  171.0 19.0 %collective-permute-start.20 = (bf16[768,768]{1,0:T(8,128)(2,1)}, bf16[768,768]{1,0:T(8,128)(2,1)}, u32[]{:S(2)}, u32[]{:S(2)}) collective-permute-start(bf16[768,768]{1,0:T(8,128)(2,1)} %collective-permute-done.18.refs_9_), channel_id=1, source_target_pairs={{0,4},{1,5},{2,6},{3,7},{4,0},{5,1},{6,2},{7,3},{8,12},{9,13},{10,... | collective-permute-start | bytes 3538952 | tf_op jit(solution)/shard_map/ppermute | solution.py:62
  174.4 19.0 %collective-permute-start.21 = (bf16[768,768]{1,0:T(8,128)(2,1)}, bf16[768,768]{1,0:T(8,128)(2,1)S(1)}, u32[]{:S(2)}, u32[]{:S(2)}) collective-permute-start(bf16[768,768]{1,0:T(8,128)(2,1)} %collective-permute-done.19.refs_10_), channel_id=1, source_target_pairs={{0,4},{1,5},{2,6},{3,7},{4,0},{5,1},{6,2},{7,3},{8,12},{9,13},{10,... | collective-permute-start | bytes 3538952 | tf_op jit(solution)/shard_map/ppermute | solution.py:62
  175.0 19.7 %collective-permute-start.22 = (bf16[768,768]{1,0:T(8,128)(2,1)}, bf16[768,768]{1,0:T(8,128)(2,1)}, u32[]{:S(2)}, u32[]{:S(2)}) collective-permute-start(bf16[768,768]{1,0:T(8,128)(2,1)} %broadcast_select_fusion.4), channel_id=1, source_target_pairs={{0,2},{1,3},{2,0},{3,1},{4,5},{5,4},{6,7},{7,6},{8,10},{9,11},{10,... | collective-permute-start | bytes 3538952 | tf_op jit(solution)/shard_map/ppermute | solution.py:62
  194.7 27.0 %collective-permute-start.23 = (bf16[768,768]{1,0:T(8,128)(2,1)}, bf16[768,768]{1,0:T(8,128)(2,1)}, u32[]{:S(2)}, u32[]{:S(2)}) collective-permute-start(bf16[768,768]{1,0:T(8,128)(2,1)} %collective-permute-done.22), channel_id=1, source_target_pairs={{0,4},{1,5},{2,6},{3,7},{4,0},{5,1},{6,2},{7,3},{8,12},{9,13},{10,... | collective-permute-start | bytes 3538952 | tf_op jit(solution)/shard_map/ppermute | solution.py:62
  195.3 25.4 %all-to-all-start.5 = ((bf16[4,128,768]{2,1,0:T(8,128)(2,1)}), bf16[4,128,768]{2,1,0:T(8,128)(2,1)S(1)}, u32[]{:S(2)}, u32[]{:S(2)}) async-start(bf16[4,128,768]{2,1,0:T(8,128)(2,1)} %bitcast.199), calls=%async_computation.5 | async-start | bytes 1572864 | tf_op jit(solution)/shard_map/all_to_all | solution.py:676
  231.8 25.5 %all-to-all-start.3 = ((bf16[4,128,768]{2,1,0:T(8,128)(2,1)}), bf16[4,128,768]{2,1,0:T(8,128)(2,1)S(1)}, u32[]{:S(2)}, u32[]{:S(2)}) async-start(bf16[4,128,768]{2,1,0:T(8,128)(2,1)} %bitcast.29), calls=%async_computation.3 | async-start | bytes 1572864 | tf_op jit(solution)/shard_map/all_to_all | solution.py:683
  270.8 51.4 %collective-permute-start.28 = (bf16[768,768]{1,0:T(8,128)(2,1)}, bf16[768,768]{1,0:T(8,128)(2,1)}, u32[]{:S(2)}, u32[]{:S(2)}) collective-permute-start(bf16[768,768]{1,0:T(8,128)(2,1)} %add_convert_fusion.9), channel_id=1, source_target_pairs={{0,2},{1,3},{2,0},{3,1},{4,5},{5,4},{6,7},{7,6},{8,10},{9,11},{10,... | collective-permute-start | bytes 3538952 | tf_op jit(solution)/shard_map/ppermute | solution.py:62
  274.3 51.5 %all-to-all-start.4 = ((bf16[4,128,768]{2,1,0:T(8,128)(2,1)}), bf16[4,128,768]{2,1,0:T(8,128)(2,1)}, u32[]{:S(2)}, u32[]{:S(2)}) async-start(bf16[4,128,768]{2,1,0:T(8,128)(2,1)} %bitcast.200), calls=%async_computation.4 | async-start | bytes 1572864 | tf_op jit(solution)/shard_map/all_to_all | solution.py:676
  278.5 126.6 %all-reduce.5.cloned.1.call-start = ((), (), s32[]{:S(2)}) async-start(), calls=%async_computation.8 | async-start | bytes 2359296 | tf_op jit(solution)/shard_map/psum | solution.py:947
  278.5 51.9 %collective-permute-start.34 = (bf16[768,768]{1,0:T(8,128)(2,1)}, bf16[768,768]{1,0:T(8,128)(2,1)}, u32[]{:S(2)}, u32[]{:S(2)}) collective-permute-start(bf16[768,768]{1,0:T(8,128)(2,1)} %add_convert_fusion.11), channel_id=1, source_target_pairs={{0,1},{1,0},{2,3},{3,2},{4,6},{5,7},{6,4},{7,5},{8,9},{9,8},{10,11... | collective-permute-start | bytes 3538952 | tf_op jit(solution)/shard_map/ppermute | solution.py:62
  329.4 18.3 %collective-permute-start.33 = (bf16[768,768]{1,0:T(8,128)(2,1)}, bf16[768,768]{1,0:T(8,128)(2,1)S(1)}, u32[]{:S(2)}, u32[]{:S(2)}) collective-permute-start(bf16[768,768]{1,0:T(8,128)(2,1)} %add_convert_fusion.7), channel_id=1, source_target_pairs={{0,1},{1,0},{2,3},{3,2},{4,6},{5,7},{6,4},{7,5},{8,9},{9,8},{10,11... | collective-permute-start | bytes 3538952 | tf_op jit(solution)/shard_map/ppermute | solution.py:62
  330.5 17.2 %collective-permute-start.35 = (bf16[768,768]{1,0:T(8,128)(2,1)}, bf16[768,768]{1,0:T(8,128)(2,1)S(1)}, u32[]{:S(2)}, u32[]{:S(2)}) collective-permute-start(bf16[768,768]{1,0:T(8,128)(2,1)} %collective-permute-done.34), channel_id=1, source_target_pairs={{0,4},{1,5},{2,6},{3,7},{4,0},{5,1},{6,2},{7,3},{8,12},{9,13},{10,... | collective-permute-start | bytes 3538952 | tf_op jit(solution)/shard_map/ppermute | solution.py:62
  341.3 26.4 %collective-permute-start.36 = (bf16[384,768]{1,0:T(8,128)(2,1)}, bf16[384,768]{1,0:T(8,128)(2,1)}, u32[]{:S(2)}, u32[]{:S(2)}) collective-permute-start(bf16[384,768]{1,0:T(8,128)(2,1)} %add_convert_fusion.15), channel_id=1, source_target_pairs={{0,2},{1,3},{2,0},{3,1},{4,5},{5,4},{6,7},{7,6},{8,10},{9,11},{10,... | collective-permute-start | bytes 1769480 | tf_op jit(solution)/shard_map/ppermute | solution.py:62
  341.8 30.0 %collective-permute-start.38 = (bf16[384,768]{1,0:T(8,128)(2,1)}, bf16[384,768]{1,0:T(8,128)(2,1)}, u32[]{:S(2)}, u32[]{:S(2)}) collective-permute-start(bf16[384,768]{1,0:T(8,128)(2,1)} %add_convert_fusion.17), channel_id=1, source_target_pairs={{0,1},{1,0},{2,3},{3,2},{4,6},{5,7},{6,4},{7,5},{8,9},{9,8},{10,11... | collective-permute-start | bytes 1769480 | tf_op jit(solution)/shard_map/ppermute | solution.py:62
  350.3 34.4 %all-to-all-start.6 = ((bf16[4,128,768]{2,1,0:T(8,128)(2,1)}), bf16[4,128,768]{2,1,0:T(8,128)(2,1)S(1)}, u32[]{:S(2)}, u32[]{:S(2)}) async-start(bf16[4,128,768]{2,1,0:T(8,128)(2,1)} %bitcast.40), calls=%async_computation.6 | async-start | bytes 1572864 | tf_op jit(solution)/shard_map/all_to_all | solution.py:683
  353.8 105.9 %all-reduce.7.cloned.1.call-start = ((), (), s32[]{:S(2)}) async-start(), calls=%async_computation.9 | async-start | bytes 1179648 | tf_op jit(solution)/shard_map/psum | solution.py:957
  369.9 15.9 %collective-permute-start.37 = (bf16[384,768]{1,0:T(8,128)(2,1)}, bf16[384,768]{1,0:T(8,128)(2,1)}, u32[]{:S(2)}, u32[]{:S(2)}) collective-permute-start(bf16[384,768]{1,0:T(8,128)(2,1)} %add_convert_fusion.13), channel_id=1, source_target_pairs={{0,1},{1,0},{2,3},{3,2},{4,6},{5,7},{6,4},{7,5},{8,9},{9,8},{10,11... | collective-permute-start | bytes 1769480 | tf_op jit(solution)/shard_map/ppermute | solution.py:62
  384.7 23.2 %collective-permute-start.43 = (bf16[768,768]{1,0:T(8,128)(2,1)}, bf16[768,768]{1,0:T(8,128)(2,1)}, u32[]{:S(2)}, u32[]{:S(2)}) collective-permute-start(bf16[768,768]{1,0:T(8,128)(2,1)} %get-tuple-element.345), channel_id=1, source_target_pairs={{0,4},{1,5},{2,6},{3,7},{4,0},{5,1},{6,2},{7,3},{8,12},{9,13},{10,... | collective-permute-start | bytes 3538952 | tf_op jit(solution)/shard_map/ppermute | solution.py:62
  385.3 26.1 %collective-permute-start.42 = (bf16[768,768]{1,0:T(8,128)(2,1)}, bf16[768,768]{1,0:T(8,128)(2,1)}, u32[]{:S(2)}, u32[]{:S(2)}) collective-permute-start(bf16[768,768]{1,0:T(8,128)(2,1)} %get-tuple-element.343), channel_id=1, source_target_pairs={{0,4},{1,5},{2,6},{3,7},{4,0},{5,1},{6,2},{7,3},{8,12},{9,13},{10,... | collective-permute-start | bytes 3538952 | tf_op jit(solution)/shard_map/ppermute | solution.py:62
  385.4 28.7 %collective-permute-start.41 = (bf16[768,768]{1,0:T(8,128)(2,1)}, bf16[768,768]{1,0:T(8,128)(2,1)}, u32[]{:S(2)}, u32[]{:S(2)}) collective-permute-start(bf16[768,768]{1,0:T(8,128)(2,1)} %get-tuple-element.341), channel_id=1, source_target_pairs={{0,4},{1,5},{2,6},{3,7},{4,0},{5,1},{6,2},{7,3},{8,12},{9,13},{10,... | collective-permute-start | bytes 3538952 | tf_op jit(solution)/shard_map/ppermute | solution.py:62
  385.8 31.0 %collective-permute-start.40 = (bf16[768,768]{1,0:T(8,128)(2,1)}, bf16[768,768]{1,0:T(8,128)(2,1)}, u32[]{:S(2)}, u32[]{:S(2)}) collective-permute-start(bf16[768,768]{1,0:T(8,128)(2,1)} %get-tuple-element.339), channel_id=1, source_target_pairs={{0,4},{1,5},{2,6},{3,7},{4,0},{5,1},{6,2},{7,3},{8,12},{9,13},{10,... | collective-permute-start | bytes 3538952 | tf_op jit(solution)/shard_map/ppermute | solution.py:62
  419.4 35.3 %collective-permute-start.44 = (bf16[768,768]{1,0:T(8,128)(2,1)}, bf16[768,768]{1,0:T(8,128)(2,1)}, u32[]{:S(2)}, u32[]{:S(2)}) collective-permute-start(bf16[768,768]{1,0:T(8,128)(2,1)} %add_convert_fusion.3), channel_id=1, source_target_pairs={{0,2},{1,3},{2,0},{3,1},{4,5},{5,4},{6,7},{7,6},{8,10},{9,11},{10,... | collective-permute-start | bytes 3538952 | tf_op jit(solution)/shard_map/ppermute | solution.py:62
  420.9 37.3 %collective-permute-start.46 = (bf16[768,768]{1,0:T(8,128)(2,1)}, bf16[768,768]{1,0:T(8,128)(2,1)}, u32[]{:S(2)}, u32[]{:S(2)}) collective-permute-start(bf16[768,768]{1,0:T(8,128)(2,1)} %add_convert_fusion.5), channel_id=1, source_target_pairs={{0,1},{1,0},{2,3},{3,2},{4,6},{5,7},{6,4},{7,5},{8,9},{9,8},{10,11... | collective-permute-start | bytes 3538952 | tf_op jit(solution)/shard_map/ppermute | solution.py:62
  457.6 34.4 %collective-permute-start.45 = (bf16[768,768]{1,0:T(8,128)(2,1)}, bf16[768,768]{1,0:T(8,128)(2,1)}, u32[]{:S(2)}, u32[]{:S(2)}) collective-permute-start(bf16[768,768]{1,0:T(8,128)(2,1)} %add_convert_fusion.1), channel_id=1, source_target_pairs={{0,1},{1,0},{2,3},{3,2},{4,6},{5,7},{6,4},{7,5},{8,9},{9,8},{10,11... | collective-permute-start | bytes 3538952 | tf_op jit(solution)/shard_map/ppermute | solution.py:62
  458.2 33.8 %collective-permute-start.47 = (bf16[768,768]{1,0:T(8,128)(2,1)}, bf16[768,768]{1,0:T(8,128)(2,1)}, u32[]{:S(2)}, u32[]{:S(2)}) collective-permute-start(bf16[768,768]{1,0:T(8,128)(2,1)} %collective-permute-done.46), channel_id=1, source_target_pairs={{0,4},{1,5},{2,6},{3,7},{4,0},{5,1},{6,2},{7,3},{8,12},{9,13},{10,... | collective-permute-start | bytes 3538952 | tf_op jit(solution)/shard_map/ppermute | solution.py:62
  459.7 34.8 %collective-permute-start.48 = (bf16[768,768]{1,0:T(8,128)(2,1)}, bf16[768,768]{1,0:T(8,128)(2,1)}, u32[]{:S(2)}, u32[]{:S(2)}) collective-permute-start(bf16[768,768]{1,0:T(8,128)(2,1)} %all-reduce.5.cloned.1.call-done), channel_id=1, source_target_pairs={{0,4},{1,5},{2,6},{3,7},{4,0},{5,1},{6,2},{7,3},{8,12},{9,13},{10,... | collective-permute-start | bytes 3538952 | tf_op jit(solution)/shard_map/ppermute | solution.py:62
  476.2 15.5 %all-to-all-start.7 = ((bf16[4,128,768]{2,1,0:T(8,128)(2,1)}), bf16[4,128,768]{2,1,0:T(8,128)(2,1)S(1)}, u32[]{:S(2)}, u32[]{:S(2)}) async-start(bf16[4,128,768]{2,1,0:T(8,128)(2,1)} %bitcast.41), calls=%async_computation.7 | async-start | bytes 1572864 | tf_op jit(solution)/shard_map/all_to_all | solution.py:683
  480.3 14.2 %collective-permute-start.49 = (bf16[384,768]{1,0:T(8,128)(2,1)S(1)}, bf16[384,768]{1,0:T(8,128)(2,1)S(1)}, u32[]{:S(2)}, u32[]{:S(2)}) collective-permute-start(bf16[384,768]{1,0:T(8,128)(2,1)S(1)} %copy-done.143), channel_id=1, source_target_pairs={{0,4},{1,5},{2,6},{3,7},{4,0},{5,1},{6,2},{7,3},{8,12},{9,13},{10,... | collective-permute-start | bytes 1769480 | tf_op jit(solution)/shard_map/ppermute | solution.py:62
  (203 other events, 1633.0 us)
Sparse Core Ops, SparseCore 0:
  349.4 55.6 all-reduce.4
  422.5 37.1 all-reduce.6
